TPU v7x, 256 devices: a whole 4x4x8 slice. The times are simulated.
256 devices in a mesh: section: 64 (over y, z, core), dp: 4 (over x).
Axes of the slice: x: 4, y: 4, z: 8, core: 2. Of those that a mesh axis runs over, the one named last changes fastest.
Arguments:
- tokens: bfloat16 [1024, 8192], P(('section', 'dp')), may hold values from -6 to 6
- norm_gain: float32 [8192], replicated, may hold values from 0.1 to 1.9
- gate_weight: bfloat16 [8192, 28672], P('dp', 'section'), may hold values from -0.0625 to 0.0625
- up_weight: bfloat16 [8192, 28672], P('dp', 'section'), may hold values from -0.0625 to 0.0625
- down_weight: bfloat16 [28672, 8192], P('section', 'dp'), may hold values from -0.03125 to 0.03125
Outputs:
- mixed: bfloat16 [1024, 8192], P(('section', 'dp'))
All inputs are finite; a program needn't handle non-finite values.
Results may differ from a plain program's by a relative error of at most 0.0046.
Values may be sent and summed in bfloat16 or wider, within the bound.
No kernel may reach another device: no remote copies, remote signals or barrier semaphores. Data moves between devices by JAX's collectives and lax.ppermute only.
A program may use at most 128 MiB of HBM per device.

v0:
```python
import jax
import jax.numpy as jnp
from jax import lax
from jax.sharding import PartitionSpec as P


def local(tokens, norm_gain, gate_weight, up_weight, down_weight):
    widened = tokens.astype(jnp.float32)
    mean_square = jnp.mean(widened * widened, axis=1, keepdims=True)
    normed_own = (widened * lax.rsqrt(mean_square + 1e-05) * norm_gain[None, :]).astype(
        jnp.bfloat16
    )
    normed = lax.all_gather(normed_own, "section", axis=0, tiled=True)
    full_gate, full_up, full_down = (
        lax.all_gather(gate_weight, "dp", axis=0, tiled=True),
        lax.all_gather(up_weight, "dp", axis=0, tiled=True),
        lax.all_gather(down_weight, "dp", axis=1, tiled=True),
    )
    gate_part = jnp.dot(normed, full_gate, preferred_element_type=jnp.float32)
    up_part = jnp.dot(normed, full_up, preferred_element_type=jnp.float32)
    hidden = (jax.nn.silu(gate_part) * up_part).astype(jnp.bfloat16)
    summed = lax.psum_scatter(
        jnp.dot(hidden, full_down, preferred_element_type=jnp.float32),
        "section",
        scatter_dimension=0,
        tiled=True,
    )
    return (widened + summed).astype(jnp.bfloat16)


def solution(mesh):
    return jax.shard_map(
        local,
        mesh=mesh,
        in_specs=(
            P(("section", "dp"), None),
            P(),
            P("dp", "section"),
            P("dp", "section"),
            P("section", "dp"),
        ),
        out_specs=P(("section", "dp"), None),
        check_vma=False,
    )
```

profile of v0, /device:TPU:1, one launch (start us, length us, event | category | flops | bytes accessed | tf_op | source)
XLA Modules:
  0.0 549.9 jit_solution(717318222495191974)
XLA Ops:
  6.5 0.0 all-gather.12.cloned.1.call-start
  6.5 1.0 fusion.1
  7.6 1.6 fusion.5
  9.1 0.0 all-gather.12.cloned.1.call-update
  9.2 0.0 all-gather.6.cloned.1.call-start
  9.2 0.7 all-gather.6.cloned.1.call-update
  9.9 0.0 all-gather.8.cloned.1.call-start
  10.0 0.7 all-gather.8.cloned.1.call-update
  10.7 0.0 all-gather.10.cloned.1.call-start
  10.7 0.5 all-gather.10.cloned.1.call-update
  11.2 0.0 all-reduce.3.cloned.1.call-start
  11.3 82.2 %all-gather.12.cloned.1.call-done = bf16[64,4,8192]{2,1,0:T(4,128)(2,1)} async-done(((bf16[1,4,8192]{2,1,0:T(4,128)(2,1)}), bf16[64,4,8192]{2,1,0:T(4,128)(2,1)}) %all-gather.12.cloned.1.call-update) | async-done | bytes 4194320 | tf_op jit(solution)/shard_map/all_gather | solution.py:13
  93.4 6.9 %reshape.10 = bf16[256,8192]{1,0:T(8,128)(2,1)} reshape(bf16[64,4,8192]{2,1,0:T(4,128)(2,1)} %all-gather.12.cloned.1.call-done) | data formatting | bytes 8388608
  100.3 68.7 %all-gather.6.cloned.1.call-done = bf16[8192,448]{0,1:T(8,128)(2,1)} async-done(((bf16[2048,448]{0,1:T(8,128)(2,1)}), bf16[8192,448]{0,1:T(8,128)(2,1)}) %all-gather.6.cloned.1.call-update) | async-done | bytes 7340048 | tf_op jit(solution)/shard_map/all_gather | solution.py:15
  169.0 6.4 %fusion.6 = f32[256,448]{0,1:T(8,128)S(1)} fusion(bf16[256,8192]{1,0:T(8,128)(2,1)} %reshape.10, bf16[8192,448]{0,1:T(8,128)(2,1)} %all-gather.6.cloned.1.call-done), kind=kOutput, calls=%fused_computation.11 | convolution fusion | flops 1879048192 | bytes 11993088 | tf_op jit(solution)/shard_map/dot_general | solution.py:19
  175.5 73.2 %all-gather.8.cloned.1.call-done = bf16[8192,448]{0,1:T(8,128)(2,1)} async-done(((bf16[2048,448]{0,1:T(8,128)(2,1)}), bf16[8192,448]{0,1:T(8,128)(2,1)}) %all-gather.8.cloned.1.call-update) | async-done | bytes 7340048 | tf_op jit(solution)/shard_map/all_gather | solution.py:16
  248.7 6.5 %fusion = bf16[256,448]{0,1:T(8,128)(2,1)S(1)} fusion(bf16[256,8192]{1,0:T(8,128)(2,1)} %reshape.10, bf16[8192,448]{0,1:T(8,128)(2,1)} %all-gather.8.cloned.1.call-done, f32[256,448]{0,1:T(8,128)S(1)} %fusion.6), kind=kOutput, calls=%fused_computation.1 | convolution fusion | flops 1879736320 | bytes 12222464 | tf_op jit(solution)/shard_map/dot_general | solution.py:20
  255.1 73.0 %all-gather.10.cloned.1.call-done = bf16[448,8192]{1,0:T(8,128)(2,1)} async-done(((bf16[448,2048]{1,0:T(8,128)(2,1)}), bf16[448,8192]{1,0:T(8,128)(2,1)}) %all-gather.10.cloned.1.call-update) | async-done | bytes 7340048 | tf_op jit(solution)/shard_map/all_gather | solution.py:17
  328.2 8.8 %fusion.7 = f32[256,8192]{1,0:T(8,128)} fusion(bf16[256,448]{0,1:T(8,128)(2,1)S(1)} %fusion, bf16[448,8192]{1,0:T(8,128)(2,1)} %all-gather.10.cloned.1.call-done), kind=kOutput, calls=%fused_computation.12 | convolution fusion | flops 1879048192 | bytes 15958016 | tf_op jit(solution)/shard_map/dot_general | solution.py:23
  336.9 0.0 copy-start.1
  336.9 0.0 copy-start
  336.9 0.0 all-reduce.3.cloned.1.call-update
  337.0 0.6 copy-done.1
  337.6 0.6 dynamic-slice
  338.8 202.9 %all-reduce.3.cloned.1.call-done = f32[256,8192]{1,0:T(8,128)} async-done(((f32[256,8192]{1,0:T(8,128)}), f32[256,8192]{1,0:T(8,128)}) %all-reduce.3.cloned.1.call-update) | async-done | bytes 8388624
  541.7 0.0 copy-done
  541.7 1.6 fusion.4
  (1 shorter events, 0.0 us)
Async XLA Ops:
  6.5 86.9 %all-gather.12.cloned.1.call-start = ((), (), s32[]{:S(2)}) async-start(), calls=%async_computation.3 | async-start | bytes 4259840 | tf_op jit(solution)/shard_map/all_gather | solution.py:13
  9.2 159.9 %all-gather.6.cloned.1.call-start = ((), (), s32[]{:S(2)}) async-start(), calls=%async_computation | async-start | bytes 9175040 | tf_op jit(solution)/shard_map/all_gather | solution.py:15
  9.9 238.7 %all-gather.8.cloned.1.call-start = ((), (), s32[]{:S(2)}) async-start(), calls=%async_computation.1 | async-start | bytes 9175040 | tf_op jit(solution)/shard_map/all_gather | solution.py:16
  10.7 317.5 %all-gather.10.cloned.1.call-start = ((), (), s32[]{:S(2)}) async-start(), calls=%async_computation.2 | async-start | bytes 9175040 | tf_op jit(solution)/shard_map/all_gather | solution.py:17
  11.2 530.5 %all-reduce.3.cloned.1.call-start = ((), (), s32[]{:S(2)}) async-start(), calls=%async_computation.4 | async-start | bytes 16777216
  336.9 0.7 copy-start.1
  336.9 204.8 %copy-start = (bf16[4,8192]{1,0:T(4,128)(2,1)S(1)}, bf16[4,8192]{1,0:T(4,128)(2,1)}, u32[]{:S(2)}) copy-start(bf16[4,8192]{1,0:T(4,128)(2,1)} %param.5) | copy-start | bytes 196612
Sparse Core Ops, SparseCore 0:
  10.1 83.2 all-gather.11
  95.2 73.7 all-gather.5
  170.8 77.7 all-gather.7
  250.3 77.7 all-gather.9
  337.1 204.6 all-reduce.2
where the time goes:
time: 551 us; the launch traced here: 550 us
  waiting for transfers between devices  502 us (91%)
  matrix products  21.7 us (4%)
  between operations  13.8 us (3%)
  local copies, waits for them, and re-layouts  8.13 us (1%)
    unnamed x6, waiting for transfers between devices  205 us
    all_gather x1, waiting for transfers between devices, local(): normed = lax.all_gather(normed_own, 'section', axis=0, tiled=True)  82.2 us
    all_gather x1, waiting for transfers between devices, local(): lax.all_gather(up_weight, 'dp', axis=0, tiled=True)  73.2 us
    all_gather x1, waiting for transfers between devices, local(): lax.all_gather(down_weight, 'dp', axis=1, tiled=True)  73 us
    all_gather x1, waiting for transfers between devices, local(): lax.all_gather(gate_weight, 'dp', axis=0, tiled=True)  68.7 us
  transfers between devices with their start and end apart: 5, of which 5 were waited for; matrix products, arithmetic and copies ran while one was open for 4% of the time, Pallas kernels for 0%

commit v1 on v0

v1 whole, which is shorter than its diff:
```python
import jax
import jax.numpy as jnp
from jax import lax
from jax.sharding import Mesh
from jax.sharding import PartitionSpec as P

F32, BF16 = jnp.float32, jnp.bfloat16
SIZES = {"y": 4, "z": 8, "c": 2, "x": 4}


def shift(value, axis, step):
    n = SIZES[axis]
    return lax.ppermute(value, axis, [(i, (i + step) % n) for i in range(n)])


def rolled(blocks, start):
    return lax.dynamic_slice_in_dim(
        jnp.concatenate([blocks, blocks], axis=0), start, blocks.shape[0], axis=0
    )


def gather_z(block):
    half = block.shape[0] // 2
    from_low, from_high = [block], [block]
    for _ in range(3):
        from_low.append(shift(from_low[-1], "z", 1))
        from_high.append(shift(from_high[-1], "z", -1))
    far = jnp.concatenate(
        [shift(from_low[3][:half], "z", 1), shift(from_high[3][half:], "z", -1)], axis=0
    )
    return from_low + [far] + from_high[:0:-1]


def scatter_z(sums):
    pieces = [sums[:, 4 * k : 4 * k + 4] for k in range(8)]
    total = pieces[0]
    for k in (4, 3, 5, 2, 6, 1, 7):
        total = total + shift(pieces[k].astype(BF16), "z", -k).astype(F32)
    return total


def local(tokens, norm_gain, gate_weight, up_weight, down_weight):
    x = lax.axis_index("x")
    gate_t, up_t = gate_weight.T, up_weight.T
    first = jnp.concatenate(
        [gate_t, shift(gate_t, "c", 1), up_t, shift(up_t, "c", 1)], axis=0
    )
    second = jnp.concatenate([down_weight, shift(down_weight, "c", 1)], axis=0)
    hidden_units = second.shape[0]
    rows, width = tokens.shape
    part = width // 4

    wide = tokens.astype(F32)
    mean_square = jnp.mean(wide * wide, axis=1, keepdims=True)
    normed = (wide * lax.rsqrt(mean_square + 1e-05) * norm_gain[None, :]).astype(BF16)
    blocks = rolled(normed.reshape(rows, 4, part).transpose(1, 0, 2), x)
    own = jnp.stack(
        [blocks[0]] + [shift(blocks[4 - r], "x", 4 - r) for r in (1, 2, 3)]
    )

    plane = jnp.concatenate(gather_z(own), axis=1)
    planes = [plane] + [shift(plane, "y", k) for k in (1, 2, 3)]

    many = jnp.concatenate(planes, axis=1)
    partial = lax.dot_general(
        many.reshape(-1, part), first, (((1,), (1,)), ((), ())), preferred_element_type=F32
    ).reshape(4, -1, 2 * hidden_units)
    both = partial[0]
    for k in (2, 1, 3):
        both = both + shift(partial[k].astype(BF16), "x", k).astype(F32)
    hidden = (jax.nn.silu(both[:, :hidden_units]) * both[:, hidden_units:]).astype(BF16)
    all_hidden = jnp.concatenate([hidden] + [shift(hidden, "x", -k) for k in (1, 2, 3)], axis=0)
    down = lax.dot_general(
        all_hidden, second, (((1,), (0,)), ((), ())), preferred_element_type=F32
    ).reshape(4, 4, -1, part)

    summed = down[:, 0]
    for k in (2, 1, 3):
        summed = summed + shift(down[:, k].astype(BF16), "y", -k).astype(F32)
    mine = scatter_z(summed)
    columns = jnp.stack([mine[0]] + [shift(mine[4 - r], "x", 4 - r) for r in (1, 2, 3)])
    ordered = rolled(columns, (4 - x) % 4).transpose(1, 0, 2).reshape(rows, width)
    return (wide + ordered).astype(BF16)


def solution(mesh):
    torus = Mesh(mesh.devices.reshape(4, 8, 2, 4), ("y", "z", "c", "x"))
    section = ("y", "z", "c")
    return jax.shard_map(
        local,
        mesh=torus,
        in_specs=(
            P(section + ("x",), None),
            P(),
            P("x", section),
            P("x", section),
            P(section, "x"),
        ),
        out_specs=P(section + ("x",), None),
        check_vma=False,
    )
```

time: 551 us -> 172 us (0.31)
  the two profiles are of different devices: /device:TPU:1 before, /device:TPU:38 now
where the time goes in v1:
time: 172 us; the launch traced here: 171 us
  waiting for transfers between devices  97.2 us (57%)
  starting transfers between devices  52.2 us (30%)
  matrix products  12.6 us (7%)
  local copies, waits for them, and re-layouts  5.24 us (3%)
  other arithmetic  3.91 us (2%)
    ppermute x36, waiting for transfers between devices, shift(): return lax.ppermute(value, axis, [(i, (i + step) % n) for i in range(n)])  97.2 us
    ppermute x36, starting transfers between devices, shift(): return lax.ppermute(value, axis, [(i, (i + step) % n) for i in range(n)])  52.2 us
    dot_general x1, matrix products, local(): lax.dot_general(many.reshape(-1, part), first, (((1,), (1,)), ((), ())),...  8.74 us
    concatenate x1, local copies, waits for them, and re-layouts, local(): many = jnp.concatenate(planes, axis=1)  4.24 us
    dot_general x1, matrix products, local(): lax.dot_general(all_hidden, second, (((1,), (0,)), ((), ())), preferred_e...  3.83 us
  transfers between devices with their start and end apart: 36, of which 23 were waited for; matrix products, arithmetic and copies ran while one was open for 9% of the time, Pallas kernels for 0%

profile of v1, /device:TPU:38, one launch (start us, length us, event | category | flops | bytes accessed | tf_op | source)
XLA Modules:
  0.0 171.4 jit_solution(6136211945968261864)
XLA Ops:
  4.1 3.2 %collective-permute-start.2 = (bf16[4,2048]{1,0:T(4,128)(2,1)S(1)}, bf16[4,2048]{1,0:T(4,128)(2,1)S(1)}, u32[]{:S(2)}, u32[]{:S(2)}) collective-permute-start(bf16[4,2048]{1,0:T(4,128)(2,1)S(1)} %get-tuple-element.27), channel_id=1, source_target_pairs={{0,1},{1,2},{2,3},{3,0},{4,5},{5,6},{6,7},{7,4},{8,9},{9,10},{10,1... | collective-permute-start | bytes 49160 | tf_op jit(solution)/shard_map/ppermute | solution.py:13
  9.1 2.0 %collective-permute-start.3 = (bf16[4,4,2048]{2,1,0:T(4,128)(2,1)S(1)}, bf16[4,4,2048]{2,1,0:T(4,128)(2,1)S(1)}, u32[]{:S(2)}, u32[]{:S(2)}) collective-permute-start(bf16[4,4,2048]{2,1,0:T(4,128)(2,1)S(1)} %pad_maximum_fusion), channel_id=1, source_target_pairs={{0,8},{8,16},{16,24},{24,32},{32,40},{40,48},{48,56},{56,0},{1,9},... | collective-permute-start | bytes 196616 | tf_op jit(solution)/shard_map/ppermute | solution.py:13
  11.2 2.2 %collective-permute-done.3 = bf16[4,4,2048]{2,1,0:T(4,128)(2,1)S(1)} collective-permute-done((bf16[4,4,2048]{2,1,0:T(4,128)(2,1)S(1)}, bf16[4,4,2048]{2,1,0:T(4,128)(2,1)S(1)}, u32[]{:S(2)}, u32[]{:S(2)}) %collective-permute-start.3) | collective-permute-done | bytes 65568 | tf_op jit(solution)/shard_map/ppermute | solution.py:13
  13.5 1.9 %collective-permute-start.4 = (bf16[4,4,2048]{2,1,0:T(4,128)(2,1)S(1)}, bf16[4,4,2048]{2,1,0:T(4,128)(2,1)S(1)}, u32[]{:S(2)}, u32[]{:S(2)}) collective-permute-start(bf16[4,4,2048]{2,1,0:T(4,128)(2,1)S(1)} %collective-permute-done.3), channel_id=1, source_target_pairs={{0,8},{8,16},{16,24},{24,32},{32,40},{40,48},{48,56},{56,0},{1,9},... | collective-permute-start | bytes 196616 | tf_op jit(solution)/shard_map/ppermute | solution.py:13
  15.4 2.0 %collective-permute-start.8 = (bf16[4,4,2048]{2,1,0:T(4,128)(2,1)S(1)}, bf16[4,4,2048]{2,1,0:T(4,128)(2,1)S(1)}, u32[]{:S(2)}, u32[]{:S(2)}) collective-permute-start(bf16[4,4,2048]{2,1,0:T(4,128)(2,1)S(1)} %collective-permute-done.7), channel_id=1, source_target_pairs={{0,56},{8,0},{16,8},{24,16},{32,24},{40,32},{48,40},{56,48},{1,57}... | collective-permute-start | bytes 196616 | tf_op jit(solution)/shard_map/ppermute | solution.py:13
  17.4 2.2 %collective-permute-done.4 = bf16[4,4,2048]{2,1,0:T(4,128)(2,1)S(1)} collective-permute-done((bf16[4,4,2048]{2,1,0:T(4,128)(2,1)S(1)}, bf16[4,4,2048]{2,1,0:T(4,128)(2,1)S(1)}, u32[]{:S(2)}, u32[]{:S(2)}) %collective-permute-start.4) | collective-permute-done | bytes 65568 | tf_op jit(solution)/shard_map/ppermute | solution.py:13
  20.7 2.3 %collective-permute-start.9 = (bf16[4,4,2048]{2,1,0:T(4,128)(2,1)S(1)}, bf16[4,4,2048]{2,1,0:T(4,128)(2,1)S(1)}, u32[]{:S(2)}, u32[]{:S(2)}) collective-permute-start(bf16[4,4,2048]{2,1,0:T(4,128)(2,1)S(1)} %collective-permute-done.8), channel_id=1, source_target_pairs={{0,56},{8,0},{16,8},{24,16},{32,24},{40,32},{48,40},{56,48},{1,57}... | collective-permute-start | bytes 196616 | tf_op jit(solution)/shard_map/ppermute | solution.py:13
  23.0 2.3 %collective-permute-done.5 = bf16[4,4,2048]{2,1,0:T(4,128)(2,1)S(1)} collective-permute-done((bf16[4,4,2048]{2,1,0:T(4,128)(2,1)S(1)}, bf16[4,4,2048]{2,1,0:T(4,128)(2,1)S(1)}, u32[]{:S(2)}, u32[]{:S(2)}) %collective-permute-start.5) | collective-permute-done | bytes 65568 | tf_op jit(solution)/shard_map/ppermute | solution.py:13
  26.5 2.4 %collective-permute-start.10 = (bf16[2,4,2048]{2,1,0:T(4,128)(2,1)S(1)}, bf16[2,4,2048]{2,1,0:T(4,128)(2,1)S(1)}, u32[]{:S(2)}, u32[]{:S(2)}) collective-permute-start(bf16[2,4,2048]{2,1,0:T(4,128)(2,1)S(1)} %slice.134), channel_id=1, source_target_pairs={{0,56},{8,0},{16,8},{24,16},{32,24},{40,32},{48,40},{56,48},{1,57}... | collective-permute-start | bytes 98312 | tf_op jit(solution)/shard_map/ppermute | solution.py:13
  32.1 3.1 %collective-permute-start.13 = (bf16[4,32,2048]{2,1,0:T(8,128)(2,1)S(1)}, bf16[4,32,2048]{2,1,0:T(8,128)(2,1)S(1)}, u32[]{:S(2)}, u32[]{:S(2)}) collective-permute-start(bf16[4,32,2048]{2,1,0:T(8,128)(2,1)S(1)} %concatenate.28), channel_id=1, source_target_pairs={{0,192},{64,0},{128,64},{192,128},{1,193},{65,1},{129,65},{193,129... | collective-permute-start | bytes 1572872 | tf_op jit(solution)/shard_map/ppermute | solution.py:13
  36.8 15.8 %collective-permute-done.13 = bf16[4,32,2048]{2,1,0:T(8,128)(2,1)S(1)} collective-permute-done((bf16[4,32,2048]{2,1,0:T(8,128)(2,1)S(1)}, bf16[4,32,2048]{2,1,0:T(8,128)(2,1)S(1)}, u32[]{:S(2)}, u32[]{:S(2)}) %collective-permute-start.13) | collective-permute-done | bytes 524320 | tf_op jit(solution)/shard_map/ppermute | solution.py:13
  52.7 3.8 %collective-permute-done.11 = bf16[4,32,2048]{2,1,0:T(8,128)(2,1)} collective-permute-done((bf16[4,32,2048]{2,1,0:T(8,128)(2,1)S(1)}, bf16[4,32,2048]{2,1,0:T(8,128)(2,1)}, u32[]{:S(2)}, u32[]{:S(2)}) %collective-permute-start.11) | collective-permute-done | bytes 524320 | tf_op jit(solution)/shard_map/ppermute | solution.py:13
  56.5 4.2 %concatenate.29 = bf16[4,128,2048]{2,1,0:T(8,128)(2,1)S(1)} concatenate(bf16[4,4,2048]{2,1,0:T(4,128)(2,1)S(1)} %pad_maximum_fusion, bf16[4,4,2048]{2,1,0:T(4,128)(2,1)S(1)} %collective-permute-done.3, bf16[4,4,2048]{2,1,0:T(4,128)(2,1)} %copy-done.1, bf16[4,4,2048]{2,1,0:T(4,128)(2,1)S(1)} %collective-permute-done.5, bf16[4,4,2048]{2,1,0:T(4,128)(2,1)S(1)} %constant_dynamic-update-slice_fusion, ...), dimensions={1} | concatenate | bytes 4194304 | tf_op jit(solution)/shard_map/concatenate | solution.py:64
  60.7 8.7 %fusion.43 = (bf16[512,1792]{1,0:T(8,128)(2,1)S(1)}, f32[512,1792]{1,0:T(8,128)S(1)}) fusion(bf16[512,2048]{1,0:T(8,128)(2,1)S(1)} %bitcast.58, bf16[448,2048]{1,0:T(8,128)(2,1)} %collective-permute-done.15, bf16[448,2048]{1,0:T(8,128)(2,1)} %bitcast.65, bf16[448,2048]{1,0:T(8,128)(2,1)} %collective-permute-done.14, bf16[448,2048]{1,0:T(8,128)(2,1)} %bitcast.67), kind=kOutput, calls=%fused_computation.73 | convolution fusion | flops 3788374016 | bytes 14942208 | tf_op jit(solution)/shard_map/dot_general | solution.py:65
  69.6 2.3 %collective-permute-start.16 = (bf16[128,1792]{1,0:T(8,128)(2,1)S(1)}, bf16[128,1792]{1,0:T(8,128)(2,1)S(1)}, u32[]{:S(2)}, u32[]{:S(2)}) collective-permute-start(bf16[128,1792]{1,0:T(8,128)(2,1)S(1)} %get-tuple-element.10), channel_id=1, source_target_pairs={{0,2},{1,3},{2,0},{3,1},{4,6},{5,7},{6,4},{7,5},{8,10},{9,11},{10,... | collective-permute-start | bytes 1376264 | tf_op jit(solution)/shard_map/ppermute | solution.py:13
  75.2 9.5 %collective-permute-done.16 = bf16[128,1792]{1,0:T(8,128)(2,1)S(1)} collective-permute-done((bf16[128,1792]{1,0:T(8,128)(2,1)S(1)}, bf16[128,1792]{1,0:T(8,128)(2,1)S(1)}, u32[]{:S(2)}, u32[]{:S(2)}) %collective-permute-start.16) | collective-permute-done | bytes 458784 | tf_op jit(solution)/shard_map/ppermute | solution.py:13
  84.7 7.8 %collective-permute-done.18 = bf16[128,1792]{1,0:T(8,128)(2,1)S(1)} collective-permute-done((bf16[128,1792]{1,0:T(8,128)(2,1)S(1)}, bf16[128,1792]{1,0:T(8,128)(2,1)S(1)}, u32[]{:S(2)}, u32[]{:S(2)}) %collective-permute-start.18) | collective-permute-done | bytes 458784 | tf_op jit(solution)/shard_map/ppermute | solution.py:13
  93.1 2.7 %collective-permute-start.21 = (bf16[128,896]{1,0:T(8,128)(2,1)S(1)}, bf16[128,896]{1,0:T(8,128)(2,1)S(1)}, u32[]{:S(2)}, u32[]{:S(2)}) collective-permute-start(bf16[128,896]{1,0:T(8,128)(2,1)S(1)} %fusion.24), channel_id=1, source_target_pairs={{0,1},{1,2},{2,3},{3,0},{4,5},{5,6},{6,7},{7,4},{8,9},{9,10},{10,1... | collective-permute-start | bytes 688136 | tf_op jit(solution)/shard_map/ppermute | solution.py:13
  96.7 9.0 %collective-permute-done.21 = bf16[128,896]{1,0:T(8,128)(2,1)S(1)} collective-permute-done((bf16[128,896]{1,0:T(8,128)(2,1)S(1)}, bf16[128,896]{1,0:T(8,128)(2,1)S(1)}, u32[]{:S(2)}, u32[]{:S(2)}) %collective-permute-start.21) | collective-permute-done | bytes 229408 | tf_op jit(solution)/shard_map/ppermute | solution.py:13
  105.8 3.4 %collective-permute-done.19 = bf16[128,896]{1,0:T(8,128)(2,1)S(1)} collective-permute-done((bf16[128,896]{1,0:T(8,128)(2,1)S(1)}, bf16[128,896]{1,0:T(8,128)(2,1)S(1)}, u32[]{:S(2)}, u32[]{:S(2)}) %collective-permute-start.19) | collective-permute-done | bytes 229408 | tf_op jit(solution)/shard_map/ppermute | solution.py:13
  109.2 3.8 %fusion.8 = f32[512,2048]{1,0:T(8,128)S(1)} fusion(bf16[448,2048]{1,0:T(8,128)(2,1)} %collective-permute-done.22, bf16[448,2048]{1,0:T(8,128)(2,1)S(1)} %copy-done.3, bf16[128,896]{1,0:T(8,128)(2,1)S(1)} %collective-permute-done.21, bf16[128,896]{1,0:T(8,128)(2,1)S(1)} %collective-permute-done.20, bf16[128,896]{1,0:T(8,128)(2,1)S(1)} %collective-permute-done.19, ...), kind=kOutput, calls=%fused_computation.8 | convolution fusion | flops 1890058240 | bytes 8781824 | tf_op jit(solution)/shard_map/dot_general | solution.py:73
  113.6 2.3 %collective-permute-start.25 = (bf16[4,32,2048]{2,1,0:T(8,128)(2,1)S(1)}, bf16[4,32,2048]{2,1,0:T(8,128)(2,1)S(1)}, u32[]{:S(2)}, u32[]{:S(2)}) collective-permute-start(bf16[4,32,2048]{2,1,0:T(8,128)(2,1)S(1)} %get-tuple-element.8), channel_id=1, source_target_pairs={{0,64},{64,128},{128,192},{192,0},{1,65},{65,129},{129,193},{193,1... | collective-permute-start | bytes 1572872 | tf_op jit(solution)/shard_map/ppermute | solution.py:13
  116.9 13.0 %collective-permute-done.23 = bf16[4,32,2048]{2,1,0:T(8,128)(2,1)S(1)} collective-permute-done((bf16[4,32,2048]{2,1,0:T(8,128)(2,1)S(1)}, bf16[4,32,2048]{2,1,0:T(8,128)(2,1)S(1)}, u32[]{:S(2)}, u32[]{:S(2)}) %collective-permute-start.23) | collective-permute-done | bytes 524320 | tf_op jit(solution)/shard_map/ppermute | solution.py:13
  129.8 9.7 %collective-permute-done.25 = bf16[4,32,2048]{2,1,0:T(8,128)(2,1)S(1)} collective-permute-done((bf16[4,32,2048]{2,1,0:T(8,128)(2,1)S(1)}, bf16[4,32,2048]{2,1,0:T(8,128)(2,1)S(1)}, u32[]{:S(2)}, u32[]{:S(2)}) %collective-permute-start.25) | collective-permute-done | bytes 524320 | tf_op jit(solution)/shard_map/ppermute | solution.py:13
  140.2 3.3 %collective-permute-start.26 = (bf16[4,4,2048]{2,1,0:T(4,128)(2,1)S(1)}, bf16[4,4,2048]{2,1,0:T(4,128)(2,1)S(1)}, u32[]{:S(2)}, u32[]{:S(2)}) collective-permute-start(bf16[4,4,2048]{2,1,0:T(4,128)(2,1)S(1)} %get-tuple-element.13), channel_id=1, source_target_pairs={{0,32},{8,40},{16,48},{24,56},{32,0},{40,8},{48,16},{56,24},{1,33}... | collective-permute-start | bytes 196616 | tf_op jit(solution)/shard_map/ppermute | solution.py:13
  143.5 2.1 %collective-permute-start.31 = (bf16[4,4,2048]{2,1,0:T(4,128)(2,1)S(1)}, bf16[4,4,2048]{2,1,0:T(4,128)(2,1)S(1)}, u32[]{:S(2)}, u32[]{:S(2)}) collective-permute-start(bf16[4,4,2048]{2,1,0:T(4,128)(2,1)S(1)} %get-tuple-element.15), channel_id=1, source_target_pairs={{0,56},{8,0},{16,8},{24,16},{32,24},{40,32},{48,40},{56,48},{1,57}... | collective-permute-start | bytes 196616 | tf_op jit(solution)/shard_map/ppermute | solution.py:13
  145.6 2.5 %collective-permute-start.30 = (bf16[4,4,2048]{2,1,0:T(4,128)(2,1)S(1)}, bf16[4,4,2048]{2,1,0:T(4,128)(2,1)S(1)}, u32[]{:S(2)}, u32[]{:S(2)}) collective-permute-start(bf16[4,4,2048]{2,1,0:T(4,128)(2,1)S(1)} %get-tuple-element.16), channel_id=1, source_target_pairs={{0,16},{8,24},{16,32},{24,40},{32,48},{40,56},{48,0},{56,8},{1,17}... | collective-permute-start | bytes 196616 | tf_op jit(solution)/shard_map/ppermute | solution.py:13
  149.8 4.6 %collective-permute-start.28 = (bf16[4,4,2048]{2,1,0:T(4,128)(2,1)S(1)}, bf16[4,4,2048]{2,1,0:T(4,128)(2,1)S(1)}, u32[]{:S(2)}, u32[]{:S(2)}) collective-permute-start(bf16[4,4,2048]{2,1,0:T(4,128)(2,1)S(1)} %get-tuple-element.18), channel_id=1, source_target_pairs={{0,24},{8,32},{16,40},{24,48},{32,56},{40,0},{48,8},{56,16},{1,25}... | collective-permute-start | bytes 196616 | tf_op jit(solution)/shard_map/ppermute | solution.py:13
  154.8 3.8 %collective-permute-done.28 = bf16[4,4,2048]{2,1,0:T(4,128)(2,1)S(1)} collective-permute-done((bf16[4,4,2048]{2,1,0:T(4,128)(2,1)S(1)}, bf16[4,4,2048]{2,1,0:T(4,128)(2,1)S(1)}, u32[]{:S(2)}, u32[]{:S(2)}) %collective-permute-start.28) | collective-permute-done | bytes 65568 | tf_op jit(solution)/shard_map/ppermute | solution.py:13
  158.6 3.0 %collective-permute-done.27 = bf16[4,4,2048]{2,1,0:T(4,128)(2,1)S(1)} collective-permute-done((bf16[4,4,2048]{2,1,0:T(4,128)(2,1)S(1)}, bf16[4,4,2048]{2,1,0:T(4,128)(2,1)S(1)}, u32[]{:S(2)}, u32[]{:S(2)}) %collective-permute-start.27) | collective-permute-done | bytes 65568 | tf_op jit(solution)/shard_map/ppermute | solution.py:13
  162.0 3.2 %collective-permute-start.35 = (f32[4,2048]{1,0:T(4,128)S(1)}, f32[4,2048]{1,0:T(4,128)S(1)}, u32[]{:S(2)}, u32[]{:S(2)}) collective-permute-start(f32[4,2048]{1,0:T(4,128)S(1)} %get-tuple-element.20), channel_id=1, source_target_pairs={{0,1},{1,2},{2,3},{3,0},{4,5},{5,6},{6,7},{7,4},{8,9},{9,10},{10,1... | collective-permute-start | bytes 98312 | tf_op jit(solution)/shard_map/ppermute | solution.py:13
  167.1 3.5 %collective-permute-done.34 = f32[4,2048]{1,0:T(4,128)S(1)} collective-permute-done((f32[4,2048]{1,0:T(4,128)S(1)}, f32[4,2048]{1,0:T(4,128)S(1)}, u32[]{:S(2)}, u32[]{:S(2)}) %collective-permute-start.34) | collective-permute-done | bytes 32800 | tf_op jit(solution)/shard_map/ppermute | solution.py:13
  (80 shorter events, 25.0 us)
Async XLA Ops:
  0.0 60.7 %collective-permute-start.14 = (bf16[448,2048]{1,0:T(8,128)(2,1)}, bf16[448,2048]{1,0:T(8,128)(2,1)}, u32[]{:S(2)}, u32[]{:S(2)}) collective-permute-start(bf16[448,2048]{1,0:T(8,128)(2,1)} %bitcast.66), channel_id=1, source_target_pairs={{0,4},{4,0},{1,5},{5,1},{2,6},{6,2},{3,7},{7,3},{8,12},{12,8},{9,1... | collective-permute-start | bytes 5505032 | tf_op jit(solution)/shard_map/ppermute | solution.py:13
  0.0 60.7 %collective-permute-start.15 = (bf16[448,2048]{1,0:T(8,128)(2,1)}, bf16[448,2048]{1,0:T(8,128)(2,1)}, u32[]{:S(2)}, u32[]{:S(2)}) collective-permute-start(bf16[448,2048]{1,0:T(8,128)(2,1)} %bitcast.64), channel_id=1, source_target_pairs={{0,4},{4,0},{1,5},{5,1},{2,6},{6,2},{3,7},{7,3},{8,12},{12,8},{9,1... | collective-permute-start | bytes 5505032 | tf_op jit(solution)/shard_map/ppermute | solution.py:13
  2.6 5.4 %collective-permute-start.1 = (bf16[4,2048]{1,0:T(4,128)(2,1)S(1)}, bf16[4,2048]{1,0:T(4,128)(2,1)S(1)}, u32[]{:S(2)}, u32[]{:S(2)}) collective-permute-start(bf16[4,2048]{1,0:T(4,128)(2,1)S(1)} %get-tuple-element.25), channel_id=1, source_target_pairs={{0,2},{1,3},{2,0},{3,1},{4,6},{5,7},{6,4},{7,5},{8,10},{9,11},{10,... | collective-permute-start | bytes 49160 | tf_op jit(solution)/shard_map/ppermute | solution.py:13
  13.5 6.2 %collective-permute-start.4 = (bf16[4,4,2048]{2,1,0:T(4,128)(2,1)S(1)}, bf16[4,4,2048]{2,1,0:T(4,128)(2,1)S(1)}, u32[]{:S(2)}, u32[]{:S(2)}) collective-permute-start(bf16[4,4,2048]{2,1,0:T(4,128)(2,1)S(1)} %collective-permute-done.3), channel_id=1, source_target_pairs={{0,8},{8,16},{16,24},{24,32},{32,40},{40,48},{48,56},{56,0},{1,9},... | collective-permute-start | bytes 196616 | tf_op jit(solution)/shard_map/ppermute | solution.py:13
  15.4 5.3 %collective-permute-start.8 = (bf16[4,4,2048]{2,1,0:T(4,128)(2,1)S(1)}, bf16[4,4,2048]{2,1,0:T(4,128)(2,1)S(1)}, u32[]{:S(2)}, u32[]{:S(2)}) collective-permute-start(bf16[4,4,2048]{2,1,0:T(4,128)(2,1)S(1)} %collective-permute-done.7), channel_id=1, source_target_pairs={{0,56},{8,0},{16,8},{24,16},{32,24},{40,32},{48,40},{56,48},{1,57}... | collective-permute-start | bytes 196616 | tf_op jit(solution)/shard_map/ppermute | solution.py:13
  19.7 5.6 %collective-permute-start.5 = (bf16[4,4,2048]{2,1,0:T(4,128)(2,1)S(1)}, bf16[4,4,2048]{2,1,0:T(4,128)(2,1)S(1)}, u32[]{:S(2)}, u32[]{:S(2)}) collective-permute-start(bf16[4,4,2048]{2,1,0:T(4,128)(2,1)S(1)} %collective-permute-done.4), channel_id=1, source_target_pairs={{0,8},{8,16},{16,24},{24,32},{32,40},{40,48},{48,56},{56,0},{1,9},... | collective-permute-start | bytes 196616 | tf_op jit(solution)/shard_map/ppermute | solution.py:13
  20.7 5.8 %collective-permute-start.9 = (bf16[4,4,2048]{2,1,0:T(4,128)(2,1)S(1)}, bf16[4,4,2048]{2,1,0:T(4,128)(2,1)S(1)}, u32[]{:S(2)}, u32[]{:S(2)}) collective-permute-start(bf16[4,4,2048]{2,1,0:T(4,128)(2,1)S(1)} %collective-permute-done.8), channel_id=1, source_target_pairs={{0,56},{8,0},{16,8},{24,16},{32,24},{40,32},{48,40},{56,48},{1,57}... | collective-permute-start | bytes 196616 | tf_op jit(solution)/shard_map/ppermute | solution.py:13
  25.3 5.4 %collective-permute-start.6 = (bf16[2,4,2048]{2,1,0:T(4,128)(2,1)S(1)}, bf16[2,4,2048]{2,1,0:T(4,128)(2,1)S(1)}, u32[]{:S(2)}, u32[]{:S(2)}) collective-permute-start(bf16[2,4,2048]{2,1,0:T(4,128)(2,1)S(1)} %slice.133), channel_id=1, source_target_pairs={{0,8},{8,16},{16,24},{24,32},{32,40},{40,48},{48,56},{56,0},{1,9},... | collective-permute-start | bytes 98312 | tf_op jit(solution)/shard_map/ppermute | solution.py:13
  26.5 5.2 %collective-permute-start.10 = (bf16[2,4,2048]{2,1,0:T(4,128)(2,1)S(1)}, bf16[2,4,2048]{2,1,0:T(4,128)(2,1)S(1)}, u32[]{:S(2)}, u32[]{:S(2)}) collective-permute-start(bf16[2,4,2048]{2,1,0:T(4,128)(2,1)S(1)} %slice.134), channel_id=1, source_target_pairs={{0,56},{8,0},{16,8},{24,16},{32,24},{40,32},{48,40},{56,48},{1,57}... | collective-permute-start | bytes 98312 | tf_op jit(solution)/shard_map/ppermute | solution.py:13
  32.1 20.5 %collective-permute-start.13 = (bf16[4,32,2048]{2,1,0:T(8,128)(2,1)S(1)}, bf16[4,32,2048]{2,1,0:T(8,128)(2,1)S(1)}, u32[]{:S(2)}, u32[]{:S(2)}) collective-permute-start(bf16[4,32,2048]{2,1,0:T(8,128)(2,1)S(1)} %concatenate.28), channel_id=1, source_target_pairs={{0,192},{64,0},{128,64},{192,128},{1,193},{65,1},{129,65},{193,129... | collective-permute-start | bytes 1572872 | tf_op jit(solution)/shard_map/ppermute | solution.py:13
  35.2 17.4 %collective-permute-start.12 = (bf16[4,32,2048]{2,1,0:T(8,128)(2,1)S(1)}, bf16[4,32,2048]{2,1,0:T(8,128)(2,1)S(1)}, u32[]{:S(2)}, u32[]{:S(2)}) collective-permute-start(bf16[4,32,2048]{2,1,0:T(8,128)(2,1)S(1)} %concatenate.28), channel_id=1, source_target_pairs={{0,128},{64,192},{128,0},{192,64},{1,129},{65,193},{129,1},{193,65... | collective-permute-start | bytes 1572872 | tf_op jit(solution)/shard_map/ppermute | solution.py:13
  35.8 20.6 %collective-permute-start.11 = (bf16[4,32,2048]{2,1,0:T(8,128)(2,1)S(1)}, bf16[4,32,2048]{2,1,0:T(8,128)(2,1)}, u32[]{:S(2)}, u32[]{:S(2)}) collective-permute-start(bf16[4,32,2048]{2,1,0:T(8,128)(2,1)S(1)} %concatenate.28), channel_id=1, source_target_pairs={{0,64},{64,128},{128,192},{192,0},{1,65},{65,129},{129,193},{193,1... | collective-permute-start | bytes 1572872 | tf_op jit(solution)/shard_map/ppermute | solution.py:13
  52.6 44.1 %collective-permute-start.22 = (bf16[448,2048]{1,0:T(8,128)(2,1)}, bf16[448,2048]{1,0:T(8,128)(2,1)}, u32[]{:S(2)}, u32[]{:S(2)}) collective-permute-start(bf16[448,2048]{1,0:T(8,128)(2,1)} %param.9), channel_id=1, source_target_pairs={{0,4},{4,0},{1,5},{5,1},{2,6},{6,2},{3,7},{7,3},{8,12},{12,8},{9,1... | collective-permute-start | bytes 5505032 | tf_op jit(solution)/shard_map/ppermute | solution.py:13
  69.6 15.1 %collective-permute-start.16 = (bf16[128,1792]{1,0:T(8,128)(2,1)S(1)}, bf16[128,1792]{1,0:T(8,128)(2,1)S(1)}, u32[]{:S(2)}, u32[]{:S(2)}) collective-permute-start(bf16[128,1792]{1,0:T(8,128)(2,1)S(1)} %get-tuple-element.10), channel_id=1, source_target_pairs={{0,2},{1,3},{2,0},{3,1},{4,6},{5,7},{6,4},{7,5},{8,10},{9,11},{10,... | collective-permute-start | bytes 1376264 | tf_op jit(solution)/shard_map/ppermute | solution.py:13
  71.9 20.6 %collective-permute-start.18 = (bf16[128,1792]{1,0:T(8,128)(2,1)S(1)}, bf16[128,1792]{1,0:T(8,128)(2,1)S(1)}, u32[]{:S(2)}, u32[]{:S(2)}) collective-permute-start(bf16[128,1792]{1,0:T(8,128)(2,1)S(1)} %get-tuple-element.11), channel_id=1, source_target_pairs={{0,3},{1,0},{2,1},{3,2},{4,7},{5,4},{6,5},{7,6},{8,11},{9,8},{10,9... | collective-permute-start | bytes 1376264 | tf_op jit(solution)/shard_map/ppermute | solution.py:13
  73.6 19.1 %collective-permute-start.17 = (bf16[128,1792]{1,0:T(8,128)(2,1)S(1)}, bf16[128,1792]{1,0:T(8,128)(2,1)S(1)}, u32[]{:S(2)}, u32[]{:S(2)}) collective-permute-start(bf16[128,1792]{1,0:T(8,128)(2,1)S(1)} %get-tuple-element.12), channel_id=1, source_target_pairs={{0,1},{1,2},{2,3},{3,0},{4,5},{5,6},{6,7},{7,4},{8,9},{9,10},{10,1... | collective-permute-start | bytes 1376264 | tf_op jit(solution)/shard_map/ppermute | solution.py:13
  93.1 12.7 %collective-permute-start.21 = (bf16[128,896]{1,0:T(8,128)(2,1)S(1)}, bf16[128,896]{1,0:T(8,128)(2,1)S(1)}, u32[]{:S(2)}, u32[]{:S(2)}) collective-permute-start(bf16[128,896]{1,0:T(8,128)(2,1)S(1)} %fusion.24), channel_id=1, source_target_pairs={{0,1},{1,2},{2,3},{3,0},{4,5},{5,6},{6,7},{7,4},{8,9},{9,10},{10,1... | collective-permute-start | bytes 688136 | tf_op jit(solution)/shard_map/ppermute | solution.py:13
  95.8 10.0 %collective-permute-start.20 = (bf16[128,896]{1,0:T(8,128)(2,1)S(1)}, bf16[128,896]{1,0:T(8,128)(2,1)S(1)}, u32[]{:S(2)}, u32[]{:S(2)}) collective-permute-start(bf16[128,896]{1,0:T(8,128)(2,1)S(1)} %fusion.24), channel_id=1, source_target_pairs={{0,2},{1,3},{2,0},{3,1},{4,6},{5,7},{6,4},{7,5},{8,10},{9,11},{10,... | collective-permute-start | bytes 688136 | tf_op jit(solution)/shard_map/ppermute | solution.py:13
  95.8 13.4 %collective-permute-start.19 = (bf16[128,896]{1,0:T(8,128)(2,1)S(1)}, bf16[128,896]{1,0:T(8,128)(2,1)S(1)}, u32[]{:S(2)}, u32[]{:S(2)}) collective-permute-start(bf16[128,896]{1,0:T(8,128)(2,1)S(1)} %fusion.24), channel_id=1, source_target_pairs={{0,3},{1,0},{2,1},{3,2},{4,7},{5,4},{6,5},{7,6},{8,11},{9,8},{10,9... | collective-permute-start | bytes 688136 | tf_op jit(solution)/shard_map/ppermute | solution.py:13
  113.4 16.4 %collective-permute-start.23 = (bf16[4,32,2048]{2,1,0:T(8,128)(2,1)S(1)}, bf16[4,32,2048]{2,1,0:T(8,128)(2,1)S(1)}, u32[]{:S(2)}, u32[]{:S(2)}) collective-permute-start(bf16[4,32,2048]{2,1,0:T(8,128)(2,1)S(1)} %get-tuple-element.7), channel_id=1, source_target_pairs={{0,128},{64,192},{128,0},{192,64},{1,129},{65,193},{129,1},{193,65... | collective-permute-start | bytes 1572872 | tf_op jit(solution)/shard_map/ppermute | solution.py:13
  113.6 25.9 %collective-permute-start.25 = (bf16[4,32,2048]{2,1,0:T(8,128)(2,1)S(1)}, bf16[4,32,2048]{2,1,0:T(8,128)(2,1)S(1)}, u32[]{:S(2)}, u32[]{:S(2)}) collective-permute-start(bf16[4,32,2048]{2,1,0:T(8,128)(2,1)S(1)} %get-tuple-element.8), channel_id=1, source_target_pairs={{0,64},{64,128},{128,192},{192,0},{1,65},{65,129},{129,193},{193,1... | collective-permute-start | bytes 1572872 | tf_op jit(solution)/shard_map/ppermute | solution.py:13
  115.9 23.6 %collective-permute-start.24 = (bf16[4,32,2048]{2,1,0:T(8,128)(2,1)S(1)}, bf16[4,32,2048]{2,1,0:T(8,128)(2,1)S(1)}, u32[]{:S(2)}, u32[]{:S(2)}) collective-permute-start(bf16[4,32,2048]{2,1,0:T(8,128)(2,1)S(1)} %get-tuple-element.9), channel_id=1, source_target_pairs={{0,192},{64,0},{128,64},{192,128},{1,193},{65,1},{129,65},{193,129... | collective-permute-start | bytes 1572872 | tf_op jit(solution)/shard_map/ppermute | solution.py:13
  140.2 9.6 %collective-permute-start.26 = (bf16[4,4,2048]{2,1,0:T(4,128)(2,1)S(1)}, bf16[4,4,2048]{2,1,0:T(4,128)(2,1)S(1)}, u32[]{:S(2)}, u32[]{:S(2)}) collective-permute-start(bf16[4,4,2048]{2,1,0:T(4,128)(2,1)S(1)} %get-tuple-element.13), channel_id=1, source_target_pairs={{0,32},{8,40},{16,48},{24,56},{32,0},{40,8},{48,16},{56,24},{1,33}... | collective-permute-start | bytes 196616 | tf_op jit(solution)/shard_map/ppermute | solution.py:13
  143.5 10.9 %collective-permute-start.32 = (bf16[4,4,2048]{2,1,0:T(4,128)(2,1)S(1)}, bf16[4,4,2048]{2,1,0:T(4,128)(2,1)S(1)}, u32[]{:S(2)}, u32[]{:S(2)}) collective-permute-start(bf16[4,4,2048]{2,1,0:T(4,128)(2,1)S(1)} %get-tuple-element.14), channel_id=1, source_target_pairs={{0,8},{8,16},{16,24},{24,32},{32,40},{40,48},{48,56},{56,0},{1,9},... | collective-permute-start | bytes 196616 | tf_op jit(solution)/shard_map/ppermute | solution.py:13
  143.5 11.4 %collective-permute-start.31 = (bf16[4,4,2048]{2,1,0:T(4,128)(2,1)S(1)}, bf16[4,4,2048]{2,1,0:T(4,128)(2,1)S(1)}, u32[]{:S(2)}, u32[]{:S(2)}) collective-permute-start(bf16[4,4,2048]{2,1,0:T(4,128)(2,1)S(1)} %get-tuple-element.15), channel_id=1, source_target_pairs={{0,56},{8,0},{16,8},{24,16},{32,24},{40,32},{48,40},{56,48},{1,57}... | collective-permute-start | bytes 196616 | tf_op jit(solution)/shard_map/ppermute | solution.py:13
  145.6 9.2 %collective-permute-start.30 = (bf16[4,4,2048]{2,1,0:T(4,128)(2,1)S(1)}, bf16[4,4,2048]{2,1,0:T(4,128)(2,1)S(1)}, u32[]{:S(2)}, u32[]{:S(2)}) collective-permute-start(bf16[4,4,2048]{2,1,0:T(4,128)(2,1)S(1)} %get-tuple-element.16), channel_id=1, source_target_pairs={{0,16},{8,24},{16,32},{24,40},{32,48},{40,56},{48,0},{56,8},{1,17}... | collective-permute-start | bytes 196616 | tf_op jit(solution)/shard_map/ppermute | solution.py:13
  148.1 6.8 %collective-permute-start.29 = (bf16[4,4,2048]{2,1,0:T(4,128)(2,1)S(1)}, bf16[4,4,2048]{2,1,0:T(4,128)(2,1)S(1)}, u32[]{:S(2)}, u32[]{:S(2)}) collective-permute-start(bf16[4,4,2048]{2,1,0:T(4,128)(2,1)S(1)} %get-tuple-element.17), channel_id=1, source_target_pairs={{0,48},{8,56},{16,0},{24,8},{32,16},{40,24},{48,32},{56,40},{1,49}... | collective-permute-start | bytes 196616 | tf_op jit(solution)/shard_map/ppermute | solution.py:13
  149.8 8.8 %collective-permute-start.28 = (bf16[4,4,2048]{2,1,0:T(4,128)(2,1)S(1)}, bf16[4,4,2048]{2,1,0:T(4,128)(2,1)S(1)}, u32[]{:S(2)}, u32[]{:S(2)}) collective-permute-start(bf16[4,4,2048]{2,1,0:T(4,128)(2,1)S(1)} %get-tuple-element.18), channel_id=1, source_target_pairs={{0,24},{8,32},{16,40},{24,48},{32,56},{40,0},{48,8},{56,16},{1,25}... | collective-permute-start | bytes 196616 | tf_op jit(solution)/shard_map/ppermute | solution.py:13
  154.4 7.3 %collective-permute-start.27 = (bf16[4,4,2048]{2,1,0:T(4,128)(2,1)S(1)}, bf16[4,4,2048]{2,1,0:T(4,128)(2,1)S(1)}, u32[]{:S(2)}, u32[]{:S(2)}) collective-permute-start(bf16[4,4,2048]{2,1,0:T(4,128)(2,1)S(1)} %get-tuple-element.19), channel_id=1, source_target_pairs={{0,40},{8,48},{16,56},{24,0},{32,8},{40,16},{48,24},{56,32},{1,41}... | collective-permute-start | bytes 196616 | tf_op jit(solution)/shard_map/ppermute | solution.py:13
  161.8 5.2 %collective-permute-start.33 = (f32[4,2048]{1,0:T(4,128)S(1)}, f32[4,2048]{1,0:T(4,128)S(1)}, u32[]{:S(2)}, u32[]{:S(2)}) collective-permute-start(f32[4,2048]{1,0:T(4,128)S(1)} %get-tuple-element.23), channel_id=1, source_target_pairs={{0,3},{1,0},{2,1},{3,2},{4,7},{5,4},{6,5},{7,6},{8,11},{9,8},{10,9... | collective-permute-start | bytes 98312 | tf_op jit(solution)/shard_map/ppermute | solution.py:13
  162.0 8.6 %collective-permute-start.35 = (f32[4,2048]{1,0:T(4,128)S(1)}, f32[4,2048]{1,0:T(4,128)S(1)}, u32[]{:S(2)}, u32[]{:S(2)}) collective-permute-start(f32[4,2048]{1,0:T(4,128)S(1)} %get-tuple-element.20), channel_id=1, source_target_pairs={{0,1},{1,2},{2,3},{3,0},{4,5},{5,6},{6,7},{7,4},{8,9},{9,10},{10,1... | collective-permute-start | bytes 98312 | tf_op jit(solution)/shard_map/ppermute | solution.py:13
  165.2 5.4 %collective-permute-start.34 = (f32[4,2048]{1,0:T(4,128)S(1)}, f32[4,2048]{1,0:T(4,128)S(1)}, u32[]{:S(2)}, u32[]{:S(2)}) collective-permute-start(f32[4,2048]{1,0:T(4,128)S(1)} %get-tuple-element.22), channel_id=1, source_target_pairs={{0,2},{1,3},{2,0},{3,1},{4,6},{5,7},{6,4},{7,5},{8,10},{9,11},{10,... | collective-permute-start | bytes 98312 | tf_op jit(solution)/shard_map/ppermute | solution.py:13
  (8 other events, 88.9 us)

commit v2 on v1

v2 whole, which is shorter than its diff:
```python
import jax
import jax.numpy as jnp
from jax import lax
from jax.sharding import Mesh
from jax.sharding import PartitionSpec as P

F32, BF16 = jnp.float32, jnp.bfloat16
SIZES = {"y": 4, "z": 8, "c": 2, "x": 4}


def shift(value, axis, step):
    n = SIZES[axis]
    return lax.ppermute(value, axis, [(i, (i + step) % n) for i in range(n)])


def along_z(value, first, second):
    steps = (first, second)
    pairs = [
        (2 * z + c, 2 * ((z + steps[c]) % 8) + c) for z in range(8) for c in range(2)
    ]
    return lax.ppermute(value, ("z", "c"), pairs)


def rolled(blocks, start):
    return lax.dynamic_slice_in_dim(
        jnp.concatenate([blocks, blocks], axis=0), start, blocks.shape[0], axis=0
    )


def together(*values):
    return lax.optimization_barrier(values)


def gather_z(pair):
    near = along_z(pair, 1, -1)
    base = along_z(pair, 0, 4)
    far = along_z(jnp.concatenate([pair, near], axis=1), 2, -2)
    return jnp.concatenate([base, near, far], axis=1)


def scatter_z(sums):
    n = sums.shape[1] // 4
    far = along_z(sums[:, 2 * n :].astype(BF16), -2, 2).astype(F32)
    base = along_z(sums[:, :n].astype(BF16), 0, 4).astype(F32)
    near = along_z((sums[:, n : 2 * n] + far[:, n:]).astype(BF16), -1, 1).astype(F32)
    return base + far[:, :n] + near


def local(tokens, norm_gain, gate_weight, up_weight, down_weight):
    x, core = lax.axis_index("x"), lax.axis_index("c")
    gate_t, up_t = gate_weight.T, up_weight.T
    first = [gate_t, shift(gate_t, "c", 1), up_t, shift(up_t, "c", 1)]
    second = jnp.concatenate([down_weight, shift(down_weight, "c", 1)], axis=0)
    units = second.shape[0]
    rows, width = tokens.shape
    part = width // 4

    wide = tokens.astype(F32)
    mean_square = jnp.mean(wide * wide, axis=1, keepdims=True)
    normed = (wide * lax.rsqrt(mean_square + 1e-05) * norm_gain[None, :]).astype(BF16)
    blocks = rolled(normed.reshape(rows, 4, part).transpose(1, 0, 2), x)
    own = jnp.stack(
        [blocks[0]] + [shift(blocks[4 - r], "x", 4 - r) for r in (1, 2, 3)]
    )
    plane = gather_z(lax.all_gather(own, "c", axis=1, tiled=True))
    tall = plane.shape[1]
    *first, own_plane = together(*first, plane)
    first = jnp.concatenate(first, axis=0)

    def project(block):
        return lax.dot_general(
            block.reshape(-1, part), first, (((1,), (1,)), ((), ())), preferred_element_type=F32
        ).reshape(4, -1, 2 * units)

    def exchange(partial):
        return [shift(partial[k].astype(BF16), "x", k) for k in (2, 1, 3)]

    def activate(both, received):
        for value in received:
            both = both + value.astype(F32)
        return (jax.nn.silu(both[:, :units]) * both[:, units:]).astype(BF16)

    def spread(hidden):
        return [shift(hidden, "x", -k) for k in (1, 2, 3)]

    def down(everyone):
        return lax.dot_general(
            jnp.concatenate(everyone, axis=0),
            second,
            (((1,), (0,)), ((), ())),
            preferred_element_type=F32,
        ).reshape(4, -1, part)

    behind, ahead, opposite = (shift(plane, "y", k) for k in (1, 3, 2))
    own_partial = project(own_plane)
    own_sums = exchange(own_partial)
    own_kept, behind, ahead = together(own_partial[0], behind, ahead)

    side_partial = project(jnp.concatenate([behind, ahead], axis=1))
    side_sums = exchange(side_partial)
    side_kept, *own_sums = together(side_partial[0], *own_sums)
    own_hidden = activate(own_kept, own_sums)
    own_spread = spread(own_hidden)
    own_hidden, opposite = together(own_hidden, opposite)

    far_partial = project(opposite)
    far_sums = exchange(far_partial)
    far_kept, *side_sums = together(far_partial[0], *side_sums)
    side_hidden = activate(side_kept, side_sums)
    side_spread = spread(side_hidden)
    side_hidden, *far_sums = together(side_hidden, *far_sums)
    far_hidden = activate(far_kept, far_sums)
    far_spread = spread(far_hidden)

    own_down = down([own_hidden] + own_spread)
    side_down = down([side_hidden] + side_spread)
    far_down = down([far_hidden] + far_spread)
    summed = own_down
    for value, k in ((side_down[:, :tall], -1), (side_down[:, tall:], -3), (far_down, -2)):
        summed = summed + shift(value.astype(BF16), "y", k).astype(F32)

    pair = scatter_z(summed)
    low, high = pair[:, :rows], pair[:, rows:]
    mine = jnp.where(core == 0, low, high)
    other = jnp.where(core == 0, high, low).astype(BF16)
    mine = mine + shift(other, "c", 1).astype(F32)
    columns = [mine[0]] + [shift(mine[k], "x", k) for k in (1, 2, 3)]
    ordered = [columns[0]] * 4
    for k in (1, 2, 3):
        ordered = [
            jnp.where((x - block) % 4 == k, columns[k], value)
            for block, value in enumerate(ordered)
        ]
    return (wide + jnp.concatenate(ordered, axis=1)).astype(BF16)


def solution(mesh):
    torus = Mesh(mesh.devices.reshape(4, 8, 2, 4), ("y", "z", "c", "x"))
    section = ("y", "z", "c")
    return jax.shard_map(
        local,
        mesh=torus,
        in_specs=(
            P(section + ("x",), None),
            P(),
            P("x", section),
            P("x", section),
            P(section, "x"),
        ),
        out_specs=P(section + ("x",), None),
        check_vma=False,
    )
```

time: 172 us -> 154 us (0.90)
  the two profiles are of different devices: /device:TPU:38 before, /device:TPU:1 now
where the time goes in v2:
time: 154 us; the launch traced here: 151 us
  starting transfers between devices  67.3 us (44%)
  waiting for transfers between devices  59.8 us (39%)
  matrix products  9.99 us (6%)
  local copies, waits for them, and re-layouts  6.02 us (4%)
  other arithmetic  3.86 us (3%)
  blocking collectives  3.72 us (2%)
    ppermute x34, starting transfers between devices, shift(): return lax.ppermute(value, axis, [(i, (i + step) % n) for i in range(n)])  55.4 us
    ppermute x34, waiting for transfers between devices, shift(): return lax.ppermute(value, axis, [(i, (i + step) % n) for i in range(n)])  39 us
    ppermute x6, waiting for transfers between devices, along_z(): return lax.ppermute(value, ('z', 'c'), pairs)  20.8 us
    ppermute x6, starting transfers between devices, along_z(): return lax.ppermute(value, ('z', 'c'), pairs)  11.8 us
    dot_general x3, matrix products, project(): lax.dot_general(block.reshape(-1, part), first, (((1,), (1,)), ((), ())),...  7.21 us
    all_gather x1, blocking collectives, local(): plane = gather_z(lax.all_gather(own, 'c', axis=1, tiled=True))  3.72 us
    unnamed x12, local copies, waits for them, and re-layouts  3.67 us
  transfers between devices with their start and end apart: 40, of which 23 were waited for; matrix products, arithmetic and copies ran while one was open for 12% of the time, Pallas kernels for 0%

profile of v2, /device:TPU:1, one launch (start us, length us, event | category | flops | bytes accessed | tf_op | source)
XLA Modules:
  0.0 151.4 jit_solution(15472354947768427688)
XLA Ops:
  0.0 3.2 %collective-permute-start = (bf16[448,2048]{1,0:T(8,128)(2,1)}, bf16[448,2048]{1,0:T(8,128)(2,1)}, u32[]{:S(2)}, u32[]{:S(2)}) collective-permute-start(bf16[448,2048]{1,0:T(8,128)(2,1)} %bitcast.46), channel_id=1, source_target_pairs={{0,4},{4,0},{1,5},{5,1},{2,6},{6,2},{3,7},{7,3},{8,12},{12,8},{9,1... | collective-permute-start | bytes 5505032 | tf_op jit(solution)/shard_map/ppermute | solution.py:13
  10.7 3.7 %all_gather.3 = bf16[4,8,2048]{2,0,1:T(4,128)(2,1)S(1)} all-gather(bf16[4,4,2048]{2,0,1:T(4,128)(2,1)S(1)} %copy.10), channel_id=1, replica_groups=mesh['y'=4,'z'=8,'c'=2,'x'=4] {'c'}, dimensions={1}, use_global_device_ids=true | all-gather | bytes 196608 | tf_op jit(solution)/shard_map/all_gather | solution.py:65
  14.5 5.7 %collective-permute-start.6 = (bf16[4,8,2048]{2,1,0:T(8,128)(2,1)S(1)}, bf16[4,8,2048]{2,1,0:T(8,128)(2,1)S(1)}, u32[]{:S(2)}, u32[]{:S(2)}) collective-permute-start(bf16[4,8,2048]{2,1,0:T(8,128)(2,1)S(1)} %copy.11), channel_id=1, source_target_pairs={{0,8},{4,60},{8,16},{12,4},{16,24},{20,12},{24,32},{28,20},{32,40}... | collective-permute-start | bytes 393224 | tf_op jit(solution)/shard_map/ppermute | solution.py:21
  21.9 3.3 %collective-permute-start.5 = (bf16[4,8,2048]{2,1,0:T(8,128)(2,1)S(1)}, bf16[4,8,2048]{2,1,0:T(8,128)(2,1)S(1)}, u32[]{:S(2)}, u32[]{:S(2)}) collective-permute-start(bf16[4,8,2048]{2,1,0:T(8,128)(2,1)S(1)} %copy.11), channel_id=1, source_target_pairs={{0,0},{4,36},{8,8},{12,44},{16,16},{20,52},{24,24},{28,60},{32,32}... | collective-permute-start | bytes 393224 | tf_op jit(solution)/shard_map/ppermute | solution.py:21
  25.3 11.0 %collective-permute-done.5 = bf16[4,8,2048]{2,1,0:T(8,128)(2,1)S(1)} collective-permute-done((bf16[4,8,2048]{2,1,0:T(8,128)(2,1)S(1)}, bf16[4,8,2048]{2,1,0:T(8,128)(2,1)S(1)}, u32[]{:S(2)}, u32[]{:S(2)}) %collective-permute-start.5) | collective-permute-done | bytes 131104 | tf_op jit(solution)/shard_map/ppermute | solution.py:21
  39.2 1.9 %collective-permute-start.13 = (bf16[4,32,2048]{2,1,0:T(8,128)(2,1)S(1)}, bf16[4,32,2048]{2,1,0:T(8,128)(2,1)S(1)}, u32[]{:S(2)}, u32[]{:S(2)}) collective-permute-start(bf16[4,32,2048]{2,1,0:T(8,128)(2,1)S(1)} %constant_dynamic-update-slice_fusion), channel_id=1, source_target_pairs={{0,128},{64,192},{128,0},{192,64},{1,129},{65,193},{129,1},{193,65... | collective-permute-start | bytes 1572872 | tf_op jit(solution)/shard_map/ppermute | solution.py:13
  41.3 1.7 %constant_dynamic-update-slice_fusion.5 = bf16[1792,2048]{1,0:T(8,128)(2,1)S(1)} fusion(bf16[1792,2048]{1,0:T(8,128)(2,1)S(1)} %constant_dynamic-update-slice_fusion.6, bf16[448,2048]{1,0:T(8,128)(2,1)} %collective-permute-done), kind=kLoop, calls=%fused_computation.66 | loop fusion | bytes 3670016
  44.8 2.5 %fusion.41 = (bf16[128,1792]{1,0:T(8,128)(2,1)S(1)}, f32[128,1792]{1,0:T(8,128)S(1)}) fusion(bf16[128,2048]{1,0:T(8,128)(2,1)S(1)} %bitcast.52, bf16[1792,2048]{1,0:T(8,128)(2,1)S(1)} %constant_dynamic-update-slice_fusion.3), kind=kOutput, calls=%fused_computation.83 | convolution fusion | flops 939753472 | bytes 9240576 | tf_op jit(solution)/shard_map/dot_general | solution.py:71
  47.4 3.4 %collective-permute-done.8 = bf16[4,32,2048]{2,1,0:T(8,128)(2,1)S(1)} collective-permute-done((bf16[4,32,2048]{2,1,0:T(8,128)(2,1)S(1)}, bf16[4,32,2048]{2,1,0:T(8,128)(2,1)S(1)}, u32[]{:S(2)}, u32[]{:S(2)}) %collective-permute-start.8) | collective-permute-done | bytes 524320 | tf_op jit(solution)/shard_map/ppermute | solution.py:13
  51.4 2.1 %fusion.42 = (bf16[256,1792]{1,0:T(8,128)(2,1)S(1)}, f32[256,1792]{1,0:T(8,128)S(1)}) fusion(bf16[256,2048]{1,0:T(8,128)(2,1)S(1)} %bitcast.51, bf16[1792,2048]{1,0:T(8,128)(2,1)S(1)} %constant_dynamic-update-slice_fusion.3), kind=kOutput, calls=%fused_computation.84 | convolution fusion | flops 1879506944 | bytes 11141120 | tf_op jit(solution)/shard_map/dot_general | solution.py:71
  55.1 2.5 %collective-permute-start.12 = (bf16[32,1792]{1,0:T(8,128)(2,1)S(1)}, bf16[32,1792]{1,0:T(8,128)(2,1)S(1)}, u32[]{:S(2)}, u32[]{:S(2)}) collective-permute-start(bf16[32,1792]{1,0:T(8,128)(2,1)S(1)} %get-tuple-element.59), channel_id=1, source_target_pairs={{0,3},{1,0},{2,1},{3,2},{4,7},{5,4},{6,5},{7,6},{8,11},{9,8},{10,9... | collective-permute-start | bytes 344072 | tf_op jit(solution)/shard_map/ppermute | solution.py:13
  57.7 2.0 %collective-permute-done.10 = bf16[32,1792]{1,0:T(8,128)(2,1)S(1)} collective-permute-done((bf16[32,1792]{1,0:T(8,128)(2,1)S(1)}, bf16[32,1792]{1,0:T(8,128)(2,1)S(1)}, u32[]{:S(2)}, u32[]{:S(2)}) %collective-permute-start.10) | collective-permute-done | bytes 114720 | tf_op jit(solution)/shard_map/ppermute | solution.py:13
  60.9 1.8 %collective-permute-done.11 = bf16[32,1792]{1,0:T(8,128)(2,1)S(1)} collective-permute-done((bf16[32,1792]{1,0:T(8,128)(2,1)S(1)}, bf16[32,1792]{1,0:T(8,128)(2,1)S(1)}, u32[]{:S(2)}, u32[]{:S(2)}) %collective-permute-start.11) | collective-permute-done | bytes 114720 | tf_op jit(solution)/shard_map/ppermute | solution.py:13
  62.7 2.7 %collective-permute-start.20 = (bf16[64,1792]{1,0:T(8,128)(2,1)S(1)}, bf16[64,1792]{1,0:T(8,128)(2,1)S(1)}, u32[]{:S(2)}, u32[]{:S(2)}) collective-permute-start(bf16[64,1792]{1,0:T(8,128)(2,1)S(1)} %get-tuple-element.53), channel_id=1, source_target_pairs={{0,3},{1,0},{2,1},{3,2},{4,7},{5,4},{6,5},{7,6},{8,11},{9,8},{10,9... | collective-permute-start | bytes 688136 | tf_op jit(solution)/shard_map/ppermute | solution.py:13
  65.5 2.5 %fusion.43 = (bf16[128,1792]{1,0:T(8,128)(2,1)S(1)}, f32[128,1792]{1,0:T(8,128)S(1)}) fusion(bf16[128,2048]{1,0:T(8,128)(2,1)S(1)} %bitcast.53, bf16[1792,2048]{1,0:T(8,128)(2,1)S(1)} %constant_dynamic-update-slice_fusion.3), kind=kOutput, calls=%fused_computation.85 | convolution fusion | flops 939753472 | bytes 9240576 | tf_op jit(solution)/shard_map/dot_general | solution.py:71
  68.8 5.3 %collective-permute-done.19 = bf16[64,1792]{1,0:T(8,128)(2,1)S(1)} collective-permute-done((bf16[64,1792]{1,0:T(8,128)(2,1)S(1)}, bf16[64,1792]{1,0:T(8,128)(2,1)S(1)}, u32[]{:S(2)}, u32[]{:S(2)}) %collective-permute-start.19) | collective-permute-done | bytes 229408 | tf_op jit(solution)/shard_map/ppermute | solution.py:13
  74.1 8.7 %collective-permute-start.23 = (bf16[32,1792]{1,0:T(8,128)(2,1)S(1)}, bf16[32,1792]{1,0:T(8,128)(2,1)S(1)}, u32[]{:S(2)}, u32[]{:S(2)}) collective-permute-start(bf16[32,1792]{1,0:T(8,128)(2,1)S(1)} %get-tuple-element.56), channel_id=1, source_target_pairs={{0,3},{1,0},{2,1},{3,2},{4,7},{5,4},{6,5},{7,6},{8,11},{9,8},{10,9... | collective-permute-start | bytes 344072 | tf_op jit(solution)/shard_map/ppermute | solution.py:13
  83.0 3.4 %collective-permute-done.23 = bf16[32,1792]{1,0:T(8,128)(2,1)S(1)} collective-permute-done((bf16[32,1792]{1,0:T(8,128)(2,1)S(1)}, bf16[32,1792]{1,0:T(8,128)(2,1)S(1)}, u32[]{:S(2)}, u32[]{:S(2)}) %collective-permute-start.23) | collective-permute-done | bytes 114720 | tf_op jit(solution)/shard_map/ppermute | solution.py:13
  90.1 2.0 %collective-permute-start.24 = (bf16[64,896]{1,0:T(8,128)(2,1)S(1)}, bf16[64,896]{1,0:T(8,128)(2,1)S(1)}, u32[]{:S(2)}, u32[]{:S(2)}) collective-permute-start(bf16[64,896]{1,0:T(8,128)(2,1)S(1)} %fusion.9), channel_id=1, source_target_pairs={{0,3},{1,0},{2,1},{3,2},{4,7},{5,4},{6,5},{7,6},{8,11},{9,8},{10,9... | collective-permute-start | bytes 344072 | tf_op jit(solution)/shard_map/ppermute | solution.py:13
  94.1 9.5 %collective-permute-start.32 = (bf16[4,32,2048]{2,1,0:T(8,128)(2,1)S(1)}, bf16[4,32,2048]{2,1,0:T(8,128)(2,1)S(1)}, u32[]{:S(2)}, u32[]{:S(2)}) collective-permute-start(bf16[4,32,2048]{2,1,0:T(8,128)(2,1)S(1)} %bitcast.54), channel_id=1, source_target_pairs={{0,128},{64,192},{128,0},{192,64},{1,129},{65,193},{129,1},{193,65... | collective-permute-start | bytes 1572872 | tf_op jit(solution)/shard_map/ppermute | solution.py:13
  105.0 4.7 %collective-permute-start.27 = (bf16[4,32,2048]{2,1,0:T(8,128)(2,1)S(1)}, bf16[4,32,2048]{2,1,0:T(8,128)(2,1)S(1)}, u32[]{:S(2)}, u32[]{:S(2)}) collective-permute-start(bf16[4,32,2048]{2,1,0:T(8,128)(2,1)S(1)} %get-tuple-element.51), channel_id=1, source_target_pairs={{0,192},{64,0},{128,64},{192,128},{1,193},{65,1},{129,65},{193,129... | collective-permute-start | bytes 1572872 | tf_op jit(solution)/shard_map/ppermute | solution.py:13
  110.6 2.4 %collective-permute-done.14 = bf16[32,896]{1,0:T(8,128)(2,1)S(1)} collective-permute-done((bf16[32,896]{1,0:T(8,128)(2,1)S(1)}, bf16[32,896]{1,0:T(8,128)(2,1)S(1)}, u32[]{:S(2)}, u32[]{:S(2)}) %collective-permute-start.14) | collective-permute-done | bytes 57376 | tf_op jit(solution)/shard_map/ppermute | solution.py:13
  113.0 1.8 %collective-permute-done.15 = bf16[32,896]{1,0:T(8,128)(2,1)S(1)} collective-permute-done((bf16[32,896]{1,0:T(8,128)(2,1)S(1)}, bf16[32,896]{1,0:T(8,128)(2,1)S(1)}, u32[]{:S(2)}, u32[]{:S(2)}) %collective-permute-start.15) | collective-permute-done | bytes 57376 | tf_op jit(solution)/shard_map/ppermute | solution.py:13
  114.8 2.7 %collective-permute-done.16 = bf16[32,896]{1,0:T(8,128)(2,1)S(1)} collective-permute-done((bf16[32,896]{1,0:T(8,128)(2,1)S(1)}, bf16[32,896]{1,0:T(8,128)(2,1)S(1)}, u32[]{:S(2)}, u32[]{:S(2)}) %collective-permute-start.16) | collective-permute-done | bytes 57376 | tf_op jit(solution)/shard_map/ppermute | solution.py:13
  118.3 6.6 %collective-permute-done.27 = bf16[4,32,2048]{2,1,0:T(8,128)(2,1)S(1)} collective-permute-done((bf16[4,32,2048]{2,1,0:T(8,128)(2,1)S(1)}, bf16[4,32,2048]{2,1,0:T(8,128)(2,1)S(1)}, u32[]{:S(2)}, u32[]{:S(2)}) %collective-permute-start.27) | collective-permute-done | bytes 524320 | tf_op jit(solution)/shard_map/ppermute | solution.py:13
  124.9 2.3 %collective-permute-done.28 = bf16[4,32,2048]{2,1,0:T(8,128)(2,1)S(1)} collective-permute-done((bf16[4,32,2048]{2,1,0:T(8,128)(2,1)S(1)}, bf16[4,32,2048]{2,1,0:T(8,128)(2,1)S(1)}, u32[]{:S(2)}, u32[]{:S(2)}) %collective-permute-start.28) | collective-permute-done | bytes 524320 | tf_op jit(solution)/shard_map/ppermute | solution.py:13
  128.2 1.9 %collective-permute-start.33 = (bf16[4,8,2048]{2,1,0:T(8,128)(2,1)S(1)}, bf16[4,8,2048]{2,1,0:T(8,128)(2,1)S(1)}, u32[]{:S(2)}, u32[]{:S(2)}) collective-permute-start(bf16[4,8,2048]{2,1,0:T(8,128)(2,1)S(1)} %slice.189), channel_id=1, source_target_pairs={{0,0},{4,36},{8,8},{12,44},{16,16},{20,52},{24,24},{28,60},{32,32}... | collective-permute-start | bytes 393224 | tf_op jit(solution)/shard_map/ppermute | solution.py:21
  130.2 4.8 %collective-permute-done.34 = bf16[4,16,2048]{2,1,0:T(8,128)(2,1)S(1)} collective-permute-done((bf16[4,16,2048]{2,1,0:T(8,128)(2,1)S(1)}, bf16[4,16,2048]{2,1,0:T(8,128)(2,1)S(1)}, u32[]{:S(2)}, u32[]{:S(2)}) %collective-permute-start.34) | collective-permute-done | bytes 262176 | tf_op jit(solution)/shard_map/ppermute | solution.py:21
  135.3 2.7 %collective-permute-done.33 = bf16[4,8,2048]{2,1,0:T(8,128)(2,1)S(1)} collective-permute-done((bf16[4,8,2048]{2,1,0:T(8,128)(2,1)S(1)}, bf16[4,8,2048]{2,1,0:T(8,128)(2,1)S(1)}, u32[]{:S(2)}, u32[]{:S(2)}) %collective-permute-start.33) | collective-permute-done | bytes 131104 | tf_op jit(solution)/shard_map/ppermute | solution.py:21
  138.0 2.3 %collective-permute-done.35 = bf16[4,8,2048]{2,1,0:T(8,128)(2,1)S(1)} collective-permute-done((bf16[4,8,2048]{2,1,0:T(8,128)(2,1)S(1)}, bf16[4,8,2048]{2,1,0:T(8,128)(2,1)S(1)}, u32[]{:S(2)}, u32[]{:S(2)}) %collective-permute-start.35) | collective-permute-done | bytes 131104 | tf_op jit(solution)/shard_map/ppermute | solution.py:21
  140.5 3.3 %collective-permute-start.36 = (bf16[4,4,2048]{2,1,0:T(4,128)(2,1)S(1)}, bf16[4,4,2048]{2,1,0:T(4,128)(2,1)S(1)}, u32[]{:S(2)}, u32[]{:S(2)}) collective-permute-start(bf16[4,4,2048]{2,1,0:T(4,128)(2,1)S(1)} %select_convert_fusion), channel_id=1, source_target_pairs={{0,4},{4,0},{1,5},{5,1},{2,6},{6,2},{3,7},{7,3},{8,12},{12,8},{9,1... | collective-permute-start | bytes 196616 | tf_op jit(solution)/shard_map/ppermute | solution.py:13
  147.6 1.8 %collective-permute-done.38 = f32[4,2048]{1,0:T(4,128)S(1)} collective-permute-done((f32[4,2048]{1,0:T(4,128)S(1)}, f32[4,2048]{1,0:T(4,128)S(1)}, u32[]{:S(2)}, u32[]{:S(2)}) %collective-permute-start.38) | collective-permute-done | bytes 32800 | tf_op jit(solution)/shard_map/ppermute | solution.py:13
  (104 shorter events, 34.5 us)
Async XLA Ops:
  0.0 39.2 %collective-permute-start = (bf16[448,2048]{1,0:T(8,128)(2,1)}, bf16[448,2048]{1,0:T(8,128)(2,1)}, u32[]{:S(2)}, u32[]{:S(2)}) collective-permute-start(bf16[448,2048]{1,0:T(8,128)(2,1)} %bitcast.46), channel_id=1, source_target_pairs={{0,4},{4,0},{1,5},{5,1},{2,6},{6,2},{3,7},{7,3},{8,12},{12,8},{9,1... | collective-permute-start | bytes 5505032 | tf_op jit(solution)/shard_map/ppermute | solution.py:13
  3.2 37.9 %collective-permute-start.1 = (bf16[448,2048]{1,0:T(8,128)(2,1)}, bf16[448,2048]{1,0:T(8,128)(2,1)}, u32[]{:S(2)}, u32[]{:S(2)}) collective-permute-start(bf16[448,2048]{1,0:T(8,128)(2,1)} %bitcast.48), channel_id=1, source_target_pairs={{0,4},{4,0},{1,5},{5,1},{2,6},{6,2},{3,7},{7,3},{8,12},{12,8},{9,1... | collective-permute-start | bytes 5505032 | tf_op jit(solution)/shard_map/ppermute | solution.py:13
  8.0 81.9 %collective-permute-start.17 = (bf16[448,2048]{1,0:T(8,128)(2,1)}, bf16[448,2048]{1,0:T(8,128)(2,1)S(1)}, u32[]{:S(2)}, u32[]{:S(2)}) collective-permute-start(bf16[448,2048]{1,0:T(8,128)(2,1)} %param.9), channel_id=1, source_target_pairs={{0,4},{4,0},{1,5},{5,1},{2,6},{6,2},{3,7},{7,3},{8,12},{12,8},{9,1... | collective-permute-start | bytes 5505032 | tf_op jit(solution)/shard_map/ppermute | solution.py:13
  14.5 10.6 %collective-permute-start.6 = (bf16[4,8,2048]{2,1,0:T(8,128)(2,1)S(1)}, bf16[4,8,2048]{2,1,0:T(8,128)(2,1)S(1)}, u32[]{:S(2)}, u32[]{:S(2)}) collective-permute-start(bf16[4,8,2048]{2,1,0:T(8,128)(2,1)S(1)} %copy.11), channel_id=1, source_target_pairs={{0,8},{4,60},{8,16},{12,4},{16,24},{20,12},{24,32},{28,20},{32,40}... | collective-permute-start | bytes 393224 | tf_op jit(solution)/shard_map/ppermute | solution.py:21
  21.9 14.4 %collective-permute-start.5 = (bf16[4,8,2048]{2,1,0:T(8,128)(2,1)S(1)}, bf16[4,8,2048]{2,1,0:T(8,128)(2,1)S(1)}, u32[]{:S(2)}, u32[]{:S(2)}) collective-permute-start(bf16[4,8,2048]{2,1,0:T(8,128)(2,1)S(1)} %copy.11), channel_id=1, source_target_pairs={{0,0},{4,36},{8,8},{12,44},{16,16},{20,52},{24,24},{28,60},{32,32}... | collective-permute-start | bytes 393224 | tf_op jit(solution)/shard_map/ppermute | solution.py:21
  25.2 11.1 %collective-permute-start.7 = (bf16[4,16,2048]{2,1,0:T(8,128)(2,1)S(1)}, bf16[4,16,2048]{2,1,0:T(8,128)(2,1)S(1)}, u32[]{:S(2)}, u32[]{:S(2)}) collective-permute-start(bf16[4,16,2048]{2,1,0:T(8,128)(2,1)S(1)} %pad_maximum_fusion.1), channel_id=1, source_target_pairs={{0,16},{4,52},{8,24},{12,60},{16,32},{20,4},{24,40},{28,12},{32,48... | collective-permute-start | bytes 786440 | tf_op jit(solution)/shard_map/ppermute | solution.py:21
  36.3 14.4 %collective-permute-start.8 = (bf16[4,32,2048]{2,1,0:T(8,128)(2,1)S(1)}, bf16[4,32,2048]{2,1,0:T(8,128)(2,1)S(1)}, u32[]{:S(2)}, u32[]{:S(2)}) collective-permute-start(bf16[4,32,2048]{2,1,0:T(8,128)(2,1)S(1)} %constant_dynamic-update-slice_fusion), channel_id=1, source_target_pairs={{0,64},{64,128},{128,192},{192,0},{1,65},{65,129},{129,193},{193,1... | collective-permute-start | bytes 1572872 | tf_op jit(solution)/shard_map/ppermute | solution.py:13
  37.7 13.6 %collective-permute-start.9 = (bf16[4,32,2048]{2,1,0:T(8,128)(2,1)S(1)}, bf16[4,32,2048]{2,1,0:T(8,128)(2,1)S(1)}, u32[]{:S(2)}, u32[]{:S(2)}) collective-permute-start(bf16[4,32,2048]{2,1,0:T(8,128)(2,1)S(1)} %constant_dynamic-update-slice_fusion), channel_id=1, source_target_pairs={{0,192},{64,0},{128,64},{192,128},{1,193},{65,1},{129,65},{193,129... | collective-permute-start | bytes 1572872 | tf_op jit(solution)/shard_map/ppermute | solution.py:13
  39.2 26.3 %collective-permute-start.13 = (bf16[4,32,2048]{2,1,0:T(8,128)(2,1)S(1)}, bf16[4,32,2048]{2,1,0:T(8,128)(2,1)S(1)}, u32[]{:S(2)}, u32[]{:S(2)}) collective-permute-start(bf16[4,32,2048]{2,1,0:T(8,128)(2,1)S(1)} %constant_dynamic-update-slice_fusion), channel_id=1, source_target_pairs={{0,128},{64,192},{128,0},{192,64},{1,129},{65,193},{129,1},{193,65... | collective-permute-start | bytes 1572872 | tf_op jit(solution)/shard_map/ppermute | solution.py:13
  53.6 6.1 %collective-permute-start.10 = (bf16[32,1792]{1,0:T(8,128)(2,1)S(1)}, bf16[32,1792]{1,0:T(8,128)(2,1)S(1)}, u32[]{:S(2)}, u32[]{:S(2)}) collective-permute-start(bf16[32,1792]{1,0:T(8,128)(2,1)S(1)} %get-tuple-element.61), channel_id=1, source_target_pairs={{0,2},{1,3},{2,0},{3,1},{4,6},{5,7},{6,4},{7,5},{8,10},{9,11},{10,... | collective-permute-start | bytes 344072 | tf_op jit(solution)/shard_map/ppermute | solution.py:13
  54.9 7.8 %collective-permute-start.11 = (bf16[32,1792]{1,0:T(8,128)(2,1)S(1)}, bf16[32,1792]{1,0:T(8,128)(2,1)S(1)}, u32[]{:S(2)}, u32[]{:S(2)}) collective-permute-start(bf16[32,1792]{1,0:T(8,128)(2,1)S(1)} %get-tuple-element.60), channel_id=1, source_target_pairs={{0,1},{1,2},{2,3},{3,0},{4,5},{5,6},{6,7},{7,4},{8,9},{9,10},{10,1... | collective-permute-start | bytes 344072 | tf_op jit(solution)/shard_map/ppermute | solution.py:13
  55.1 7.6 %collective-permute-start.12 = (bf16[32,1792]{1,0:T(8,128)(2,1)S(1)}, bf16[32,1792]{1,0:T(8,128)(2,1)S(1)}, u32[]{:S(2)}, u32[]{:S(2)}) collective-permute-start(bf16[32,1792]{1,0:T(8,128)(2,1)S(1)} %get-tuple-element.59), channel_id=1, source_target_pairs={{0,3},{1,0},{2,1},{3,2},{4,7},{5,4},{6,5},{7,6},{8,11},{9,8},{10,9... | collective-permute-start | bytes 344072 | tf_op jit(solution)/shard_map/ppermute | solution.py:13
  59.7 8.5 %collective-permute-start.18 = (bf16[64,1792]{1,0:T(8,128)(2,1)S(1)}, bf16[64,1792]{1,0:T(8,128)(2,1)S(1)}, u32[]{:S(2)}, u32[]{:S(2)}) collective-permute-start(bf16[64,1792]{1,0:T(8,128)(2,1)S(1)} %get-tuple-element.55), channel_id=1, source_target_pairs={{0,2},{1,3},{2,0},{3,1},{4,6},{5,7},{6,4},{7,5},{8,10},{9,11},{10,... | collective-permute-start | bytes 688136 | tf_op jit(solution)/shard_map/ppermute | solution.py:13
  62.7 11.4 %collective-permute-start.19 = (bf16[64,1792]{1,0:T(8,128)(2,1)S(1)}, bf16[64,1792]{1,0:T(8,128)(2,1)S(1)}, u32[]{:S(2)}, u32[]{:S(2)}) collective-permute-start(bf16[64,1792]{1,0:T(8,128)(2,1)S(1)} %get-tuple-element.54), channel_id=1, source_target_pairs={{0,1},{1,2},{2,3},{3,0},{4,5},{5,6},{6,7},{7,4},{8,9},{9,10},{10,1... | collective-permute-start | bytes 688136 | tf_op jit(solution)/shard_map/ppermute | solution.py:13
  62.7 20.1 %collective-permute-start.20 = (bf16[64,1792]{1,0:T(8,128)(2,1)S(1)}, bf16[64,1792]{1,0:T(8,128)(2,1)S(1)}, u32[]{:S(2)}, u32[]{:S(2)}) collective-permute-start(bf16[64,1792]{1,0:T(8,128)(2,1)S(1)} %get-tuple-element.53), channel_id=1, source_target_pairs={{0,3},{1,0},{2,1},{3,2},{4,7},{5,4},{6,5},{7,6},{8,11},{9,8},{10,9... | collective-permute-start | bytes 688136 | tf_op jit(solution)/shard_map/ppermute | solution.py:13
  68.1 14.9 %collective-permute-start.21 = (bf16[32,1792]{1,0:T(8,128)(2,1)S(1)}, bf16[32,1792]{1,0:T(8,128)(2,1)S(1)}, u32[]{:S(2)}, u32[]{:S(2)}) collective-permute-start(bf16[32,1792]{1,0:T(8,128)(2,1)S(1)} %get-tuple-element.58), channel_id=1, source_target_pairs={{0,2},{1,3},{2,0},{3,1},{4,6},{5,7},{6,4},{7,5},{8,10},{9,11},{10,... | collective-permute-start | bytes 344072 | tf_op jit(solution)/shard_map/ppermute | solution.py:13
  68.2 14.8 %collective-permute-start.22 = (bf16[32,1792]{1,0:T(8,128)(2,1)S(1)}, bf16[32,1792]{1,0:T(8,128)(2,1)S(1)}, u32[]{:S(2)}, u32[]{:S(2)}) collective-permute-start(bf16[32,1792]{1,0:T(8,128)(2,1)S(1)} %get-tuple-element.57), channel_id=1, source_target_pairs={{0,1},{1,2},{2,3},{3,0},{4,5},{5,6},{6,7},{7,4},{8,9},{9,10},{10,1... | collective-permute-start | bytes 344072 | tf_op jit(solution)/shard_map/ppermute | solution.py:13
  74.1 12.3 %collective-permute-start.23 = (bf16[32,1792]{1,0:T(8,128)(2,1)S(1)}, bf16[32,1792]{1,0:T(8,128)(2,1)S(1)}, u32[]{:S(2)}, u32[]{:S(2)}) collective-permute-start(bf16[32,1792]{1,0:T(8,128)(2,1)S(1)} %get-tuple-element.56), channel_id=1, source_target_pairs={{0,3},{1,0},{2,1},{3,2},{4,7},{5,4},{6,5},{7,6},{8,11},{9,8},{10,9... | collective-permute-start | bytes 344072 | tf_op jit(solution)/shard_map/ppermute | solution.py:13
  86.5 6.0 %collective-permute-start.29 = (bf16[32,896]{1,0:T(8,128)(2,1)S(1)}, bf16[32,896]{1,0:T(8,128)(2,1)S(1)}, u32[]{:S(2)}, u32[]{:S(2)}) collective-permute-start(bf16[32,896]{1,0:T(8,128)(2,1)S(1)} %fusion.29), channel_id=1, source_target_pairs={{0,3},{1,0},{2,1},{3,2},{4,7},{5,4},{6,5},{7,6},{8,11},{9,8},{10,9... | collective-permute-start | bytes 172040 | tf_op jit(solution)/shard_map/ppermute | solution.py:13
  87.8 5.0 %collective-permute-start.30 = (bf16[32,896]{1,0:T(8,128)(2,1)S(1)}, bf16[32,896]{1,0:T(8,128)(2,1)S(1)}, u32[]{:S(2)}, u32[]{:S(2)}) collective-permute-start(bf16[32,896]{1,0:T(8,128)(2,1)S(1)} %fusion.29), channel_id=1, source_target_pairs={{0,2},{1,3},{2,0},{3,1},{4,6},{5,7},{6,4},{7,5},{8,10},{9,11},{10,... | collective-permute-start | bytes 172040 | tf_op jit(solution)/shard_map/ppermute | solution.py:13
  90.1 13.5 %collective-permute-start.24 = (bf16[64,896]{1,0:T(8,128)(2,1)S(1)}, bf16[64,896]{1,0:T(8,128)(2,1)S(1)}, u32[]{:S(2)}, u32[]{:S(2)}) collective-permute-start(bf16[64,896]{1,0:T(8,128)(2,1)S(1)} %fusion.9), channel_id=1, source_target_pairs={{0,3},{1,0},{2,1},{3,2},{4,7},{5,4},{6,5},{7,6},{8,11},{9,8},{10,9... | collective-permute-start | bytes 344072 | tf_op jit(solution)/shard_map/ppermute | solution.py:13
  92.1 11.5 %collective-permute-start.25 = (bf16[64,896]{1,0:T(8,128)(2,1)S(1)}, bf16[64,896]{1,0:T(8,128)(2,1)S(1)}, u32[]{:S(2)}, u32[]{:S(2)}) collective-permute-start(bf16[64,896]{1,0:T(8,128)(2,1)S(1)} %fusion.9), channel_id=1, source_target_pairs={{0,2},{1,3},{2,0},{3,1},{4,6},{5,7},{6,4},{7,5},{8,10},{9,11},{10,... | collective-permute-start | bytes 344072 | tf_op jit(solution)/shard_map/ppermute | solution.py:13
  92.6 11.1 %collective-permute-start.26 = (bf16[64,896]{1,0:T(8,128)(2,1)S(1)}, bf16[64,896]{1,0:T(8,128)(2,1)S(1)}, u32[]{:S(2)}, u32[]{:S(2)}) collective-permute-start(bf16[64,896]{1,0:T(8,128)(2,1)S(1)} %fusion.9), channel_id=1, source_target_pairs={{0,1},{1,2},{2,3},{3,0},{4,5},{5,6},{6,7},{7,4},{8,9},{9,10},{10,1... | collective-permute-start | bytes 344072 | tf_op jit(solution)/shard_map/ppermute | solution.py:13
  94.1 24.2 %collective-permute-start.32 = (bf16[4,32,2048]{2,1,0:T(8,128)(2,1)S(1)}, bf16[4,32,2048]{2,1,0:T(8,128)(2,1)S(1)}, u32[]{:S(2)}, u32[]{:S(2)}) collective-permute-start(bf16[4,32,2048]{2,1,0:T(8,128)(2,1)S(1)} %bitcast.54), channel_id=1, source_target_pairs={{0,128},{64,192},{128,0},{192,64},{1,129},{65,193},{129,1},{193,65... | collective-permute-start | bytes 1572872 | tf_op jit(solution)/shard_map/ppermute | solution.py:13
  105.0 19.9 %collective-permute-start.27 = (bf16[4,32,2048]{2,1,0:T(8,128)(2,1)S(1)}, bf16[4,32,2048]{2,1,0:T(8,128)(2,1)S(1)}, u32[]{:S(2)}, u32[]{:S(2)}) collective-permute-start(bf16[4,32,2048]{2,1,0:T(8,128)(2,1)S(1)} %get-tuple-element.51), channel_id=1, source_target_pairs={{0,192},{64,0},{128,64},{192,128},{1,193},{65,1},{129,65},{193,129... | collective-permute-start | bytes 1572872 | tf_op jit(solution)/shard_map/ppermute | solution.py:13
  109.7 17.5 %collective-permute-start.28 = (bf16[4,32,2048]{2,1,0:T(8,128)(2,1)S(1)}, bf16[4,32,2048]{2,1,0:T(8,128)(2,1)S(1)}, u32[]{:S(2)}, u32[]{:S(2)}) collective-permute-start(bf16[4,32,2048]{2,1,0:T(8,128)(2,1)S(1)} %get-tuple-element.52), channel_id=1, source_target_pairs={{0,64},{64,128},{128,192},{192,0},{1,65},{65,129},{129,193},{193,1... | collective-permute-start | bytes 1572872 | tf_op jit(solution)/shard_map/ppermute | solution.py:13
  110.0 4.8 %collective-permute-start.15 = (bf16[32,896]{1,0:T(8,128)(2,1)S(1)}, bf16[32,896]{1,0:T(8,128)(2,1)S(1)}, u32[]{:S(2)}, u32[]{:S(2)}) collective-permute-start(bf16[32,896]{1,0:T(8,128)(2,1)S(1)} %fusion.30), channel_id=1, source_target_pairs={{0,2},{1,3},{2,0},{3,1},{4,6},{5,7},{6,4},{7,5},{8,10},{9,11},{10,... | collective-permute-start | bytes 172040 | tf_op jit(solution)/shard_map/ppermute | solution.py:13
  113.0 4.5 %collective-permute-start.16 = (bf16[32,896]{1,0:T(8,128)(2,1)S(1)}, bf16[32,896]{1,0:T(8,128)(2,1)S(1)}, u32[]{:S(2)}, u32[]{:S(2)}) collective-permute-start(bf16[32,896]{1,0:T(8,128)(2,1)S(1)} %fusion.30), channel_id=1, source_target_pairs={{0,1},{1,2},{2,3},{3,0},{4,5},{5,6},{6,7},{7,4},{8,9},{9,10},{10,1... | collective-permute-start | bytes 172040 | tf_op jit(solution)/shard_map/ppermute | solution.py:13
  127.6 7.4 %collective-permute-start.34 = (bf16[4,16,2048]{2,1,0:T(8,128)(2,1)S(1)}, bf16[4,16,2048]{2,1,0:T(8,128)(2,1)S(1)}, u32[]{:S(2)}, u32[]{:S(2)}) collective-permute-start(bf16[4,16,2048]{2,1,0:T(8,128)(2,1)S(1)} %slice.190), channel_id=1, source_target_pairs={{0,48},{4,20},{8,56},{12,28},{16,0},{20,36},{24,8},{28,44},{32,16}... | collective-permute-start | bytes 786440 | tf_op jit(solution)/shard_map/ppermute | solution.py:21
  128.2 9.8 %collective-permute-start.33 = (bf16[4,8,2048]{2,1,0:T(8,128)(2,1)S(1)}, bf16[4,8,2048]{2,1,0:T(8,128)(2,1)S(1)}, u32[]{:S(2)}, u32[]{:S(2)}) collective-permute-start(bf16[4,8,2048]{2,1,0:T(8,128)(2,1)S(1)} %slice.189), channel_id=1, source_target_pairs={{0,0},{4,36},{8,8},{12,44},{16,16},{20,52},{24,24},{28,60},{32,32}... | collective-permute-start | bytes 393224 | tf_op jit(solution)/shard_map/ppermute | solution.py:21
  135.1 5.3 %collective-permute-start.35 = (bf16[4,8,2048]{2,1,0:T(8,128)(2,1)S(1)}, bf16[4,8,2048]{2,1,0:T(8,128)(2,1)S(1)}, u32[]{:S(2)}, u32[]{:S(2)}) collective-permute-start(bf16[4,8,2048]{2,1,0:T(8,128)(2,1)S(1)} %fusion.7), channel_id=1, source_target_pairs={{0,56},{4,12},{8,0},{12,20},{16,8},{20,28},{24,16},{28,36},{32,24}... | collective-permute-start | bytes 393224 | tf_op jit(solution)/shard_map/ppermute | solution.py:21
  146.1 4.3 %collective-permute-start.39 = (f32[4,2048]{1,0:T(4,128)S(1)}, f32[4,2048]{1,0:T(4,128)S(1)}, u32[]{:S(2)}, u32[]{:S(2)}) collective-permute-start(f32[4,2048]{1,0:T(4,128)S(1)} %get-tuple-element.66), channel_id=1, source_target_pairs={{0,1},{1,2},{2,3},{3,0},{4,5},{5,6},{6,7},{7,4},{8,9},{9,10},{10,1... | collective-permute-start | bytes 98312 | tf_op jit(solution)/shard_map/ppermute | solution.py:13
  (11 other events, 100.5 us)

commit v3 on v2

--- a/solution.py
+++ b/solution.py
@@ -31,21 +31,6 @@
     return lax.optimization_barrier(values)
 
 
-def gather_z(pair):
-    near = along_z(pair, 1, -1)
-    base = along_z(pair, 0, 4)
-    far = along_z(jnp.concatenate([pair, near], axis=1), 2, -2)
-    return jnp.concatenate([base, near, far], axis=1)
-
-
-def scatter_z(sums):
-    n = sums.shape[1] // 4
-    far = along_z(sums[:, 2 * n :].astype(BF16), -2, 2).astype(F32)
-    base = along_z(sums[:, :n].astype(BF16), 0, 4).astype(F32)
-    near = along_z((sums[:, n : 2 * n] + far[:, n:]).astype(BF16), -1, 1).astype(F32)
-    return base + far[:, :n] + near
-
-
 def local(tokens, norm_gain, gate_weight, up_weight, down_weight):
     x, core = lax.axis_index("x"), lax.axis_index("c")
     gate_t, up_t = gate_weight.T, up_weight.T
@@ -62,10 +47,10 @@
     own = jnp.stack(
         [blocks[0]] + [shift(blocks[4 - r], "x", 4 - r) for r in (1, 2, 3)]
     )
-    plane = gather_z(lax.all_gather(own, "c", axis=1, tiled=True))
-    tall = plane.shape[1]
-    *first, own_plane = together(*first, plane)
-    first = jnp.concatenate(first, axis=0)
+    pair = lax.all_gather(own, "c", axis=1, tiled=True)
+    near, base = along_z(pair, 1, -1), along_z(pair, 0, 4)
+    far = along_z(jnp.concatenate([pair, near], axis=1), 2, -2)
+    near = jnp.concatenate([base, near], axis=1)
 
     def project(block):
         return lax.dot_general(
@@ -91,35 +76,57 @@
             preferred_element_type=F32,
         ).reshape(4, -1, part)
 
-    behind, ahead, opposite = (shift(plane, "y", k) for k in (1, 3, 2))
-    own_partial = project(own_plane)
-    own_sums = exchange(own_partial)
-    own_kept, behind, ahead = together(own_partial[0], behind, ahead)
+    def sum_over_y(blocks, received):
+        return sum((value.astype(F32) for value in received), blocks[0])
 
-    side_partial = project(jnp.concatenate([behind, ahead], axis=1))
-    side_sums = exchange(side_partial)
-    side_kept, *own_sums = together(side_partial[0], *own_sums)
-    own_hidden = activate(own_kept, own_sums)
-    own_spread = spread(own_hidden)
-    own_hidden, opposite = together(own_hidden, opposite)
+    def over_y(value):
+        return [shift(value, "y", k) for k in (1, 3, 2)]
 
-    far_partial = project(opposite)
+    def back_over_y(blocks):
+        return [shift(blocks[k].astype(BF16), "y", -k) for k in (1, 3, 2)]
+
+    def by_y(value):
+        return [value[:, k * slots : (k + 1) * slots] for k in range(4)]
+
+    slots = near.shape[1]
+    near_y = over_y(near)
+    *first, far_own = together(*first, far)
+    first = jnp.concatenate(first, axis=0)
+    far_y = over_y(far)
+
+    first, near_1, near_3, near_2 = together(first, *near_y)
+    near_partial = project(jnp.concatenate([near, near_1, near_2, near_3], axis=1))
+    near_sums = exchange(near_partial)
+    near_hidden = activate(near_partial[0], near_sums)
+    near_spread = spread(near_hidden)
+
+    near_hidden, far_1, far_3, far_2 = together(near_hidden, *far_y)
+    far_partial = project(jnp.concatenate([far_own, far_1, far_2, far_3], axis=1))
     far_sums = exchange(far_partial)
-    far_kept, *side_sums = together(far_partial[0], *side_sums)
-    side_hidden = activate(side_kept, side_sums)
-    side_spread = spread(side_hidden)
-    side_hidden, *far_sums = together(side_hidden, *far_sums)
+    far_kept, *near_spread = together(far_partial[0], *near_spread)
+
+    near_down = by_y(down([near_hidden] + near_spread))
+    near_back = back_over_y(near_down)
+    near_down[0], *far_sums = together(near_down[0], *far_sums)
     far_hidden = activate(far_kept, far_sums)
     far_spread = spread(far_hidden)
+    far_hidden, *near_back = together(far_hidden, *near_back)
 
-    own_down = down([own_hidden] + own_spread)
-    side_down = down([side_hidden] + side_spread)
-    far_down = down([far_hidden] + far_spread)
-    summed = own_down
-    for value, k in ((side_down[:, :tall], -1), (side_down[:, tall:], -3), (far_down, -2)):
-        summed = summed + shift(value.astype(BF16), "y", k).astype(F32)
-
-    pair = scatter_z(summed)
+    near_total = sum_over_y(near_down, near_back)
+    half = slots // 2
+    near_pieces = [
+        along_z(near_total[:, half:].astype(BF16), -1, 1),
+        along_z(near_total[:, :half].astype(BF16), 0, 4),
+    ]
+    far_down = by_y(down([far_hidden] + far_spread))
+    far_back = back_over_y(far_down)
+    *near_pieces, back_1, back_3, back_2 = together(*near_pieces, *far_back)
+    far_total = sum_over_y(far_down, (back_1, back_3, back_2))
+    far_pieces = [
+        along_z(far_total[:, half:].astype(BF16), -3, 3),
+        along_z(far_total[:, :half].astype(BF16), -2, 2),
+    ]
+    pair = sum(piece.astype(F32) for piece in near_pieces + far_pieces)
     low, high = pair[:, :rows], pair[:, rows:]
     mine = jnp.where(core == 0, low, high)
     other = jnp.where(core == 0, high, low).astype(BF16)

time: 154 us -> 131 us (0.85); the launches traced: 151 us -> 131 us
  waiting for transfers between devices: 59.8 us -> 50.3 us
  starting transfers between devices: 67.3 us -> 59.8 us
  local copies, waits for them, and re-layouts: 6.02 us -> 2.48 us
  other arithmetic: 3.86 us -> 7.31 us
  matrix products: 9.99 us -> 6.76 us
    ppermute x34, waiting for transfers between devices: 39 us -> 22.6 us  [shift(): return lax.ppermute(value, axis, [(i, (i + step) % n) for i in range(n)])]
    ppermute x34, starting transfers between devices: 55.4 us -> 46.9 us  [shift(): return lax.ppermute(value, axis, [(i, (i + step) % n) for i in range(n)])]
    ppermute x6 -> x7, waiting for transfers between devices: 20.8 us -> 27.7 us  [along_z(): return lax.ppermute(value, ('z', 'c'), pairs)]
    concatenate x2 -> x3, other arithmetic: 0.11 us -> 3.28 us  [the longest x1 3.17 us: local(): first = jnp.concatenate(first, axis=0)]
    dot_general x3 -> x2, matrix products: 7.21 us -> 4.23 us  [project(): lax.dot_general(block.reshape(-1, part), first, (((1,), (1,)), ((), ())),...]
    unnamed x12 -> x10, local copies, waits for them, and re-layouts: 3.67 us -> 1.77 us
    concatenate x2, local copies, waits for them, and re-layouts: 1.72 us -> 0.04 us  [the longest x1 0.02 us: local(): near = jnp.concatenate([base, near], axis=1)]
    ppermute x6 -> x7, starting transfers between devices: 11.8 us -> 12.9 us  [along_z(): return lax.ppermute(value, ('z', 'c'), pairs)]
  transfers between devices with their start and end apart: 40 -> 41, of which waited for: 23 -> 21; matrix products, arithmetic and copies ran while one was open for 12% -> 11% of each run, Pallas kernels for 0% -> 0%
where the time goes in v3:
time: 131 us
  starting transfers between devices  59.8 us (46%)
  waiting for transfers between devices  50.3 us (38%)
  other arithmetic  7.31 us (6%)
  matrix products  6.76 us (5%)
  blocking collectives  3.72 us (3%)
  local copies, waits for them, and re-layouts  2.48 us (2%)
    ppermute x34, starting transfers between devices, shift(): return lax.ppermute(value, axis, [(i, (i + step) % n) for i in range(n)])  46.9 us
    ppermute x7, waiting for transfers between devices, along_z(): return lax.ppermute(value, ('z', 'c'), pairs)  27.7 us
    ppermute x34, waiting for transfers between devices, shift(): return lax.ppermute(value, axis, [(i, (i + step) % n) for i in range(n)])  22.6 us
    ppermute x7, starting transfers between devices, along_z(): return lax.ppermute(value, ('z', 'c'), pairs)  12.9 us
    dot_general x2, matrix products, project(): lax.dot_general(block.reshape(-1, part), first, (((1,), (1,)), ((), ())),...  4.23 us
    all_gather x1, blocking collectives, local(): pair = lax.all_gather(own, 'c', axis=1, tiled=True)  3.72 us
    concatenate x1, other arithmetic, local(): first = jnp.concatenate(first, axis=0)  3.17 us
  transfers between devices with their start and end apart: 41, of which 21 were waited for; matrix products, arithmetic and copies ran while one was open for 11% of the time, Pallas kernels for 0%

profile of v3, /device:TPU:1, one launch (start us, length us, event | category | flops | bytes accessed | tf_op | source)
XLA Modules:
  0.0 130.8 jit_solution(8856417059227917154)
XLA Ops:
  0.0 3.2 %collective-permute-start.5 = (bf16[448,2048]{1,0:T(8,128)(2,1)}, bf16[448,2048]{1,0:T(8,128)(2,1)}, u32[]{:S(2)}, u32[]{:S(2)}) collective-permute-start(bf16[448,2048]{1,0:T(8,128)(2,1)} %bitcast.46), channel_id=1, source_target_pairs={{0,4},{4,0},{1,5},{5,1},{2,6},{6,2},{3,7},{7,3},{8,12},{12,8},{9,1... | collective-permute-start | bytes 5505032 | tf_op jit(solution)/shard_map/ppermute | solution.py:13
  8.2 1.7 %collective-permute-start.20 = (bf16[448,2048]{1,0:T(8,128)(2,1)}, bf16[448,2048]{1,0:T(8,128)(2,1)S(1)}, u32[]{:S(2)}, u32[]{:S(2)}) collective-permute-start(bf16[448,2048]{1,0:T(8,128)(2,1)} %param.9), channel_id=1, source_target_pairs={{0,4},{4,0},{1,5},{5,1},{2,6},{6,2},{3,7},{7,3},{8,12},{12,8},{9,1... | collective-permute-start | bytes 5505032 | tf_op jit(solution)/shard_map/ppermute | solution.py:13
  10.9 3.7 %all_gather.3 = bf16[4,8,2048]{2,0,1:T(4,128)(2,1)S(1)} all-gather(bf16[4,4,2048]{2,0,1:T(4,128)(2,1)S(1)} %copy.10), channel_id=1, replica_groups=mesh['y'=4,'z'=8,'c'=2,'x'=4] {'c'}, dimensions={1}, use_global_device_ids=true | all-gather | bytes 196608 | tf_op jit(solution)/shard_map/all_gather | solution.py:50
  14.7 5.7 %collective-permute-start.4 = (bf16[4,8,2048]{2,1,0:T(8,128)(2,1)S(1)}, bf16[4,8,2048]{2,1,0:T(8,128)(2,1)S(1)}, u32[]{:S(2)}, u32[]{:S(2)}) collective-permute-start(bf16[4,8,2048]{2,1,0:T(8,128)(2,1)S(1)} %copy.11), channel_id=1, source_target_pairs={{0,8},{4,60},{8,16},{12,4},{16,24},{20,12},{24,32},{28,20},{32,40}... | collective-permute-start | bytes 393224 | tf_op jit(solution)/shard_map/ppermute | solution.py:21
  20.3 1.7 %constant_dynamic-update-slice_fusion.8 = bf16[896,2048]{1,0:T(8,128)(2,1)S(1)} fusion(bf16[448,2048]{1,0:T(8,128)(2,1)} %param.9), kind=kLoop, calls=%fused_computation.62 | loop fusion | bytes 3670016
  22.0 3.3 %collective-permute-start.3 = (bf16[4,8,2048]{2,1,0:T(8,128)(2,1)S(1)}, bf16[4,8,2048]{2,1,0:T(8,128)(2,1)S(1)}, u32[]{:S(2)}, u32[]{:S(2)}) collective-permute-start(bf16[4,8,2048]{2,1,0:T(8,128)(2,1)S(1)} %copy.11), channel_id=1, source_target_pairs={{0,0},{4,36},{8,8},{12,44},{16,16},{20,52},{24,24},{28,60},{32,32}... | collective-permute-start | bytes 393224 | tf_op jit(solution)/shard_map/ppermute | solution.py:21
  25.4 11.0 %collective-permute-done.3 = bf16[4,8,2048]{2,1,0:T(8,128)(2,1)S(1)} collective-permute-done((bf16[4,8,2048]{2,1,0:T(8,128)(2,1)S(1)}, bf16[4,8,2048]{2,1,0:T(8,128)(2,1)S(1)}, u32[]{:S(2)}, u32[]{:S(2)}) %collective-permute-start.3) | collective-permute-done | bytes 131104 | tf_op jit(solution)/shard_map/ppermute | solution.py:21
  36.4 3.0 %collective-permute-start.10 = (bf16[4,16,2048]{2,1,0:T(8,128)(2,1)S(1)}, bf16[4,16,2048]{2,1,0:T(8,128)(2,1)S(1)}, u32[]{:S(2)}, u32[]{:S(2)}) collective-permute-start(bf16[4,16,2048]{2,1,0:T(8,128)(2,1)S(1)} %get-tuple-element.88), channel_id=1, source_target_pairs={{0,128},{64,192},{128,0},{192,64},{1,129},{65,193},{129,1},{193,65... | collective-permute-start | bytes 786440 | tf_op jit(solution)/shard_map/ppermute | solution.py:13
  39.8 2.3 %collective-permute-start.9 = (bf16[4,16,2048]{2,1,0:T(8,128)(2,1)S(1)}, bf16[4,16,2048]{2,1,0:T(8,128)(2,1)S(1)}, u32[]{:S(2)}, u32[]{:S(2)}) collective-permute-start(bf16[4,16,2048]{2,1,0:T(8,128)(2,1)S(1)} %get-tuple-element.88), channel_id=1, source_target_pairs={{0,192},{64,0},{128,64},{192,128},{1,193},{65,1},{129,65},{193,129... | collective-permute-start | bytes 786440 | tf_op jit(solution)/shard_map/ppermute | solution.py:13
  42.1 3.2 %pad_maximum_fusion = bf16[1792,2048]{1,0:T(8,128)(2,1)S(1)} fusion(bf16[448,2048]{1,0:T(8,128)(2,1)} %collective-permute-done.6, bf16[448,2048]{1,0:T(8,128)(2,1)S(1)} %bitcast.45, bf16[448,2048]{1,0:T(8,128)(2,1)} %collective-permute-done.5, bf16[448,2048]{1,0:T(8,128)(2,1)S(1)} %bitcast.47), kind=kLoop, calls=%fused_computation | loop fusion | flops 29360128 | bytes 14680064 | tf_op jit(solution)/shard_map/concatenate | solution.py:94
  45.8 2.4 %collective-permute-start.15 = (bf16[4,16,2048]{2,1,0:T(8,128)(2,1)S(1)}, bf16[4,16,2048]{2,1,0:T(8,128)(2,1)S(1)}, u32[]{:S(2)}, u32[]{:S(2)}) collective-permute-start(bf16[4,16,2048]{2,1,0:T(8,128)(2,1)S(1)} %collective-permute-done.7), channel_id=1, source_target_pairs={{0,192},{64,0},{128,64},{192,128},{1,193},{65,1},{129,65},{193,129... | collective-permute-start | bytes 786440 | tf_op jit(solution)/shard_map/ppermute | solution.py:13
  48.2 2.2 %collective-permute-done.8 = bf16[4,16,2048]{2,1,0:T(8,128)(2,1)S(1)} collective-permute-done((bf16[4,16,2048]{2,1,0:T(8,128)(2,1)S(1)}, bf16[4,16,2048]{2,1,0:T(8,128)(2,1)S(1)}, u32[]{:S(2)}, u32[]{:S(2)}) %collective-permute-start.8) | collective-permute-done | bytes 262176 | tf_op jit(solution)/shard_map/ppermute | solution.py:13
  51.5 2.1 %fusion.37 = (bf16[256,1792]{1,0:T(8,128)(2,1)S(1)}, f32[256,1792]{1,0:T(8,128)S(1)}) fusion(bf16[256,2048]{1,0:T(8,128)(2,1)S(1)} %bitcast.50, bf16[1792,2048]{1,0:T(8,128)(2,1)S(1)} %pad_maximum_fusion), kind=kOutput, calls=%fused_computation.76 | convolution fusion | flops 1879506944 | bytes 11141120 | tf_op jit(solution)/shard_map/dot_general | solution.py:56
  55.5 2.4 %collective-permute-start.13 = (bf16[64,1792]{1,0:T(8,128)(2,1)S(1)}, bf16[64,1792]{1,0:T(8,128)(2,1)S(1)}, u32[]{:S(2)}, u32[]{:S(2)}) collective-permute-start(bf16[64,1792]{1,0:T(8,128)(2,1)S(1)} %get-tuple-element.75), channel_id=1, source_target_pairs={{0,3},{1,0},{2,1},{3,2},{4,7},{5,4},{6,5},{7,6},{8,11},{9,8},{10,9... | collective-permute-start | bytes 688136 | tf_op jit(solution)/shard_map/ppermute | solution.py:13
  58.1 2.8 %collective-permute-done.11 = bf16[64,1792]{1,0:T(8,128)(2,1)S(1)} collective-permute-done((bf16[64,1792]{1,0:T(8,128)(2,1)S(1)}, bf16[64,1792]{1,0:T(8,128)(2,1)S(1)}, u32[]{:S(2)}, u32[]{:S(2)}) %collective-permute-start.11) | collective-permute-done | bytes 229408 | tf_op jit(solution)/shard_map/ppermute | solution.py:13
  60.9 2.7 %collective-permute-start.16 = (bf16[4,16,2048]{2,1,0:T(8,128)(2,1)S(1)}, bf16[4,16,2048]{2,1,0:T(8,128)(2,1)S(1)}, u32[]{:S(2)}, u32[]{:S(2)}) collective-permute-start(bf16[4,16,2048]{2,1,0:T(8,128)(2,1)S(1)} %collective-permute-done.7), channel_id=1, source_target_pairs={{0,128},{64,192},{128,0},{192,64},{1,129},{65,193},{129,1},{193,65... | collective-permute-start | bytes 786440 | tf_op jit(solution)/shard_map/ppermute | solution.py:13
  66.0 1.6 %collective-permute-done.16 = bf16[4,16,2048]{2,1,0:T(8,128)(2,1)S(1)} collective-permute-done((bf16[4,16,2048]{2,1,0:T(8,128)(2,1)S(1)}, bf16[4,16,2048]{2,1,0:T(8,128)(2,1)S(1)}, u32[]{:S(2)}, u32[]{:S(2)}) %collective-permute-start.16) | collective-permute-done | bytes 262176 | tf_op jit(solution)/shard_map/ppermute | solution.py:13
  67.8 2.1 %fusion.38 = (bf16[256,1792]{1,0:T(8,128)(2,1)S(1)}, f32[256,1792]{1,0:T(8,128)S(1)}) fusion(bf16[256,2048]{1,0:T(8,128)(2,1)S(1)} %bitcast.48, bf16[1792,2048]{1,0:T(8,128)(2,1)S(1)} %pad_maximum_fusion), kind=kOutput, calls=%fused_computation.77 | convolution fusion | flops 1879506944 | bytes 11141120 | tf_op jit(solution)/shard_map/dot_general | solution.py:56
  71.9 2.1 %collective-permute-start.23 = (bf16[64,1792]{1,0:T(8,128)(2,1)S(1)}, bf16[64,1792]{1,0:T(8,128)(2,1)S(1)}, u32[]{:S(2)}, u32[]{:S(2)}) collective-permute-start(bf16[64,1792]{1,0:T(8,128)(2,1)S(1)} %get-tuple-element.71), channel_id=1, source_target_pairs={{0,3},{1,0},{2,1},{3,2},{4,7},{5,4},{6,5},{7,6},{8,11},{9,8},{10,9... | collective-permute-start | bytes 688136 | tf_op jit(solution)/shard_map/ppermute | solution.py:13
  75.5 3.3 %collective-permute-start.24 = (bf16[4,16,2048]{2,1,0:T(8,128)(2,1)S(1)}, bf16[4,16,2048]{2,1,0:T(8,128)(2,1)S(1)}, u32[]{:S(2)}, u32[]{:S(2)}) collective-permute-start(bf16[4,16,2048]{2,1,0:T(8,128)(2,1)S(1)} %get-tuple-element.70), channel_id=1, source_target_pairs={{0,192},{64,0},{128,64},{192,128},{1,193},{65,1},{129,65},{193,129... | collective-permute-start | bytes 786440 | tf_op jit(solution)/shard_map/ppermute | solution.py:13
  79.1 2.6 %collective-permute-start.26 = (bf16[4,16,2048]{2,1,0:T(8,128)(2,1)S(1)}, bf16[4,16,2048]{2,1,0:T(8,128)(2,1)S(1)}, u32[]{:S(2)}, u32[]{:S(2)}) collective-permute-start(bf16[4,16,2048]{2,1,0:T(8,128)(2,1)S(1)} %get-tuple-element.68), channel_id=1, source_target_pairs={{0,128},{64,192},{128,0},{192,64},{1,129},{65,193},{129,1},{193,65... | collective-permute-start | bytes 786440 | tf_op jit(solution)/shard_map/ppermute | solution.py:13
  81.8 2.0 %collective-permute-done.22 = bf16[64,1792]{1,0:T(8,128)(2,1)S(1)} collective-permute-done((bf16[64,1792]{1,0:T(8,128)(2,1)S(1)}, bf16[64,1792]{1,0:T(8,128)(2,1)S(1)}, u32[]{:S(2)}, u32[]{:S(2)}) %collective-permute-start.22) | collective-permute-done | bytes 229408 | tf_op jit(solution)/shard_map/ppermute | solution.py:13
  84.7 2.1 %collective-permute-start.30 = (bf16[64,896]{1,0:T(8,128)(2,1)S(1)}, bf16[64,896]{1,0:T(8,128)(2,1)S(1)}, u32[]{:S(2)}, u32[]{:S(2)}) collective-permute-start(bf16[64,896]{1,0:T(8,128)(2,1)S(1)} %fusion.21), channel_id=1, source_target_pairs={{0,2},{1,3},{2,0},{3,1},{4,6},{5,7},{6,4},{7,5},{8,10},{9,11},{10,... | collective-permute-start | bytes 344072 | tf_op jit(solution)/shard_map/ppermute | solution.py:13
  88.2 3.0 %collective-permute-done.26 = bf16[4,16,2048]{2,1,0:T(8,128)(2,1)S(1)} collective-permute-done((bf16[4,16,2048]{2,1,0:T(8,128)(2,1)S(1)}, bf16[4,16,2048]{2,1,0:T(8,128)(2,1)S(1)}, u32[]{:S(2)}, u32[]{:S(2)}) %collective-permute-start.26) | collective-permute-done | bytes 262176 | tf_op jit(solution)/shard_map/ppermute | solution.py:13
  94.2 3.5 %collective-permute-start.32 = (bf16[4,16,2048]{2,1,0:T(8,128)(2,1)S(1)}, bf16[4,16,2048]{2,1,0:T(8,128)(2,1)S(1)}, u32[]{:S(2)}, u32[]{:S(2)}) collective-permute-start(bf16[4,16,2048]{2,1,0:T(8,128)(2,1)S(1)} %get-tuple-element.67), channel_id=1, source_target_pairs={{0,192},{64,0},{128,64},{192,128},{1,193},{65,1},{129,65},{193,129... | collective-permute-start | bytes 786440 | tf_op jit(solution)/shard_map/ppermute | solution.py:13
  98.6 1.7 %collective-permute-start.34 = (bf16[4,16,2048]{2,1,0:T(8,128)(2,1)S(1)}, bf16[4,16,2048]{2,1,0:T(8,128)(2,1)S(1)}, u32[]{:S(2)}, u32[]{:S(2)}) collective-permute-start(bf16[4,16,2048]{2,1,0:T(8,128)(2,1)S(1)} %get-tuple-element.65), channel_id=1, source_target_pairs={{0,128},{64,192},{128,0},{192,64},{1,129},{65,193},{129,1},{193,65... | collective-permute-start | bytes 786440 | tf_op jit(solution)/shard_map/ppermute | solution.py:13
  100.5 2.2 %collective-permute-start.28 = (bf16[4,8,2048]{2,1,0:T(8,128)(2,1)S(1)}, bf16[4,8,2048]{2,1,0:T(8,128)(2,1)S(1)}, u32[]{:S(2)}, u32[]{:S(2)}) collective-permute-start(bf16[4,8,2048]{2,1,0:T(8,128)(2,1)S(1)} %get-tuple-element.79), channel_id=1, source_target_pairs={{0,0},{4,36},{8,8},{12,44},{16,16},{20,52},{24,24},{28,60},{32,32}... | collective-permute-start | bytes 393224 | tf_op jit(solution)/shard_map/ppermute | solution.py:21
  102.7 4.2 %collective-permute-done.27 = bf16[4,8,2048]{2,1,0:T(8,128)(2,1)S(1)} collective-permute-done((bf16[4,8,2048]{2,1,0:T(8,128)(2,1)S(1)}, bf16[4,8,2048]{2,1,0:T(8,128)(2,1)S(1)}, u32[]{:S(2)}, u32[]{:S(2)}) %collective-permute-start.27) | collective-permute-done | bytes 131104 | tf_op jit(solution)/shard_map/ppermute | solution.py:21
  107.0 3.2 %collective-permute-done.28 = bf16[4,8,2048]{2,1,0:T(8,128)(2,1)S(1)} collective-permute-done((bf16[4,8,2048]{2,1,0:T(8,128)(2,1)S(1)}, bf16[4,8,2048]{2,1,0:T(8,128)(2,1)S(1)}, u32[]{:S(2)}, u32[]{:S(2)}) %collective-permute-start.28) | collective-permute-done | bytes 131104 | tf_op jit(solution)/shard_map/ppermute | solution.py:21
  110.3 1.7 %collective-permute-start.35 = (bf16[4,8,2048]{2,1,0:T(8,128)(2,1)S(1)}, bf16[4,8,2048]{2,1,0:T(8,128)(2,1)S(1)}, u32[]{:S(2)}, u32[]{:S(2)}) collective-permute-start(bf16[4,8,2048]{2,1,0:T(8,128)(2,1)S(1)} %get-tuple-element.77), channel_id=1, source_target_pairs={{0,40},{4,28},{8,48},{12,36},{16,56},{20,44},{24,0},{28,52},{32,8}... | collective-permute-start | bytes 393224 | tf_op jit(solution)/shard_map/ppermute | solution.py:21
  112.0 8.2 %collective-permute-done.35 = bf16[4,8,2048]{2,1,0:T(8,128)(2,1)S(1)} collective-permute-done((bf16[4,8,2048]{2,1,0:T(8,128)(2,1)S(1)}, bf16[4,8,2048]{2,1,0:T(8,128)(2,1)S(1)}, u32[]{:S(2)}, u32[]{:S(2)}) %collective-permute-start.35) | collective-permute-done | bytes 131104 | tf_op jit(solution)/shard_map/ppermute | solution.py:21
  121.4 2.0 %collective-permute-start.37 = (bf16[4,4,2048]{2,1,0:T(4,128)(2,1)S(1)}, bf16[4,4,2048]{2,1,0:T(4,128)(2,1)S(1)}, u32[]{:S(2)}, u32[]{:S(2)}) collective-permute-start(bf16[4,4,2048]{2,1,0:T(4,128)(2,1)S(1)} %select_convert_fusion), channel_id=1, source_target_pairs={{0,4},{4,0},{1,5},{5,1},{2,6},{6,2},{3,7},{7,3},{8,12},{12,8},{9,1... | collective-permute-start | bytes 196616 | tf_op jit(solution)/shard_map/ppermute | solution.py:13
  (101 shorter events, 31.6 us)
Async XLA Ops:
  0.0 39.8 %collective-permute-start.5 = (bf16[448,2048]{1,0:T(8,128)(2,1)}, bf16[448,2048]{1,0:T(8,128)(2,1)}, u32[]{:S(2)}, u32[]{:S(2)}) collective-permute-start(bf16[448,2048]{1,0:T(8,128)(2,1)} %bitcast.46), channel_id=1, source_target_pairs={{0,4},{4,0},{1,5},{5,1},{2,6},{6,2},{3,7},{7,3},{8,12},{12,8},{9,1... | collective-permute-start | bytes 5505032 | tf_op jit(solution)/shard_map/ppermute | solution.py:13
  3.2 38.9 %collective-permute-start.6 = (bf16[448,2048]{1,0:T(8,128)(2,1)}, bf16[448,2048]{1,0:T(8,128)(2,1)}, u32[]{:S(2)}, u32[]{:S(2)}) collective-permute-start(bf16[448,2048]{1,0:T(8,128)(2,1)} %bitcast.44), channel_id=1, source_target_pairs={{0,4},{4,0},{1,5},{5,1},{2,6},{6,2},{3,7},{7,3},{8,12},{12,8},{9,1... | collective-permute-start | bytes 5505032 | tf_op jit(solution)/shard_map/ppermute | solution.py:13
  8.2 47.3 %collective-permute-start.20 = (bf16[448,2048]{1,0:T(8,128)(2,1)}, bf16[448,2048]{1,0:T(8,128)(2,1)S(1)}, u32[]{:S(2)}, u32[]{:S(2)}) collective-permute-start(bf16[448,2048]{1,0:T(8,128)(2,1)} %param.9), channel_id=1, source_target_pairs={{0,4},{4,0},{1,5},{5,1},{2,6},{6,2},{3,7},{7,3},{8,12},{12,8},{9,1... | collective-permute-start | bytes 5505032 | tf_op jit(solution)/shard_map/ppermute | solution.py:13
  14.7 10.6 %collective-permute-start.4 = (bf16[4,8,2048]{2,1,0:T(8,128)(2,1)S(1)}, bf16[4,8,2048]{2,1,0:T(8,128)(2,1)S(1)}, u32[]{:S(2)}, u32[]{:S(2)}) collective-permute-start(bf16[4,8,2048]{2,1,0:T(8,128)(2,1)S(1)} %copy.11), channel_id=1, source_target_pairs={{0,8},{4,60},{8,16},{12,4},{16,24},{20,12},{24,32},{28,20},{32,40}... | collective-permute-start | bytes 393224 | tf_op jit(solution)/shard_map/ppermute | solution.py:21
  22.0 14.4 %collective-permute-start.3 = (bf16[4,8,2048]{2,1,0:T(8,128)(2,1)S(1)}, bf16[4,8,2048]{2,1,0:T(8,128)(2,1)S(1)}, u32[]{:S(2)}, u32[]{:S(2)}) collective-permute-start(bf16[4,8,2048]{2,1,0:T(8,128)(2,1)S(1)} %copy.11), channel_id=1, source_target_pairs={{0,0},{4,36},{8,8},{12,44},{16,16},{20,52},{24,24},{28,60},{32,32}... | collective-permute-start | bytes 393224 | tf_op jit(solution)/shard_map/ppermute | solution.py:21
  25.3 14.1 %collective-permute-start.7 = (bf16[4,16,2048]{2,1,0:T(8,128)(2,1)S(1)}, bf16[4,16,2048]{2,1,0:T(8,128)(2,1)S(1)}, u32[]{:S(2)}, u32[]{:S(2)}) collective-permute-start(bf16[4,16,2048]{2,1,0:T(8,128)(2,1)S(1)} %pad_maximum_fusion.2), channel_id=1, source_target_pairs={{0,16},{4,52},{8,24},{12,60},{16,32},{20,4},{24,40},{28,12},{32,48... | collective-permute-start | bytes 786440 | tf_op jit(solution)/shard_map/ppermute | solution.py:21
  36.4 9.4 %collective-permute-start.10 = (bf16[4,16,2048]{2,1,0:T(8,128)(2,1)S(1)}, bf16[4,16,2048]{2,1,0:T(8,128)(2,1)S(1)}, u32[]{:S(2)}, u32[]{:S(2)}) collective-permute-start(bf16[4,16,2048]{2,1,0:T(8,128)(2,1)S(1)} %get-tuple-element.88), channel_id=1, source_target_pairs={{0,128},{64,192},{128,0},{192,64},{1,129},{65,193},{129,1},{193,65... | collective-permute-start | bytes 786440 | tf_op jit(solution)/shard_map/ppermute | solution.py:13
  39.4 11.0 %collective-permute-start.8 = (bf16[4,16,2048]{2,1,0:T(8,128)(2,1)S(1)}, bf16[4,16,2048]{2,1,0:T(8,128)(2,1)S(1)}, u32[]{:S(2)}, u32[]{:S(2)}) collective-permute-start(bf16[4,16,2048]{2,1,0:T(8,128)(2,1)S(1)} %get-tuple-element.88), channel_id=1, source_target_pairs={{0,64},{64,128},{128,192},{192,0},{1,65},{65,129},{129,193},{193,1... | collective-permute-start | bytes 786440 | tf_op jit(solution)/shard_map/ppermute | solution.py:13
  39.8 11.6 %collective-permute-start.9 = (bf16[4,16,2048]{2,1,0:T(8,128)(2,1)S(1)}, bf16[4,16,2048]{2,1,0:T(8,128)(2,1)S(1)}, u32[]{:S(2)}, u32[]{:S(2)}) collective-permute-start(bf16[4,16,2048]{2,1,0:T(8,128)(2,1)S(1)} %get-tuple-element.88), channel_id=1, source_target_pairs={{0,192},{64,0},{128,64},{192,128},{1,193},{65,1},{129,65},{193,129... | collective-permute-start | bytes 786440 | tf_op jit(solution)/shard_map/ppermute | solution.py:13
  42.1 23.3 %collective-permute-start.14 = (bf16[4,16,2048]{2,1,0:T(8,128)(2,1)S(1)}, bf16[4,16,2048]{2,1,0:T(8,128)(2,1)S(1)}, u32[]{:S(2)}, u32[]{:S(2)}) collective-permute-start(bf16[4,16,2048]{2,1,0:T(8,128)(2,1)S(1)} %collective-permute-done.7), channel_id=1, source_target_pairs={{0,64},{64,128},{128,192},{192,0},{1,65},{65,129},{129,193},{193,1... | collective-permute-start | bytes 786440 | tf_op jit(solution)/shard_map/ppermute | solution.py:13
  45.8 20.2 %collective-permute-start.15 = (bf16[4,16,2048]{2,1,0:T(8,128)(2,1)S(1)}, bf16[4,16,2048]{2,1,0:T(8,128)(2,1)S(1)}, u32[]{:S(2)}, u32[]{:S(2)}) collective-permute-start(bf16[4,16,2048]{2,1,0:T(8,128)(2,1)S(1)} %collective-permute-done.7), channel_id=1, source_target_pairs={{0,192},{64,0},{128,64},{192,128},{1,193},{65,1},{129,65},{193,129... | collective-permute-start | bytes 786440 | tf_op jit(solution)/shard_map/ppermute | solution.py:13
  53.7 7.2 %collective-permute-start.11 = (bf16[64,1792]{1,0:T(8,128)(2,1)S(1)}, bf16[64,1792]{1,0:T(8,128)(2,1)S(1)}, u32[]{:S(2)}, u32[]{:S(2)}) collective-permute-start(bf16[64,1792]{1,0:T(8,128)(2,1)S(1)} %get-tuple-element.74), channel_id=1, source_target_pairs={{0,2},{1,3},{2,0},{3,1},{4,6},{5,7},{6,4},{7,5},{8,10},{9,11},{10,... | collective-permute-start | bytes 688136 | tf_op jit(solution)/shard_map/ppermute | solution.py:13
  55.2 8.4 %collective-permute-start.12 = (bf16[64,1792]{1,0:T(8,128)(2,1)S(1)}, bf16[64,1792]{1,0:T(8,128)(2,1)S(1)}, u32[]{:S(2)}, u32[]{:S(2)}) collective-permute-start(bf16[64,1792]{1,0:T(8,128)(2,1)S(1)} %get-tuple-element.76), channel_id=1, source_target_pairs={{0,1},{1,2},{2,3},{3,0},{4,5},{5,6},{6,7},{7,4},{8,9},{9,10},{10,1... | collective-permute-start | bytes 688136 | tf_op jit(solution)/shard_map/ppermute | solution.py:13
  55.5 8.1 %collective-permute-start.13 = (bf16[64,1792]{1,0:T(8,128)(2,1)S(1)}, bf16[64,1792]{1,0:T(8,128)(2,1)S(1)}, u32[]{:S(2)}, u32[]{:S(2)}) collective-permute-start(bf16[64,1792]{1,0:T(8,128)(2,1)S(1)} %get-tuple-element.75), channel_id=1, source_target_pairs={{0,3},{1,0},{2,1},{3,2},{4,7},{5,4},{6,5},{7,6},{8,11},{9,8},{10,9... | collective-permute-start | bytes 688136 | tf_op jit(solution)/shard_map/ppermute | solution.py:13
  60.9 6.7 %collective-permute-start.16 = (bf16[4,16,2048]{2,1,0:T(8,128)(2,1)S(1)}, bf16[4,16,2048]{2,1,0:T(8,128)(2,1)S(1)}, u32[]{:S(2)}, u32[]{:S(2)}) collective-permute-start(bf16[4,16,2048]{2,1,0:T(8,128)(2,1)S(1)} %collective-permute-done.7), channel_id=1, source_target_pairs={{0,128},{64,192},{128,0},{192,64},{1,129},{65,193},{129,1},{193,65... | collective-permute-start | bytes 786440 | tf_op jit(solution)/shard_map/ppermute | solution.py:13
  63.8 8.2 %collective-permute-start.17 = (bf16[64,896]{1,0:T(8,128)(2,1)S(1)}, bf16[64,896]{1,0:T(8,128)(2,1)S(1)}, u32[]{:S(2)}, u32[]{:S(2)}) collective-permute-start(bf16[64,896]{1,0:T(8,128)(2,1)S(1)} %fusion.22), channel_id=1, source_target_pairs={{0,3},{1,0},{2,1},{3,2},{4,7},{5,4},{6,5},{7,6},{8,11},{9,8},{10,9... | collective-permute-start | bytes 344072 | tf_op jit(solution)/shard_map/ppermute | solution.py:13
  65.3 8.7 %collective-permute-start.18 = (bf16[64,896]{1,0:T(8,128)(2,1)S(1)}, bf16[64,896]{1,0:T(8,128)(2,1)S(1)}, u32[]{:S(2)}, u32[]{:S(2)}) collective-permute-start(bf16[64,896]{1,0:T(8,128)(2,1)S(1)} %fusion.22), channel_id=1, source_target_pairs={{0,2},{1,3},{2,0},{3,1},{4,6},{5,7},{6,4},{7,5},{8,10},{9,11},{10,... | collective-permute-start | bytes 344072 | tf_op jit(solution)/shard_map/ppermute | solution.py:13
  65.4 8.6 %collective-permute-start.19 = (bf16[64,896]{1,0:T(8,128)(2,1)S(1)}, bf16[64,896]{1,0:T(8,128)(2,1)S(1)}, u32[]{:S(2)}, u32[]{:S(2)}) collective-permute-start(bf16[64,896]{1,0:T(8,128)(2,1)S(1)} %fusion.22), channel_id=1, source_target_pairs={{0,1},{1,2},{2,3},{3,0},{4,5},{5,6},{6,7},{7,4},{8,9},{9,10},{10,1... | collective-permute-start | bytes 344072 | tf_op jit(solution)/shard_map/ppermute | solution.py:13
  70.0 9.1 %collective-permute-start.21 = (bf16[64,1792]{1,0:T(8,128)(2,1)S(1)}, bf16[64,1792]{1,0:T(8,128)(2,1)S(1)}, u32[]{:S(2)}, u32[]{:S(2)}) collective-permute-start(bf16[64,1792]{1,0:T(8,128)(2,1)S(1)} %get-tuple-element.73), channel_id=1, source_target_pairs={{0,2},{1,3},{2,0},{3,1},{4,6},{5,7},{6,4},{7,5},{8,10},{9,11},{10,... | collective-permute-start | bytes 688136 | tf_op jit(solution)/shard_map/ppermute | solution.py:13
  71.3 12.4 %collective-permute-start.22 = (bf16[64,1792]{1,0:T(8,128)(2,1)S(1)}, bf16[64,1792]{1,0:T(8,128)(2,1)S(1)}, u32[]{:S(2)}, u32[]{:S(2)}) collective-permute-start(bf16[64,1792]{1,0:T(8,128)(2,1)S(1)} %get-tuple-element.72), channel_id=1, source_target_pairs={{0,1},{1,2},{2,3},{3,0},{4,5},{5,6},{6,7},{7,4},{8,9},{9,10},{10,1... | collective-permute-start | bytes 688136 | tf_op jit(solution)/shard_map/ppermute | solution.py:13
  71.9 11.8 %collective-permute-start.23 = (bf16[64,1792]{1,0:T(8,128)(2,1)S(1)}, bf16[64,1792]{1,0:T(8,128)(2,1)S(1)}, u32[]{:S(2)}, u32[]{:S(2)}) collective-permute-start(bf16[64,1792]{1,0:T(8,128)(2,1)S(1)} %get-tuple-element.71), channel_id=1, source_target_pairs={{0,3},{1,0},{2,1},{3,2},{4,7},{5,4},{6,5},{7,6},{8,11},{9,8},{10,9... | collective-permute-start | bytes 688136 | tf_op jit(solution)/shard_map/ppermute | solution.py:13
  75.5 11.2 %collective-permute-start.24 = (bf16[4,16,2048]{2,1,0:T(8,128)(2,1)S(1)}, bf16[4,16,2048]{2,1,0:T(8,128)(2,1)S(1)}, u32[]{:S(2)}, u32[]{:S(2)}) collective-permute-start(bf16[4,16,2048]{2,1,0:T(8,128)(2,1)S(1)} %get-tuple-element.70), channel_id=1, source_target_pairs={{0,192},{64,0},{128,64},{192,128},{1,193},{65,1},{129,65},{193,129... | collective-permute-start | bytes 786440 | tf_op jit(solution)/shard_map/ppermute | solution.py:13
  78.9 9.3 %collective-permute-start.25 = (bf16[4,16,2048]{2,1,0:T(8,128)(2,1)S(1)}, bf16[4,16,2048]{2,1,0:T(8,128)(2,1)S(1)}, u32[]{:S(2)}, u32[]{:S(2)}) collective-permute-start(bf16[4,16,2048]{2,1,0:T(8,128)(2,1)S(1)} %get-tuple-element.69), channel_id=1, source_target_pairs={{0,64},{64,128},{128,192},{192,0},{1,65},{65,129},{129,193},{193,1... | collective-permute-start | bytes 786440 | tf_op jit(solution)/shard_map/ppermute | solution.py:13
  79.1 12.1 %collective-permute-start.26 = (bf16[4,16,2048]{2,1,0:T(8,128)(2,1)S(1)}, bf16[4,16,2048]{2,1,0:T(8,128)(2,1)S(1)}, u32[]{:S(2)}, u32[]{:S(2)}) collective-permute-start(bf16[4,16,2048]{2,1,0:T(8,128)(2,1)S(1)} %get-tuple-element.68), channel_id=1, source_target_pairs={{0,128},{64,192},{128,0},{192,64},{1,129},{65,193},{129,1},{193,65... | collective-permute-start | bytes 786440 | tf_op jit(solution)/shard_map/ppermute | solution.py:13
  83.9 7.3 %collective-permute-start.29 = (bf16[64,896]{1,0:T(8,128)(2,1)S(1)}, bf16[64,896]{1,0:T(8,128)(2,1)S(1)}, u32[]{:S(2)}, u32[]{:S(2)}) collective-permute-start(bf16[64,896]{1,0:T(8,128)(2,1)S(1)} %fusion.21), channel_id=1, source_target_pairs={{0,3},{1,0},{2,1},{3,2},{4,7},{5,4},{6,5},{7,6},{8,11},{9,8},{10,9... | collective-permute-start | bytes 344072 | tf_op jit(solution)/shard_map/ppermute | solution.py:13
  84.7 6.5 %collective-permute-start.30 = (bf16[64,896]{1,0:T(8,128)(2,1)S(1)}, bf16[64,896]{1,0:T(8,128)(2,1)S(1)}, u32[]{:S(2)}, u32[]{:S(2)}) collective-permute-start(bf16[64,896]{1,0:T(8,128)(2,1)S(1)} %fusion.21), channel_id=1, source_target_pairs={{0,2},{1,3},{2,0},{3,1},{4,6},{5,7},{6,4},{7,5},{8,10},{9,11},{10,... | collective-permute-start | bytes 344072 | tf_op jit(solution)/shard_map/ppermute | solution.py:13
  94.2 16.0 %collective-permute-start.32 = (bf16[4,16,2048]{2,1,0:T(8,128)(2,1)S(1)}, bf16[4,16,2048]{2,1,0:T(8,128)(2,1)S(1)}, u32[]{:S(2)}, u32[]{:S(2)}) collective-permute-start(bf16[4,16,2048]{2,1,0:T(8,128)(2,1)S(1)} %get-tuple-element.67), channel_id=1, source_target_pairs={{0,192},{64,0},{128,64},{192,128},{1,193},{65,1},{129,65},{193,129... | collective-permute-start | bytes 786440 | tf_op jit(solution)/shard_map/ppermute | solution.py:13
  97.7 12.4 %collective-permute-start.33 = (bf16[4,16,2048]{2,1,0:T(8,128)(2,1)S(1)}, bf16[4,16,2048]{2,1,0:T(8,128)(2,1)S(1)}, u32[]{:S(2)}, u32[]{:S(2)}) collective-permute-start(bf16[4,16,2048]{2,1,0:T(8,128)(2,1)S(1)} %get-tuple-element.66), channel_id=1, source_target_pairs={{0,64},{64,128},{128,192},{192,0},{1,65},{65,129},{129,193},{193,1... | collective-permute-start | bytes 786440 | tf_op jit(solution)/shard_map/ppermute | solution.py:13
  98.6 11.6 %collective-permute-start.34 = (bf16[4,16,2048]{2,1,0:T(8,128)(2,1)S(1)}, bf16[4,16,2048]{2,1,0:T(8,128)(2,1)S(1)}, u32[]{:S(2)}, u32[]{:S(2)}) collective-permute-start(bf16[4,16,2048]{2,1,0:T(8,128)(2,1)S(1)} %get-tuple-element.65), channel_id=1, source_target_pairs={{0,128},{64,192},{128,0},{192,64},{1,129},{65,193},{129,1},{193,65... | collective-permute-start | bytes 786440 | tf_op jit(solution)/shard_map/ppermute | solution.py:13
  100.5 9.6 %collective-permute-start.28 = (bf16[4,8,2048]{2,1,0:T(8,128)(2,1)S(1)}, bf16[4,8,2048]{2,1,0:T(8,128)(2,1)S(1)}, u32[]{:S(2)}, u32[]{:S(2)}) collective-permute-start(bf16[4,8,2048]{2,1,0:T(8,128)(2,1)S(1)} %get-tuple-element.79), channel_id=1, source_target_pairs={{0,0},{4,36},{8,8},{12,44},{16,16},{20,52},{24,24},{28,60},{32,32}... | collective-permute-start | bytes 393224 | tf_op jit(solution)/shard_map/ppermute | solution.py:21
  110.3 9.8 %collective-permute-start.35 = (bf16[4,8,2048]{2,1,0:T(8,128)(2,1)S(1)}, bf16[4,8,2048]{2,1,0:T(8,128)(2,1)S(1)}, u32[]{:S(2)}, u32[]{:S(2)}) collective-permute-start(bf16[4,8,2048]{2,1,0:T(8,128)(2,1)S(1)} %get-tuple-element.77), channel_id=1, source_target_pairs={{0,40},{4,28},{8,48},{12,36},{16,56},{20,44},{24,0},{28,52},{32,8}... | collective-permute-start | bytes 393224 | tf_op jit(solution)/shard_map/ppermute | solution.py:21
  112.0 9.3 %collective-permute-start.36 = (bf16[4,8,2048]{2,1,0:T(8,128)(2,1)S(1)}, bf16[4,8,2048]{2,1,0:T(8,128)(2,1)S(1)}, u32[]{:S(2)}, u32[]{:S(2)}) collective-permute-start(bf16[4,8,2048]{2,1,0:T(8,128)(2,1)S(1)} %get-tuple-element.78), channel_id=1, source_target_pairs={{0,48},{4,20},{8,56},{12,28},{16,0},{20,36},{24,8},{28,44},{32,16}... | collective-permute-start | bytes 393224 | tf_op jit(solution)/shard_map/ppermute | solution.py:21
  (12 other events, 153.3 us)

commit v4 on v3

--- a/solution.py
+++ b/solution.py
@@ -35,8 +35,8 @@
     x, core = lax.axis_index("x"), lax.axis_index("c")
     gate_t, up_t = gate_weight.T, up_weight.T
     first = [gate_t, shift(gate_t, "c", 1), up_t, shift(up_t, "c", 1)]
-    second = jnp.concatenate([down_weight, shift(down_weight, "c", 1)], axis=0)
-    units = second.shape[0]
+    second = [down_weight, shift(down_weight, "c", 1)]
+    units = 2 * down_weight.shape[0]
     rows, width = tokens.shape
     part = width // 4
 
@@ -52,9 +52,9 @@
     far = along_z(jnp.concatenate([pair, near], axis=1), 2, -2)
     near = jnp.concatenate([base, near], axis=1)
 
-    def project(block):
+    def project(weights, block):
         return lax.dot_general(
-            block.reshape(-1, part), first, (((1,), (1,)), ((), ())), preferred_element_type=F32
+            block.reshape(-1, part), weights, (((1,), (1,)), ((), ())), preferred_element_type=F32
         ).reshape(4, -1, 2 * units)
 
     def exchange(partial):
@@ -68,10 +68,10 @@
     def spread(hidden):
         return [shift(hidden, "x", -k) for k in (1, 2, 3)]
 
-    def down(everyone):
+    def down(weights, everyone):
         return lax.dot_general(
             jnp.concatenate(everyone, axis=0),
-            second,
+            weights,
             (((1,), (0,)), ((), ())),
             preferred_element_type=F32,
         ).reshape(4, -1, part)
@@ -90,22 +90,24 @@
 
     slots = near.shape[1]
     near_y = over_y(near)
-    *first, far_own = together(*first, far)
-    first = jnp.concatenate(first, axis=0)
+    *first, near_own = together(*first, near)
+    first, far = together(jnp.concatenate(first, axis=0), far)
     far_y = over_y(far)
+    *second, far_own = together(*second, far)
+    second = jnp.concatenate(second, axis=0)
 
-    first, near_1, near_3, near_2 = together(first, *near_y)
-    near_partial = project(jnp.concatenate([near, near_1, near_2, near_3], axis=1))
+    first, second, near_1, near_3, near_2 = together(first, second, *near_y)
+    near_partial = project(first, jnp.concatenate([near_own, near_1, near_2, near_3], axis=1))
     near_sums = exchange(near_partial)
     near_hidden = activate(near_partial[0], near_sums)
     near_spread = spread(near_hidden)
 
     near_hidden, far_1, far_3, far_2 = together(near_hidden, *far_y)
-    far_partial = project(jnp.concatenate([far_own, far_1, far_2, far_3], axis=1))
+    far_partial = project(first, jnp.concatenate([far_own, far_1, far_2, far_3], axis=1))
     far_sums = exchange(far_partial)
     far_kept, *near_spread = together(far_partial[0], *near_spread)
 
-    near_down = by_y(down([near_hidden] + near_spread))
+    near_down = by_y(down(second, [near_hidden] + near_spread))
     near_back = back_over_y(near_down)
     near_down[0], *far_sums = together(near_down[0], *far_sums)
     far_hidden = activate(far_kept, far_sums)
@@ -118,7 +120,7 @@
         along_z(near_total[:, half:].astype(BF16), -1, 1),
         along_z(near_total[:, :half].astype(BF16), 0, 4),
     ]
-    far_down = by_y(down([far_hidden] + far_spread))
+    far_down = by_y(down(second, [far_hidden] + far_spread))
     far_back = back_over_y(far_down)
     *near_pieces, back_1, back_3, back_2 = together(*near_pieces, *far_back)
     far_total = sum_over_y(far_down, (back_1, back_3, back_2))

time: 131 us -> 131 us (level)
  starting transfers between devices: 59.8 us -> 69.6 us
  waiting for transfers between devices: 50.3 us -> 41.6 us
  local copies, waits for them, and re-layouts: 2.48 us -> 0.52 us
    ppermute x7, starting transfers between devices: 12.9 us -> 25.9 us  [along_z(): return lax.ppermute(value, ('z', 'c'), pairs)]
    ppermute x34, waiting for transfers between devices: 22.6 us -> 17.1 us  [shift(): return lax.ppermute(value, axis, [(i, (i + step) % n) for i in range(n)])]
    ppermute x7, waiting for transfers between devices: 27.7 us -> 24.5 us  [along_z(): return lax.ppermute(value, ('z', 'c'), pairs)]
    ppermute x34, starting transfers between devices: 46.9 us -> 43.7 us  [shift(): return lax.ppermute(value, axis, [(i, (i + step) % n) for i in range(n)])]
    unnamed x10 -> x7, local copies, waits for them, and re-layouts: 1.77 us -> 0.03 us
    concatenate x1 -> x3, other arithmetic: 3.17 us -> 4.2 us  [the longest x1 3.61 us: local(): first, far = together(jnp.concatenate(first, axis=0), far)]
  transfers between devices with their start and end apart: 41 -> 41, of which waited for: 21 -> 17; matrix products, arithmetic and copies ran while one was open for 11% -> 8% of each run, Pallas kernels for 0% -> 0%
where the time goes in v4:
time: 131 us; the launch traced here: 130 us
  starting transfers between devices  69.6 us (53%)
  waiting for transfers between devices  41.6 us (32%)
  other arithmetic  8.17 us (6%)
  matrix products  6.77 us (5%)
  blocking collectives  3.38 us (3%)
    ppermute x34, starting transfers between devices, shift(): return lax.ppermute(value, axis, [(i, (i + step) % n) for i in range(n)])  43.7 us
    ppermute x7, starting transfers between devices, along_z(): return lax.ppermute(value, ('z', 'c'), pairs)  25.9 us
    ppermute x7, waiting for transfers between devices, along_z(): return lax.ppermute(value, ('z', 'c'), pairs)  24.5 us
    ppermute x34, waiting for transfers between devices, shift(): return lax.ppermute(value, axis, [(i, (i + step) % n) for i in range(n)])  17.1 us
    dot_general x2, matrix products, project(): lax.dot_general(block.reshape(-1, part), weights, (((1,), (1,)), ((), ())...  4.23 us
    concatenate x1, other arithmetic, local(): first, far = together(jnp.concatenate(first, axis=0), far)  3.61 us
    all_gather x1, blocking collectives, local(): pair = lax.all_gather(own, 'c', axis=1, tiled=True)  3.38 us
  transfers between devices with their start and end apart: 41, of which 17 were waited for; matrix products, arithmetic and copies ran while one was open for 8% of the time, Pallas kernels for 0%

profile of v4, /device:TPU:1, one launch (start us, length us, event | category | flops | bytes accessed | tf_op | source)
XLA Modules:
  0.0 130.5 jit_solution(4188690134908158235)
XLA Ops:
  0.0 3.2 %collective-permute-start = (bf16[448,2048]{1,0:T(8,128)(2,1)}, bf16[448,2048]{1,0:T(8,128)(2,1)}, u32[]{:S(2)}, u32[]{:S(2)}) collective-permute-start(bf16[448,2048]{1,0:T(8,128)(2,1)} %bitcast.46), channel_id=1, source_target_pairs={{0,4},{4,0},{1,5},{5,1},{2,6},{6,2},{3,7},{7,3},{8,12},{12,8},{9,1... | collective-permute-start | bytes 5505032 | tf_op jit(solution)/shard_map/ppermute | solution.py:13
  5.5 2.0 %collective-permute-start.3 = (bf16[4,2048]{1,0:T(4,128)(2,1)S(1)}, bf16[4,2048]{1,0:T(4,128)(2,1)S(1)}, u32[]{:S(2)}, u32[]{:S(2)}) collective-permute-start(bf16[4,2048]{1,0:T(4,128)(2,1)S(1)} %get-tuple-element.101), channel_id=1, source_target_pairs={{0,2},{1,3},{2,0},{3,1},{4,6},{5,7},{6,4},{7,5},{8,10},{9,11},{10,... | collective-permute-start | bytes 49160 | tf_op jit(solution)/shard_map/ppermute | solution.py:13
  9.3 1.7 %collective-permute-start.8 = (bf16[448,2048]{1,0:T(8,128)(2,1)}, bf16[448,2048]{1,0:T(8,128)(2,1)S(1)}, u32[]{:S(2)}, u32[]{:S(2)}) collective-permute-start(bf16[448,2048]{1,0:T(8,128)(2,1)} %param.9), channel_id=1, source_target_pairs={{0,4},{4,0},{1,5},{5,1},{2,6},{6,2},{3,7},{7,3},{8,12},{12,8},{9,1... | collective-permute-start | bytes 5505032 | tf_op jit(solution)/shard_map/ppermute | solution.py:13
  11.1 3.4 %all_gather.3 = bf16[4,8,2048]{2,0,1:T(4,128)(2,1)S(1)} all-gather(bf16[4,4,2048]{2,0,1:T(4,128)(2,1)S(1)} %copy.10), channel_id=1, replica_groups=mesh['y'=4,'z'=8,'c'=2,'x'=4] {'c'}, dimensions={1}, use_global_device_ids=true | all-gather | bytes 196608 | tf_op jit(solution)/shard_map/all_gather | solution.py:50
  14.5 8.3 %collective-permute-start.5 = (bf16[4,8,2048]{2,1,0:T(8,128)(2,1)S(1)}, bf16[4,8,2048]{2,1,0:T(8,128)(2,1)S(1)}, u32[]{:S(2)}, u32[]{:S(2)}) collective-permute-start(bf16[4,8,2048]{2,1,0:T(8,128)(2,1)S(1)} %copy.11), channel_id=1, source_target_pairs={{0,0},{4,36},{8,8},{12,44},{16,16},{20,52},{24,24},{28,60},{32,32}... | collective-permute-start | bytes 393224 | tf_op jit(solution)/shard_map/ppermute | solution.py:21
  22.9 3.4 %collective-permute-done.5 = bf16[4,8,2048]{2,1,0:T(8,128)(2,1)S(1)} collective-permute-done((bf16[4,8,2048]{2,1,0:T(8,128)(2,1)S(1)}, bf16[4,8,2048]{2,1,0:T(8,128)(2,1)S(1)}, u32[]{:S(2)}, u32[]{:S(2)}) %collective-permute-start.5) | collective-permute-done | bytes 131104 | tf_op jit(solution)/shard_map/ppermute | solution.py:21
  26.2 2.8 %collective-permute-done.6 = bf16[4,8,2048]{2,1,0:T(8,128)(2,1)S(1)} collective-permute-done((bf16[4,8,2048]{2,1,0:T(8,128)(2,1)S(1)}, bf16[4,8,2048]{2,1,0:T(8,128)(2,1)S(1)}, u32[]{:S(2)}, u32[]{:S(2)}) %collective-permute-start.6) | collective-permute-done | bytes 131104 | tf_op jit(solution)/shard_map/ppermute | solution.py:21
  32.0 1.6 %collective-permute-start.11 = (bf16[4,16,2048]{2,1,0:T(8,128)(2,1)S(1)}, bf16[4,16,2048]{2,1,0:T(8,128)(2,1)S(1)}, u32[]{:S(2)}, u32[]{:S(2)}) collective-permute-start(bf16[4,16,2048]{2,1,0:T(8,128)(2,1)S(1)} %constant_dynamic-update-slice_fusion), channel_id=1, source_target_pairs={{0,128},{64,192},{128,0},{192,64},{1,129},{65,193},{129,1},{193,65... | collective-permute-start | bytes 786440 | tf_op jit(solution)/shard_map/ppermute | solution.py:13
  33.6 2.0 %collective-permute-start.7 = (bf16[4,16,2048]{2,1,0:T(8,128)(2,1)S(1)}, bf16[4,16,2048]{2,1,0:T(8,128)(2,1)S(1)}, u32[]{:S(2)}, u32[]{:S(2)}) collective-permute-start(bf16[4,16,2048]{2,1,0:T(8,128)(2,1)S(1)} %pad_maximum_fusion.4), channel_id=1, source_target_pairs={{0,16},{4,52},{8,24},{12,60},{16,32},{20,4},{24,40},{28,12},{32,48... | collective-permute-start | bytes 786440 | tf_op jit(solution)/shard_map/ppermute | solution.py:21
  35.6 3.6 %pad_maximum_fusion = bf16[1792,2048]{1,0:T(8,128)(2,1)S(1)} fusion(bf16[448,2048]{1,0:T(8,128)(2,1)} %collective-permute-done.1, bf16[448,2048]{1,0:T(8,128)(2,1)S(1)} %bitcast.45, bf16[448,2048]{1,0:T(8,128)(2,1)} %collective-permute-done, bf16[448,2048]{1,0:T(8,128)(2,1)} %bitcast.47), kind=kLoop, calls=%fused_computation | loop fusion | flops 29360128 | bytes 14680064 | tf_op jit(solution)/shard_map/concatenate | solution.py:94
  39.3 3.1 %collective-permute-done.7 = bf16[4,16,2048]{2,1,0:T(8,128)(2,1)S(1)} collective-permute-done((bf16[4,16,2048]{2,1,0:T(8,128)(2,1)S(1)}, bf16[4,16,2048]{2,1,0:T(8,128)(2,1)S(1)}, u32[]{:S(2)}, u32[]{:S(2)}) %collective-permute-start.7) | collective-permute-done | bytes 262176 | tf_op jit(solution)/shard_map/ppermute | solution.py:21
  43.0 2.1 %fusion.37 = (bf16[256,1792]{1,0:T(8,128)(2,1)S(1)}, f32[256,1792]{1,0:T(8,128)S(1)}) fusion(bf16[256,2048]{1,0:T(8,128)(2,1)S(1)} %bitcast.49, bf16[1792,2048]{1,0:T(8,128)(2,1)S(1)} %pad_maximum_fusion), kind=kOutput, calls=%fused_computation.71 | convolution fusion | flops 1879506944 | bytes 11141120 | tf_op jit(solution)/shard_map/dot_general | solution.py:56
  45.1 2.4 %collective-permute-start.14 = (bf16[64,1792]{1,0:T(8,128)(2,1)S(1)}, bf16[64,1792]{1,0:T(8,128)(2,1)S(1)}, u32[]{:S(2)}, u32[]{:S(2)}) collective-permute-start(bf16[64,1792]{1,0:T(8,128)(2,1)S(1)} %get-tuple-element.87), channel_id=1, source_target_pairs={{0,3},{1,0},{2,1},{3,2},{4,7},{5,4},{6,5},{7,6},{8,11},{9,8},{10,9... | collective-permute-start | bytes 688136 | tf_op jit(solution)/shard_map/ppermute | solution.py:13
  49.3 2.2 %collective-permute-start.16 = (bf16[4,16,2048]{2,1,0:T(8,128)(2,1)S(1)}, bf16[4,16,2048]{2,1,0:T(8,128)(2,1)S(1)}, u32[]{:S(2)}, u32[]{:S(2)}) collective-permute-start(bf16[4,16,2048]{2,1,0:T(8,128)(2,1)S(1)} %collective-permute-done.7), channel_id=1, source_target_pairs={{0,192},{64,0},{128,64},{192,128},{1,193},{65,1},{129,65},{193,129... | collective-permute-start | bytes 786440 | tf_op jit(solution)/shard_map/ppermute | solution.py:13
  51.5 3.7 %collective-permute-done.14 = bf16[64,1792]{1,0:T(8,128)(2,1)S(1)} collective-permute-done((bf16[64,1792]{1,0:T(8,128)(2,1)S(1)}, bf16[64,1792]{1,0:T(8,128)(2,1)S(1)}, u32[]{:S(2)}, u32[]{:S(2)}) %collective-permute-start.14) | collective-permute-done | bytes 229408 | tf_op jit(solution)/shard_map/ppermute | solution.py:13
  57.9 2.3 %collective-permute-start.18 = (bf16[64,896]{1,0:T(8,128)(2,1)S(1)}, bf16[64,896]{1,0:T(8,128)(2,1)S(1)}, u32[]{:S(2)}, u32[]{:S(2)}) collective-permute-start(bf16[64,896]{1,0:T(8,128)(2,1)S(1)} %fusion.22), channel_id=1, source_target_pairs={{0,3},{1,0},{2,1},{3,2},{4,7},{5,4},{6,5},{7,6},{8,11},{9,8},{10,9... | collective-permute-start | bytes 344072 | tf_op jit(solution)/shard_map/ppermute | solution.py:13
  60.1 2.8 %collective-permute-start.20 = (bf16[64,896]{1,0:T(8,128)(2,1)S(1)}, bf16[64,896]{1,0:T(8,128)(2,1)S(1)}, u32[]{:S(2)}, u32[]{:S(2)}) collective-permute-start(bf16[64,896]{1,0:T(8,128)(2,1)S(1)} %fusion.22), channel_id=1, source_target_pairs={{0,1},{1,2},{2,3},{3,0},{4,5},{5,6},{6,7},{7,4},{8,9},{9,10},{10,1... | collective-permute-start | bytes 344072 | tf_op jit(solution)/shard_map/ppermute | solution.py:13
  63.0 2.1 %fusion.38 = (bf16[256,1792]{1,0:T(8,128)(2,1)S(1)}, f32[256,1792]{1,0:T(8,128)S(1)}) fusion(bf16[256,2048]{1,0:T(8,128)(2,1)S(1)} %bitcast.48, bf16[1792,2048]{1,0:T(8,128)(2,1)S(1)} %pad_maximum_fusion), kind=kOutput, calls=%fused_computation.72 | convolution fusion | flops 1879506944 | bytes 11141120 | tf_op jit(solution)/shard_map/dot_general | solution.py:56
  65.5 2.9 %collective-permute-start.22 = (bf16[64,1792]{1,0:T(8,128)(2,1)S(1)}, bf16[64,1792]{1,0:T(8,128)(2,1)S(1)}, u32[]{:S(2)}, u32[]{:S(2)}) collective-permute-start(bf16[64,1792]{1,0:T(8,128)(2,1)S(1)} %get-tuple-element.84), channel_id=1, source_target_pairs={{0,1},{1,2},{2,3},{3,0},{4,5},{5,6},{6,7},{7,4},{8,9},{9,10},{10,1... | collective-permute-start | bytes 688136 | tf_op jit(solution)/shard_map/ppermute | solution.py:13
  69.9 2.1 %collective-permute-start.24 = (bf16[4,16,2048]{2,1,0:T(8,128)(2,1)S(1)}, bf16[4,16,2048]{2,1,0:T(8,128)(2,1)S(1)}, u32[]{:S(2)}, u32[]{:S(2)}) collective-permute-start(bf16[4,16,2048]{2,1,0:T(8,128)(2,1)S(1)} %get-tuple-element.82), channel_id=1, source_target_pairs={{0,192},{64,0},{128,64},{192,128},{1,193},{65,1},{129,65},{193,129... | collective-permute-start | bytes 786440 | tf_op jit(solution)/shard_map/ppermute | solution.py:13
  72.0 2.0 %collective-permute-done.21 = bf16[64,1792]{1,0:T(8,128)(2,1)S(1)} collective-permute-done((bf16[64,1792]{1,0:T(8,128)(2,1)S(1)}, bf16[64,1792]{1,0:T(8,128)(2,1)S(1)}, u32[]{:S(2)}, u32[]{:S(2)}) %collective-permute-start.21) | collective-permute-done | bytes 229408 | tf_op jit(solution)/shard_map/ppermute | solution.py:13
  76.6 2.2 %collective-permute-start.31 = (bf16[64,896]{1,0:T(8,128)(2,1)S(1)}, bf16[64,896]{1,0:T(8,128)(2,1)S(1)}, u32[]{:S(2)}, u32[]{:S(2)}) collective-permute-start(bf16[64,896]{1,0:T(8,128)(2,1)S(1)} %fusion.21), channel_id=1, source_target_pairs={{0,1},{1,2},{2,3},{3,0},{4,5},{5,6},{6,7},{7,4},{8,9},{9,10},{10,1... | collective-permute-start | bytes 344072 | tf_op jit(solution)/shard_map/ppermute | solution.py:13
  79.8 1.6 %collective-permute-start.29 = (bf16[64,896]{1,0:T(8,128)(2,1)S(1)}, bf16[64,896]{1,0:T(8,128)(2,1)S(1)}, u32[]{:S(2)}, u32[]{:S(2)}) collective-permute-start(bf16[64,896]{1,0:T(8,128)(2,1)S(1)} %fusion.21), channel_id=1, source_target_pairs={{0,3},{1,0},{2,1},{3,2},{4,7},{5,4},{6,5},{7,6},{8,11},{9,8},{10,9... | collective-permute-start | bytes 344072 | tf_op jit(solution)/shard_map/ppermute | solution.py:13
  81.4 3.6 %collective-permute-done.25 = bf16[4,16,2048]{2,1,0:T(8,128)(2,1)S(1)} collective-permute-done((bf16[4,16,2048]{2,1,0:T(8,128)(2,1)S(1)}, bf16[4,16,2048]{2,1,0:T(8,128)(2,1)S(1)}, u32[]{:S(2)}, u32[]{:S(2)}) %collective-permute-start.25) | collective-permute-done | bytes 262176 | tf_op jit(solution)/shard_map/ppermute | solution.py:13
  90.3 7.6 %collective-permute-start.27 = (bf16[4,8,2048]{2,1,0:T(8,128)(2,1)S(1)}, bf16[4,8,2048]{2,1,0:T(8,128)(2,1)S(1)}, u32[]{:S(2)}, u32[]{:S(2)}) collective-permute-start(bf16[4,8,2048]{2,1,0:T(8,128)(2,1)S(1)} %get-tuple-element.92), channel_id=1, source_target_pairs={{0,56},{4,12},{8,0},{12,20},{16,8},{20,28},{24,16},{28,36},{32,24}... | collective-permute-start | bytes 393224 | tf_op jit(solution)/shard_map/ppermute | solution.py:21
  97.9 4.2 %collective-permute-start.28 = (bf16[4,8,2048]{2,1,0:T(8,128)(2,1)S(1)}, bf16[4,8,2048]{2,1,0:T(8,128)(2,1)S(1)}, u32[]{:S(2)}, u32[]{:S(2)}) collective-permute-start(bf16[4,8,2048]{2,1,0:T(8,128)(2,1)S(1)} %get-tuple-element.91), channel_id=1, source_target_pairs={{0,0},{4,36},{8,8},{12,44},{16,16},{20,52},{24,24},{28,60},{32,32}... | collective-permute-start | bytes 393224 | tf_op jit(solution)/shard_map/ppermute | solution.py:21
  102.7 4.8 %collective-permute-done.28 = bf16[4,8,2048]{2,1,0:T(8,128)(2,1)S(1)} collective-permute-done((bf16[4,8,2048]{2,1,0:T(8,128)(2,1)S(1)}, bf16[4,8,2048]{2,1,0:T(8,128)(2,1)S(1)}, u32[]{:S(2)}, u32[]{:S(2)}) %collective-permute-start.28) | collective-permute-done | bytes 131104 | tf_op jit(solution)/shard_map/ppermute | solution.py:21
  108.9 2.5 %collective-permute-start.35 = (bf16[4,8,2048]{2,1,0:T(8,128)(2,1)S(1)}, bf16[4,8,2048]{2,1,0:T(8,128)(2,1)S(1)}, u32[]{:S(2)}, u32[]{:S(2)}) collective-permute-start(bf16[4,8,2048]{2,1,0:T(8,128)(2,1)S(1)} %get-tuple-element.89), channel_id=1, source_target_pairs={{0,40},{4,28},{8,48},{12,36},{16,56},{20,44},{24,0},{28,52},{32,8}... | collective-permute-start | bytes 393224 | tf_op jit(solution)/shard_map/ppermute | solution.py:21
  111.4 2.7 %collective-permute-done.36 = bf16[4,8,2048]{2,1,0:T(8,128)(2,1)S(1)} collective-permute-done((bf16[4,8,2048]{2,1,0:T(8,128)(2,1)S(1)}, bf16[4,8,2048]{2,1,0:T(8,128)(2,1)S(1)}, u32[]{:S(2)}, u32[]{:S(2)}) %collective-permute-start.36) | collective-permute-done | bytes 131104 | tf_op jit(solution)/shard_map/ppermute | solution.py:21
  114.2 7.2 %collective-permute-done.35 = bf16[4,8,2048]{2,1,0:T(8,128)(2,1)S(1)} collective-permute-done((bf16[4,8,2048]{2,1,0:T(8,128)(2,1)S(1)}, bf16[4,8,2048]{2,1,0:T(8,128)(2,1)S(1)}, u32[]{:S(2)}, u32[]{:S(2)}) %collective-permute-start.35) | collective-permute-done | bytes 131104 | tf_op jit(solution)/shard_map/ppermute | solution.py:21
  123.0 2.4 %collective-permute-start.38 = (f32[4,2048]{1,0:T(4,128)S(1)}, f32[4,2048]{1,0:T(4,128)S(1)}, u32[]{:S(2)}, u32[]{:S(2)}) collective-permute-start(f32[4,2048]{1,0:T(4,128)S(1)} %get-tuple-element.99), channel_id=1, source_target_pairs={{0,3},{1,0},{2,1},{3,2},{4,7},{5,4},{6,5},{7,6},{8,11},{9,8},{10,9... | collective-permute-start | bytes 98312 | tf_op jit(solution)/shard_map/ppermute | solution.py:13
  126.4 3.3 %collective-permute-done.39 = f32[4,2048]{1,0:T(4,128)S(1)} collective-permute-done((f32[4,2048]{1,0:T(4,128)S(1)}, f32[4,2048]{1,0:T(4,128)S(1)}, u32[]{:S(2)}, u32[]{:S(2)}) %collective-permute-start.39) | collective-permute-done | bytes 32800 | tf_op jit(solution)/shard_map/ppermute | solution.py:13
  (98 shorter events, 28.3 us)
Async XLA Ops:
  0.0 32.0 %collective-permute-start = (bf16[448,2048]{1,0:T(8,128)(2,1)}, bf16[448,2048]{1,0:T(8,128)(2,1)}, u32[]{:S(2)}, u32[]{:S(2)}) collective-permute-start(bf16[448,2048]{1,0:T(8,128)(2,1)} %bitcast.46), channel_id=1, source_target_pairs={{0,4},{4,0},{1,5},{5,1},{2,6},{6,2},{3,7},{7,3},{8,12},{12,8},{9,1... | collective-permute-start | bytes 5505032 | tf_op jit(solution)/shard_map/ppermute | solution.py:13
  3.2 30.4 %collective-permute-start.1 = (bf16[448,2048]{1,0:T(8,128)(2,1)}, bf16[448,2048]{1,0:T(8,128)(2,1)}, u32[]{:S(2)}, u32[]{:S(2)}) collective-permute-start(bf16[448,2048]{1,0:T(8,128)(2,1)} %bitcast.44), channel_id=1, source_target_pairs={{0,4},{4,0},{1,5},{5,1},{2,6},{6,2},{3,7},{7,3},{8,12},{12,8},{9,1... | collective-permute-start | bytes 5505032 | tf_op jit(solution)/shard_map/ppermute | solution.py:13
  9.3 33.1 %collective-permute-start.8 = (bf16[448,2048]{1,0:T(8,128)(2,1)}, bf16[448,2048]{1,0:T(8,128)(2,1)S(1)}, u32[]{:S(2)}, u32[]{:S(2)}) collective-permute-start(bf16[448,2048]{1,0:T(8,128)(2,1)} %param.9), channel_id=1, source_target_pairs={{0,4},{4,0},{1,5},{5,1},{2,6},{6,2},{3,7},{7,3},{8,12},{12,8},{9,1... | collective-permute-start | bytes 5505032 | tf_op jit(solution)/shard_map/ppermute | solution.py:13
  14.5 11.7 %collective-permute-start.5 = (bf16[4,8,2048]{2,1,0:T(8,128)(2,1)S(1)}, bf16[4,8,2048]{2,1,0:T(8,128)(2,1)S(1)}, u32[]{:S(2)}, u32[]{:S(2)}) collective-permute-start(bf16[4,8,2048]{2,1,0:T(8,128)(2,1)S(1)} %copy.11), channel_id=1, source_target_pairs={{0,0},{4,36},{8,8},{12,44},{16,16},{20,52},{24,24},{28,60},{32,32}... | collective-permute-start | bytes 393224 | tf_op jit(solution)/shard_map/ppermute | solution.py:21
  29.0 13.8 %collective-permute-start.9 = (bf16[4,16,2048]{2,1,0:T(8,128)(2,1)S(1)}, bf16[4,16,2048]{2,1,0:T(8,128)(2,1)S(1)}, u32[]{:S(2)}, u32[]{:S(2)}) collective-permute-start(bf16[4,16,2048]{2,1,0:T(8,128)(2,1)S(1)} %constant_dynamic-update-slice_fusion), channel_id=1, source_target_pairs={{0,64},{64,128},{128,192},{192,0},{1,65},{65,129},{129,193},{193,1... | collective-permute-start | bytes 786440 | tf_op jit(solution)/shard_map/ppermute | solution.py:13
  30.4 12.4 %collective-permute-start.10 = (bf16[4,16,2048]{2,1,0:T(8,128)(2,1)S(1)}, bf16[4,16,2048]{2,1,0:T(8,128)(2,1)S(1)}, u32[]{:S(2)}, u32[]{:S(2)}) collective-permute-start(bf16[4,16,2048]{2,1,0:T(8,128)(2,1)S(1)} %constant_dynamic-update-slice_fusion), channel_id=1, source_target_pairs={{0,192},{64,0},{128,64},{192,128},{1,193},{65,1},{129,65},{193,129... | collective-permute-start | bytes 786440 | tf_op jit(solution)/shard_map/ppermute | solution.py:13
  32.0 10.9 %collective-permute-start.11 = (bf16[4,16,2048]{2,1,0:T(8,128)(2,1)S(1)}, bf16[4,16,2048]{2,1,0:T(8,128)(2,1)S(1)}, u32[]{:S(2)}, u32[]{:S(2)}) collective-permute-start(bf16[4,16,2048]{2,1,0:T(8,128)(2,1)S(1)} %constant_dynamic-update-slice_fusion), channel_id=1, source_target_pairs={{0,128},{64,192},{128,0},{192,64},{1,129},{65,193},{129,1},{193,65... | collective-permute-start | bytes 786440 | tf_op jit(solution)/shard_map/ppermute | solution.py:13
  33.6 8.7 %collective-permute-start.7 = (bf16[4,16,2048]{2,1,0:T(8,128)(2,1)S(1)}, bf16[4,16,2048]{2,1,0:T(8,128)(2,1)S(1)}, u32[]{:S(2)}, u32[]{:S(2)}) collective-permute-start(bf16[4,16,2048]{2,1,0:T(8,128)(2,1)S(1)} %pad_maximum_fusion.4), channel_id=1, source_target_pairs={{0,16},{4,52},{8,24},{12,60},{16,32},{20,4},{24,40},{28,12},{32,48... | collective-permute-start | bytes 786440 | tf_op jit(solution)/shard_map/ppermute | solution.py:21
  45.1 10.1 %collective-permute-start.14 = (bf16[64,1792]{1,0:T(8,128)(2,1)S(1)}, bf16[64,1792]{1,0:T(8,128)(2,1)S(1)}, u32[]{:S(2)}, u32[]{:S(2)}) collective-permute-start(bf16[64,1792]{1,0:T(8,128)(2,1)S(1)} %get-tuple-element.87), channel_id=1, source_target_pairs={{0,3},{1,0},{2,1},{3,2},{4,7},{5,4},{6,5},{7,6},{8,11},{9,8},{10,9... | collective-permute-start | bytes 688136 | tf_op jit(solution)/shard_map/ppermute | solution.py:13
  47.6 10.1 %collective-permute-start.13 = (bf16[64,1792]{1,0:T(8,128)(2,1)S(1)}, bf16[64,1792]{1,0:T(8,128)(2,1)S(1)}, u32[]{:S(2)}, u32[]{:S(2)}) collective-permute-start(bf16[64,1792]{1,0:T(8,128)(2,1)S(1)} %get-tuple-element.88), channel_id=1, source_target_pairs={{0,1},{1,2},{2,3},{3,0},{4,5},{5,6},{6,7},{7,4},{8,9},{9,10},{10,1... | collective-permute-start | bytes 688136 | tf_op jit(solution)/shard_map/ppermute | solution.py:13
  47.6 10.1 %collective-permute-start.12 = (bf16[64,1792]{1,0:T(8,128)(2,1)S(1)}, bf16[64,1792]{1,0:T(8,128)(2,1)S(1)}, u32[]{:S(2)}, u32[]{:S(2)}) collective-permute-start(bf16[64,1792]{1,0:T(8,128)(2,1)S(1)} %get-tuple-element.86), channel_id=1, source_target_pairs={{0,2},{1,3},{2,0},{3,1},{4,6},{5,7},{6,4},{7,5},{8,10},{9,11},{10,... | collective-permute-start | bytes 688136 | tf_op jit(solution)/shard_map/ppermute | solution.py:13
  48.9 11.2 %collective-permute-start.15 = (bf16[4,16,2048]{2,1,0:T(8,128)(2,1)S(1)}, bf16[4,16,2048]{2,1,0:T(8,128)(2,1)S(1)}, u32[]{:S(2)}, u32[]{:S(2)}) collective-permute-start(bf16[4,16,2048]{2,1,0:T(8,128)(2,1)S(1)} %collective-permute-done.7), channel_id=1, source_target_pairs={{0,64},{64,128},{128,192},{192,0},{1,65},{65,129},{129,193},{193,1... | collective-permute-start | bytes 786440 | tf_op jit(solution)/shard_map/ppermute | solution.py:13
  49.3 13.6 %collective-permute-start.16 = (bf16[4,16,2048]{2,1,0:T(8,128)(2,1)S(1)}, bf16[4,16,2048]{2,1,0:T(8,128)(2,1)S(1)}, u32[]{:S(2)}, u32[]{:S(2)}) collective-permute-start(bf16[4,16,2048]{2,1,0:T(8,128)(2,1)S(1)} %collective-permute-done.7), channel_id=1, source_target_pairs={{0,192},{64,0},{128,64},{192,128},{1,193},{65,1},{129,65},{193,129... | collective-permute-start | bytes 786440 | tf_op jit(solution)/shard_map/ppermute | solution.py:13
  55.2 7.7 %collective-permute-start.17 = (bf16[4,16,2048]{2,1,0:T(8,128)(2,1)S(1)}, bf16[4,16,2048]{2,1,0:T(8,128)(2,1)S(1)}, u32[]{:S(2)}, u32[]{:S(2)}) collective-permute-start(bf16[4,16,2048]{2,1,0:T(8,128)(2,1)S(1)} %collective-permute-done.7), channel_id=1, source_target_pairs={{0,128},{64,192},{128,0},{192,64},{1,129},{65,193},{129,1},{193,65... | collective-permute-start | bytes 786440 | tf_op jit(solution)/shard_map/ppermute | solution.py:13
  57.9 10.5 %collective-permute-start.18 = (bf16[64,896]{1,0:T(8,128)(2,1)S(1)}, bf16[64,896]{1,0:T(8,128)(2,1)S(1)}, u32[]{:S(2)}, u32[]{:S(2)}) collective-permute-start(bf16[64,896]{1,0:T(8,128)(2,1)S(1)} %fusion.22), channel_id=1, source_target_pairs={{0,3},{1,0},{2,1},{3,2},{4,7},{5,4},{6,5},{7,6},{8,11},{9,8},{10,9... | collective-permute-start | bytes 344072 | tf_op jit(solution)/shard_map/ppermute | solution.py:13
  60.1 8.3 %collective-permute-start.19 = (bf16[64,896]{1,0:T(8,128)(2,1)S(1)}, bf16[64,896]{1,0:T(8,128)(2,1)S(1)}, u32[]{:S(2)}, u32[]{:S(2)}) collective-permute-start(bf16[64,896]{1,0:T(8,128)(2,1)S(1)} %fusion.22), channel_id=1, source_target_pairs={{0,2},{1,3},{2,0},{3,1},{4,6},{5,7},{6,4},{7,5},{8,10},{9,11},{10,... | collective-permute-start | bytes 344072 | tf_op jit(solution)/shard_map/ppermute | solution.py:13
  60.1 8.3 %collective-permute-start.20 = (bf16[64,896]{1,0:T(8,128)(2,1)S(1)}, bf16[64,896]{1,0:T(8,128)(2,1)S(1)}, u32[]{:S(2)}, u32[]{:S(2)}) collective-permute-start(bf16[64,896]{1,0:T(8,128)(2,1)S(1)} %fusion.22), channel_id=1, source_target_pairs={{0,1},{1,2},{2,3},{3,0},{4,5},{5,6},{6,7},{7,4},{8,9},{9,10},{10,1... | collective-permute-start | bytes 344072 | tf_op jit(solution)/shard_map/ppermute | solution.py:13
  65.2 8.7 %collective-permute-start.21 = (bf16[64,1792]{1,0:T(8,128)(2,1)S(1)}, bf16[64,1792]{1,0:T(8,128)(2,1)S(1)}, u32[]{:S(2)}, u32[]{:S(2)}) collective-permute-start(bf16[64,1792]{1,0:T(8,128)(2,1)S(1)} %get-tuple-element.85), channel_id=1, source_target_pairs={{0,2},{1,3},{2,0},{3,1},{4,6},{5,7},{6,4},{7,5},{8,10},{9,11},{10,... | collective-permute-start | bytes 688136 | tf_op jit(solution)/shard_map/ppermute | solution.py:13
  65.5 10.9 %collective-permute-start.22 = (bf16[64,1792]{1,0:T(8,128)(2,1)S(1)}, bf16[64,1792]{1,0:T(8,128)(2,1)S(1)}, u32[]{:S(2)}, u32[]{:S(2)}) collective-permute-start(bf16[64,1792]{1,0:T(8,128)(2,1)S(1)} %get-tuple-element.84), channel_id=1, source_target_pairs={{0,1},{1,2},{2,3},{3,0},{4,5},{5,6},{6,7},{7,4},{8,9},{9,10},{10,1... | collective-permute-start | bytes 688136 | tf_op jit(solution)/shard_map/ppermute | solution.py:13
  68.4 8.0 %collective-permute-start.23 = (bf16[64,1792]{1,0:T(8,128)(2,1)S(1)}, bf16[64,1792]{1,0:T(8,128)(2,1)S(1)}, u32[]{:S(2)}, u32[]{:S(2)}) collective-permute-start(bf16[64,1792]{1,0:T(8,128)(2,1)S(1)} %get-tuple-element.83), channel_id=1, source_target_pairs={{0,3},{1,0},{2,1},{3,2},{4,7},{5,4},{6,5},{7,6},{8,11},{9,8},{10,9... | collective-permute-start | bytes 688136 | tf_op jit(solution)/shard_map/ppermute | solution.py:13
  69.9 9.9 %collective-permute-start.24 = (bf16[4,16,2048]{2,1,0:T(8,128)(2,1)S(1)}, bf16[4,16,2048]{2,1,0:T(8,128)(2,1)S(1)}, u32[]{:S(2)}, u32[]{:S(2)}) collective-permute-start(bf16[4,16,2048]{2,1,0:T(8,128)(2,1)S(1)} %get-tuple-element.82), channel_id=1, source_target_pairs={{0,192},{64,0},{128,64},{192,128},{1,193},{65,1},{129,65},{193,129... | collective-permute-start | bytes 786440 | tf_op jit(solution)/shard_map/ppermute | solution.py:13
  72.0 13.1 %collective-permute-start.25 = (bf16[4,16,2048]{2,1,0:T(8,128)(2,1)S(1)}, bf16[4,16,2048]{2,1,0:T(8,128)(2,1)S(1)}, u32[]{:S(2)}, u32[]{:S(2)}) collective-permute-start(bf16[4,16,2048]{2,1,0:T(8,128)(2,1)S(1)} %get-tuple-element.81), channel_id=1, source_target_pairs={{0,64},{64,128},{128,192},{192,0},{1,65},{65,129},{129,193},{193,1... | collective-permute-start | bytes 786440 | tf_op jit(solution)/shard_map/ppermute | solution.py:13
  73.9 11.1 %collective-permute-start.26 = (bf16[4,16,2048]{2,1,0:T(8,128)(2,1)S(1)}, bf16[4,16,2048]{2,1,0:T(8,128)(2,1)S(1)}, u32[]{:S(2)}, u32[]{:S(2)}) collective-permute-start(bf16[4,16,2048]{2,1,0:T(8,128)(2,1)S(1)} %get-tuple-element.80), channel_id=1, source_target_pairs={{0,128},{64,192},{128,0},{192,64},{1,129},{65,193},{129,1},{193,65... | collective-permute-start | bytes 786440 | tf_op jit(solution)/shard_map/ppermute | solution.py:13
  76.6 8.5 %collective-permute-start.31 = (bf16[64,896]{1,0:T(8,128)(2,1)S(1)}, bf16[64,896]{1,0:T(8,128)(2,1)S(1)}, u32[]{:S(2)}, u32[]{:S(2)}) collective-permute-start(bf16[64,896]{1,0:T(8,128)(2,1)S(1)} %fusion.21), channel_id=1, source_target_pairs={{0,1},{1,2},{2,3},{3,0},{4,5},{5,6},{6,7},{7,4},{8,9},{9,10},{10,1... | collective-permute-start | bytes 344072 | tf_op jit(solution)/shard_map/ppermute | solution.py:13
  78.7 6.4 %collective-permute-start.30 = (bf16[64,896]{1,0:T(8,128)(2,1)S(1)}, bf16[64,896]{1,0:T(8,128)(2,1)S(1)}, u32[]{:S(2)}, u32[]{:S(2)}) collective-permute-start(bf16[64,896]{1,0:T(8,128)(2,1)S(1)} %fusion.21), channel_id=1, source_target_pairs={{0,2},{1,3},{2,0},{3,1},{4,6},{5,7},{6,4},{7,5},{8,10},{9,11},{10,... | collective-permute-start | bytes 344072 | tf_op jit(solution)/shard_map/ppermute | solution.py:13
  87.2 20.3 %collective-permute-start.32 = (bf16[4,16,2048]{2,1,0:T(8,128)(2,1)S(1)}, bf16[4,16,2048]{2,1,0:T(8,128)(2,1)S(1)}, u32[]{:S(2)}, u32[]{:S(2)}) collective-permute-start(bf16[4,16,2048]{2,1,0:T(8,128)(2,1)S(1)} %get-tuple-element.79), channel_id=1, source_target_pairs={{0,192},{64,0},{128,64},{192,128},{1,193},{65,1},{129,65},{193,129... | collective-permute-start | bytes 786440 | tf_op jit(solution)/shard_map/ppermute | solution.py:13
  88.2 19.3 %collective-permute-start.33 = (bf16[4,16,2048]{2,1,0:T(8,128)(2,1)S(1)}, bf16[4,16,2048]{2,1,0:T(8,128)(2,1)S(1)}, u32[]{:S(2)}, u32[]{:S(2)}) collective-permute-start(bf16[4,16,2048]{2,1,0:T(8,128)(2,1)S(1)} %get-tuple-element.78), channel_id=1, source_target_pairs={{0,64},{64,128},{128,192},{192,0},{1,65},{65,129},{129,193},{193,1... | collective-permute-start | bytes 786440 | tf_op jit(solution)/shard_map/ppermute | solution.py:13
  88.7 18.8 %collective-permute-start.34 = (bf16[4,16,2048]{2,1,0:T(8,128)(2,1)S(1)}, bf16[4,16,2048]{2,1,0:T(8,128)(2,1)S(1)}, u32[]{:S(2)}, u32[]{:S(2)}) collective-permute-start(bf16[4,16,2048]{2,1,0:T(8,128)(2,1)S(1)} %get-tuple-element.77), channel_id=1, source_target_pairs={{0,128},{64,192},{128,0},{192,64},{1,129},{65,193},{129,1},{193,65... | collective-permute-start | bytes 786440 | tf_op jit(solution)/shard_map/ppermute | solution.py:13
  90.3 12.4 %collective-permute-start.27 = (bf16[4,8,2048]{2,1,0:T(8,128)(2,1)S(1)}, bf16[4,8,2048]{2,1,0:T(8,128)(2,1)S(1)}, u32[]{:S(2)}, u32[]{:S(2)}) collective-permute-start(bf16[4,8,2048]{2,1,0:T(8,128)(2,1)S(1)} %get-tuple-element.92), channel_id=1, source_target_pairs={{0,56},{4,12},{8,0},{12,20},{16,8},{20,28},{24,16},{28,36},{32,24}... | collective-permute-start | bytes 393224 | tf_op jit(solution)/shard_map/ppermute | solution.py:21
  97.9 9.6 %collective-permute-start.28 = (bf16[4,8,2048]{2,1,0:T(8,128)(2,1)S(1)}, bf16[4,8,2048]{2,1,0:T(8,128)(2,1)S(1)}, u32[]{:S(2)}, u32[]{:S(2)}) collective-permute-start(bf16[4,8,2048]{2,1,0:T(8,128)(2,1)S(1)} %get-tuple-element.91), channel_id=1, source_target_pairs={{0,0},{4,36},{8,8},{12,44},{16,16},{20,52},{24,24},{28,60},{32,32}... | collective-permute-start | bytes 393224 | tf_op jit(solution)/shard_map/ppermute | solution.py:21
  107.7 6.5 %collective-permute-start.36 = (bf16[4,8,2048]{2,1,0:T(8,128)(2,1)S(1)}, bf16[4,8,2048]{2,1,0:T(8,128)(2,1)S(1)}, u32[]{:S(2)}, u32[]{:S(2)}) collective-permute-start(bf16[4,8,2048]{2,1,0:T(8,128)(2,1)S(1)} %get-tuple-element.90), channel_id=1, source_target_pairs={{0,48},{4,20},{8,56},{12,28},{16,0},{20,36},{24,8},{28,44},{32,16}... | collective-permute-start | bytes 393224 | tf_op jit(solution)/shard_map/ppermute | solution.py:21
  108.9 12.5 %collective-permute-start.35 = (bf16[4,8,2048]{2,1,0:T(8,128)(2,1)S(1)}, bf16[4,8,2048]{2,1,0:T(8,128)(2,1)S(1)}, u32[]{:S(2)}, u32[]{:S(2)}) collective-permute-start(bf16[4,8,2048]{2,1,0:T(8,128)(2,1)S(1)} %get-tuple-element.89), channel_id=1, source_target_pairs={{0,40},{4,28},{8,48},{12,36},{16,56},{20,44},{24,0},{28,52},{32,8}... | collective-permute-start | bytes 393224 | tf_op jit(solution)/shard_map/ppermute | solution.py:21
  (12 other events, 124.0 us)

commit v5 on v4

--- a/solution.py
+++ b/solution.py
@@ -47,10 +47,11 @@
     own = jnp.stack(
         [blocks[0]] + [shift(blocks[4 - r], "x", 4 - r) for r in (1, 2, 3)]
     )
+    opposite = along_z(own, 4, 4)
     pair = lax.all_gather(own, "c", axis=1, tiled=True)
-    near, base = along_z(pair, 1, -1), along_z(pair, 0, 4)
+    near = along_z(pair, 1, -1)
     far = along_z(jnp.concatenate([pair, near], axis=1), 2, -2)
-    near = jnp.concatenate([base, near], axis=1)
+    near = jnp.concatenate([own, opposite, near], axis=1)
 
     def project(weights, block):
         return lax.dot_general(
@@ -93,19 +94,19 @@
     *first, near_own = together(*first, near)
     first, far = together(jnp.concatenate(first, axis=0), far)
     far_y = over_y(far)
-    *second, far_own = together(*second, far)
+
+    first, near_1, near_3, near_2 = together(first, *near_y)
+    near_partial = project(first, jnp.concatenate([near_own, near_1, near_2, near_3], axis=1))
+    near_sums = exchange(near_partial)
+    *second, near_kept = together(*second, near_partial[0])
     second = jnp.concatenate(second, axis=0)
 
-    first, second, near_1, near_3, near_2 = together(first, second, *near_y)
-    near_partial = project(first, jnp.concatenate([near_own, near_1, near_2, near_3], axis=1))
-    near_sums = exchange(near_partial)
-    near_hidden = activate(near_partial[0], near_sums)
+    second, far_1, far_3, far_2 = together(second, *far_y)
+    far_partial = project(first, jnp.concatenate([far, far_1, far_2, far_3], axis=1))
+    far_sums = exchange(far_partial)
+    far_kept, *near_sums = together(far_partial[0], *near_sums)
+    near_hidden = activate(near_kept, near_sums)
     near_spread = spread(near_hidden)
-
-    near_hidden, far_1, far_3, far_2 = together(near_hidden, *far_y)
-    far_partial = project(first, jnp.concatenate([far_own, far_1, far_2, far_3], axis=1))
-    far_sums = exchange(far_partial)
-    far_kept, *near_spread = together(far_partial[0], *near_spread)
 
     near_down = by_y(down(second, [near_hidden] + near_spread))
     near_back = back_over_y(near_down)
@@ -115,22 +116,24 @@
     far_hidden, *near_back = together(far_hidden, *near_back)
 
     near_total = sum_over_y(near_down, near_back)
-    half = slots // 2
     near_pieces = [
-        along_z(near_total[:, half:].astype(BF16), -1, 1),
-        along_z(near_total[:, :half].astype(BF16), 0, 4),
+        along_z(near_total[:, 2 * rows :].astype(BF16), -1, 1),
+        along_z(near_total[:, rows : 2 * rows].astype(BF16), 4, 4),
     ]
     far_down = by_y(down(second, [far_hidden] + far_spread))
     far_back = back_over_y(far_down)
     *near_pieces, back_1, back_3, back_2 = together(*near_pieces, *far_back)
     far_total = sum_over_y(far_down, (back_1, back_3, back_2))
-    far_pieces = [
-        along_z(far_total[:, half:].astype(BF16), -3, 3),
-        along_z(far_total[:, :half].astype(BF16), -2, 2),
-    ]
-    pair = sum(piece.astype(F32) for piece in near_pieces + far_pieces)
+    pair = sum(
+        piece.astype(F32)
+        for piece in (
+            near_pieces[0],
+            along_z(far_total[:, 2 * rows :].astype(BF16), -3, 3),
+            along_z(far_total[:, : 2 * rows].astype(BF16), -2, 2),
+        )
+    )
     low, high = pair[:, :rows], pair[:, rows:]
-    mine = jnp.where(core == 0, low, high)
+    mine = near_total[:, :rows] + near_pieces[1].astype(F32) + jnp.where(core == 0, low, high)
     other = jnp.where(core == 0, high, low).astype(BF16)
     mine = mine + shift(other, "c", 1).astype(F32)
     columns = [mine[0]] + [shift(mine[k], "x", k) for k in (1, 2, 3)]

time: 131 us -> 129 us (0.985)
  starting transfers between devices: 69.6 us -> 67.3 us
    ppermute x7, starting transfers between devices: 25.9 us -> 13.6 us  [along_z(): return lax.ppermute(value, ('z', 'c'), pairs)]
    ppermute x34, starting transfers between devices: 43.7 us -> 53.7 us  [shift(): return lax.ppermute(value, axis, [(i, (i + step) % n) for i in range(n)])]
    ppermute x7, waiting for transfers between devices: 24.5 us -> 21.6 us  [along_z(): return lax.ppermute(value, ('z', 'c'), pairs)]
    ppermute x34, waiting for transfers between devices: 17.1 us -> 18.9 us  [shift(): return lax.ppermute(value, axis, [(i, (i + step) % n) for i in range(n)])]
  transfers between devices with their start and end apart: 41 -> 41, of which waited for: 17 -> 19; matrix products, arithmetic and copies ran while one was open for 8% -> 10% of each run, Pallas kernels for 0% -> 0%
where the time goes in v5:
time: 129 us; the launch traced here: 128 us
  starting transfers between devices  67.3 us (52%)
  waiting for transfers between devices  40.5 us (31%)
  other arithmetic  8.29 us (6%)
  matrix products  6.82 us (5%)
  blocking collectives  3.72 us (3%)
    ppermute x34, starting transfers between devices, shift(): return lax.ppermute(value, axis, [(i, (i + step) % n) for i in range(n)])  53.7 us
    ppermute x7, waiting for transfers between devices, along_z(): return lax.ppermute(value, ('z', 'c'), pairs)  21.6 us
    ppermute x34, waiting for transfers between devices, shift(): return lax.ppermute(value, axis, [(i, (i + step) % n) for i in range(n)])  18.9 us
    ppermute x7, starting transfers between devices, along_z(): return lax.ppermute(value, ('z', 'c'), pairs)  13.6 us
    dot_general x2, matrix products, project(): lax.dot_general(block.reshape(-1, part), weights, (((1,), (1,)), ((), ())...  4.24 us
    all_gather x1, blocking collectives, local(): pair = lax.all_gather(own, 'c', axis=1, tiled=True)  3.72 us
    concatenate x1, other arithmetic, local(): first, far = together(jnp.concatenate(first, axis=0), far)  3.61 us
  transfers between devices with their start and end apart: 41, of which 19 were waited for; matrix products, arithmetic and copies ran while one was open for 10% of the time, Pallas kernels for 0%

profile of v5, /device:TPU:1, one launch (start us, length us, event | category | flops | bytes accessed | tf_op | source)
XLA Modules:
  0.0 127.6 jit_solution(2986983512481413739)
XLA Ops:
  0.0 3.2 %collective-permute-start.1 = (bf16[448,2048]{1,0:T(8,128)(2,1)}, bf16[448,2048]{1,0:T(8,128)(2,1)}, u32[]{:S(2)}, u32[]{:S(2)}) collective-permute-start(bf16[448,2048]{1,0:T(8,128)(2,1)} %bitcast.46), channel_id=1, source_target_pairs={{0,4},{4,0},{1,5},{5,1},{2,6},{6,2},{3,7},{7,3},{8,12},{12,8},{9,1... | collective-permute-start | bytes 5505032 | tf_op jit(solution)/shard_map/ppermute | solution.py:13
  8.0 1.5 %collective-permute-done.4 = bf16[4,2048]{1,0:T(4,128)(2,1)S(1)} collective-permute-done((bf16[4,2048]{1,0:T(4,128)(2,1)S(1)}, bf16[4,2048]{1,0:T(4,128)(2,1)S(1)}, u32[]{:S(2)}, u32[]{:S(2)}) %collective-permute-start.4) | collective-permute-done | bytes 16416 | tf_op jit(solution)/shard_map/ppermute | solution.py:13
  9.6 1.7 %collective-permute-done.5 = bf16[4,2048]{1,0:T(4,128)(2,1)S(1)} collective-permute-done((bf16[4,2048]{1,0:T(4,128)(2,1)S(1)}, bf16[4,2048]{1,0:T(4,128)(2,1)S(1)}, u32[]{:S(2)}, u32[]{:S(2)}) %collective-permute-start.5) | collective-permute-done | bytes 16416 | tf_op jit(solution)/shard_map/ppermute | solution.py:13
  11.3 3.7 %all_gather.3 = bf16[4,8,2048]{2,0,1:T(4,128)(2,1)S(1)} all-gather(bf16[4,4,2048]{2,0,1:T(4,128)(2,1)S(1)} %copy.12), channel_id=1, replica_groups=mesh['y'=4,'z'=8,'c'=2,'x'=4] {'c'}, dimensions={1}, use_global_device_ids=true | all-gather | bytes 196608 | tf_op jit(solution)/shard_map/all_gather | solution.py:51
  15.1 5.7 %collective-permute-start.7 = (bf16[4,8,2048]{2,1,0:T(8,128)(2,1)S(1)}, bf16[4,8,2048]{2,1,0:T(8,128)(2,1)S(1)}, u32[]{:S(2)}, u32[]{:S(2)}) collective-permute-start(bf16[4,8,2048]{2,1,0:T(8,128)(2,1)S(1)} %copy.13), channel_id=1, source_target_pairs={{0,8},{4,60},{8,16},{12,4},{16,24},{20,12},{24,32},{28,20},{32,40}... | collective-permute-start | bytes 393224 | tf_op jit(solution)/shard_map/ppermute | solution.py:21
  22.2 1.6 %collective-permute-start = (bf16[448,2048]{1,0:T(8,128)(2,1)}, bf16[448,2048]{1,0:T(8,128)(2,1)S(1)}, u32[]{:S(2)}, u32[]{:S(2)}) collective-permute-start(bf16[448,2048]{1,0:T(8,128)(2,1)} %param.9), channel_id=1, source_target_pairs={{0,4},{4,0},{1,5},{5,1},{2,6},{6,2},{3,7},{7,3},{8,12},{12,8},{9,1... | collective-permute-start | bytes 5505032 | tf_op jit(solution)/shard_map/ppermute | solution.py:13
  23.8 4.0 %collective-permute-done.6 = bf16[4,4,2048]{2,1,0:T(4,128)(2,1)S(1)} collective-permute-done((bf16[4,4,2048]{2,1,0:T(4,128)(2,1)S(1)}, bf16[4,4,2048]{2,1,0:T(4,128)(2,1)S(1)}, u32[]{:S(2)}, u32[]{:S(2)}) %collective-permute-start.6) | collective-permute-done | bytes 65568 | tf_op jit(solution)/shard_map/ppermute | solution.py:21
  27.9 3.0 %collective-permute-start.11 = (bf16[4,16,2048]{2,1,0:T(8,128)(2,1)S(1)}, bf16[4,16,2048]{2,1,0:T(8,128)(2,1)S(1)}, u32[]{:S(2)}, u32[]{:S(2)}) collective-permute-start(bf16[4,16,2048]{2,1,0:T(8,128)(2,1)S(1)} %get-tuple-element.40), channel_id=1, source_target_pairs={{0,128},{64,192},{128,0},{192,64},{1,129},{65,193},{129,1},{193,65... | collective-permute-start | bytes 786440 | tf_op jit(solution)/shard_map/ppermute | solution.py:13
  32.4 2.2 %collective-permute-start.8 = (bf16[4,16,2048]{2,1,0:T(8,128)(2,1)S(1)}, bf16[4,16,2048]{2,1,0:T(8,128)(2,1)S(1)}, u32[]{:S(2)}, u32[]{:S(2)}) collective-permute-start(bf16[4,16,2048]{2,1,0:T(8,128)(2,1)S(1)} %get-tuple-element.98), channel_id=1, source_target_pairs={{0,16},{4,52},{8,24},{12,60},{16,32},{20,4},{24,40},{28,12},{32,48... | collective-permute-start | bytes 786440 | tf_op jit(solution)/shard_map/ppermute | solution.py:21
  34.6 3.6 %pad_maximum_fusion = bf16[1792,2048]{1,0:T(8,128)(2,1)S(1)} fusion(bf16[448,2048]{1,0:T(8,128)(2,1)} %collective-permute-done.2, bf16[448,2048]{1,0:T(8,128)(2,1)S(1)} %bitcast.45, bf16[448,2048]{1,0:T(8,128)(2,1)} %collective-permute-done.1, bf16[448,2048]{1,0:T(8,128)(2,1)} %bitcast.47), kind=kLoop, calls=%fused_computation | loop fusion | flops 29360128 | bytes 14680064 | tf_op jit(solution)/shard_map/concatenate | solution.py:95
  38.3 3.4 %collective-permute-done.8 = bf16[4,16,2048]{2,1,0:T(8,128)(2,1)S(1)} collective-permute-done((bf16[4,16,2048]{2,1,0:T(8,128)(2,1)S(1)}, bf16[4,16,2048]{2,1,0:T(8,128)(2,1)S(1)}, u32[]{:S(2)}, u32[]{:S(2)}) %collective-permute-start.8) | collective-permute-done | bytes 262176 | tf_op jit(solution)/shard_map/ppermute | solution.py:21
  42.3 2.0 %collective-permute-start.13 = (bf16[4,16,2048]{2,1,0:T(8,128)(2,1)S(1)}, bf16[4,16,2048]{2,1,0:T(8,128)(2,1)S(1)}, u32[]{:S(2)}, u32[]{:S(2)}) collective-permute-start(bf16[4,16,2048]{2,1,0:T(8,128)(2,1)S(1)} %collective-permute-done.8), channel_id=1, source_target_pairs={{0,192},{64,0},{128,64},{192,128},{1,193},{65,1},{129,65},{193,129... | collective-permute-start | bytes 786440 | tf_op jit(solution)/shard_map/ppermute | solution.py:13
  44.8 2.1 %fusion.37 = (bf16[256,1792]{1,0:T(8,128)(2,1)S(1)}, f32[256,1792]{1,0:T(8,128)S(1)}) fusion(bf16[256,2048]{1,0:T(8,128)(2,1)S(1)} %bitcast.49, bf16[1792,2048]{1,0:T(8,128)(2,1)S(1)} %pad_maximum_fusion), kind=kOutput, calls=%fused_computation.70 | convolution fusion | flops 1879506944 | bytes 11141120 | tf_op jit(solution)/shard_map/dot_general | solution.py:57
  47.2 1.5 %collective-permute-start.16 = (bf16[64,1792]{1,0:T(8,128)(2,1)S(1)}, bf16[64,1792]{1,0:T(8,128)(2,1)S(1)}, u32[]{:S(2)}, u32[]{:S(2)}) collective-permute-start(bf16[64,1792]{1,0:T(8,128)(2,1)S(1)} %get-tuple-element.87), channel_id=1, source_target_pairs={{0,1},{1,2},{2,3},{3,0},{4,5},{5,6},{6,7},{7,4},{8,9},{9,10},{10,1... | collective-permute-start | bytes 688136 | tf_op jit(solution)/shard_map/ppermute | solution.py:13
  49.2 2.1 %collective-permute-done.14 = bf16[4,16,2048]{2,1,0:T(8,128)(2,1)S(1)} collective-permute-done((bf16[4,16,2048]{2,1,0:T(8,128)(2,1)S(1)}, bf16[4,16,2048]{2,1,0:T(8,128)(2,1)S(1)}, u32[]{:S(2)}, u32[]{:S(2)}) %collective-permute-start.14) | collective-permute-done | bytes 262176 | tf_op jit(solution)/shard_map/ppermute | solution.py:13
  51.4 5.2 %collective-permute-done.13 = bf16[4,16,2048]{2,1,0:T(8,128)(2,1)S(1)} collective-permute-done((bf16[4,16,2048]{2,1,0:T(8,128)(2,1)S(1)}, bf16[4,16,2048]{2,1,0:T(8,128)(2,1)S(1)}, u32[]{:S(2)}, u32[]{:S(2)}) %collective-permute-start.13) | collective-permute-done | bytes 262176 | tf_op jit(solution)/shard_map/ppermute | solution.py:13
  57.1 2.1 %fusion.38 = (bf16[256,1792]{1,0:T(8,128)(2,1)S(1)}, f32[256,1792]{1,0:T(8,128)S(1)}) fusion(bf16[256,2048]{1,0:T(8,128)(2,1)S(1)} %bitcast.48, bf16[1792,2048]{1,0:T(8,128)(2,1)S(1)} %pad_maximum_fusion), kind=kOutput, calls=%fused_computation.71 | convolution fusion | flops 1879506944 | bytes 11141120 | tf_op jit(solution)/shard_map/dot_general | solution.py:57
  59.6 2.7 %collective-permute-start.19 = (bf16[64,896]{1,0:T(8,128)(2,1)S(1)}, bf16[64,896]{1,0:T(8,128)(2,1)S(1)}, u32[]{:S(2)}, u32[]{:S(2)}) collective-permute-start(bf16[64,896]{1,0:T(8,128)(2,1)S(1)} %fusion.20), channel_id=1, source_target_pairs={{0,2},{1,3},{2,0},{3,1},{4,6},{5,7},{6,4},{7,5},{8,10},{9,11},{10,... | collective-permute-start | bytes 344072 | tf_op jit(solution)/shard_map/ppermute | solution.py:13
  68.1 2.6 %collective-permute-start.26 = (bf16[4,16,2048]{2,1,0:T(8,128)(2,1)S(1)}, bf16[4,16,2048]{2,1,0:T(8,128)(2,1)S(1)}, u32[]{:S(2)}, u32[]{:S(2)}) collective-permute-start(bf16[4,16,2048]{2,1,0:T(8,128)(2,1)S(1)} %get-tuple-element.80), channel_id=1, source_target_pairs={{0,128},{64,192},{128,0},{192,64},{1,129},{65,193},{129,1},{193,65... | collective-permute-start | bytes 786440 | tf_op jit(solution)/shard_map/ppermute | solution.py:13
  71.1 2.3 %collective-permute-start.24 = (bf16[4,16,2048]{2,1,0:T(8,128)(2,1)S(1)}, bf16[4,16,2048]{2,1,0:T(8,128)(2,1)S(1)}, u32[]{:S(2)}, u32[]{:S(2)}) collective-permute-start(bf16[4,16,2048]{2,1,0:T(8,128)(2,1)S(1)} %get-tuple-element.82), channel_id=1, source_target_pairs={{0,192},{64,0},{128,64},{192,128},{1,193},{65,1},{129,65},{193,129... | collective-permute-start | bytes 786440 | tf_op jit(solution)/shard_map/ppermute | solution.py:13
  73.4 1.9 %collective-permute-done.21 = bf16[64,1792]{1,0:T(8,128)(2,1)S(1)} collective-permute-done((bf16[64,1792]{1,0:T(8,128)(2,1)S(1)}, bf16[64,1792]{1,0:T(8,128)(2,1)S(1)}, u32[]{:S(2)}, u32[]{:S(2)}) %collective-permute-start.21) | collective-permute-done | bytes 229408 | tf_op jit(solution)/shard_map/ppermute | solution.py:13
  75.4 1.9 %collective-permute-start.31 = (bf16[64,896]{1,0:T(8,128)(2,1)S(1)}, bf16[64,896]{1,0:T(8,128)(2,1)S(1)}, u32[]{:S(2)}, u32[]{:S(2)}) collective-permute-start(bf16[64,896]{1,0:T(8,128)(2,1)S(1)} %fusion.19), channel_id=1, source_target_pairs={{0,1},{1,2},{2,3},{3,0},{4,5},{5,6},{6,7},{7,4},{8,9},{9,10},{10,1... | collective-permute-start | bytes 344072 | tf_op jit(solution)/shard_map/ppermute | solution.py:13
  77.4 2.1 %collective-permute-start.30 = (bf16[64,896]{1,0:T(8,128)(2,1)S(1)}, bf16[64,896]{1,0:T(8,128)(2,1)S(1)}, u32[]{:S(2)}, u32[]{:S(2)}) collective-permute-start(bf16[64,896]{1,0:T(8,128)(2,1)S(1)} %fusion.19), channel_id=1, source_target_pairs={{0,2},{1,3},{2,0},{3,1},{4,6},{5,7},{6,4},{7,5},{8,10},{9,11},{10,... | collective-permute-start | bytes 344072 | tf_op jit(solution)/shard_map/ppermute | solution.py:13
  80.8 2.1 %collective-permute-done.30 = bf16[64,896]{1,0:T(8,128)(2,1)S(1)} collective-permute-done((bf16[64,896]{1,0:T(8,128)(2,1)S(1)}, bf16[64,896]{1,0:T(8,128)(2,1)S(1)}, u32[]{:S(2)}, u32[]{:S(2)}) %collective-permute-start.30) | collective-permute-done | bytes 114720 | tf_op jit(solution)/shard_map/ppermute | solution.py:13
  85.0 2.5 %collective-permute-start.34 = (bf16[4,16,2048]{2,1,0:T(8,128)(2,1)S(1)}, bf16[4,16,2048]{2,1,0:T(8,128)(2,1)S(1)}, u32[]{:S(2)}, u32[]{:S(2)}) collective-permute-start(bf16[4,16,2048]{2,1,0:T(8,128)(2,1)S(1)} %get-tuple-element.77), channel_id=1, source_target_pairs={{0,128},{64,192},{128,0},{192,64},{1,129},{65,193},{129,1},{193,65... | collective-permute-start | bytes 786440 | tf_op jit(solution)/shard_map/ppermute | solution.py:13
  87.7 2.5 %collective-permute-start.32 = (bf16[4,16,2048]{2,1,0:T(8,128)(2,1)S(1)}, bf16[4,16,2048]{2,1,0:T(8,128)(2,1)S(1)}, u32[]{:S(2)}, u32[]{:S(2)}) collective-permute-start(bf16[4,16,2048]{2,1,0:T(8,128)(2,1)S(1)} %get-tuple-element.79), channel_id=1, source_target_pairs={{0,192},{64,0},{128,64},{192,128},{1,193},{65,1},{129,65},{193,129... | collective-permute-start | bytes 786440 | tf_op jit(solution)/shard_map/ppermute | solution.py:13
  91.5 6.0 %collective-permute-done.28 = bf16[4,4,2048]{2,1,0:T(4,128)(2,1)S(1)} collective-permute-done((bf16[4,4,2048]{2,1,0:T(4,128)(2,1)S(1)}, bf16[4,4,2048]{2,1,0:T(4,128)(2,1)S(1)}, u32[]{:S(2)}, u32[]{:S(2)}) %collective-permute-start.28) | collective-permute-done | bytes 65568 | tf_op jit(solution)/shard_map/ppermute | solution.py:21
  98.1 2.7 %collective-permute-start.36 = (bf16[4,8,2048]{2,1,0:T(8,128)(2,1)S(1)}, bf16[4,8,2048]{2,1,0:T(8,128)(2,1)S(1)}, u32[]{:S(2)}, u32[]{:S(2)}) collective-permute-start(bf16[4,8,2048]{2,1,0:T(8,128)(2,1)S(1)} %get-tuple-element.90), channel_id=1, source_target_pairs={{0,48},{4,20},{8,56},{12,28},{16,0},{20,36},{24,8},{28,44},{32,16}... | collective-permute-start | bytes 393224 | tf_op jit(solution)/shard_map/ppermute | solution.py:21
  100.8 7.1 %collective-permute-done.35 = bf16[4,8,2048]{2,1,0:T(8,128)(2,1)S(1)} collective-permute-done((bf16[4,8,2048]{2,1,0:T(8,128)(2,1)S(1)}, bf16[4,8,2048]{2,1,0:T(8,128)(2,1)S(1)}, u32[]{:S(2)}, u32[]{:S(2)}) %collective-permute-start.35) | collective-permute-done | bytes 131104 | tf_op jit(solution)/shard_map/ppermute | solution.py:21
  109.0 10.5 %collective-permute-start.37 = (bf16[4,4,2048]{2,1,0:T(4,128)(2,1)S(1)}, bf16[4,4,2048]{2,1,0:T(4,128)(2,1)S(1)}, u32[]{:S(2)}, u32[]{:S(2)}) collective-permute-start(bf16[4,4,2048]{2,1,0:T(4,128)(2,1)S(1)} %select_convert_fusion), channel_id=1, source_target_pairs={{0,4},{4,0},{1,5},{5,1},{2,6},{6,2},{3,7},{7,3},{8,12},{12,8},{9,1... | collective-permute-start | bytes 196616 | tf_op jit(solution)/shard_map/ppermute | solution.py:13
  120.9 3.2 %collective-permute-start.39 = (f32[4,2048]{1,0:T(4,128)S(1)}, f32[4,2048]{1,0:T(4,128)S(1)}, u32[]{:S(2)}, u32[]{:S(2)}) collective-permute-start(f32[4,2048]{1,0:T(4,128)S(1)} %get-tuple-element.96), channel_id=1, source_target_pairs={{0,2},{1,3},{2,0},{3,1},{4,6},{5,7},{6,4},{7,5},{8,10},{9,11},{10,... | collective-permute-start | bytes 98312 | tf_op jit(solution)/shard_map/ppermute | solution.py:13
  124.1 1.6 %collective-permute-start.38 = (f32[4,2048]{1,0:T(4,128)S(1)}, f32[4,2048]{1,0:T(4,128)S(1)}, u32[]{:S(2)}, u32[]{:S(2)}) collective-permute-start(f32[4,2048]{1,0:T(4,128)S(1)} %get-tuple-element.97), channel_id=1, source_target_pairs={{0,3},{1,0},{2,1},{3,2},{4,7},{5,4},{6,5},{7,6},{8,11},{9,8},{10,9... | collective-permute-start | bytes 98312 | tf_op jit(solution)/shard_map/ppermute | solution.py:13
  (98 shorter events, 26.7 us)
Async XLA Ops:
  0.0 31.7 %collective-permute-start.1 = (bf16[448,2048]{1,0:T(8,128)(2,1)}, bf16[448,2048]{1,0:T(8,128)(2,1)}, u32[]{:S(2)}, u32[]{:S(2)}) collective-permute-start(bf16[448,2048]{1,0:T(8,128)(2,1)} %bitcast.46), channel_id=1, source_target_pairs={{0,4},{4,0},{1,5},{5,1},{2,6},{6,2},{3,7},{7,3},{8,12},{12,8},{9,1... | collective-permute-start | bytes 5505032 | tf_op jit(solution)/shard_map/ppermute | solution.py:13
  3.2 29.2 %collective-permute-start.2 = (bf16[448,2048]{1,0:T(8,128)(2,1)}, bf16[448,2048]{1,0:T(8,128)(2,1)}, u32[]{:S(2)}, u32[]{:S(2)}) collective-permute-start(bf16[448,2048]{1,0:T(8,128)(2,1)} %bitcast.44), channel_id=1, source_target_pairs={{0,4},{4,0},{1,5},{5,1},{2,6},{6,2},{3,7},{7,3},{8,12},{12,8},{9,1... | collective-permute-start | bytes 5505032 | tf_op jit(solution)/shard_map/ppermute | solution.py:13
  15.1 12.7 %collective-permute-start.7 = (bf16[4,8,2048]{2,1,0:T(8,128)(2,1)S(1)}, bf16[4,8,2048]{2,1,0:T(8,128)(2,1)S(1)}, u32[]{:S(2)}, u32[]{:S(2)}) collective-permute-start(bf16[4,8,2048]{2,1,0:T(8,128)(2,1)S(1)} %copy.13), channel_id=1, source_target_pairs={{0,8},{4,60},{8,16},{12,4},{16,24},{20,12},{24,32},{28,20},{32,40}... | collective-permute-start | bytes 393224 | tf_op jit(solution)/shard_map/ppermute | solution.py:21
  20.8 7.0 %collective-permute-start.6 = (bf16[4,4,2048]{2,1,0:T(4,128)(2,1)S(1)}, bf16[4,4,2048]{2,1,0:T(4,128)(2,1)S(1)}, u32[]{:S(2)}, u32[]{:S(2)}) collective-permute-start(bf16[4,4,2048]{2,1,0:T(4,128)(2,1)S(1)} %pad_maximum_fusion.6), channel_id=1, source_target_pairs={{0,32},{4,36},{8,40},{12,44},{16,48},{20,52},{24,56},{28,60},{32,0... | collective-permute-start | bytes 196616 | tf_op jit(solution)/shard_map/ppermute | solution.py:21
  22.2 24.9 %collective-permute-start = (bf16[448,2048]{1,0:T(8,128)(2,1)}, bf16[448,2048]{1,0:T(8,128)(2,1)S(1)}, u32[]{:S(2)}, u32[]{:S(2)}) collective-permute-start(bf16[448,2048]{1,0:T(8,128)(2,1)} %param.9), channel_id=1, source_target_pairs={{0,4},{4,0},{1,5},{5,1},{2,6},{6,2},{3,7},{7,3},{8,12},{12,8},{9,1... | collective-permute-start | bytes 5505032 | tf_op jit(solution)/shard_map/ppermute | solution.py:13
  27.9 14.4 %collective-permute-start.11 = (bf16[4,16,2048]{2,1,0:T(8,128)(2,1)S(1)}, bf16[4,16,2048]{2,1,0:T(8,128)(2,1)S(1)}, u32[]{:S(2)}, u32[]{:S(2)}) collective-permute-start(bf16[4,16,2048]{2,1,0:T(8,128)(2,1)S(1)} %get-tuple-element.40), channel_id=1, source_target_pairs={{0,128},{64,192},{128,0},{192,64},{1,129},{65,193},{129,1},{193,65... | collective-permute-start | bytes 786440 | tf_op jit(solution)/shard_map/ppermute | solution.py:13
  30.9 13.4 %collective-permute-start.10 = (bf16[4,16,2048]{2,1,0:T(8,128)(2,1)S(1)}, bf16[4,16,2048]{2,1,0:T(8,128)(2,1)S(1)}, u32[]{:S(2)}, u32[]{:S(2)}) collective-permute-start(bf16[4,16,2048]{2,1,0:T(8,128)(2,1)S(1)} %get-tuple-element.40), channel_id=1, source_target_pairs={{0,192},{64,0},{128,64},{192,128},{1,193},{65,1},{129,65},{193,129... | collective-permute-start | bytes 786440 | tf_op jit(solution)/shard_map/ppermute | solution.py:13
  31.7 13.0 %collective-permute-start.9 = (bf16[4,16,2048]{2,1,0:T(8,128)(2,1)S(1)}, bf16[4,16,2048]{2,1,0:T(8,128)(2,1)S(1)}, u32[]{:S(2)}, u32[]{:S(2)}) collective-permute-start(bf16[4,16,2048]{2,1,0:T(8,128)(2,1)S(1)} %get-tuple-element.40), channel_id=1, source_target_pairs={{0,64},{64,128},{128,192},{192,0},{1,65},{65,129},{129,193},{193,1... | collective-permute-start | bytes 786440 | tf_op jit(solution)/shard_map/ppermute | solution.py:13
  32.4 9.3 %collective-permute-start.8 = (bf16[4,16,2048]{2,1,0:T(8,128)(2,1)S(1)}, bf16[4,16,2048]{2,1,0:T(8,128)(2,1)S(1)}, u32[]{:S(2)}, u32[]{:S(2)}) collective-permute-start(bf16[4,16,2048]{2,1,0:T(8,128)(2,1)S(1)} %get-tuple-element.98), channel_id=1, source_target_pairs={{0,16},{4,52},{8,24},{12,60},{16,32},{20,4},{24,40},{28,12},{32,48... | collective-permute-start | bytes 786440 | tf_op jit(solution)/shard_map/ppermute | solution.py:21
  41.7 9.7 %collective-permute-start.14 = (bf16[4,16,2048]{2,1,0:T(8,128)(2,1)S(1)}, bf16[4,16,2048]{2,1,0:T(8,128)(2,1)S(1)}, u32[]{:S(2)}, u32[]{:S(2)}) collective-permute-start(bf16[4,16,2048]{2,1,0:T(8,128)(2,1)S(1)} %collective-permute-done.8), channel_id=1, source_target_pairs={{0,128},{64,192},{128,0},{192,64},{1,129},{65,193},{129,1},{193,65... | collective-permute-start | bytes 786440 | tf_op jit(solution)/shard_map/ppermute | solution.py:13
  42.3 14.3 %collective-permute-start.13 = (bf16[4,16,2048]{2,1,0:T(8,128)(2,1)S(1)}, bf16[4,16,2048]{2,1,0:T(8,128)(2,1)S(1)}, u32[]{:S(2)}, u32[]{:S(2)}) collective-permute-start(bf16[4,16,2048]{2,1,0:T(8,128)(2,1)S(1)} %collective-permute-done.8), channel_id=1, source_target_pairs={{0,192},{64,0},{128,64},{192,128},{1,193},{65,1},{129,65},{193,129... | collective-permute-start | bytes 786440 | tf_op jit(solution)/shard_map/ppermute | solution.py:13
  44.3 12.8 %collective-permute-start.12 = (bf16[4,16,2048]{2,1,0:T(8,128)(2,1)S(1)}, bf16[4,16,2048]{2,1,0:T(8,128)(2,1)S(1)}, u32[]{:S(2)}, u32[]{:S(2)}) collective-permute-start(bf16[4,16,2048]{2,1,0:T(8,128)(2,1)S(1)} %collective-permute-done.8), channel_id=1, source_target_pairs={{0,64},{64,128},{128,192},{192,0},{1,65},{65,129},{129,193},{193,1... | collective-permute-start | bytes 786440 | tf_op jit(solution)/shard_map/ppermute | solution.py:13
  47.0 12.3 %collective-permute-start.17 = (bf16[64,1792]{1,0:T(8,128)(2,1)S(1)}, bf16[64,1792]{1,0:T(8,128)(2,1)S(1)}, u32[]{:S(2)}, u32[]{:S(2)}) collective-permute-start(bf16[64,1792]{1,0:T(8,128)(2,1)S(1)} %get-tuple-element.86), channel_id=1, source_target_pairs={{0,3},{1,0},{2,1},{3,2},{4,7},{5,4},{6,5},{7,6},{8,11},{9,8},{10,9... | collective-permute-start | bytes 688136 | tf_op jit(solution)/shard_map/ppermute | solution.py:13
  47.2 12.1 %collective-permute-start.16 = (bf16[64,1792]{1,0:T(8,128)(2,1)S(1)}, bf16[64,1792]{1,0:T(8,128)(2,1)S(1)}, u32[]{:S(2)}, u32[]{:S(2)}) collective-permute-start(bf16[64,1792]{1,0:T(8,128)(2,1)S(1)} %get-tuple-element.87), channel_id=1, source_target_pairs={{0,1},{1,2},{2,3},{3,0},{4,5},{5,6},{6,7},{7,4},{8,9},{9,10},{10,1... | collective-permute-start | bytes 688136 | tf_op jit(solution)/shard_map/ppermute | solution.py:13
  51.3 8.0 %collective-permute-start.15 = (bf16[64,1792]{1,0:T(8,128)(2,1)S(1)}, bf16[64,1792]{1,0:T(8,128)(2,1)S(1)}, u32[]{:S(2)}, u32[]{:S(2)}) collective-permute-start(bf16[64,1792]{1,0:T(8,128)(2,1)S(1)} %get-tuple-element.88), channel_id=1, source_target_pairs={{0,2},{1,3},{2,0},{3,1},{4,6},{5,7},{6,4},{7,5},{8,10},{9,11},{10,... | collective-permute-start | bytes 688136 | tf_op jit(solution)/shard_map/ppermute | solution.py:13
  59.5 5.6 %collective-permute-start.20 = (bf16[64,896]{1,0:T(8,128)(2,1)S(1)}, bf16[64,896]{1,0:T(8,128)(2,1)S(1)}, u32[]{:S(2)}, u32[]{:S(2)}) collective-permute-start(bf16[64,896]{1,0:T(8,128)(2,1)S(1)} %fusion.20), channel_id=1, source_target_pairs={{0,1},{1,2},{2,3},{3,0},{4,5},{5,6},{6,7},{7,4},{8,9},{9,10},{10,1... | collective-permute-start | bytes 344072 | tf_op jit(solution)/shard_map/ppermute | solution.py:13
  59.6 6.6 %collective-permute-start.19 = (bf16[64,896]{1,0:T(8,128)(2,1)S(1)}, bf16[64,896]{1,0:T(8,128)(2,1)S(1)}, u32[]{:S(2)}, u32[]{:S(2)}) collective-permute-start(bf16[64,896]{1,0:T(8,128)(2,1)S(1)} %fusion.20), channel_id=1, source_target_pairs={{0,2},{1,3},{2,0},{3,1},{4,6},{5,7},{6,4},{7,5},{8,10},{9,11},{10,... | collective-permute-start | bytes 344072 | tf_op jit(solution)/shard_map/ppermute | solution.py:13
  63.6 7.4 %collective-permute-start.23 = (bf16[64,1792]{1,0:T(8,128)(2,1)S(1)}, bf16[64,1792]{1,0:T(8,128)(2,1)S(1)}, u32[]{:S(2)}, u32[]{:S(2)}) collective-permute-start(bf16[64,1792]{1,0:T(8,128)(2,1)S(1)} %get-tuple-element.83), channel_id=1, source_target_pairs={{0,3},{1,0},{2,1},{3,2},{4,7},{5,4},{6,5},{7,6},{8,11},{9,8},{10,9... | collective-permute-start | bytes 688136 | tf_op jit(solution)/shard_map/ppermute | solution.py:13
  63.7 9.7 %collective-permute-start.22 = (bf16[64,1792]{1,0:T(8,128)(2,1)S(1)}, bf16[64,1792]{1,0:T(8,128)(2,1)S(1)}, u32[]{:S(2)}, u32[]{:S(2)}) collective-permute-start(bf16[64,1792]{1,0:T(8,128)(2,1)S(1)} %get-tuple-element.84), channel_id=1, source_target_pairs={{0,1},{1,2},{2,3},{3,0},{4,5},{5,6},{6,7},{7,4},{8,9},{9,10},{10,1... | collective-permute-start | bytes 688136 | tf_op jit(solution)/shard_map/ppermute | solution.py:13
  65.2 10.1 %collective-permute-start.21 = (bf16[64,1792]{1,0:T(8,128)(2,1)S(1)}, bf16[64,1792]{1,0:T(8,128)(2,1)S(1)}, u32[]{:S(2)}, u32[]{:S(2)}) collective-permute-start(bf16[64,1792]{1,0:T(8,128)(2,1)S(1)} %get-tuple-element.85), channel_id=1, source_target_pairs={{0,2},{1,3},{2,0},{3,1},{4,6},{5,7},{6,4},{7,5},{8,10},{9,11},{10,... | collective-permute-start | bytes 688136 | tf_op jit(solution)/shard_map/ppermute | solution.py:13
  68.1 11.4 %collective-permute-start.26 = (bf16[4,16,2048]{2,1,0:T(8,128)(2,1)S(1)}, bf16[4,16,2048]{2,1,0:T(8,128)(2,1)S(1)}, u32[]{:S(2)}, u32[]{:S(2)}) collective-permute-start(bf16[4,16,2048]{2,1,0:T(8,128)(2,1)S(1)} %get-tuple-element.80), channel_id=1, source_target_pairs={{0,128},{64,192},{128,0},{192,64},{1,129},{65,193},{129,1},{193,65... | collective-permute-start | bytes 786440 | tf_op jit(solution)/shard_map/ppermute | solution.py:13
  70.7 9.2 %collective-permute-start.25 = (bf16[4,16,2048]{2,1,0:T(8,128)(2,1)S(1)}, bf16[4,16,2048]{2,1,0:T(8,128)(2,1)S(1)}, u32[]{:S(2)}, u32[]{:S(2)}) collective-permute-start(bf16[4,16,2048]{2,1,0:T(8,128)(2,1)S(1)} %get-tuple-element.81), channel_id=1, source_target_pairs={{0,64},{64,128},{128,192},{192,0},{1,65},{65,129},{129,193},{193,1... | collective-permute-start | bytes 786440 | tf_op jit(solution)/shard_map/ppermute | solution.py:13
  71.1 8.8 %collective-permute-start.24 = (bf16[4,16,2048]{2,1,0:T(8,128)(2,1)S(1)}, bf16[4,16,2048]{2,1,0:T(8,128)(2,1)S(1)}, u32[]{:S(2)}, u32[]{:S(2)}) collective-permute-start(bf16[4,16,2048]{2,1,0:T(8,128)(2,1)S(1)} %get-tuple-element.82), channel_id=1, source_target_pairs={{0,192},{64,0},{128,64},{192,128},{1,193},{65,1},{129,65},{193,129... | collective-permute-start | bytes 786440 | tf_op jit(solution)/shard_map/ppermute | solution.py:13
  77.4 5.5 %collective-permute-start.30 = (bf16[64,896]{1,0:T(8,128)(2,1)S(1)}, bf16[64,896]{1,0:T(8,128)(2,1)S(1)}, u32[]{:S(2)}, u32[]{:S(2)}) collective-permute-start(bf16[64,896]{1,0:T(8,128)(2,1)S(1)} %fusion.19), channel_id=1, source_target_pairs={{0,2},{1,3},{2,0},{3,1},{4,6},{5,7},{6,4},{7,5},{8,10},{9,11},{10,... | collective-permute-start | bytes 344072 | tf_op jit(solution)/shard_map/ppermute | solution.py:13
  85.0 12.6 %collective-permute-start.34 = (bf16[4,16,2048]{2,1,0:T(8,128)(2,1)S(1)}, bf16[4,16,2048]{2,1,0:T(8,128)(2,1)S(1)}, u32[]{:S(2)}, u32[]{:S(2)}) collective-permute-start(bf16[4,16,2048]{2,1,0:T(8,128)(2,1)S(1)} %get-tuple-element.77), channel_id=1, source_target_pairs={{0,128},{64,192},{128,0},{192,64},{1,129},{65,193},{129,1},{193,65... | collective-permute-start | bytes 786440 | tf_op jit(solution)/shard_map/ppermute | solution.py:13
  87.5 10.1 %collective-permute-start.33 = (bf16[4,16,2048]{2,1,0:T(8,128)(2,1)S(1)}, bf16[4,16,2048]{2,1,0:T(8,128)(2,1)S(1)}, u32[]{:S(2)}, u32[]{:S(2)}) collective-permute-start(bf16[4,16,2048]{2,1,0:T(8,128)(2,1)S(1)} %get-tuple-element.78), channel_id=1, source_target_pairs={{0,64},{64,128},{128,192},{192,0},{1,65},{65,129},{129,193},{193,1... | collective-permute-start | bytes 786440 | tf_op jit(solution)/shard_map/ppermute | solution.py:13
  87.7 9.9 %collective-permute-start.32 = (bf16[4,16,2048]{2,1,0:T(8,128)(2,1)S(1)}, bf16[4,16,2048]{2,1,0:T(8,128)(2,1)S(1)}, u32[]{:S(2)}, u32[]{:S(2)}) collective-permute-start(bf16[4,16,2048]{2,1,0:T(8,128)(2,1)S(1)} %get-tuple-element.79), channel_id=1, source_target_pairs={{0,192},{64,0},{128,64},{192,128},{1,193},{65,1},{129,65},{193,129... | collective-permute-start | bytes 786440 | tf_op jit(solution)/shard_map/ppermute | solution.py:13
  90.3 7.3 %collective-permute-start.27 = (bf16[4,8,2048]{2,1,0:T(8,128)(2,1)S(1)}, bf16[4,8,2048]{2,1,0:T(8,128)(2,1)S(1)}, u32[]{:S(2)}, u32[]{:S(2)}) collective-permute-start(bf16[4,8,2048]{2,1,0:T(8,128)(2,1)S(1)} %slice.185), channel_id=1, source_target_pairs={{0,56},{4,12},{8,0},{12,20},{16,8},{20,28},{24,16},{28,36},{32,24}... | collective-permute-start | bytes 393224 | tf_op jit(solution)/shard_map/ppermute | solution.py:21
  90.5 7.1 %collective-permute-start.28 = (bf16[4,4,2048]{2,1,0:T(4,128)(2,1)S(1)}, bf16[4,4,2048]{2,1,0:T(4,128)(2,1)S(1)}, u32[]{:S(2)}, u32[]{:S(2)}) collective-permute-start(bf16[4,4,2048]{2,1,0:T(4,128)(2,1)S(1)} %slice.186), channel_id=1, source_target_pairs={{0,32},{4,36},{8,40},{12,44},{16,48},{20,52},{24,56},{28,60},{32,0... | collective-permute-start | bytes 196616 | tf_op jit(solution)/shard_map/ppermute | solution.py:21
  97.8 10.2 %collective-permute-start.35 = (bf16[4,8,2048]{2,1,0:T(8,128)(2,1)S(1)}, bf16[4,8,2048]{2,1,0:T(8,128)(2,1)S(1)}, u32[]{:S(2)}, u32[]{:S(2)}) collective-permute-start(bf16[4,8,2048]{2,1,0:T(8,128)(2,1)S(1)} %get-tuple-element.89), channel_id=1, source_target_pairs={{0,40},{4,28},{8,48},{12,36},{16,56},{20,44},{24,0},{28,52},{32,8}... | collective-permute-start | bytes 393224 | tf_op jit(solution)/shard_map/ppermute | solution.py:21
  98.1 10.8 %collective-permute-start.36 = (bf16[4,8,2048]{2,1,0:T(8,128)(2,1)S(1)}, bf16[4,8,2048]{2,1,0:T(8,128)(2,1)S(1)}, u32[]{:S(2)}, u32[]{:S(2)}) collective-permute-start(bf16[4,8,2048]{2,1,0:T(8,128)(2,1)S(1)} %get-tuple-element.90), channel_id=1, source_target_pairs={{0,48},{4,20},{8,56},{12,28},{16,0},{20,36},{24,8},{28,44},{32,16}... | collective-permute-start | bytes 393224 | tf_op jit(solution)/shard_map/ppermute | solution.py:21
  109.0 11.4 %collective-permute-start.37 = (bf16[4,4,2048]{2,1,0:T(4,128)(2,1)S(1)}, bf16[4,4,2048]{2,1,0:T(4,128)(2,1)S(1)}, u32[]{:S(2)}, u32[]{:S(2)}) collective-permute-start(bf16[4,4,2048]{2,1,0:T(4,128)(2,1)S(1)} %select_convert_fusion), channel_id=1, source_target_pairs={{0,4},{4,0},{1,5},{5,1},{2,6},{6,2},{3,7},{7,3},{8,12},{12,8},{9,1... | collective-permute-start | bytes 196616 | tf_op jit(solution)/shard_map/ppermute | solution.py:13
  (12 other events, 110.1 us)

commit v6 on v5

--- a/solution.py
+++ b/solution.py
@@ -108,21 +108,24 @@
     near_hidden = activate(near_kept, near_sums)
     near_spread = spread(near_hidden)
 
+    near_hidden, *far_sums = together(near_hidden, *far_sums)
+    far_hidden = activate(far_kept, far_sums)
+    far_spread = spread(far_hidden)
+    far_hidden, *near_spread = together(far_hidden, *near_spread)
+
     near_down = by_y(down(second, [near_hidden] + near_spread))
     near_back = back_over_y(near_down)
-    near_down[0], *far_sums = together(near_down[0], *far_sums)
-    far_hidden = activate(far_kept, far_sums)
-    far_spread = spread(far_hidden)
-    far_hidden, *near_back = together(far_hidden, *near_back)
+    near_down[0], *far_spread = together(near_down[0], *far_spread)
+    far_down = by_y(down(second, [far_hidden] + far_spread))
+    far_back = back_over_y(far_down)
+    far_down[0], *near_back = together(far_down[0], *near_back)
 
     near_total = sum_over_y(near_down, near_back)
     near_pieces = [
         along_z(near_total[:, 2 * rows :].astype(BF16), -1, 1),
         along_z(near_total[:, rows : 2 * rows].astype(BF16), 4, 4),
     ]
-    far_down = by_y(down(second, [far_hidden] + far_spread))
-    far_back = back_over_y(far_down)
-    *near_pieces, back_1, back_3, back_2 = together(*near_pieces, *far_back)
+    near_pieces[0], back_1, back_3, back_2 = together(near_pieces[0], *far_back)
     far_total = sum_over_y(far_down, (back_1, back_3, back_2))
     pair = sum(
         piece.astype(F32)

time: 129 us -> 130 us (level)
  waiting for transfers between devices: 40.5 us -> 48.5 us
  starting transfers between devices: 67.3 us -> 61.2 us
    ppermute x34, waiting for transfers between devices: 18.9 us -> 36.5 us  [shift(): return lax.ppermute(value, axis, [(i, (i + step) % n) for i in range(n)])]
    ppermute x7, waiting for transfers between devices: 21.6 us -> 12.1 us  [along_z(): return lax.ppermute(value, ('z', 'c'), pairs)]
    ppermute x34, starting transfers between devices: 53.7 us -> 46.1 us  [shift(): return lax.ppermute(value, axis, [(i, (i + step) % n) for i in range(n)])]
    ppermute x7, starting transfers between devices: 13.6 us -> 15.1 us  [along_z(): return lax.ppermute(value, ('z', 'c'), pairs)]
  transfers between devices with their start and end apart: 41 -> 41, of which waited for: 19 -> 21; matrix products, arithmetic and copies ran while one was open for 10% -> 11% of each run, Pallas kernels for 0% -> 0%
where the time goes in v6:
time: 130 us
  starting transfers between devices  61.2 us (47%)
  waiting for transfers between devices  48.5 us (37%)
  other arithmetic  8.28 us (6%)
  matrix products  6.82 us (5%)
  blocking collectives  3.72 us (3%)
    ppermute x34, starting transfers between devices, shift(): return lax.ppermute(value, axis, [(i, (i + step) % n) for i in range(n)])  46.1 us
    ppermute x34, waiting for transfers between devices, shift(): return lax.ppermute(value, axis, [(i, (i + step) % n) for i in range(n)])  36.5 us
    ppermute x7, starting transfers between devices, along_z(): return lax.ppermute(value, ('z', 'c'), pairs)  15.1 us
    ppermute x7, waiting for transfers between devices, along_z(): return lax.ppermute(value, ('z', 'c'), pairs)  12.1 us
    dot_general x2, matrix products, project(): lax.dot_general(block.reshape(-1, part), weights, (((1,), (1,)), ((), ())...  4.24 us
    all_gather x1, blocking collectives, local(): pair = lax.all_gather(own, 'c', axis=1, tiled=True)  3.72 us
    concatenate x1, other arithmetic, local(): first, far = together(jnp.concatenate(first, axis=0), far)  3.61 us
  transfers between devices with their start and end apart: 41, of which 21 were waited for; matrix products, arithmetic and copies ran while one was open for 11% of the time, Pallas kernels for 0%

profile of v6, /device:TPU:1, one launch (start us, length us, event | category | flops | bytes accessed | tf_op | source)
XLA Modules:
  0.0 129.5 jit_solution(11601348692813746746)
XLA Ops:
  0.0 3.2 %collective-permute-start.1 = (bf16[448,2048]{1,0:T(8,128)(2,1)}, bf16[448,2048]{1,0:T(8,128)(2,1)}, u32[]{:S(2)}, u32[]{:S(2)}) collective-permute-start(bf16[448,2048]{1,0:T(8,128)(2,1)} %bitcast.46), channel_id=1, source_target_pairs={{0,4},{4,0},{1,5},{5,1},{2,6},{6,2},{3,7},{7,3},{8,12},{12,8},{9,1... | collective-permute-start | bytes 5505032 | tf_op jit(solution)/shard_map/ppermute | solution.py:13
  8.0 1.5 %collective-permute-done.4 = bf16[4,2048]{1,0:T(4,128)(2,1)S(1)} collective-permute-done((bf16[4,2048]{1,0:T(4,128)(2,1)S(1)}, bf16[4,2048]{1,0:T(4,128)(2,1)S(1)}, u32[]{:S(2)}, u32[]{:S(2)}) %collective-permute-start.4) | collective-permute-done | bytes 16416 | tf_op jit(solution)/shard_map/ppermute | solution.py:13
  9.6 1.7 %collective-permute-done.5 = bf16[4,2048]{1,0:T(4,128)(2,1)S(1)} collective-permute-done((bf16[4,2048]{1,0:T(4,128)(2,1)S(1)}, bf16[4,2048]{1,0:T(4,128)(2,1)S(1)}, u32[]{:S(2)}, u32[]{:S(2)}) %collective-permute-start.5) | collective-permute-done | bytes 16416 | tf_op jit(solution)/shard_map/ppermute | solution.py:13
  11.3 3.7 %all_gather.3 = bf16[4,8,2048]{2,0,1:T(4,128)(2,1)S(1)} all-gather(bf16[4,4,2048]{2,0,1:T(4,128)(2,1)S(1)} %copy.12), channel_id=1, replica_groups=mesh['y'=4,'z'=8,'c'=2,'x'=4] {'c'}, dimensions={1}, use_global_device_ids=true | all-gather | bytes 196608 | tf_op jit(solution)/shard_map/all_gather | solution.py:51
  15.1 5.7 %collective-permute-start.7 = (bf16[4,8,2048]{2,1,0:T(8,128)(2,1)S(1)}, bf16[4,8,2048]{2,1,0:T(8,128)(2,1)S(1)}, u32[]{:S(2)}, u32[]{:S(2)}) collective-permute-start(bf16[4,8,2048]{2,1,0:T(8,128)(2,1)S(1)} %copy.13), channel_id=1, source_target_pairs={{0,8},{4,60},{8,16},{12,4},{16,24},{20,12},{24,32},{28,20},{32,40}... | collective-permute-start | bytes 393224 | tf_op jit(solution)/shard_map/ppermute | solution.py:21
  22.2 1.6 %collective-permute-start = (bf16[448,2048]{1,0:T(8,128)(2,1)}, bf16[448,2048]{1,0:T(8,128)(2,1)S(1)}, u32[]{:S(2)}, u32[]{:S(2)}) collective-permute-start(bf16[448,2048]{1,0:T(8,128)(2,1)} %param.9), channel_id=1, source_target_pairs={{0,4},{4,0},{1,5},{5,1},{2,6},{6,2},{3,7},{7,3},{8,12},{12,8},{9,1... | collective-permute-start | bytes 5505032 | tf_op jit(solution)/shard_map/ppermute | solution.py:13
  23.8 4.0 %collective-permute-done.6 = bf16[4,4,2048]{2,1,0:T(4,128)(2,1)S(1)} collective-permute-done((bf16[4,4,2048]{2,1,0:T(4,128)(2,1)S(1)}, bf16[4,4,2048]{2,1,0:T(4,128)(2,1)S(1)}, u32[]{:S(2)}, u32[]{:S(2)}) %collective-permute-start.6) | collective-permute-done | bytes 65568 | tf_op jit(solution)/shard_map/ppermute | solution.py:21
  27.9 3.0 %collective-permute-start.11 = (bf16[4,16,2048]{2,1,0:T(8,128)(2,1)S(1)}, bf16[4,16,2048]{2,1,0:T(8,128)(2,1)S(1)}, u32[]{:S(2)}, u32[]{:S(2)}) collective-permute-start(bf16[4,16,2048]{2,1,0:T(8,128)(2,1)S(1)} %get-tuple-element.47), channel_id=1, source_target_pairs={{0,128},{64,192},{128,0},{192,64},{1,129},{65,193},{129,1},{193,65... | collective-permute-start | bytes 786440 | tf_op jit(solution)/shard_map/ppermute | solution.py:13
  32.4 2.2 %collective-permute-start.8 = (bf16[4,16,2048]{2,1,0:T(8,128)(2,1)S(1)}, bf16[4,16,2048]{2,1,0:T(8,128)(2,1)S(1)}, u32[]{:S(2)}, u32[]{:S(2)}) collective-permute-start(bf16[4,16,2048]{2,1,0:T(8,128)(2,1)S(1)} %get-tuple-element.112), channel_id=1, source_target_pairs={{0,16},{4,52},{8,24},{12,60},{16,32},{20,4},{24,40},{28,12},{32,48... | collective-permute-start | bytes 786440 | tf_op jit(solution)/shard_map/ppermute | solution.py:21
  34.6 3.6 %pad_maximum_fusion = bf16[1792,2048]{1,0:T(8,128)(2,1)S(1)} fusion(bf16[448,2048]{1,0:T(8,128)(2,1)} %collective-permute-done.2, bf16[448,2048]{1,0:T(8,128)(2,1)S(1)} %bitcast.45, bf16[448,2048]{1,0:T(8,128)(2,1)} %collective-permute-done.1, bf16[448,2048]{1,0:T(8,128)(2,1)} %bitcast.47), kind=kLoop, calls=%fused_computation | loop fusion | flops 29360128 | bytes 14680064 | tf_op jit(solution)/shard_map/concatenate | solution.py:95
  38.3 3.4 %collective-permute-done.8 = bf16[4,16,2048]{2,1,0:T(8,128)(2,1)S(1)} collective-permute-done((bf16[4,16,2048]{2,1,0:T(8,128)(2,1)S(1)}, bf16[4,16,2048]{2,1,0:T(8,128)(2,1)S(1)}, u32[]{:S(2)}, u32[]{:S(2)}) %collective-permute-start.8) | collective-permute-done | bytes 262176 | tf_op jit(solution)/shard_map/ppermute | solution.py:21
  42.3 2.0 %collective-permute-start.13 = (bf16[4,16,2048]{2,1,0:T(8,128)(2,1)S(1)}, bf16[4,16,2048]{2,1,0:T(8,128)(2,1)S(1)}, u32[]{:S(2)}, u32[]{:S(2)}) collective-permute-start(bf16[4,16,2048]{2,1,0:T(8,128)(2,1)S(1)} %collective-permute-done.8), channel_id=1, source_target_pairs={{0,192},{64,0},{128,64},{192,128},{1,193},{65,1},{129,65},{193,129... | collective-permute-start | bytes 786440 | tf_op jit(solution)/shard_map/ppermute | solution.py:13
  44.8 2.1 %fusion.34 = (bf16[256,1792]{1,0:T(8,128)(2,1)S(1)}, f32[256,1792]{1,0:T(8,128)S(1)}) fusion(bf16[256,2048]{1,0:T(8,128)(2,1)S(1)} %bitcast.49, bf16[1792,2048]{1,0:T(8,128)(2,1)S(1)} %pad_maximum_fusion), kind=kOutput, calls=%fused_computation.67 | convolution fusion | flops 1879506944 | bytes 11141120 | tf_op jit(solution)/shard_map/dot_general | solution.py:57
  49.2 2.1 %collective-permute-done.14 = bf16[4,16,2048]{2,1,0:T(8,128)(2,1)S(1)} collective-permute-done((bf16[4,16,2048]{2,1,0:T(8,128)(2,1)S(1)}, bf16[4,16,2048]{2,1,0:T(8,128)(2,1)S(1)}, u32[]{:S(2)}, u32[]{:S(2)}) %collective-permute-start.14) | collective-permute-done | bytes 262176 | tf_op jit(solution)/shard_map/ppermute | solution.py:13
  51.4 5.2 %collective-permute-done.13 = bf16[4,16,2048]{2,1,0:T(8,128)(2,1)S(1)} collective-permute-done((bf16[4,16,2048]{2,1,0:T(8,128)(2,1)S(1)}, bf16[4,16,2048]{2,1,0:T(8,128)(2,1)S(1)}, u32[]{:S(2)}, u32[]{:S(2)}) %collective-permute-start.13) | collective-permute-done | bytes 262176 | tf_op jit(solution)/shard_map/ppermute | solution.py:13
  57.1 2.1 %fusion.35 = (bf16[256,1792]{1,0:T(8,128)(2,1)S(1)}, f32[256,1792]{1,0:T(8,128)S(1)}) fusion(bf16[256,2048]{1,0:T(8,128)(2,1)S(1)} %bitcast.48, bf16[1792,2048]{1,0:T(8,128)(2,1)S(1)} %pad_maximum_fusion), kind=kOutput, calls=%fused_computation.68 | convolution fusion | flops 1879506944 | bytes 11141120 | tf_op jit(solution)/shard_map/dot_general | solution.py:57
  61.2 1.9 %collective-permute-start.23 = (bf16[64,896]{1,0:T(8,128)(2,1)S(1)}, bf16[64,896]{1,0:T(8,128)(2,1)S(1)}, u32[]{:S(2)}, u32[]{:S(2)}) collective-permute-start(bf16[64,896]{1,0:T(8,128)(2,1)S(1)} %fusion.17), channel_id=1, source_target_pairs={{0,1},{1,2},{2,3},{3,0},{4,5},{5,6},{6,7},{7,4},{8,9},{9,10},{10,1... | collective-permute-start | bytes 344072 | tf_op jit(solution)/shard_map/ppermute | solution.py:13
  63.1 1.7 %collective-permute-start.22 = (bf16[64,896]{1,0:T(8,128)(2,1)S(1)}, bf16[64,896]{1,0:T(8,128)(2,1)S(1)}, u32[]{:S(2)}, u32[]{:S(2)}) collective-permute-start(bf16[64,896]{1,0:T(8,128)(2,1)S(1)} %fusion.17), channel_id=1, source_target_pairs={{0,2},{1,3},{2,0},{3,1},{4,6},{5,7},{6,4},{7,5},{8,10},{9,11},{10,... | collective-permute-start | bytes 344072 | tf_op jit(solution)/shard_map/ppermute | solution.py:13
  67.6 3.7 %collective-permute-done.19 = bf16[64,1792]{1,0:T(8,128)(2,1)S(1)} collective-permute-done((bf16[64,1792]{1,0:T(8,128)(2,1)S(1)}, bf16[64,1792]{1,0:T(8,128)(2,1)S(1)}, u32[]{:S(2)}, u32[]{:S(2)}) %collective-permute-start.19) | collective-permute-done | bytes 229408 | tf_op jit(solution)/shard_map/ppermute | solution.py:13
  71.6 3.3 %collective-permute-start.25 = (bf16[64,896]{1,0:T(8,128)(2,1)S(1)}, bf16[64,896]{1,0:T(8,128)(2,1)S(1)}, u32[]{:S(2)}, u32[]{:S(2)}) collective-permute-start(bf16[64,896]{1,0:T(8,128)(2,1)S(1)} %fusion.16), channel_id=1, source_target_pairs={{0,2},{1,3},{2,0},{3,1},{4,6},{5,7},{6,4},{7,5},{8,10},{9,11},{10,... | collective-permute-start | bytes 344072 | tf_op jit(solution)/shard_map/ppermute | solution.py:13
  74.9 1.9 %collective-permute-done.23 = bf16[64,896]{1,0:T(8,128)(2,1)S(1)} collective-permute-done((bf16[64,896]{1,0:T(8,128)(2,1)S(1)}, bf16[64,896]{1,0:T(8,128)(2,1)S(1)}, u32[]{:S(2)}, u32[]{:S(2)}) %collective-permute-start.23) | collective-permute-done | bytes 114720 | tf_op jit(solution)/shard_map/ppermute | solution.py:13
  78.6 2.6 %collective-permute-start.28 = (bf16[4,16,2048]{2,1,0:T(8,128)(2,1)S(1)}, bf16[4,16,2048]{2,1,0:T(8,128)(2,1)S(1)}, u32[]{:S(2)}, u32[]{:S(2)}) collective-permute-start(bf16[4,16,2048]{2,1,0:T(8,128)(2,1)S(1)} %get-tuple-element.95), channel_id=1, source_target_pairs={{0,64},{64,128},{128,192},{192,0},{1,65},{65,129},{129,193},{193,1... | collective-permute-start | bytes 786440 | tf_op jit(solution)/shard_map/ppermute | solution.py:13
  82.1 2.1 %collective-permute-start.27 = (bf16[4,16,2048]{2,1,0:T(8,128)(2,1)S(1)}, bf16[4,16,2048]{2,1,0:T(8,128)(2,1)S(1)}, u32[]{:S(2)}, u32[]{:S(2)}) collective-permute-start(bf16[4,16,2048]{2,1,0:T(8,128)(2,1)S(1)} %get-tuple-element.96), channel_id=1, source_target_pairs={{0,192},{64,0},{128,64},{192,128},{1,193},{65,1},{129,65},{193,129... | collective-permute-start | bytes 786440 | tf_op jit(solution)/shard_map/ppermute | solution.py:13
  86.4 2.2 %collective-permute-start.32 = (bf16[4,16,2048]{2,1,0:T(8,128)(2,1)S(1)}, bf16[4,16,2048]{2,1,0:T(8,128)(2,1)S(1)}, u32[]{:S(2)}, u32[]{:S(2)}) collective-permute-start(bf16[4,16,2048]{2,1,0:T(8,128)(2,1)S(1)} %get-tuple-element.93), channel_id=1, source_target_pairs={{0,192},{64,0},{128,64},{192,128},{1,193},{65,1},{129,65},{193,129... | collective-permute-start | bytes 786440 | tf_op jit(solution)/shard_map/ppermute | solution.py:13
  88.6 4.1 %collective-permute-done.28 = bf16[4,16,2048]{2,1,0:T(8,128)(2,1)S(1)} collective-permute-done((bf16[4,16,2048]{2,1,0:T(8,128)(2,1)S(1)}, bf16[4,16,2048]{2,1,0:T(8,128)(2,1)S(1)}, u32[]{:S(2)}, u32[]{:S(2)}) %collective-permute-start.28) | collective-permute-done | bytes 262176 | tf_op jit(solution)/shard_map/ppermute | solution.py:13
  93.8 1.7 %collective-permute-done.34 = bf16[4,16,2048]{2,1,0:T(8,128)(2,1)S(1)} collective-permute-done((bf16[4,16,2048]{2,1,0:T(8,128)(2,1)S(1)}, bf16[4,16,2048]{2,1,0:T(8,128)(2,1)S(1)}, u32[]{:S(2)}, u32[]{:S(2)}) %collective-permute-start.34) | collective-permute-done | bytes 262176 | tf_op jit(solution)/shard_map/ppermute | solution.py:13
  95.5 7.2 %collective-permute-done.33 = bf16[4,16,2048]{2,1,0:T(8,128)(2,1)S(1)} collective-permute-done((bf16[4,16,2048]{2,1,0:T(8,128)(2,1)S(1)}, bf16[4,16,2048]{2,1,0:T(8,128)(2,1)S(1)}, u32[]{:S(2)}, u32[]{:S(2)}) %collective-permute-start.33) | collective-permute-done | bytes 262176 | tf_op jit(solution)/shard_map/ppermute | solution.py:13
  104.4 4.2 %collective-permute-start.30 = (bf16[4,4,2048]{2,1,0:T(4,128)(2,1)S(1)}, bf16[4,4,2048]{2,1,0:T(4,128)(2,1)S(1)}, u32[]{:S(2)}, u32[]{:S(2)}) collective-permute-start(bf16[4,4,2048]{2,1,0:T(4,128)(2,1)S(1)} %slice.186), channel_id=1, source_target_pairs={{0,32},{4,36},{8,40},{12,44},{16,48},{20,52},{24,56},{28,60},{32,0... | collective-permute-start | bytes 196616 | tf_op jit(solution)/shard_map/ppermute | solution.py:21
  108.6 3.0 %collective-permute-done.35 = bf16[4,8,2048]{2,1,0:T(8,128)(2,1)S(1)} collective-permute-done((bf16[4,8,2048]{2,1,0:T(8,128)(2,1)S(1)}, bf16[4,8,2048]{2,1,0:T(8,128)(2,1)S(1)}, u32[]{:S(2)}, u32[]{:S(2)}) %collective-permute-start.35) | collective-permute-done | bytes 131104 | tf_op jit(solution)/shard_map/ppermute | solution.py:21
  111.6 1.6 %collective-permute-done.36 = bf16[4,8,2048]{2,1,0:T(8,128)(2,1)S(1)} collective-permute-done((bf16[4,8,2048]{2,1,0:T(8,128)(2,1)S(1)}, bf16[4,8,2048]{2,1,0:T(8,128)(2,1)S(1)}, u32[]{:S(2)}, u32[]{:S(2)}) %collective-permute-start.36) | collective-permute-done | bytes 131104 | tf_op jit(solution)/shard_map/ppermute | solution.py:21
  113.3 8.1 %collective-permute-start.37 = (bf16[4,4,2048]{2,1,0:T(4,128)(2,1)S(1)}, bf16[4,4,2048]{2,1,0:T(4,128)(2,1)S(1)}, u32[]{:S(2)}, u32[]{:S(2)}) collective-permute-start(bf16[4,4,2048]{2,1,0:T(4,128)(2,1)S(1)} %select_convert_fusion), channel_id=1, source_target_pairs={{0,4},{4,0},{1,5},{5,1},{2,6},{6,2},{3,7},{7,3},{8,12},{12,8},{9,1... | collective-permute-start | bytes 196616 | tf_op jit(solution)/shard_map/ppermute | solution.py:13
  123.2 2.8 %collective-permute-start.39 = (f32[4,2048]{1,0:T(4,128)S(1)}, f32[4,2048]{1,0:T(4,128)S(1)}, u32[]{:S(2)}, u32[]{:S(2)}) collective-permute-start(f32[4,2048]{1,0:T(4,128)S(1)} %get-tuple-element.110), channel_id=1, source_target_pairs={{0,2},{1,3},{2,0},{3,1},{4,6},{5,7},{6,4},{7,5},{8,10},{9,11},{10,... | collective-permute-start | bytes 98312 | tf_op jit(solution)/shard_map/ppermute | solution.py:13
  (99 shorter events, 30.0 us)
Async XLA Ops:
  0.0 31.7 %collective-permute-start.1 = (bf16[448,2048]{1,0:T(8,128)(2,1)}, bf16[448,2048]{1,0:T(8,128)(2,1)}, u32[]{:S(2)}, u32[]{:S(2)}) collective-permute-start(bf16[448,2048]{1,0:T(8,128)(2,1)} %bitcast.46), channel_id=1, source_target_pairs={{0,4},{4,0},{1,5},{5,1},{2,6},{6,2},{3,7},{7,3},{8,12},{12,8},{9,1... | collective-permute-start | bytes 5505032 | tf_op jit(solution)/shard_map/ppermute | solution.py:13
  3.2 29.2 %collective-permute-start.2 = (bf16[448,2048]{1,0:T(8,128)(2,1)}, bf16[448,2048]{1,0:T(8,128)(2,1)}, u32[]{:S(2)}, u32[]{:S(2)}) collective-permute-start(bf16[448,2048]{1,0:T(8,128)(2,1)} %bitcast.44), channel_id=1, source_target_pairs={{0,4},{4,0},{1,5},{5,1},{2,6},{6,2},{3,7},{7,3},{8,12},{12,8},{9,1... | collective-permute-start | bytes 5505032 | tf_op jit(solution)/shard_map/ppermute | solution.py:13
  15.1 12.7 %collective-permute-start.7 = (bf16[4,8,2048]{2,1,0:T(8,128)(2,1)S(1)}, bf16[4,8,2048]{2,1,0:T(8,128)(2,1)S(1)}, u32[]{:S(2)}, u32[]{:S(2)}) collective-permute-start(bf16[4,8,2048]{2,1,0:T(8,128)(2,1)S(1)} %copy.13), channel_id=1, source_target_pairs={{0,8},{4,60},{8,16},{12,4},{16,24},{20,12},{24,32},{28,20},{32,40}... | collective-permute-start | bytes 393224 | tf_op jit(solution)/shard_map/ppermute | solution.py:21
  22.2 24.9 %collective-permute-start = (bf16[448,2048]{1,0:T(8,128)(2,1)}, bf16[448,2048]{1,0:T(8,128)(2,1)S(1)}, u32[]{:S(2)}, u32[]{:S(2)}) collective-permute-start(bf16[448,2048]{1,0:T(8,128)(2,1)} %param.9), channel_id=1, source_target_pairs={{0,4},{4,0},{1,5},{5,1},{2,6},{6,2},{3,7},{7,3},{8,12},{12,8},{9,1... | collective-permute-start | bytes 5505032 | tf_op jit(solution)/shard_map/ppermute | solution.py:13
  27.9 14.4 %collective-permute-start.11 = (bf16[4,16,2048]{2,1,0:T(8,128)(2,1)S(1)}, bf16[4,16,2048]{2,1,0:T(8,128)(2,1)S(1)}, u32[]{:S(2)}, u32[]{:S(2)}) collective-permute-start(bf16[4,16,2048]{2,1,0:T(8,128)(2,1)S(1)} %get-tuple-element.47), channel_id=1, source_target_pairs={{0,128},{64,192},{128,0},{192,64},{1,129},{65,193},{129,1},{193,65... | collective-permute-start | bytes 786440 | tf_op jit(solution)/shard_map/ppermute | solution.py:13
  30.9 13.4 %collective-permute-start.10 = (bf16[4,16,2048]{2,1,0:T(8,128)(2,1)S(1)}, bf16[4,16,2048]{2,1,0:T(8,128)(2,1)S(1)}, u32[]{:S(2)}, u32[]{:S(2)}) collective-permute-start(bf16[4,16,2048]{2,1,0:T(8,128)(2,1)S(1)} %get-tuple-element.47), channel_id=1, source_target_pairs={{0,192},{64,0},{128,64},{192,128},{1,193},{65,1},{129,65},{193,129... | collective-permute-start | bytes 786440 | tf_op jit(solution)/shard_map/ppermute | solution.py:13
  31.7 13.0 %collective-permute-start.9 = (bf16[4,16,2048]{2,1,0:T(8,128)(2,1)S(1)}, bf16[4,16,2048]{2,1,0:T(8,128)(2,1)S(1)}, u32[]{:S(2)}, u32[]{:S(2)}) collective-permute-start(bf16[4,16,2048]{2,1,0:T(8,128)(2,1)S(1)} %get-tuple-element.47), channel_id=1, source_target_pairs={{0,64},{64,128},{128,192},{192,0},{1,65},{65,129},{129,193},{193,1... | collective-permute-start | bytes 786440 | tf_op jit(solution)/shard_map/ppermute | solution.py:13
  32.4 9.3 %collective-permute-start.8 = (bf16[4,16,2048]{2,1,0:T(8,128)(2,1)S(1)}, bf16[4,16,2048]{2,1,0:T(8,128)(2,1)S(1)}, u32[]{:S(2)}, u32[]{:S(2)}) collective-permute-start(bf16[4,16,2048]{2,1,0:T(8,128)(2,1)S(1)} %get-tuple-element.112), channel_id=1, source_target_pairs={{0,16},{4,52},{8,24},{12,60},{16,32},{20,4},{24,40},{28,12},{32,48... | collective-permute-start | bytes 786440 | tf_op jit(solution)/shard_map/ppermute | solution.py:21
  41.7 9.7 %collective-permute-start.14 = (bf16[4,16,2048]{2,1,0:T(8,128)(2,1)S(1)}, bf16[4,16,2048]{2,1,0:T(8,128)(2,1)S(1)}, u32[]{:S(2)}, u32[]{:S(2)}) collective-permute-start(bf16[4,16,2048]{2,1,0:T(8,128)(2,1)S(1)} %collective-permute-done.8), channel_id=1, source_target_pairs={{0,128},{64,192},{128,0},{192,64},{1,129},{65,193},{129,1},{193,65... | collective-permute-start | bytes 786440 | tf_op jit(solution)/shard_map/ppermute | solution.py:13
  42.3 14.3 %collective-permute-start.13 = (bf16[4,16,2048]{2,1,0:T(8,128)(2,1)S(1)}, bf16[4,16,2048]{2,1,0:T(8,128)(2,1)S(1)}, u32[]{:S(2)}, u32[]{:S(2)}) collective-permute-start(bf16[4,16,2048]{2,1,0:T(8,128)(2,1)S(1)} %collective-permute-done.8), channel_id=1, source_target_pairs={{0,192},{64,0},{128,64},{192,128},{1,193},{65,1},{129,65},{193,129... | collective-permute-start | bytes 786440 | tf_op jit(solution)/shard_map/ppermute | solution.py:13
  44.3 12.8 %collective-permute-start.12 = (bf16[4,16,2048]{2,1,0:T(8,128)(2,1)S(1)}, bf16[4,16,2048]{2,1,0:T(8,128)(2,1)S(1)}, u32[]{:S(2)}, u32[]{:S(2)}) collective-permute-start(bf16[4,16,2048]{2,1,0:T(8,128)(2,1)S(1)} %collective-permute-done.8), channel_id=1, source_target_pairs={{0,64},{64,128},{128,192},{192,0},{1,65},{65,129},{129,193},{193,1... | collective-permute-start | bytes 786440 | tf_op jit(solution)/shard_map/ppermute | solution.py:13
  47.0 13.9 %collective-permute-start.17 = (bf16[64,1792]{1,0:T(8,128)(2,1)S(1)}, bf16[64,1792]{1,0:T(8,128)(2,1)S(1)}, u32[]{:S(2)}, u32[]{:S(2)}) collective-permute-start(bf16[64,1792]{1,0:T(8,128)(2,1)S(1)} %get-tuple-element.100), channel_id=1, source_target_pairs={{0,3},{1,0},{2,1},{3,2},{4,7},{5,4},{6,5},{7,6},{8,11},{9,8},{10,9... | collective-permute-start | bytes 688136 | tf_op jit(solution)/shard_map/ppermute | solution.py:13
  47.2 13.9 %collective-permute-start.16 = (bf16[64,1792]{1,0:T(8,128)(2,1)S(1)}, bf16[64,1792]{1,0:T(8,128)(2,1)S(1)}, u32[]{:S(2)}, u32[]{:S(2)}) collective-permute-start(bf16[64,1792]{1,0:T(8,128)(2,1)S(1)} %get-tuple-element.101), channel_id=1, source_target_pairs={{0,1},{1,2},{2,3},{3,0},{4,5},{5,6},{6,7},{7,4},{8,9},{9,10},{10,1... | collective-permute-start | bytes 688136 | tf_op jit(solution)/shard_map/ppermute | solution.py:13
  51.3 9.7 %collective-permute-start.15 = (bf16[64,1792]{1,0:T(8,128)(2,1)S(1)}, bf16[64,1792]{1,0:T(8,128)(2,1)S(1)}, u32[]{:S(2)}, u32[]{:S(2)}) collective-permute-start(bf16[64,1792]{1,0:T(8,128)(2,1)S(1)} %get-tuple-element.102), channel_id=1, source_target_pairs={{0,2},{1,3},{2,0},{3,1},{4,6},{5,7},{6,4},{7,5},{8,10},{9,11},{10,... | collective-permute-start | bytes 688136 | tf_op jit(solution)/shard_map/ppermute | solution.py:13
  59.4 11.9 %collective-permute-start.19 = (bf16[64,1792]{1,0:T(8,128)(2,1)S(1)}, bf16[64,1792]{1,0:T(8,128)(2,1)S(1)}, u32[]{:S(2)}, u32[]{:S(2)}) collective-permute-start(bf16[64,1792]{1,0:T(8,128)(2,1)S(1)} %get-tuple-element.98), channel_id=1, source_target_pairs={{0,1},{1,2},{2,3},{3,0},{4,5},{5,6},{6,7},{7,4},{8,9},{9,10},{10,1... | collective-permute-start | bytes 688136 | tf_op jit(solution)/shard_map/ppermute | solution.py:13
  60.9 10.4 %collective-permute-start.18 = (bf16[64,1792]{1,0:T(8,128)(2,1)S(1)}, bf16[64,1792]{1,0:T(8,128)(2,1)S(1)}, u32[]{:S(2)}, u32[]{:S(2)}) collective-permute-start(bf16[64,1792]{1,0:T(8,128)(2,1)S(1)} %get-tuple-element.99), channel_id=1, source_target_pairs={{0,2},{1,3},{2,0},{3,1},{4,6},{5,7},{6,4},{7,5},{8,10},{9,11},{10,... | collective-permute-start | bytes 688136 | tf_op jit(solution)/shard_map/ppermute | solution.py:13
  61.2 15.5 %collective-permute-start.23 = (bf16[64,896]{1,0:T(8,128)(2,1)S(1)}, bf16[64,896]{1,0:T(8,128)(2,1)S(1)}, u32[]{:S(2)}, u32[]{:S(2)}) collective-permute-start(bf16[64,896]{1,0:T(8,128)(2,1)S(1)} %fusion.17), channel_id=1, source_target_pairs={{0,1},{1,2},{2,3},{3,0},{4,5},{5,6},{6,7},{7,4},{8,9},{9,10},{10,1... | collective-permute-start | bytes 344072 | tf_op jit(solution)/shard_map/ppermute | solution.py:13
  63.1 13.6 %collective-permute-start.22 = (bf16[64,896]{1,0:T(8,128)(2,1)S(1)}, bf16[64,896]{1,0:T(8,128)(2,1)S(1)}, u32[]{:S(2)}, u32[]{:S(2)}) collective-permute-start(bf16[64,896]{1,0:T(8,128)(2,1)S(1)} %fusion.17), channel_id=1, source_target_pairs={{0,2},{1,3},{2,0},{3,1},{4,6},{5,7},{6,4},{7,5},{8,10},{9,11},{10,... | collective-permute-start | bytes 344072 | tf_op jit(solution)/shard_map/ppermute | solution.py:13
  66.1 10.7 %collective-permute-start.21 = (bf16[64,896]{1,0:T(8,128)(2,1)S(1)}, bf16[64,896]{1,0:T(8,128)(2,1)S(1)}, u32[]{:S(2)}, u32[]{:S(2)}) collective-permute-start(bf16[64,896]{1,0:T(8,128)(2,1)S(1)} %fusion.17), channel_id=1, source_target_pairs={{0,3},{1,0},{2,1},{3,2},{4,7},{5,4},{6,5},{7,6},{8,11},{9,8},{10,9... | collective-permute-start | bytes 344072 | tf_op jit(solution)/shard_map/ppermute | solution.py:13
  71.5 10.6 %collective-permute-start.26 = (bf16[64,896]{1,0:T(8,128)(2,1)S(1)}, bf16[64,896]{1,0:T(8,128)(2,1)S(1)}, u32[]{:S(2)}, u32[]{:S(2)}) collective-permute-start(bf16[64,896]{1,0:T(8,128)(2,1)S(1)} %fusion.16), channel_id=1, source_target_pairs={{0,1},{1,2},{2,3},{3,0},{4,5},{5,6},{6,7},{7,4},{8,9},{9,10},{10,1... | collective-permute-start | bytes 344072 | tf_op jit(solution)/shard_map/ppermute | solution.py:13
  71.6 12.6 %collective-permute-start.25 = (bf16[64,896]{1,0:T(8,128)(2,1)S(1)}, bf16[64,896]{1,0:T(8,128)(2,1)S(1)}, u32[]{:S(2)}, u32[]{:S(2)}) collective-permute-start(bf16[64,896]{1,0:T(8,128)(2,1)S(1)} %fusion.16), channel_id=1, source_target_pairs={{0,2},{1,3},{2,0},{3,1},{4,6},{5,7},{6,4},{7,5},{8,10},{9,11},{10,... | collective-permute-start | bytes 344072 | tf_op jit(solution)/shard_map/ppermute | solution.py:13
  78.3 8.1 %collective-permute-start.29 = (bf16[4,16,2048]{2,1,0:T(8,128)(2,1)S(1)}, bf16[4,16,2048]{2,1,0:T(8,128)(2,1)S(1)}, u32[]{:S(2)}, u32[]{:S(2)}) collective-permute-start(bf16[4,16,2048]{2,1,0:T(8,128)(2,1)S(1)} %get-tuple-element.94), channel_id=1, source_target_pairs={{0,128},{64,192},{128,0},{192,64},{1,129},{65,193},{129,1},{193,65... | collective-permute-start | bytes 786440 | tf_op jit(solution)/shard_map/ppermute | solution.py:13
  78.6 14.1 %collective-permute-start.28 = (bf16[4,16,2048]{2,1,0:T(8,128)(2,1)S(1)}, bf16[4,16,2048]{2,1,0:T(8,128)(2,1)S(1)}, u32[]{:S(2)}, u32[]{:S(2)}) collective-permute-start(bf16[4,16,2048]{2,1,0:T(8,128)(2,1)S(1)} %get-tuple-element.95), channel_id=1, source_target_pairs={{0,64},{64,128},{128,192},{192,0},{1,65},{65,129},{129,193},{193,1... | collective-permute-start | bytes 786440 | tf_op jit(solution)/shard_map/ppermute | solution.py:13
  82.1 11.4 %collective-permute-start.27 = (bf16[4,16,2048]{2,1,0:T(8,128)(2,1)S(1)}, bf16[4,16,2048]{2,1,0:T(8,128)(2,1)S(1)}, u32[]{:S(2)}, u32[]{:S(2)}) collective-permute-start(bf16[4,16,2048]{2,1,0:T(8,128)(2,1)S(1)} %get-tuple-element.96), channel_id=1, source_target_pairs={{0,192},{64,0},{128,64},{192,128},{1,193},{65,1},{129,65},{193,129... | collective-permute-start | bytes 786440 | tf_op jit(solution)/shard_map/ppermute | solution.py:13
  85.8 9.7 %collective-permute-start.34 = (bf16[4,16,2048]{2,1,0:T(8,128)(2,1)S(1)}, bf16[4,16,2048]{2,1,0:T(8,128)(2,1)S(1)}, u32[]{:S(2)}, u32[]{:S(2)}) collective-permute-start(bf16[4,16,2048]{2,1,0:T(8,128)(2,1)S(1)} %get-tuple-element.91), channel_id=1, source_target_pairs={{0,128},{64,192},{128,0},{192,64},{1,129},{65,193},{129,1},{193,65... | collective-permute-start | bytes 786440 | tf_op jit(solution)/shard_map/ppermute | solution.py:13
  85.9 16.8 %collective-permute-start.33 = (bf16[4,16,2048]{2,1,0:T(8,128)(2,1)S(1)}, bf16[4,16,2048]{2,1,0:T(8,128)(2,1)S(1)}, u32[]{:S(2)}, u32[]{:S(2)}) collective-permute-start(bf16[4,16,2048]{2,1,0:T(8,128)(2,1)S(1)} %get-tuple-element.92), channel_id=1, source_target_pairs={{0,64},{64,128},{128,192},{192,0},{1,65},{65,129},{129,193},{193,1... | collective-permute-start | bytes 786440 | tf_op jit(solution)/shard_map/ppermute | solution.py:13
  86.4 16.2 %collective-permute-start.32 = (bf16[4,16,2048]{2,1,0:T(8,128)(2,1)S(1)}, bf16[4,16,2048]{2,1,0:T(8,128)(2,1)S(1)}, u32[]{:S(2)}, u32[]{:S(2)}) collective-permute-start(bf16[4,16,2048]{2,1,0:T(8,128)(2,1)S(1)} %get-tuple-element.93), channel_id=1, source_target_pairs={{0,192},{64,0},{128,64},{192,128},{1,193},{65,1},{129,65},{193,129... | collective-permute-start | bytes 786440 | tf_op jit(solution)/shard_map/ppermute | solution.py:13
  93.7 9.0 %collective-permute-start.31 = (bf16[4,8,2048]{2,1,0:T(8,128)(2,1)S(1)}, bf16[4,8,2048]{2,1,0:T(8,128)(2,1)S(1)}, u32[]{:S(2)}, u32[]{:S(2)}) collective-permute-start(bf16[4,8,2048]{2,1,0:T(8,128)(2,1)S(1)} %slice.187), channel_id=1, source_target_pairs={{0,56},{4,12},{8,0},{12,20},{16,8},{20,28},{24,16},{28,36},{32,24}... | collective-permute-start | bytes 393224 | tf_op jit(solution)/shard_map/ppermute | solution.py:21
  102.8 8.8 %collective-permute-start.35 = (bf16[4,8,2048]{2,1,0:T(8,128)(2,1)S(1)}, bf16[4,8,2048]{2,1,0:T(8,128)(2,1)S(1)}, u32[]{:S(2)}, u32[]{:S(2)}) collective-permute-start(bf16[4,8,2048]{2,1,0:T(8,128)(2,1)S(1)} %get-tuple-element.103), channel_id=1, source_target_pairs={{0,40},{4,28},{8,48},{12,36},{16,56},{20,44},{24,0},{28,52},{32,8}... | collective-permute-start | bytes 393224 | tf_op jit(solution)/shard_map/ppermute | solution.py:21
  102.9 10.3 %collective-permute-start.36 = (bf16[4,8,2048]{2,1,0:T(8,128)(2,1)S(1)}, bf16[4,8,2048]{2,1,0:T(8,128)(2,1)S(1)}, u32[]{:S(2)}, u32[]{:S(2)}) collective-permute-start(bf16[4,8,2048]{2,1,0:T(8,128)(2,1)S(1)} %get-tuple-element.104), channel_id=1, source_target_pairs={{0,48},{4,20},{8,56},{12,28},{16,0},{20,36},{24,8},{28,44},{32,16}... | collective-permute-start | bytes 393224 | tf_op jit(solution)/shard_map/ppermute | solution.py:21
  104.4 17.1 %collective-permute-start.30 = (bf16[4,4,2048]{2,1,0:T(4,128)(2,1)S(1)}, bf16[4,4,2048]{2,1,0:T(4,128)(2,1)S(1)}, u32[]{:S(2)}, u32[]{:S(2)}) collective-permute-start(bf16[4,4,2048]{2,1,0:T(4,128)(2,1)S(1)} %slice.186), channel_id=1, source_target_pairs={{0,32},{4,36},{8,40},{12,44},{16,48},{20,52},{24,56},{28,60},{32,0... | collective-permute-start | bytes 196616 | tf_op jit(solution)/shard_map/ppermute | solution.py:21
  113.3 9.0 %collective-permute-start.37 = (bf16[4,4,2048]{2,1,0:T(4,128)(2,1)S(1)}, bf16[4,4,2048]{2,1,0:T(4,128)(2,1)S(1)}, u32[]{:S(2)}, u32[]{:S(2)}) collective-permute-start(bf16[4,4,2048]{2,1,0:T(4,128)(2,1)S(1)} %select_convert_fusion), channel_id=1, source_target_pairs={{0,4},{4,0},{1,5},{5,1},{2,6},{6,2},{3,7},{7,3},{8,12},{12,8},{9,1... | collective-permute-start | bytes 196616 | tf_op jit(solution)/shard_map/ppermute | solution.py:13
  (12 other events, 115.3 us)

commit v7 on v6

--- a/solution.py
+++ b/solution.py
@@ -47,11 +47,9 @@
     own = jnp.stack(
         [blocks[0]] + [shift(blocks[4 - r], "x", 4 - r) for r in (1, 2, 3)]
     )
-    opposite = along_z(own, 4, 4)
     pair = lax.all_gather(own, "c", axis=1, tiled=True)
-    near = along_z(pair, 1, -1)
-    far = along_z(jnp.concatenate([pair, near], axis=1), 2, -2)
-    near = jnp.concatenate([own, opposite, near], axis=1)
+    near = jnp.concatenate([along_z(pair, 0, -2), along_z(pair, 1, -1)], axis=1)
+    far = along_z(near, 2, -2)
 
     def project(weights, block):
         return lax.dot_general(
@@ -121,22 +119,20 @@
     far_down[0], *near_back = together(far_down[0], *near_back)
 
     near_total = sum_over_y(near_down, near_back)
+    half = 2 * rows
     near_pieces = [
-        along_z(near_total[:, 2 * rows :].astype(BF16), -1, 1),
-        along_z(near_total[:, rows : 2 * rows].astype(BF16), 4, 4),
+        along_z(near_total[:, :half].astype(BF16), 0, 2),
+        along_z(near_total[:, half:].astype(BF16), -1, 1),
     ]
-    near_pieces[0], back_1, back_3, back_2 = together(near_pieces[0], *far_back)
+    *near_pieces, back_1, back_3, back_2 = together(*near_pieces, *far_back)
     far_total = sum_over_y(far_down, (back_1, back_3, back_2))
-    pair = sum(
-        piece.astype(F32)
-        for piece in (
-            near_pieces[0],
-            along_z(far_total[:, 2 * rows :].astype(BF16), -3, 3),
-            along_z(far_total[:, : 2 * rows].astype(BF16), -2, 2),
-        )
-    )
+    far_pieces = [
+        along_z(far_total[:, :half].astype(BF16), -2, 4),
+        along_z(far_total[:, half:].astype(BF16), -3, 3),
+    ]
+    pair = sum(piece.astype(F32) for piece in near_pieces + far_pieces)
     low, high = pair[:, :rows], pair[:, rows:]
-    mine = near_total[:, :rows] + near_pieces[1].astype(F32) + jnp.where(core == 0, low, high)
+    mine = jnp.where(core == 0, low, high)
     other = jnp.where(core == 0, high, low).astype(BF16)
     mine = mine + shift(other, "c", 1).astype(F32)
     columns = [mine[0]] + [shift(mine[k], "x", k) for k in (1, 2, 3)]

time: 130 us -> 131 us (level)
  the two profiles are of different devices: /device:TPU:1 before, /device:TPU:56 now
where the time goes in v7:
time: 131 us
  waiting for transfers between devices  57.8 us (44%)
  starting transfers between devices  55.1 us (42%)
  other arithmetic  8.16 us (6%)
  matrix products  6.8 us (5%)
  blocking collectives  1.9 us (1%)
    ppermute x34, starting transfers between devices, shift(): return lax.ppermute(value, axis, [(i, (i + step) % n) for i in range(n)])  48.2 us
    ppermute x34, waiting for transfers between devices, shift(): return lax.ppermute(value, axis, [(i, (i + step) % n) for i in range(n)])  39.2 us
    ppermute x7, waiting for transfers between devices, along_z(): return lax.ppermute(value, ('z', 'c'), pairs)  18.6 us
    ppermute x7, starting transfers between devices, along_z(): return lax.ppermute(value, ('z', 'c'), pairs)  6.91 us
    dot_general x2, matrix products, project(): lax.dot_general(block.reshape(-1, part), weights, (((1,), (1,)), ((), ())...  4.23 us
    concatenate x1, other arithmetic, local(): first, far = together(jnp.concatenate(first, axis=0), far)  3.61 us
  transfers between devices with their start and end apart: 41, of which 20 were waited for; matrix products, arithmetic and copies ran while one was open for 11% of the time, Pallas kernels for 0%

profile of v7, /device:TPU:56, one launch (start us, length us, event | category | flops | bytes accessed | tf_op | source)
XLA Modules:
  0.0 130.7 jit_solution(16326751128810713233)
XLA Ops:
  2.6 3.1 %collective-permute-start.4 = (bf16[4,2048]{1,0:T(4,128)(2,1)S(1)}, bf16[4,2048]{1,0:T(4,128)(2,1)S(1)}, u32[]{:S(2)}, u32[]{:S(2)}) collective-permute-start(bf16[4,2048]{1,0:T(4,128)(2,1)S(1)} %get-tuple-element.115), channel_id=1, source_target_pairs={{0,2},{1,3},{2,0},{3,1},{4,6},{5,7},{6,4},{7,5},{8,10},{9,11},{10,... | collective-permute-start | bytes 49160 | tf_op jit(solution)/shard_map/ppermute | solution.py:13
  8.0 1.5 %collective-permute-done.3 = bf16[4,2048]{1,0:T(4,128)(2,1)S(1)} collective-permute-done((bf16[4,2048]{1,0:T(4,128)(2,1)S(1)}, bf16[4,2048]{1,0:T(4,128)(2,1)S(1)}, u32[]{:S(2)}, u32[]{:S(2)}) %collective-permute-start.3) | collective-permute-done | bytes 16416 | tf_op jit(solution)/shard_map/ppermute | solution.py:13
  9.5 2.4 %collective-permute-done.5 = bf16[4,2048]{1,0:T(4,128)(2,1)S(1)} collective-permute-done((bf16[4,2048]{1,0:T(4,128)(2,1)S(1)}, bf16[4,2048]{1,0:T(4,128)(2,1)S(1)}, u32[]{:S(2)}, u32[]{:S(2)}) %collective-permute-start.5) | collective-permute-done | bytes 16416 | tf_op jit(solution)/shard_map/ppermute | solution.py:13
  12.0 1.9 %all_gather.3 = bf16[4,8,2048]{2,0,1:T(4,128)(2,1)S(1)} all-gather(bf16[4,4,2048]{2,0,1:T(4,128)(2,1)S(1)} %copy.10), channel_id=1, replica_groups=mesh['y'=4,'z'=8,'c'=2,'x'=4] {'c'}, dimensions={1}, use_global_device_ids=true | all-gather | bytes 196608 | tf_op jit(solution)/shard_map/all_gather | solution.py:50
  14.6 6.6 %collective-permute-start = (bf16[448,2048]{1,0:T(8,128)(2,1)}, bf16[448,2048]{1,0:T(8,128)(2,1)S(1)}, u32[]{:S(2)}, u32[]{:S(2)}) collective-permute-start(bf16[448,2048]{1,0:T(8,128)(2,1)} %param.9), channel_id=1, source_target_pairs={{0,4},{4,0},{1,5},{5,1},{2,6},{6,2},{3,7},{7,3},{8,12},{12,8},{9,1... | collective-permute-start | bytes 5505032 | tf_op jit(solution)/shard_map/ppermute | solution.py:13
  21.2 4.9 %collective-permute-done.7 = bf16[4,8,2048]{2,1,0:T(8,128)(2,1)S(1)} collective-permute-done((bf16[4,8,2048]{2,1,0:T(8,128)(2,1)S(1)}, bf16[4,8,2048]{2,1,0:T(8,128)(2,1)S(1)}, u32[]{:S(2)}, u32[]{:S(2)}) %collective-permute-start.7) | collective-permute-done | bytes 131104 | tf_op jit(solution)/shard_map/ppermute | solution.py:21
  27.5 3.2 %collective-permute-start.9 = (bf16[4,16,2048]{2,1,0:T(8,128)(2,1)S(1)}, bf16[4,16,2048]{2,1,0:T(8,128)(2,1)S(1)}, u32[]{:S(2)}, u32[]{:S(2)}) collective-permute-start(bf16[4,16,2048]{2,1,0:T(8,128)(2,1)S(1)} %constant_dynamic-update-slice_fusion), channel_id=1, source_target_pairs={{0,64},{64,128},{128,192},{192,0},{1,65},{65,129},{129,193},{193,1... | collective-permute-start | bytes 786440 | tf_op jit(solution)/shard_map/ppermute | solution.py:13
  30.8 3.6 %pad_maximum_fusion = bf16[1792,2048]{1,0:T(8,128)(2,1)S(1)} fusion(bf16[448,2048]{1,0:T(8,128)(2,1)} %collective-permute-done.2, bf16[448,2048]{1,0:T(8,128)(2,1)} %bitcast.45, bf16[448,2048]{1,0:T(8,128)(2,1)S(1)} %collective-permute-done.1, bf16[448,2048]{1,0:T(8,128)(2,1)} %bitcast.47), kind=kLoop, calls=%fused_computation | loop fusion | flops 29360128 | bytes 14680064 | tf_op jit(solution)/shard_map/concatenate | solution.py:93
  34.4 5.0 %collective-permute-done.8 = bf16[4,16,2048]{2,1,0:T(8,128)(2,1)S(1)} collective-permute-done((bf16[4,16,2048]{2,1,0:T(8,128)(2,1)S(1)}, bf16[4,16,2048]{2,1,0:T(8,128)(2,1)S(1)}, u32[]{:S(2)}, u32[]{:S(2)}) %collective-permute-start.8) | collective-permute-done | bytes 262176 | tf_op jit(solution)/shard_map/ppermute | solution.py:21
  41.2 2.5 %collective-permute-start.12 = (bf16[4,16,2048]{2,1,0:T(8,128)(2,1)S(1)}, bf16[4,16,2048]{2,1,0:T(8,128)(2,1)S(1)}, u32[]{:S(2)}, u32[]{:S(2)}) collective-permute-start(bf16[4,16,2048]{2,1,0:T(8,128)(2,1)S(1)} %collective-permute-done.8), channel_id=1, source_target_pairs={{0,64},{64,128},{128,192},{192,0},{1,65},{65,129},{129,193},{193,1... | collective-permute-start | bytes 786440 | tf_op jit(solution)/shard_map/ppermute | solution.py:13
  43.8 2.1 %fusion.32 = (bf16[256,1792]{1,0:T(8,128)(2,1)S(1)}, f32[256,1792]{1,0:T(8,128)S(1)}) fusion(bf16[256,2048]{1,0:T(8,128)(2,1)S(1)} %bitcast.49, bf16[1792,2048]{1,0:T(8,128)(2,1)S(1)} %pad_maximum_fusion), kind=kOutput, calls=%fused_computation.65 | convolution fusion | flops 1879506944 | bytes 11141120 | tf_op jit(solution)/shard_map/dot_general | solution.py:55
  46.1 2.1 %collective-permute-start.16 = (bf16[64,1792]{1,0:T(8,128)(2,1)S(1)}, bf16[64,1792]{1,0:T(8,128)(2,1)S(1)}, u32[]{:S(2)}, u32[]{:S(2)}) collective-permute-start(bf16[64,1792]{1,0:T(8,128)(2,1)S(1)} %get-tuple-element.101), channel_id=1, source_target_pairs={{0,1},{1,2},{2,3},{3,0},{4,5},{5,6},{6,7},{7,4},{8,9},{9,10},{10,1... | collective-permute-start | bytes 688136 | tf_op jit(solution)/shard_map/ppermute | solution.py:13
  50.5 3.4 %collective-permute-done.13 = bf16[4,16,2048]{2,1,0:T(8,128)(2,1)S(1)} collective-permute-done((bf16[4,16,2048]{2,1,0:T(8,128)(2,1)S(1)}, bf16[4,16,2048]{2,1,0:T(8,128)(2,1)S(1)}, u32[]{:S(2)}, u32[]{:S(2)}) %collective-permute-start.13) | collective-permute-done | bytes 262176 | tf_op jit(solution)/shard_map/ppermute | solution.py:13
  54.0 2.1 %fusion.33 = (bf16[256,1792]{1,0:T(8,128)(2,1)S(1)}, f32[256,1792]{1,0:T(8,128)S(1)}) fusion(bf16[256,2048]{1,0:T(8,128)(2,1)S(1)} %bitcast.48, bf16[1792,2048]{1,0:T(8,128)(2,1)S(1)} %pad_maximum_fusion), kind=kOutput, calls=%fused_computation.66 | convolution fusion | flops 1879506944 | bytes 11141120 | tf_op jit(solution)/shard_map/dot_general | solution.py:55
  56.2 2.0 %collective-permute-start.19 = (bf16[64,1792]{1,0:T(8,128)(2,1)S(1)}, bf16[64,1792]{1,0:T(8,128)(2,1)S(1)}, u32[]{:S(2)}, u32[]{:S(2)}) collective-permute-start(bf16[64,1792]{1,0:T(8,128)(2,1)S(1)} %get-tuple-element.98), channel_id=1, source_target_pairs={{0,1},{1,2},{2,3},{3,0},{4,5},{5,6},{6,7},{7,4},{8,9},{9,10},{10,1... | collective-permute-start | bytes 688136 | tf_op jit(solution)/shard_map/ppermute | solution.py:13
  58.9 1.9 %collective-permute-start.23 = (bf16[64,896]{1,0:T(8,128)(2,1)S(1)}, bf16[64,896]{1,0:T(8,128)(2,1)S(1)}, u32[]{:S(2)}, u32[]{:S(2)}) collective-permute-start(bf16[64,896]{1,0:T(8,128)(2,1)S(1)} %fusion.17), channel_id=1, source_target_pairs={{0,1},{1,2},{2,3},{3,0},{4,5},{5,6},{6,7},{7,4},{8,9},{9,10},{10,1... | collective-permute-start | bytes 344072 | tf_op jit(solution)/shard_map/ppermute | solution.py:13
  60.8 2.0 %collective-permute-start.22 = (bf16[64,896]{1,0:T(8,128)(2,1)S(1)}, bf16[64,896]{1,0:T(8,128)(2,1)S(1)}, u32[]{:S(2)}, u32[]{:S(2)}) collective-permute-start(bf16[64,896]{1,0:T(8,128)(2,1)S(1)} %fusion.17), channel_id=1, source_target_pairs={{0,2},{1,3},{2,0},{3,1},{4,6},{5,7},{6,4},{7,5},{8,10},{9,11},{10,... | collective-permute-start | bytes 344072 | tf_op jit(solution)/shard_map/ppermute | solution.py:13
  62.8 1.9 %collective-permute-done.20 = bf16[64,1792]{1,0:T(8,128)(2,1)S(1)} collective-permute-done((bf16[64,1792]{1,0:T(8,128)(2,1)S(1)}, bf16[64,1792]{1,0:T(8,128)(2,1)S(1)}, u32[]{:S(2)}, u32[]{:S(2)}) %collective-permute-start.20) | collective-permute-done | bytes 229408 | tf_op jit(solution)/shard_map/ppermute | solution.py:13
  65.2 6.6 %collective-permute-done.19 = bf16[64,1792]{1,0:T(8,128)(2,1)S(1)} collective-permute-done((bf16[64,1792]{1,0:T(8,128)(2,1)S(1)}, bf16[64,1792]{1,0:T(8,128)(2,1)S(1)}, u32[]{:S(2)}, u32[]{:S(2)}) %collective-permute-start.19) | collective-permute-done | bytes 229408 | tf_op jit(solution)/shard_map/ppermute | solution.py:13
  72.1 2.0 %collective-permute-start.25 = (bf16[64,896]{1,0:T(8,128)(2,1)S(1)}, bf16[64,896]{1,0:T(8,128)(2,1)S(1)}, u32[]{:S(2)}, u32[]{:S(2)}) collective-permute-start(bf16[64,896]{1,0:T(8,128)(2,1)S(1)} %fusion.16), channel_id=1, source_target_pairs={{0,2},{1,3},{2,0},{3,1},{4,6},{5,7},{6,4},{7,5},{8,10},{9,11},{10,... | collective-permute-start | bytes 344072 | tf_op jit(solution)/shard_map/ppermute | solution.py:13
  74.1 3.0 %collective-permute-done.23 = bf16[64,896]{1,0:T(8,128)(2,1)S(1)} collective-permute-done((bf16[64,896]{1,0:T(8,128)(2,1)S(1)}, bf16[64,896]{1,0:T(8,128)(2,1)S(1)}, u32[]{:S(2)}, u32[]{:S(2)}) %collective-permute-start.23) | collective-permute-done | bytes 114720 | tf_op jit(solution)/shard_map/ppermute | solution.py:13
  83.4 2.5 %collective-permute-start.34 = (bf16[4,16,2048]{2,1,0:T(8,128)(2,1)S(1)}, bf16[4,16,2048]{2,1,0:T(8,128)(2,1)S(1)}, u32[]{:S(2)}, u32[]{:S(2)}) collective-permute-start(bf16[4,16,2048]{2,1,0:T(8,128)(2,1)S(1)} %get-tuple-element.91), channel_id=1, source_target_pairs={{0,128},{64,192},{128,0},{192,64},{1,129},{65,193},{129,1},{193,65... | collective-permute-start | bytes 786440 | tf_op jit(solution)/shard_map/ppermute | solution.py:13
  86.6 2.9 %collective-permute-done.29 = bf16[4,16,2048]{2,1,0:T(8,128)(2,1)S(1)} collective-permute-done((bf16[4,16,2048]{2,1,0:T(8,128)(2,1)S(1)}, bf16[4,16,2048]{2,1,0:T(8,128)(2,1)S(1)}, u32[]{:S(2)}, u32[]{:S(2)}) %collective-permute-start.29) | collective-permute-done | bytes 262176 | tf_op jit(solution)/shard_map/ppermute | solution.py:13
  89.6 4.8 %collective-permute-done.28 = bf16[4,16,2048]{2,1,0:T(8,128)(2,1)S(1)} collective-permute-done((bf16[4,16,2048]{2,1,0:T(8,128)(2,1)S(1)}, bf16[4,16,2048]{2,1,0:T(8,128)(2,1)S(1)}, u32[]{:S(2)}, u32[]{:S(2)}) %collective-permute-start.28) | collective-permute-done | bytes 262176 | tf_op jit(solution)/shard_map/ppermute | solution.py:13
  94.3 2.7 %collective-permute-done.27 = bf16[4,16,2048]{2,1,0:T(8,128)(2,1)S(1)} collective-permute-done((bf16[4,16,2048]{2,1,0:T(8,128)(2,1)S(1)}, bf16[4,16,2048]{2,1,0:T(8,128)(2,1)S(1)}, u32[]{:S(2)}, u32[]{:S(2)}) %collective-permute-start.27) | collective-permute-done | bytes 262176 | tf_op jit(solution)/shard_map/ppermute | solution.py:13
  99.4 3.0 %collective-permute-done.32 = bf16[4,16,2048]{2,1,0:T(8,128)(2,1)S(1)} collective-permute-done((bf16[4,16,2048]{2,1,0:T(8,128)(2,1)S(1)}, bf16[4,16,2048]{2,1,0:T(8,128)(2,1)S(1)}, u32[]{:S(2)}, u32[]{:S(2)}) %collective-permute-start.32) | collective-permute-done | bytes 262176 | tf_op jit(solution)/shard_map/ppermute | solution.py:13
  102.6 5.5 %collective-permute-start.35 = (bf16[4,8,2048]{2,1,0:T(8,128)(2,1)S(1)}, bf16[4,8,2048]{2,1,0:T(8,128)(2,1)S(1)}, u32[]{:S(2)}, u32[]{:S(2)}) collective-permute-start(bf16[4,8,2048]{2,1,0:T(8,128)(2,1)S(1)} %get-tuple-element.103), channel_id=1, source_target_pairs={{0,48},{4,36},{8,56},{12,44},{16,0},{20,52},{24,8},{28,60},{32,16}... | collective-permute-start | bytes 393224 | tf_op jit(solution)/shard_map/ppermute | solution.py:21
  108.1 4.0 %collective-permute-done.35 = bf16[4,8,2048]{2,1,0:T(8,128)(2,1)S(1)} collective-permute-done((bf16[4,8,2048]{2,1,0:T(8,128)(2,1)S(1)}, bf16[4,8,2048]{2,1,0:T(8,128)(2,1)S(1)}, u32[]{:S(2)}, u32[]{:S(2)}) %collective-permute-start.35) | collective-permute-done | bytes 131104 | tf_op jit(solution)/shard_map/ppermute | solution.py:21
  112.1 4.7 %collective-permute-done.36 = bf16[4,8,2048]{2,1,0:T(8,128)(2,1)S(1)} collective-permute-done((bf16[4,8,2048]{2,1,0:T(8,128)(2,1)S(1)}, bf16[4,8,2048]{2,1,0:T(8,128)(2,1)S(1)}, u32[]{:S(2)}, u32[]{:S(2)}) %collective-permute-start.36) | collective-permute-done | bytes 131104 | tf_op jit(solution)/shard_map/ppermute | solution.py:21
  118.3 6.2 %collective-permute-start.40 = (f32[4,2048]{1,0:T(4,128)S(1)}, f32[4,2048]{1,0:T(4,128)S(1)}, u32[]{:S(2)}, u32[]{:S(2)}) collective-permute-start(f32[4,2048]{1,0:T(4,128)S(1)} %get-tuple-element.111), channel_id=1, source_target_pairs={{0,1},{1,2},{2,3},{3,0},{4,5},{5,6},{6,7},{7,4},{8,9},{9,10},{10,1... | collective-permute-start | bytes 98312 | tf_op jit(solution)/shard_map/ppermute | solution.py:13
  124.5 2.8 %collective-permute-start.38 = (f32[4,2048]{1,0:T(4,128)S(1)}, f32[4,2048]{1,0:T(4,128)S(1)}, u32[]{:S(2)}, u32[]{:S(2)}) collective-permute-start(f32[4,2048]{1,0:T(4,128)S(1)} %get-tuple-element.113), channel_id=1, source_target_pairs={{0,3},{1,0},{2,1},{3,2},{4,7},{5,4},{6,5},{7,6},{8,11},{9,8},{10,9... | collective-permute-start | bytes 98312 | tf_op jit(solution)/shard_map/ppermute | solution.py:13
  127.3 2.6 %collective-permute-done.39 = f32[4,2048]{1,0:T(4,128)S(1)} collective-permute-done((f32[4,2048]{1,0:T(4,128)S(1)}, f32[4,2048]{1,0:T(4,128)S(1)}, u32[]{:S(2)}, u32[]{:S(2)}) %collective-permute-start.39) | collective-permute-done | bytes 32800 | tf_op jit(solution)/shard_map/ppermute | solution.py:13
  (97 shorter events, 24.8 us)
Async XLA Ops:
  0.0 27.5 %collective-permute-start.1 = (bf16[448,2048]{1,0:T(8,128)(2,1)}, bf16[448,2048]{1,0:T(8,128)(2,1)S(1)}, u32[]{:S(2)}, u32[]{:S(2)}) collective-permute-start(bf16[448,2048]{1,0:T(8,128)(2,1)} %bitcast.46), channel_id=1, source_target_pairs={{0,4},{4,0},{1,5},{5,1},{2,6},{6,2},{3,7},{7,3},{8,12},{12,8},{9,1... | collective-permute-start | bytes 5505032 | tf_op jit(solution)/shard_map/ppermute | solution.py:13
  0.0 30.8 %collective-permute-start.2 = (bf16[448,2048]{1,0:T(8,128)(2,1)}, bf16[448,2048]{1,0:T(8,128)(2,1)}, u32[]{:S(2)}, u32[]{:S(2)}) collective-permute-start(bf16[448,2048]{1,0:T(8,128)(2,1)} %bitcast.44), channel_id=1, source_target_pairs={{0,4},{4,0},{1,5},{5,1},{2,6},{6,2},{3,7},{7,3},{8,12},{12,8},{9,1... | collective-permute-start | bytes 5505032 | tf_op jit(solution)/shard_map/ppermute | solution.py:13
  13.9 7.3 %collective-permute-start.6 = (bf16[4,8,2048]{2,1,0:T(8,128)(2,1)S(1)}, bf16[4,8,2048]{2,1,0:T(8,128)(2,1)S(1)}, u32[]{:S(2)}, u32[]{:S(2)}) collective-permute-start(bf16[4,8,2048]{2,1,0:T(8,128)(2,1)S(1)} %copy.11), channel_id=1, source_target_pairs={{0,0},{4,52},{8,8},{12,60},{16,16},{20,4},{24,24},{28,12},{32,32},... | collective-permute-start | bytes 393224 | tf_op jit(solution)/shard_map/ppermute | solution.py:21
  14.6 31.5 %collective-permute-start = (bf16[448,2048]{1,0:T(8,128)(2,1)}, bf16[448,2048]{1,0:T(8,128)(2,1)S(1)}, u32[]{:S(2)}, u32[]{:S(2)}) collective-permute-start(bf16[448,2048]{1,0:T(8,128)(2,1)} %param.9), channel_id=1, source_target_pairs={{0,4},{4,0},{1,5},{5,1},{2,6},{6,2},{3,7},{7,3},{8,12},{12,8},{9,1... | collective-permute-start | bytes 5505032 | tf_op jit(solution)/shard_map/ppermute | solution.py:13
  26.2 14.2 %collective-permute-start.11 = (bf16[4,16,2048]{2,1,0:T(8,128)(2,1)S(1)}, bf16[4,16,2048]{2,1,0:T(8,128)(2,1)S(1)}, u32[]{:S(2)}, u32[]{:S(2)}) collective-permute-start(bf16[4,16,2048]{2,1,0:T(8,128)(2,1)S(1)} %constant_dynamic-update-slice_fusion), channel_id=1, source_target_pairs={{0,128},{64,192},{128,0},{192,64},{1,129},{65,193},{129,1},{193,65... | collective-permute-start | bytes 786440 | tf_op jit(solution)/shard_map/ppermute | solution.py:13
  27.5 13.7 %collective-permute-start.10 = (bf16[4,16,2048]{2,1,0:T(8,128)(2,1)S(1)}, bf16[4,16,2048]{2,1,0:T(8,128)(2,1)S(1)}, u32[]{:S(2)}, u32[]{:S(2)}) collective-permute-start(bf16[4,16,2048]{2,1,0:T(8,128)(2,1)S(1)} %constant_dynamic-update-slice_fusion), channel_id=1, source_target_pairs={{0,192},{64,0},{128,64},{192,128},{1,193},{65,1},{129,65},{193,129... | collective-permute-start | bytes 786440 | tf_op jit(solution)/shard_map/ppermute | solution.py:13
  27.5 16.2 %collective-permute-start.9 = (bf16[4,16,2048]{2,1,0:T(8,128)(2,1)S(1)}, bf16[4,16,2048]{2,1,0:T(8,128)(2,1)S(1)}, u32[]{:S(2)}, u32[]{:S(2)}) collective-permute-start(bf16[4,16,2048]{2,1,0:T(8,128)(2,1)S(1)} %constant_dynamic-update-slice_fusion), channel_id=1, source_target_pairs={{0,64},{64,128},{128,192},{192,0},{1,65},{65,129},{129,193},{193,1... | collective-permute-start | bytes 786440 | tf_op jit(solution)/shard_map/ppermute | solution.py:13
  30.8 8.6 %collective-permute-start.8 = (bf16[4,16,2048]{2,1,0:T(8,128)(2,1)S(1)}, bf16[4,16,2048]{2,1,0:T(8,128)(2,1)S(1)}, u32[]{:S(2)}, u32[]{:S(2)}) collective-permute-start(bf16[4,16,2048]{2,1,0:T(8,128)(2,1)S(1)} %constant_dynamic-update-slice_fusion), channel_id=1, source_target_pairs={{0,16},{4,52},{8,24},{12,60},{16,32},{20,4},{24,40},{28,12},{32,48... | collective-permute-start | bytes 786440 | tf_op jit(solution)/shard_map/ppermute | solution.py:21
  39.4 10.8 %collective-permute-start.14 = (bf16[4,16,2048]{2,1,0:T(8,128)(2,1)S(1)}, bf16[4,16,2048]{2,1,0:T(8,128)(2,1)S(1)}, u32[]{:S(2)}, u32[]{:S(2)}) collective-permute-start(bf16[4,16,2048]{2,1,0:T(8,128)(2,1)S(1)} %collective-permute-done.8), channel_id=1, source_target_pairs={{0,128},{64,192},{128,0},{192,64},{1,129},{65,193},{129,1},{193,65... | collective-permute-start | bytes 786440 | tf_op jit(solution)/shard_map/ppermute | solution.py:13
  40.4 13.4 %collective-permute-start.13 = (bf16[4,16,2048]{2,1,0:T(8,128)(2,1)S(1)}, bf16[4,16,2048]{2,1,0:T(8,128)(2,1)S(1)}, u32[]{:S(2)}, u32[]{:S(2)}) collective-permute-start(bf16[4,16,2048]{2,1,0:T(8,128)(2,1)S(1)} %collective-permute-done.8), channel_id=1, source_target_pairs={{0,192},{64,0},{128,64},{192,128},{1,193},{65,1},{129,65},{193,129... | collective-permute-start | bytes 786440 | tf_op jit(solution)/shard_map/ppermute | solution.py:13
  41.2 12.7 %collective-permute-start.12 = (bf16[4,16,2048]{2,1,0:T(8,128)(2,1)S(1)}, bf16[4,16,2048]{2,1,0:T(8,128)(2,1)S(1)}, u32[]{:S(2)}, u32[]{:S(2)}) collective-permute-start(bf16[4,16,2048]{2,1,0:T(8,128)(2,1)S(1)} %collective-permute-done.8), channel_id=1, source_target_pairs={{0,64},{64,128},{128,192},{192,0},{1,65},{65,129},{129,193},{193,1... | collective-permute-start | bytes 786440 | tf_op jit(solution)/shard_map/ppermute | solution.py:13
  46.0 12.3 %collective-permute-start.17 = (bf16[64,1792]{1,0:T(8,128)(2,1)S(1)}, bf16[64,1792]{1,0:T(8,128)(2,1)S(1)}, u32[]{:S(2)}, u32[]{:S(2)}) collective-permute-start(bf16[64,1792]{1,0:T(8,128)(2,1)S(1)} %get-tuple-element.100), channel_id=1, source_target_pairs={{0,3},{1,0},{2,1},{3,2},{4,7},{5,4},{6,5},{7,6},{8,11},{9,8},{10,9... | collective-permute-start | bytes 688136 | tf_op jit(solution)/shard_map/ppermute | solution.py:13
  46.1 12.6 %collective-permute-start.16 = (bf16[64,1792]{1,0:T(8,128)(2,1)S(1)}, bf16[64,1792]{1,0:T(8,128)(2,1)S(1)}, u32[]{:S(2)}, u32[]{:S(2)}) collective-permute-start(bf16[64,1792]{1,0:T(8,128)(2,1)S(1)} %get-tuple-element.101), channel_id=1, source_target_pairs={{0,1},{1,2},{2,3},{3,0},{4,5},{5,6},{6,7},{7,4},{8,9},{9,10},{10,1... | collective-permute-start | bytes 688136 | tf_op jit(solution)/shard_map/ppermute | solution.py:13
  50.1 8.5 %collective-permute-start.15 = (bf16[64,1792]{1,0:T(8,128)(2,1)S(1)}, bf16[64,1792]{1,0:T(8,128)(2,1)S(1)}, u32[]{:S(2)}, u32[]{:S(2)}) collective-permute-start(bf16[64,1792]{1,0:T(8,128)(2,1)S(1)} %get-tuple-element.102), channel_id=1, source_target_pairs={{0,2},{1,3},{2,0},{3,1},{4,6},{5,7},{6,4},{7,5},{8,10},{9,11},{10,... | collective-permute-start | bytes 688136 | tf_op jit(solution)/shard_map/ppermute | solution.py:13
  56.1 8.5 %collective-permute-start.20 = (bf16[64,1792]{1,0:T(8,128)(2,1)S(1)}, bf16[64,1792]{1,0:T(8,128)(2,1)S(1)}, u32[]{:S(2)}, u32[]{:S(2)}) collective-permute-start(bf16[64,1792]{1,0:T(8,128)(2,1)S(1)} %get-tuple-element.97), channel_id=1, source_target_pairs={{0,3},{1,0},{2,1},{3,2},{4,7},{5,4},{6,5},{7,6},{8,11},{9,8},{10,9... | collective-permute-start | bytes 688136 | tf_op jit(solution)/shard_map/ppermute | solution.py:13
  56.2 15.6 %collective-permute-start.19 = (bf16[64,1792]{1,0:T(8,128)(2,1)S(1)}, bf16[64,1792]{1,0:T(8,128)(2,1)S(1)}, u32[]{:S(2)}, u32[]{:S(2)}) collective-permute-start(bf16[64,1792]{1,0:T(8,128)(2,1)S(1)} %get-tuple-element.98), channel_id=1, source_target_pairs={{0,1},{1,2},{2,3},{3,0},{4,5},{5,6},{6,7},{7,4},{8,9},{9,10},{10,1... | collective-permute-start | bytes 688136 | tf_op jit(solution)/shard_map/ppermute | solution.py:13
  58.3 13.6 %collective-permute-start.18 = (bf16[64,1792]{1,0:T(8,128)(2,1)S(1)}, bf16[64,1792]{1,0:T(8,128)(2,1)S(1)}, u32[]{:S(2)}, u32[]{:S(2)}) collective-permute-start(bf16[64,1792]{1,0:T(8,128)(2,1)S(1)} %get-tuple-element.99), channel_id=1, source_target_pairs={{0,2},{1,3},{2,0},{3,1},{4,6},{5,7},{6,4},{7,5},{8,10},{9,11},{10,... | collective-permute-start | bytes 688136 | tf_op jit(solution)/shard_map/ppermute | solution.py:13
  58.9 18.2 %collective-permute-start.23 = (bf16[64,896]{1,0:T(8,128)(2,1)S(1)}, bf16[64,896]{1,0:T(8,128)(2,1)S(1)}, u32[]{:S(2)}, u32[]{:S(2)}) collective-permute-start(bf16[64,896]{1,0:T(8,128)(2,1)S(1)} %fusion.17), channel_id=1, source_target_pairs={{0,1},{1,2},{2,3},{3,0},{4,5},{5,6},{6,7},{7,4},{8,9},{9,10},{10,1... | collective-permute-start | bytes 344072 | tf_op jit(solution)/shard_map/ppermute | solution.py:13
  60.8 16.3 %collective-permute-start.22 = (bf16[64,896]{1,0:T(8,128)(2,1)S(1)}, bf16[64,896]{1,0:T(8,128)(2,1)S(1)}, u32[]{:S(2)}, u32[]{:S(2)}) collective-permute-start(bf16[64,896]{1,0:T(8,128)(2,1)S(1)} %fusion.17), channel_id=1, source_target_pairs={{0,2},{1,3},{2,0},{3,1},{4,6},{5,7},{6,4},{7,5},{8,10},{9,11},{10,... | collective-permute-start | bytes 344072 | tf_op jit(solution)/shard_map/ppermute | solution.py:13
  64.7 12.4 %collective-permute-start.21 = (bf16[64,896]{1,0:T(8,128)(2,1)S(1)}, bf16[64,896]{1,0:T(8,128)(2,1)S(1)}, u32[]{:S(2)}, u32[]{:S(2)}) collective-permute-start(bf16[64,896]{1,0:T(8,128)(2,1)S(1)} %fusion.17), channel_id=1, source_target_pairs={{0,3},{1,0},{2,1},{3,2},{4,7},{5,4},{6,5},{7,6},{8,11},{9,8},{10,9... | collective-permute-start | bytes 344072 | tf_op jit(solution)/shard_map/ppermute | solution.py:13
  72.0 8.9 %collective-permute-start.26 = (bf16[64,896]{1,0:T(8,128)(2,1)S(1)}, bf16[64,896]{1,0:T(8,128)(2,1)S(1)}, u32[]{:S(2)}, u32[]{:S(2)}) collective-permute-start(bf16[64,896]{1,0:T(8,128)(2,1)S(1)} %fusion.16), channel_id=1, source_target_pairs={{0,1},{1,2},{2,3},{3,0},{4,5},{5,6},{6,7},{7,4},{8,9},{9,10},{10,1... | collective-permute-start | bytes 344072 | tf_op jit(solution)/shard_map/ppermute | solution.py:13
  72.1 9.7 %collective-permute-start.25 = (bf16[64,896]{1,0:T(8,128)(2,1)S(1)}, bf16[64,896]{1,0:T(8,128)(2,1)S(1)}, u32[]{:S(2)}, u32[]{:S(2)}) collective-permute-start(bf16[64,896]{1,0:T(8,128)(2,1)S(1)} %fusion.16), channel_id=1, source_target_pairs={{0,2},{1,3},{2,0},{3,1},{4,6},{5,7},{6,4},{7,5},{8,10},{9,11},{10,... | collective-permute-start | bytes 344072 | tf_op jit(solution)/shard_map/ppermute | solution.py:13
  78.6 10.9 %collective-permute-start.29 = (bf16[4,16,2048]{2,1,0:T(8,128)(2,1)S(1)}, bf16[4,16,2048]{2,1,0:T(8,128)(2,1)S(1)}, u32[]{:S(2)}, u32[]{:S(2)}) collective-permute-start(bf16[4,16,2048]{2,1,0:T(8,128)(2,1)S(1)} %get-tuple-element.94), channel_id=1, source_target_pairs={{0,128},{64,192},{128,0},{192,64},{1,129},{65,193},{129,1},{193,65... | collective-permute-start | bytes 786440 | tf_op jit(solution)/shard_map/ppermute | solution.py:13
  79.8 14.5 %collective-permute-start.28 = (bf16[4,16,2048]{2,1,0:T(8,128)(2,1)S(1)}, bf16[4,16,2048]{2,1,0:T(8,128)(2,1)S(1)}, u32[]{:S(2)}, u32[]{:S(2)}) collective-permute-start(bf16[4,16,2048]{2,1,0:T(8,128)(2,1)S(1)} %get-tuple-element.95), channel_id=1, source_target_pairs={{0,64},{64,128},{128,192},{192,0},{1,65},{65,129},{129,193},{193,1... | collective-permute-start | bytes 786440 | tf_op jit(solution)/shard_map/ppermute | solution.py:13
  80.9 16.1 %collective-permute-start.27 = (bf16[4,16,2048]{2,1,0:T(8,128)(2,1)S(1)}, bf16[4,16,2048]{2,1,0:T(8,128)(2,1)S(1)}, u32[]{:S(2)}, u32[]{:S(2)}) collective-permute-start(bf16[4,16,2048]{2,1,0:T(8,128)(2,1)S(1)} %get-tuple-element.96), channel_id=1, source_target_pairs={{0,192},{64,0},{128,64},{192,128},{1,193},{65,1},{129,65},{193,129... | collective-permute-start | bytes 786440 | tf_op jit(solution)/shard_map/ppermute | solution.py:13
  83.4 15.8 %collective-permute-start.34 = (bf16[4,16,2048]{2,1,0:T(8,128)(2,1)S(1)}, bf16[4,16,2048]{2,1,0:T(8,128)(2,1)S(1)}, u32[]{:S(2)}, u32[]{:S(2)}) collective-permute-start(bf16[4,16,2048]{2,1,0:T(8,128)(2,1)S(1)} %get-tuple-element.91), channel_id=1, source_target_pairs={{0,128},{64,192},{128,0},{192,64},{1,129},{65,193},{129,1},{193,65... | collective-permute-start | bytes 786440 | tf_op jit(solution)/shard_map/ppermute | solution.py:13
  85.9 13.5 %collective-permute-start.33 = (bf16[4,16,2048]{2,1,0:T(8,128)(2,1)S(1)}, bf16[4,16,2048]{2,1,0:T(8,128)(2,1)S(1)}, u32[]{:S(2)}, u32[]{:S(2)}) collective-permute-start(bf16[4,16,2048]{2,1,0:T(8,128)(2,1)S(1)} %get-tuple-element.92), channel_id=1, source_target_pairs={{0,64},{64,128},{128,192},{192,0},{1,65},{65,129},{129,193},{193,1... | collective-permute-start | bytes 786440 | tf_op jit(solution)/shard_map/ppermute | solution.py:13
  89.6 12.9 %collective-permute-start.32 = (bf16[4,16,2048]{2,1,0:T(8,128)(2,1)S(1)}, bf16[4,16,2048]{2,1,0:T(8,128)(2,1)S(1)}, u32[]{:S(2)}, u32[]{:S(2)}) collective-permute-start(bf16[4,16,2048]{2,1,0:T(8,128)(2,1)S(1)} %get-tuple-element.93), channel_id=1, source_target_pairs={{0,192},{64,0},{128,64},{192,128},{1,193},{65,1},{129,65},{193,129... | collective-permute-start | bytes 786440 | tf_op jit(solution)/shard_map/ppermute | solution.py:13
  102.6 9.5 %collective-permute-start.35 = (bf16[4,8,2048]{2,1,0:T(8,128)(2,1)S(1)}, bf16[4,8,2048]{2,1,0:T(8,128)(2,1)S(1)}, u32[]{:S(2)}, u32[]{:S(2)}) collective-permute-start(bf16[4,8,2048]{2,1,0:T(8,128)(2,1)S(1)} %get-tuple-element.103), channel_id=1, source_target_pairs={{0,48},{4,36},{8,56},{12,44},{16,0},{20,52},{24,8},{28,60},{32,16}... | collective-permute-start | bytes 393224 | tf_op jit(solution)/shard_map/ppermute | solution.py:21
  108.1 8.7 %collective-permute-start.36 = (bf16[4,8,2048]{2,1,0:T(8,128)(2,1)S(1)}, bf16[4,8,2048]{2,1,0:T(8,128)(2,1)S(1)}, u32[]{:S(2)}, u32[]{:S(2)}) collective-permute-start(bf16[4,8,2048]{2,1,0:T(8,128)(2,1)S(1)} %get-tuple-element.104), channel_id=1, source_target_pairs={{0,40},{4,28},{8,48},{12,36},{16,56},{20,44},{24,0},{28,52},{32,8}... | collective-permute-start | bytes 393224 | tf_op jit(solution)/shard_map/ppermute | solution.py:21
  118.3 9.0 %collective-permute-start.40 = (f32[4,2048]{1,0:T(4,128)S(1)}, f32[4,2048]{1,0:T(4,128)S(1)}, u32[]{:S(2)}, u32[]{:S(2)}) collective-permute-start(f32[4,2048]{1,0:T(4,128)S(1)} %get-tuple-element.111), channel_id=1, source_target_pairs={{0,1},{1,2},{2,3},{3,0},{4,5},{5,6},{6,7},{7,4},{8,9},{9,10},{10,1... | collective-permute-start | bytes 98312 | tf_op jit(solution)/shard_map/ppermute | solution.py:13
  124.5 5.4 %collective-permute-start.39 = (f32[4,2048]{1,0:T(4,128)S(1)}, f32[4,2048]{1,0:T(4,128)S(1)}, u32[]{:S(2)}, u32[]{:S(2)}) collective-permute-start(f32[4,2048]{1,0:T(4,128)S(1)} %get-tuple-element.112), channel_id=1, source_target_pairs={{0,2},{1,3},{2,0},{3,1},{4,6},{5,7},{6,4},{7,5},{8,10},{9,11},{10,... | collective-permute-start | bytes 98312 | tf_op jit(solution)/shard_map/ppermute | solution.py:13
  (11 other events, 76.1 us)

commit v8 on v7

--- a/solution.py
+++ b/solution.py
@@ -89,7 +89,8 @@
 
     slots = near.shape[1]
     near_y = over_y(near)
-    *first, near_own = together(*first, near)
+    *first, down_own, down_other, near_own = together(*first, *second, near)
+    second = [down_own, down_other]
     first, far = together(jnp.concatenate(first, axis=0), far)
     far_y = over_y(far)
 

time: 131 us -> 129 us (0.985)
  the two profiles are of different devices: /device:TPU:56 before, /device:TPU:1 now
where the time goes in v8:
time: 129 us; the launch traced here: 127 us
  starting transfers between devices  69.2 us (54%)
  waiting for transfers between devices  37.8 us (29%)
  other arithmetic  8.58 us (7%)
  matrix products  6.77 us (5%)
  blocking collectives  3.85 us (3%)
    ppermute x34, starting transfers between devices, shift(): return lax.ppermute(value, axis, [(i, (i + step) % n) for i in range(n)])  40.5 us
    ppermute x7, starting transfers between devices, along_z(): return lax.ppermute(value, ('z', 'c'), pairs)  28.8 us
    ppermute x34, waiting for transfers between devices, shift(): return lax.ppermute(value, axis, [(i, (i + step) % n) for i in range(n)])  22.8 us
    ppermute x7, waiting for transfers between devices, along_z(): return lax.ppermute(value, ('z', 'c'), pairs)  15 us
    dot_general x2, matrix products, project(): lax.dot_general(block.reshape(-1, part), weights, (((1,), (1,)), ((), ())...  4.23 us
    concatenate x1, other arithmetic, local(): first, far = together(jnp.concatenate(first, axis=0), far)  4.07 us
    all_gather x1, blocking collectives, local(): pair = lax.all_gather(own, 'c', axis=1, tiled=True)  3.85 us
  transfers between devices with their start and end apart: 41, of which 21 were waited for; matrix products, arithmetic and copies ran while one was open for 12% of the time, Pallas kernels for 0%

profile of v8, /device:TPU:1, one launch (start us, length us, event | category | flops | bytes accessed | tf_op | source)
XLA Modules:
  0.0 127.2 jit_solution(17493180597434359382)
XLA Ops:
  0.0 3.2 %collective-permute-start = (bf16[448,2048]{1,0:T(8,128)(2,1)}, bf16[448,2048]{1,0:T(8,128)(2,1)}, u32[]{:S(2)}, u32[]{:S(2)}) collective-permute-start(bf16[448,2048]{1,0:T(8,128)(2,1)} %bitcast.46), channel_id=1, source_target_pairs={{0,4},{4,0},{1,5},{5,1},{2,6},{6,2},{3,7},{7,3},{8,12},{12,8},{9,1... | collective-permute-start | bytes 5505032 | tf_op jit(solution)/shard_map/ppermute | solution.py:13
  7.8 2.2 %collective-permute-done.4 = bf16[4,2048]{1,0:T(4,128)(2,1)S(1)} collective-permute-done((bf16[4,2048]{1,0:T(4,128)(2,1)S(1)}, bf16[4,2048]{1,0:T(4,128)(2,1)S(1)}, u32[]{:S(2)}, u32[]{:S(2)}) %collective-permute-start.4) | collective-permute-done | bytes 16416 | tf_op jit(solution)/shard_map/ppermute | solution.py:13
  10.1 3.8 %collective-permute-done.5 = bf16[4,2048]{1,0:T(4,128)(2,1)S(1)} collective-permute-done((bf16[4,2048]{1,0:T(4,128)(2,1)S(1)}, bf16[4,2048]{1,0:T(4,128)(2,1)S(1)}, u32[]{:S(2)}, u32[]{:S(2)}) %collective-permute-start.5) | collective-permute-done | bytes 16416 | tf_op jit(solution)/shard_map/ppermute | solution.py:13
  14.0 3.9 %all_gather.3 = bf16[4,8,2048]{2,0,1:T(4,128)(2,1)S(1)} all-gather(bf16[4,4,2048]{2,0,1:T(4,128)(2,1)S(1)} %copy.10), channel_id=1, replica_groups=mesh['y'=4,'z'=8,'c'=2,'x'=4] {'c'}, dimensions={1}, use_global_device_ids=true | all-gather | bytes 196608 | tf_op jit(solution)/shard_map/all_gather | solution.py:50
  17.9 6.2 %collective-permute-start.6 = (bf16[4,8,2048]{2,1,0:T(8,128)(2,1)S(1)}, bf16[4,8,2048]{2,1,0:T(8,128)(2,1)S(1)}, u32[]{:S(2)}, u32[]{:S(2)}) collective-permute-start(bf16[4,8,2048]{2,1,0:T(8,128)(2,1)S(1)} %copy.11), channel_id=1, source_target_pairs={{0,0},{4,52},{8,8},{12,60},{16,16},{20,4},{24,24},{28,12},{32,32},... | collective-permute-start | bytes 393224 | tf_op jit(solution)/shard_map/ppermute | solution.py:21
  24.9 2.5 %collective-permute-done.6 = bf16[4,8,2048]{2,1,0:T(8,128)(2,1)S(1)} collective-permute-done((bf16[4,8,2048]{2,1,0:T(8,128)(2,1)S(1)}, bf16[4,8,2048]{2,1,0:T(8,128)(2,1)S(1)}, u32[]{:S(2)}, u32[]{:S(2)}) %collective-permute-start.6) | collective-permute-done | bytes 131104 | tf_op jit(solution)/shard_map/ppermute | solution.py:21
  28.8 3.0 %collective-permute-start.11 = (bf16[4,16,2048]{2,1,0:T(8,128)(2,1)S(1)}, bf16[4,16,2048]{2,1,0:T(8,128)(2,1)S(1)}, u32[]{:S(2)}, u32[]{:S(2)}) collective-permute-start(bf16[4,16,2048]{2,1,0:T(8,128)(2,1)S(1)} %constant_dynamic-update-slice_fusion), channel_id=1, source_target_pairs={{0,128},{64,192},{128,0},{192,64},{1,129},{65,193},{129,1},{193,65... | collective-permute-start | bytes 786440 | tf_op jit(solution)/shard_map/ppermute | solution.py:13
  33.3 2.6 %collective-permute-start.8 = (bf16[4,16,2048]{2,1,0:T(8,128)(2,1)S(1)}, bf16[4,16,2048]{2,1,0:T(8,128)(2,1)S(1)}, u32[]{:S(2)}, u32[]{:S(2)}) collective-permute-start(bf16[4,16,2048]{2,1,0:T(8,128)(2,1)S(1)} %constant_dynamic-update-slice_fusion), channel_id=1, source_target_pairs={{0,16},{4,52},{8,24},{12,60},{16,32},{20,4},{24,40},{28,12},{32,48... | collective-permute-start | bytes 786440 | tf_op jit(solution)/shard_map/ppermute | solution.py:21
  35.9 4.1 %pad_maximum_fusion = bf16[1792,2048]{1,0:T(8,128)(2,1)S(1)} fusion(bf16[448,2048]{1,0:T(8,128)(2,1)} %collective-permute-done.1, bf16[448,2048]{1,0:T(8,128)(2,1)} %bitcast.45, bf16[448,2048]{1,0:T(8,128)(2,1)} %collective-permute-done, bf16[448,2048]{1,0:T(8,128)(2,1)} %bitcast.47), kind=kLoop, calls=%fused_computation | loop fusion | flops 29360128 | bytes 14680064 | tf_op jit(solution)/shard_map/concatenate | solution.py:94
  40.0 2.3 %collective-permute-done.8 = bf16[4,16,2048]{2,1,0:T(8,128)(2,1)S(1)} collective-permute-done((bf16[4,16,2048]{2,1,0:T(8,128)(2,1)S(1)}, bf16[4,16,2048]{2,1,0:T(8,128)(2,1)S(1)}, u32[]{:S(2)}, u32[]{:S(2)}) %collective-permute-start.8) | collective-permute-done | bytes 262176 | tf_op jit(solution)/shard_map/ppermute | solution.py:21
  43.1 2.0 %collective-permute-start.13 = (bf16[4,16,2048]{2,1,0:T(8,128)(2,1)S(1)}, bf16[4,16,2048]{2,1,0:T(8,128)(2,1)S(1)}, u32[]{:S(2)}, u32[]{:S(2)}) collective-permute-start(bf16[4,16,2048]{2,1,0:T(8,128)(2,1)S(1)} %collective-permute-done.8), channel_id=1, source_target_pairs={{0,192},{64,0},{128,64},{192,128},{1,193},{65,1},{129,65},{193,129... | collective-permute-start | bytes 786440 | tf_op jit(solution)/shard_map/ppermute | solution.py:13
  45.2 2.1 %fusion.32 = (bf16[256,1792]{1,0:T(8,128)(2,1)S(1)}, f32[256,1792]{1,0:T(8,128)S(1)}) fusion(bf16[256,2048]{1,0:T(8,128)(2,1)S(1)} %bitcast.49, bf16[1792,2048]{1,0:T(8,128)(2,1)S(1)} %pad_maximum_fusion), kind=kOutput, calls=%fused_computation.65 | convolution fusion | flops 1879506944 | bytes 11141120 | tf_op jit(solution)/shard_map/dot_general | solution.py:55
  49.5 1.9 %collective-permute-done.14 = bf16[4,16,2048]{2,1,0:T(8,128)(2,1)S(1)} collective-permute-done((bf16[4,16,2048]{2,1,0:T(8,128)(2,1)S(1)}, bf16[4,16,2048]{2,1,0:T(8,128)(2,1)S(1)}, u32[]{:S(2)}, u32[]{:S(2)}) %collective-permute-start.14) | collective-permute-done | bytes 262176 | tf_op jit(solution)/shard_map/ppermute | solution.py:13
  52.9 4.1 %collective-permute-done.13 = bf16[4,16,2048]{2,1,0:T(8,128)(2,1)S(1)} collective-permute-done((bf16[4,16,2048]{2,1,0:T(8,128)(2,1)S(1)}, bf16[4,16,2048]{2,1,0:T(8,128)(2,1)S(1)}, u32[]{:S(2)}, u32[]{:S(2)}) %collective-permute-start.13) | collective-permute-done | bytes 262176 | tf_op jit(solution)/shard_map/ppermute | solution.py:13
  57.8 2.1 %fusion.33 = (bf16[256,1792]{1,0:T(8,128)(2,1)S(1)}, f32[256,1792]{1,0:T(8,128)S(1)}) fusion(bf16[256,2048]{1,0:T(8,128)(2,1)S(1)} %bitcast.48, bf16[1792,2048]{1,0:T(8,128)(2,1)S(1)} %pad_maximum_fusion), kind=kOutput, calls=%fused_computation.66 | convolution fusion | flops 1879506944 | bytes 11141120 | tf_op jit(solution)/shard_map/dot_general | solution.py:55
  66.7 2.6 %collective-permute-start.21 = (bf16[64,896]{1,0:T(8,128)(2,1)S(1)}, bf16[64,896]{1,0:T(8,128)(2,1)S(1)}, u32[]{:S(2)}, u32[]{:S(2)}) collective-permute-start(bf16[64,896]{1,0:T(8,128)(2,1)S(1)} %fusion.17), channel_id=1, source_target_pairs={{0,3},{1,0},{2,1},{3,2},{4,7},{5,4},{6,5},{7,6},{8,11},{9,8},{10,9... | collective-permute-start | bytes 344072 | tf_op jit(solution)/shard_map/ppermute | solution.py:13
  69.8 3.0 %collective-permute-done.18 = bf16[64,1792]{1,0:T(8,128)(2,1)S(1)} collective-permute-done((bf16[64,1792]{1,0:T(8,128)(2,1)S(1)}, bf16[64,1792]{1,0:T(8,128)(2,1)S(1)}, u32[]{:S(2)}, u32[]{:S(2)}) %collective-permute-start.18) | collective-permute-done | bytes 229408 | tf_op jit(solution)/shard_map/ppermute | solution.py:13
  73.1 2.4 %collective-permute-start.25 = (bf16[64,896]{1,0:T(8,128)(2,1)S(1)}, bf16[64,896]{1,0:T(8,128)(2,1)S(1)}, u32[]{:S(2)}, u32[]{:S(2)}) collective-permute-start(bf16[64,896]{1,0:T(8,128)(2,1)S(1)} %fusion.16), channel_id=1, source_target_pairs={{0,2},{1,3},{2,0},{3,1},{4,6},{5,7},{6,4},{7,5},{8,10},{9,11},{10,... | collective-permute-start | bytes 344072 | tf_op jit(solution)/shard_map/ppermute | solution.py:13
  75.5 1.7 %collective-permute-done.23 = bf16[64,896]{1,0:T(8,128)(2,1)S(1)} collective-permute-done((bf16[64,896]{1,0:T(8,128)(2,1)S(1)}, bf16[64,896]{1,0:T(8,128)(2,1)S(1)}, u32[]{:S(2)}, u32[]{:S(2)}) %collective-permute-start.23) | collective-permute-done | bytes 114720 | tf_op jit(solution)/shard_map/ppermute | solution.py:13
  79.6 2.2 %collective-permute-start.28 = (bf16[4,16,2048]{2,1,0:T(8,128)(2,1)S(1)}, bf16[4,16,2048]{2,1,0:T(8,128)(2,1)S(1)}, u32[]{:S(2)}, u32[]{:S(2)}) collective-permute-start(bf16[4,16,2048]{2,1,0:T(8,128)(2,1)S(1)} %get-tuple-element.99), channel_id=1, source_target_pairs={{0,64},{64,128},{128,192},{192,0},{1,65},{65,129},{129,193},{193,1... | collective-permute-start | bytes 786440 | tf_op jit(solution)/shard_map/ppermute | solution.py:13
  82.1 2.2 %collective-permute-start.27 = (bf16[4,16,2048]{2,1,0:T(8,128)(2,1)S(1)}, bf16[4,16,2048]{2,1,0:T(8,128)(2,1)S(1)}, u32[]{:S(2)}, u32[]{:S(2)}) collective-permute-start(bf16[4,16,2048]{2,1,0:T(8,128)(2,1)S(1)} %get-tuple-element.100), channel_id=1, source_target_pairs={{0,192},{64,0},{128,64},{192,128},{1,193},{65,1},{129,65},{193,129... | collective-permute-start | bytes 786440 | tf_op jit(solution)/shard_map/ppermute | solution.py:13
  86.8 1.9 %collective-permute-start.32 = (bf16[4,16,2048]{2,1,0:T(8,128)(2,1)S(1)}, bf16[4,16,2048]{2,1,0:T(8,128)(2,1)S(1)}, u32[]{:S(2)}, u32[]{:S(2)}) collective-permute-start(bf16[4,16,2048]{2,1,0:T(8,128)(2,1)S(1)} %get-tuple-element.97), channel_id=1, source_target_pairs={{0,192},{64,0},{128,64},{192,128},{1,193},{65,1},{129,65},{193,129... | collective-permute-start | bytes 786440 | tf_op jit(solution)/shard_map/ppermute | solution.py:13
  89.1 5.5 %collective-permute-start.31 = (bf16[4,8,2048]{2,1,0:T(8,128)(2,1)S(1)}, bf16[4,8,2048]{2,1,0:T(8,128)(2,1)S(1)}, u32[]{:S(2)}, u32[]{:S(2)}) collective-permute-start(bf16[4,8,2048]{2,1,0:T(8,128)(2,1)S(1)} %get-tuple-element.109), channel_id=1, source_target_pairs={{0,56},{4,12},{8,0},{12,20},{16,8},{20,28},{24,16},{28,36},{32,24}... | collective-permute-start | bytes 393224 | tf_op jit(solution)/shard_map/ppermute | solution.py:21
  94.6 6.5 %collective-permute-start.30 = (bf16[4,8,2048]{2,1,0:T(8,128)(2,1)S(1)}, bf16[4,8,2048]{2,1,0:T(8,128)(2,1)S(1)}, u32[]{:S(2)}, u32[]{:S(2)}) collective-permute-start(bf16[4,8,2048]{2,1,0:T(8,128)(2,1)S(1)} %get-tuple-element.110), channel_id=1, source_target_pairs={{0,0},{4,20},{8,8},{12,28},{16,16},{20,36},{24,24},{28,44},{32,32}... | collective-permute-start | bytes 393224 | tf_op jit(solution)/shard_map/ppermute | solution.py:21
  101.4 3.3 %collective-permute-done.30 = bf16[4,8,2048]{2,1,0:T(8,128)(2,1)S(1)} collective-permute-done((bf16[4,8,2048]{2,1,0:T(8,128)(2,1)S(1)}, bf16[4,8,2048]{2,1,0:T(8,128)(2,1)S(1)}, u32[]{:S(2)}, u32[]{:S(2)}) %collective-permute-start.30) | collective-permute-done | bytes 131104 | tf_op jit(solution)/shard_map/ppermute | solution.py:21
  104.8 4.5 %collective-permute-start.35 = (bf16[4,8,2048]{2,1,0:T(8,128)(2,1)S(1)}, bf16[4,8,2048]{2,1,0:T(8,128)(2,1)S(1)}, u32[]{:S(2)}, u32[]{:S(2)}) collective-permute-start(bf16[4,8,2048]{2,1,0:T(8,128)(2,1)S(1)} %get-tuple-element.107), channel_id=1, source_target_pairs={{0,48},{4,36},{8,56},{12,44},{16,0},{20,52},{24,8},{28,60},{32,16}... | collective-permute-start | bytes 393224 | tf_op jit(solution)/shard_map/ppermute | solution.py:21
  109.3 2.6 %collective-permute-start.36 = (bf16[4,8,2048]{2,1,0:T(8,128)(2,1)S(1)}, bf16[4,8,2048]{2,1,0:T(8,128)(2,1)S(1)}, u32[]{:S(2)}, u32[]{:S(2)}) collective-permute-start(bf16[4,8,2048]{2,1,0:T(8,128)(2,1)S(1)} %get-tuple-element.108), channel_id=1, source_target_pairs={{0,40},{4,28},{8,48},{12,36},{16,56},{20,44},{24,0},{28,52},{32,8}... | collective-permute-start | bytes 393224 | tf_op jit(solution)/shard_map/ppermute | solution.py:21
  111.9 2.3 %collective-permute-done.35 = bf16[4,8,2048]{2,1,0:T(8,128)(2,1)S(1)} collective-permute-done((bf16[4,8,2048]{2,1,0:T(8,128)(2,1)S(1)}, bf16[4,8,2048]{2,1,0:T(8,128)(2,1)S(1)}, u32[]{:S(2)}, u32[]{:S(2)}) %collective-permute-start.35) | collective-permute-done | bytes 131104 | tf_op jit(solution)/shard_map/ppermute | solution.py:21
  114.2 3.2 %collective-permute-done.36 = bf16[4,8,2048]{2,1,0:T(8,128)(2,1)S(1)} collective-permute-done((bf16[4,8,2048]{2,1,0:T(8,128)(2,1)S(1)}, bf16[4,8,2048]{2,1,0:T(8,128)(2,1)S(1)}, u32[]{:S(2)}, u32[]{:S(2)}) %collective-permute-start.36) | collective-permute-done | bytes 131104 | tf_op jit(solution)/shard_map/ppermute | solution.py:21
  119.7 2.4 %collective-permute-start.40 = (f32[4,2048]{1,0:T(4,128)S(1)}, f32[4,2048]{1,0:T(4,128)S(1)}, u32[]{:S(2)}, u32[]{:S(2)}) collective-permute-start(f32[4,2048]{1,0:T(4,128)S(1)} %get-tuple-element.115), channel_id=1, source_target_pairs={{0,1},{1,2},{2,3},{3,0},{4,5},{5,6},{6,7},{7,4},{8,9},{9,10},{10,1... | collective-permute-start | bytes 98312 | tf_op jit(solution)/shard_map/ppermute | solution.py:13
  122.2 2.5 %collective-permute-start.38 = (f32[4,2048]{1,0:T(4,128)S(1)}, f32[4,2048]{1,0:T(4,128)S(1)}, u32[]{:S(2)}, u32[]{:S(2)}) collective-permute-start(f32[4,2048]{1,0:T(4,128)S(1)} %get-tuple-element.117), channel_id=1, source_target_pairs={{0,3},{1,0},{2,1},{3,2},{4,7},{5,4},{6,5},{7,6},{8,11},{9,8},{10,9... | collective-permute-start | bytes 98312 | tf_op jit(solution)/shard_map/ppermute | solution.py:13
  124.7 1.8 %collective-permute-done.39 = f32[4,2048]{1,0:T(4,128)S(1)} collective-permute-done((f32[4,2048]{1,0:T(4,128)S(1)}, f32[4,2048]{1,0:T(4,128)S(1)}, u32[]{:S(2)}, u32[]{:S(2)}) %collective-permute-start.39) | collective-permute-done | bytes 32800 | tf_op jit(solution)/shard_map/ppermute | solution.py:13
  (97 shorter events, 30.2 us)
Async XLA Ops:
  0.0 32.6 %collective-permute-start = (bf16[448,2048]{1,0:T(8,128)(2,1)}, bf16[448,2048]{1,0:T(8,128)(2,1)}, u32[]{:S(2)}, u32[]{:S(2)}) collective-permute-start(bf16[448,2048]{1,0:T(8,128)(2,1)} %bitcast.46), channel_id=1, source_target_pairs={{0,4},{4,0},{1,5},{5,1},{2,6},{6,2},{3,7},{7,3},{8,12},{12,8},{9,1... | collective-permute-start | bytes 5505032 | tf_op jit(solution)/shard_map/ppermute | solution.py:13
  3.2 30.1 %collective-permute-start.1 = (bf16[448,2048]{1,0:T(8,128)(2,1)}, bf16[448,2048]{1,0:T(8,128)(2,1)}, u32[]{:S(2)}, u32[]{:S(2)}) collective-permute-start(bf16[448,2048]{1,0:T(8,128)(2,1)} %bitcast.44), channel_id=1, source_target_pairs={{0,4},{4,0},{1,5},{5,1},{2,6},{6,2},{3,7},{7,3},{8,12},{12,8},{9,1... | collective-permute-start | bytes 5505032 | tf_op jit(solution)/shard_map/ppermute | solution.py:13
  3.2 32.7 %collective-permute-start.2 = (bf16[448,2048]{1,0:T(8,128)(2,1)}, bf16[448,2048]{1,0:T(8,128)(2,1)S(1)}, u32[]{:S(2)}, u32[]{:S(2)}) collective-permute-start(bf16[448,2048]{1,0:T(8,128)(2,1)} %param.9), channel_id=1, source_target_pairs={{0,4},{4,0},{1,5},{5,1},{2,6},{6,2},{3,7},{7,3},{8,12},{12,8},{9,1... | collective-permute-start | bytes 5505032 | tf_op jit(solution)/shard_map/ppermute | solution.py:13
  17.9 9.5 %collective-permute-start.6 = (bf16[4,8,2048]{2,1,0:T(8,128)(2,1)S(1)}, bf16[4,8,2048]{2,1,0:T(8,128)(2,1)S(1)}, u32[]{:S(2)}, u32[]{:S(2)}) collective-permute-start(bf16[4,8,2048]{2,1,0:T(8,128)(2,1)S(1)} %copy.11), channel_id=1, source_target_pairs={{0,0},{4,52},{8,8},{12,60},{16,16},{20,4},{24,24},{28,12},{32,32},... | collective-permute-start | bytes 393224 | tf_op jit(solution)/shard_map/ppermute | solution.py:21
  28.8 16.3 %collective-permute-start.11 = (bf16[4,16,2048]{2,1,0:T(8,128)(2,1)S(1)}, bf16[4,16,2048]{2,1,0:T(8,128)(2,1)S(1)}, u32[]{:S(2)}, u32[]{:S(2)}) collective-permute-start(bf16[4,16,2048]{2,1,0:T(8,128)(2,1)S(1)} %constant_dynamic-update-slice_fusion), channel_id=1, source_target_pairs={{0,128},{64,192},{128,0},{192,64},{1,129},{65,193},{129,1},{193,65... | collective-permute-start | bytes 786440 | tf_op jit(solution)/shard_map/ppermute | solution.py:13
  31.8 13.3 %collective-permute-start.10 = (bf16[4,16,2048]{2,1,0:T(8,128)(2,1)S(1)}, bf16[4,16,2048]{2,1,0:T(8,128)(2,1)S(1)}, u32[]{:S(2)}, u32[]{:S(2)}) collective-permute-start(bf16[4,16,2048]{2,1,0:T(8,128)(2,1)S(1)} %constant_dynamic-update-slice_fusion), channel_id=1, source_target_pairs={{0,192},{64,0},{128,64},{192,128},{1,193},{65,1},{129,65},{193,129... | collective-permute-start | bytes 786440 | tf_op jit(solution)/shard_map/ppermute | solution.py:13
  32.6 12.5 %collective-permute-start.9 = (bf16[4,16,2048]{2,1,0:T(8,128)(2,1)S(1)}, bf16[4,16,2048]{2,1,0:T(8,128)(2,1)S(1)}, u32[]{:S(2)}, u32[]{:S(2)}) collective-permute-start(bf16[4,16,2048]{2,1,0:T(8,128)(2,1)S(1)} %constant_dynamic-update-slice_fusion), channel_id=1, source_target_pairs={{0,64},{64,128},{128,192},{192,0},{1,65},{65,129},{129,193},{193,1... | collective-permute-start | bytes 786440 | tf_op jit(solution)/shard_map/ppermute | solution.py:13
  33.3 9.0 %collective-permute-start.8 = (bf16[4,16,2048]{2,1,0:T(8,128)(2,1)S(1)}, bf16[4,16,2048]{2,1,0:T(8,128)(2,1)S(1)}, u32[]{:S(2)}, u32[]{:S(2)}) collective-permute-start(bf16[4,16,2048]{2,1,0:T(8,128)(2,1)S(1)} %constant_dynamic-update-slice_fusion), channel_id=1, source_target_pairs={{0,16},{4,52},{8,24},{12,60},{16,32},{20,4},{24,40},{28,12},{32,48... | collective-permute-start | bytes 786440 | tf_op jit(solution)/shard_map/ppermute | solution.py:21
  42.3 9.0 %collective-permute-start.14 = (bf16[4,16,2048]{2,1,0:T(8,128)(2,1)S(1)}, bf16[4,16,2048]{2,1,0:T(8,128)(2,1)S(1)}, u32[]{:S(2)}, u32[]{:S(2)}) collective-permute-start(bf16[4,16,2048]{2,1,0:T(8,128)(2,1)S(1)} %collective-permute-done.8), channel_id=1, source_target_pairs={{0,128},{64,192},{128,0},{192,64},{1,129},{65,193},{129,1},{193,65... | collective-permute-start | bytes 786440 | tf_op jit(solution)/shard_map/ppermute | solution.py:13
  43.1 13.9 %collective-permute-start.13 = (bf16[4,16,2048]{2,1,0:T(8,128)(2,1)S(1)}, bf16[4,16,2048]{2,1,0:T(8,128)(2,1)S(1)}, u32[]{:S(2)}, u32[]{:S(2)}) collective-permute-start(bf16[4,16,2048]{2,1,0:T(8,128)(2,1)S(1)} %collective-permute-done.8), channel_id=1, source_target_pairs={{0,192},{64,0},{128,64},{192,128},{1,193},{65,1},{129,65},{193,129... | collective-permute-start | bytes 786440 | tf_op jit(solution)/shard_map/ppermute | solution.py:13
  45.1 12.6 %collective-permute-start.12 = (bf16[4,16,2048]{2,1,0:T(8,128)(2,1)S(1)}, bf16[4,16,2048]{2,1,0:T(8,128)(2,1)S(1)}, u32[]{:S(2)}, u32[]{:S(2)}) collective-permute-start(bf16[4,16,2048]{2,1,0:T(8,128)(2,1)S(1)} %collective-permute-done.8), channel_id=1, source_target_pairs={{0,64},{64,128},{128,192},{192,0},{1,65},{65,129},{129,193},{193,1... | collective-permute-start | bytes 786440 | tf_op jit(solution)/shard_map/ppermute | solution.py:13
  47.4 14.1 %collective-permute-start.17 = (bf16[64,1792]{1,0:T(8,128)(2,1)S(1)}, bf16[64,1792]{1,0:T(8,128)(2,1)S(1)}, u32[]{:S(2)}, u32[]{:S(2)}) collective-permute-start(bf16[64,1792]{1,0:T(8,128)(2,1)S(1)} %get-tuple-element.104), channel_id=1, source_target_pairs={{0,3},{1,0},{2,1},{3,2},{4,7},{5,4},{6,5},{7,6},{8,11},{9,8},{10,9... | collective-permute-start | bytes 688136 | tf_op jit(solution)/shard_map/ppermute | solution.py:13
  48.8 14.4 %collective-permute-start.16 = (bf16[64,1792]{1,0:T(8,128)(2,1)S(1)}, bf16[64,1792]{1,0:T(8,128)(2,1)S(1)}, u32[]{:S(2)}, u32[]{:S(2)}) collective-permute-start(bf16[64,1792]{1,0:T(8,128)(2,1)S(1)} %get-tuple-element.105), channel_id=1, source_target_pairs={{0,1},{1,2},{2,3},{3,0},{4,5},{5,6},{6,7},{7,4},{8,9},{9,10},{10,1... | collective-permute-start | bytes 688136 | tf_op jit(solution)/shard_map/ppermute | solution.py:13
  51.3 11.8 %collective-permute-start.15 = (bf16[64,1792]{1,0:T(8,128)(2,1)S(1)}, bf16[64,1792]{1,0:T(8,128)(2,1)S(1)}, u32[]{:S(2)}, u32[]{:S(2)}) collective-permute-start(bf16[64,1792]{1,0:T(8,128)(2,1)S(1)} %get-tuple-element.106), channel_id=1, source_target_pairs={{0,2},{1,3},{2,0},{3,1},{4,6},{5,7},{6,4},{7,5},{8,10},{9,11},{10,... | collective-permute-start | bytes 688136 | tf_op jit(solution)/shard_map/ppermute | solution.py:13
  61.3 8.6 %collective-permute-start.19 = (bf16[64,1792]{1,0:T(8,128)(2,1)S(1)}, bf16[64,1792]{1,0:T(8,128)(2,1)S(1)}, u32[]{:S(2)}, u32[]{:S(2)}) collective-permute-start(bf16[64,1792]{1,0:T(8,128)(2,1)S(1)} %get-tuple-element.102), channel_id=1, source_target_pairs={{0,1},{1,2},{2,3},{3,0},{4,5},{5,6},{6,7},{7,4},{8,9},{9,10},{10,1... | collective-permute-start | bytes 688136 | tf_op jit(solution)/shard_map/ppermute | solution.py:13
  61.5 11.3 %collective-permute-start.18 = (bf16[64,1792]{1,0:T(8,128)(2,1)S(1)}, bf16[64,1792]{1,0:T(8,128)(2,1)S(1)}, u32[]{:S(2)}, u32[]{:S(2)}) collective-permute-start(bf16[64,1792]{1,0:T(8,128)(2,1)S(1)} %get-tuple-element.103), channel_id=1, source_target_pairs={{0,2},{1,3},{2,0},{3,1},{4,6},{5,7},{6,4},{7,5},{8,10},{9,11},{10,... | collective-permute-start | bytes 688136 | tf_op jit(solution)/shard_map/ppermute | solution.py:13
  63.3 13.8 %collective-permute-start.23 = (bf16[64,896]{1,0:T(8,128)(2,1)S(1)}, bf16[64,896]{1,0:T(8,128)(2,1)S(1)}, u32[]{:S(2)}, u32[]{:S(2)}) collective-permute-start(bf16[64,896]{1,0:T(8,128)(2,1)S(1)} %fusion.17), channel_id=1, source_target_pairs={{0,1},{1,2},{2,3},{3,0},{4,5},{5,6},{6,7},{7,4},{8,9},{9,10},{10,1... | collective-permute-start | bytes 344072 | tf_op jit(solution)/shard_map/ppermute | solution.py:13
  64.9 12.5 %collective-permute-start.22 = (bf16[64,896]{1,0:T(8,128)(2,1)S(1)}, bf16[64,896]{1,0:T(8,128)(2,1)S(1)}, u32[]{:S(2)}, u32[]{:S(2)}) collective-permute-start(bf16[64,896]{1,0:T(8,128)(2,1)S(1)} %fusion.17), channel_id=1, source_target_pairs={{0,2},{1,3},{2,0},{3,1},{4,6},{5,7},{6,4},{7,5},{8,10},{9,11},{10,... | collective-permute-start | bytes 344072 | tf_op jit(solution)/shard_map/ppermute | solution.py:13
  66.7 10.8 %collective-permute-start.21 = (bf16[64,896]{1,0:T(8,128)(2,1)S(1)}, bf16[64,896]{1,0:T(8,128)(2,1)S(1)}, u32[]{:S(2)}, u32[]{:S(2)}) collective-permute-start(bf16[64,896]{1,0:T(8,128)(2,1)S(1)} %fusion.17), channel_id=1, source_target_pairs={{0,3},{1,0},{2,1},{3,2},{4,7},{5,4},{6,5},{7,6},{8,11},{9,8},{10,9... | collective-permute-start | bytes 344072 | tf_op jit(solution)/shard_map/ppermute | solution.py:13
  73.0 9.1 %collective-permute-start.26 = (bf16[64,896]{1,0:T(8,128)(2,1)S(1)}, bf16[64,896]{1,0:T(8,128)(2,1)S(1)}, u32[]{:S(2)}, u32[]{:S(2)}) collective-permute-start(bf16[64,896]{1,0:T(8,128)(2,1)S(1)} %fusion.16), channel_id=1, source_target_pairs={{0,1},{1,2},{2,3},{3,0},{4,5},{5,6},{6,7},{7,4},{8,9},{9,10},{10,1... | collective-permute-start | bytes 344072 | tf_op jit(solution)/shard_map/ppermute | solution.py:13
  73.1 11.1 %collective-permute-start.25 = (bf16[64,896]{1,0:T(8,128)(2,1)S(1)}, bf16[64,896]{1,0:T(8,128)(2,1)S(1)}, u32[]{:S(2)}, u32[]{:S(2)}) collective-permute-start(bf16[64,896]{1,0:T(8,128)(2,1)S(1)} %fusion.16), channel_id=1, source_target_pairs={{0,2},{1,3},{2,0},{3,1},{4,6},{5,7},{6,4},{7,5},{8,10},{9,11},{10,... | collective-permute-start | bytes 344072 | tf_op jit(solution)/shard_map/ppermute | solution.py:13
  77.2 7.1 %collective-permute-start.24 = (bf16[64,896]{1,0:T(8,128)(2,1)S(1)}, bf16[64,896]{1,0:T(8,128)(2,1)S(1)}, u32[]{:S(2)}, u32[]{:S(2)}) collective-permute-start(bf16[64,896]{1,0:T(8,128)(2,1)S(1)} %fusion.16), channel_id=1, source_target_pairs={{0,3},{1,0},{2,1},{3,2},{4,7},{5,4},{6,5},{7,6},{8,11},{9,8},{10,9... | collective-permute-start | bytes 344072 | tf_op jit(solution)/shard_map/ppermute | solution.py:13
  79.0 7.8 %collective-permute-start.29 = (bf16[4,16,2048]{2,1,0:T(8,128)(2,1)S(1)}, bf16[4,16,2048]{2,1,0:T(8,128)(2,1)S(1)}, u32[]{:S(2)}, u32[]{:S(2)}) collective-permute-start(bf16[4,16,2048]{2,1,0:T(8,128)(2,1)S(1)} %get-tuple-element.98), channel_id=1, source_target_pairs={{0,128},{64,192},{128,0},{192,64},{1,129},{65,193},{129,1},{193,65... | collective-permute-start | bytes 786440 | tf_op jit(solution)/shard_map/ppermute | solution.py:13
  79.6 9.3 %collective-permute-start.28 = (bf16[4,16,2048]{2,1,0:T(8,128)(2,1)S(1)}, bf16[4,16,2048]{2,1,0:T(8,128)(2,1)S(1)}, u32[]{:S(2)}, u32[]{:S(2)}) collective-permute-start(bf16[4,16,2048]{2,1,0:T(8,128)(2,1)S(1)} %get-tuple-element.99), channel_id=1, source_target_pairs={{0,64},{64,128},{128,192},{192,0},{1,65},{65,129},{129,193},{193,1... | collective-permute-start | bytes 786440 | tf_op jit(solution)/shard_map/ppermute | solution.py:13
  82.1 6.9 %collective-permute-start.27 = (bf16[4,16,2048]{2,1,0:T(8,128)(2,1)S(1)}, bf16[4,16,2048]{2,1,0:T(8,128)(2,1)S(1)}, u32[]{:S(2)}, u32[]{:S(2)}) collective-permute-start(bf16[4,16,2048]{2,1,0:T(8,128)(2,1)S(1)} %get-tuple-element.100), channel_id=1, source_target_pairs={{0,192},{64,0},{128,64},{192,128},{1,193},{65,1},{129,65},{193,129... | collective-permute-start | bytes 786440 | tf_op jit(solution)/shard_map/ppermute | solution.py:13
  85.8 15.3 %collective-permute-start.34 = (bf16[4,16,2048]{2,1,0:T(8,128)(2,1)S(1)}, bf16[4,16,2048]{2,1,0:T(8,128)(2,1)S(1)}, u32[]{:S(2)}, u32[]{:S(2)}) collective-permute-start(bf16[4,16,2048]{2,1,0:T(8,128)(2,1)S(1)} %get-tuple-element.95), channel_id=1, source_target_pairs={{0,128},{64,192},{128,0},{192,64},{1,129},{65,193},{129,1},{193,65... | collective-permute-start | bytes 786440 | tf_op jit(solution)/shard_map/ppermute | solution.py:13
  85.9 15.4 %collective-permute-start.33 = (bf16[4,16,2048]{2,1,0:T(8,128)(2,1)S(1)}, bf16[4,16,2048]{2,1,0:T(8,128)(2,1)S(1)}, u32[]{:S(2)}, u32[]{:S(2)}) collective-permute-start(bf16[4,16,2048]{2,1,0:T(8,128)(2,1)S(1)} %get-tuple-element.96), channel_id=1, source_target_pairs={{0,64},{64,128},{128,192},{192,0},{1,65},{65,129},{129,193},{193,1... | collective-permute-start | bytes 786440 | tf_op jit(solution)/shard_map/ppermute | solution.py:13
  86.8 14.6 %collective-permute-start.32 = (bf16[4,16,2048]{2,1,0:T(8,128)(2,1)S(1)}, bf16[4,16,2048]{2,1,0:T(8,128)(2,1)S(1)}, u32[]{:S(2)}, u32[]{:S(2)}) collective-permute-start(bf16[4,16,2048]{2,1,0:T(8,128)(2,1)S(1)} %get-tuple-element.97), channel_id=1, source_target_pairs={{0,192},{64,0},{128,64},{192,128},{1,193},{65,1},{129,65},{193,129... | collective-permute-start | bytes 786440 | tf_op jit(solution)/shard_map/ppermute | solution.py:13
  89.1 12.2 %collective-permute-start.31 = (bf16[4,8,2048]{2,1,0:T(8,128)(2,1)S(1)}, bf16[4,8,2048]{2,1,0:T(8,128)(2,1)S(1)}, u32[]{:S(2)}, u32[]{:S(2)}) collective-permute-start(bf16[4,8,2048]{2,1,0:T(8,128)(2,1)S(1)} %get-tuple-element.109), channel_id=1, source_target_pairs={{0,56},{4,12},{8,0},{12,20},{16,8},{20,28},{24,16},{28,36},{32,24}... | collective-permute-start | bytes 393224 | tf_op jit(solution)/shard_map/ppermute | solution.py:21
  94.6 10.0 %collective-permute-start.30 = (bf16[4,8,2048]{2,1,0:T(8,128)(2,1)S(1)}, bf16[4,8,2048]{2,1,0:T(8,128)(2,1)S(1)}, u32[]{:S(2)}, u32[]{:S(2)}) collective-permute-start(bf16[4,8,2048]{2,1,0:T(8,128)(2,1)S(1)} %get-tuple-element.110), channel_id=1, source_target_pairs={{0,0},{4,20},{8,8},{12,28},{16,16},{20,36},{24,24},{28,44},{32,32}... | collective-permute-start | bytes 393224 | tf_op jit(solution)/shard_map/ppermute | solution.py:21
  104.8 9.4 %collective-permute-start.35 = (bf16[4,8,2048]{2,1,0:T(8,128)(2,1)S(1)}, bf16[4,8,2048]{2,1,0:T(8,128)(2,1)S(1)}, u32[]{:S(2)}, u32[]{:S(2)}) collective-permute-start(bf16[4,8,2048]{2,1,0:T(8,128)(2,1)S(1)} %get-tuple-element.107), channel_id=1, source_target_pairs={{0,48},{4,36},{8,56},{12,44},{16,0},{20,52},{24,8},{28,60},{32,16}... | collective-permute-start | bytes 393224 | tf_op jit(solution)/shard_map/ppermute | solution.py:21
  109.3 8.1 %collective-permute-start.36 = (bf16[4,8,2048]{2,1,0:T(8,128)(2,1)S(1)}, bf16[4,8,2048]{2,1,0:T(8,128)(2,1)S(1)}, u32[]{:S(2)}, u32[]{:S(2)}) collective-permute-start(bf16[4,8,2048]{2,1,0:T(8,128)(2,1)S(1)} %get-tuple-element.108), channel_id=1, source_target_pairs={{0,40},{4,28},{8,48},{12,36},{16,56},{20,44},{24,0},{28,52},{32,8}... | collective-permute-start | bytes 393224 | tf_op jit(solution)/shard_map/ppermute | solution.py:21
  (11 other events, 77.2 us)

commit v9 on v7

--- a/solution.py
+++ b/solution.py
@@ -35,7 +35,6 @@
     x, core = lax.axis_index("x"), lax.axis_index("c")
     gate_t, up_t = gate_weight.T, up_weight.T
     first = [gate_t, shift(gate_t, "c", 1), up_t, shift(up_t, "c", 1)]
-    second = [down_weight, shift(down_weight, "c", 1)]
     units = 2 * down_weight.shape[0]
     rows, width = tokens.shape
     part = width // 4
@@ -89,7 +88,8 @@
 
     slots = near.shape[1]
     near_y = over_y(near)
-    *first, near_own = together(*first, near)
+    *first, down_own, near_own = together(*first, down_weight, near)
+    second = [down_own, shift(down_own, "c", 1)]
     first, far = together(jnp.concatenate(first, axis=0), far)
     far_y = over_y(far)
 

time: 131 us -> 128 us (0.977)
  the two profiles are of different devices: /device:TPU:56 before, /device:TPU:1 now
where the time goes in v9:
time: 128 us
  starting transfers between devices  63.2 us (49%)
  waiting for transfers between devices  44.7 us (35%)
  other arithmetic  8.16 us (6%)
  matrix products  6.81 us (5%)
  blocking collectives  3.76 us (3%)
    ppermute x34, starting transfers between devices, shift(): return lax.ppermute(value, axis, [(i, (i + step) % n) for i in range(n)])  39.9 us
    ppermute x34, waiting for transfers between devices, shift(): return lax.ppermute(value, axis, [(i, (i + step) % n) for i in range(n)])  30.4 us
    ppermute x7, starting transfers between devices, along_z(): return lax.ppermute(value, ('z', 'c'), pairs)  23.3 us
    ppermute x7, waiting for transfers between devices, along_z(): return lax.ppermute(value, ('z', 'c'), pairs)  14.3 us
    dot_general x2, matrix products, project(): lax.dot_general(block.reshape(-1, part), weights, (((1,), (1,)), ((), ())...  4.23 us
    all_gather x1, blocking collectives, local(): pair = lax.all_gather(own, 'c', axis=1, tiled=True)  3.76 us
    concatenate x1, other arithmetic, local(): first, far = together(jnp.concatenate(first, axis=0), far)  3.61 us
    dot_general x2, matrix products, down(): lax.dot_general(jnp.concatenate(everyone, axis=0), weights, (((1,), (0,))...  2.58 us
  transfers between devices with their start and end apart: 41, of which 21 were waited for; matrix products, arithmetic and copies ran while one was open for 11% of the time, Pallas kernels for 0%

profile of v9, /device:TPU:1, one launch (start us, length us, event | category | flops | bytes accessed | tf_op | source)
XLA Modules:
  0.0 127.6 jit_solution(9503842588361304404)
XLA Ops:
  0.0 3.2 %collective-permute-start = (bf16[448,2048]{1,0:T(8,128)(2,1)}, bf16[448,2048]{1,0:T(8,128)(2,1)S(1)}, u32[]{:S(2)}, u32[]{:S(2)}) collective-permute-start(bf16[448,2048]{1,0:T(8,128)(2,1)} %bitcast.46), channel_id=1, source_target_pairs={{0,4},{4,0},{1,5},{5,1},{2,6},{6,2},{3,7},{7,3},{8,12},{12,8},{9,1... | collective-permute-start | bytes 5505032 | tf_op jit(solution)/shard_map/ppermute | solution.py:13
  11.2 3.8 %all_gather.3 = bf16[4,8,2048]{2,0,1:T(4,128)(2,1)S(1)} all-gather(bf16[4,4,2048]{2,0,1:T(4,128)(2,1)S(1)} %copy.10), channel_id=1, replica_groups=mesh['y'=4,'z'=8,'c'=2,'x'=4] {'c'}, dimensions={1}, use_global_device_ids=true | all-gather | bytes 196608 | tf_op jit(solution)/shard_map/all_gather | solution.py:49
  15.1 7.9 %collective-permute-start.5 = (bf16[4,8,2048]{2,1,0:T(8,128)(2,1)S(1)}, bf16[4,8,2048]{2,1,0:T(8,128)(2,1)S(1)}, u32[]{:S(2)}, u32[]{:S(2)}) collective-permute-start(bf16[4,8,2048]{2,1,0:T(8,128)(2,1)S(1)} %copy.11), channel_id=1, source_target_pairs={{0,0},{4,52},{8,8},{12,60},{16,16},{20,4},{24,24},{28,12},{32,32},... | collective-permute-start | bytes 393224 | tf_op jit(solution)/shard_map/ppermute | solution.py:21
  23.8 2.5 %collective-permute-done.5 = bf16[4,8,2048]{2,1,0:T(8,128)(2,1)S(1)} collective-permute-done((bf16[4,8,2048]{2,1,0:T(8,128)(2,1)S(1)}, bf16[4,8,2048]{2,1,0:T(8,128)(2,1)S(1)}, u32[]{:S(2)}, u32[]{:S(2)}) %collective-permute-start.5) | collective-permute-done | bytes 131104 | tf_op jit(solution)/shard_map/ppermute | solution.py:21
  27.7 3.0 %collective-permute-start.11 = (bf16[4,16,2048]{2,1,0:T(8,128)(2,1)S(1)}, bf16[4,16,2048]{2,1,0:T(8,128)(2,1)S(1)}, u32[]{:S(2)}, u32[]{:S(2)}) collective-permute-start(bf16[4,16,2048]{2,1,0:T(8,128)(2,1)S(1)} %constant_dynamic-update-slice_fusion), channel_id=1, source_target_pairs={{0,128},{64,192},{128,0},{192,64},{1,129},{65,193},{129,1},{193,65... | collective-permute-start | bytes 786440 | tf_op jit(solution)/shard_map/ppermute | solution.py:13
  32.2 2.6 %collective-permute-start.8 = (bf16[4,16,2048]{2,1,0:T(8,128)(2,1)S(1)}, bf16[4,16,2048]{2,1,0:T(8,128)(2,1)S(1)}, u32[]{:S(2)}, u32[]{:S(2)}) collective-permute-start(bf16[4,16,2048]{2,1,0:T(8,128)(2,1)S(1)} %constant_dynamic-update-slice_fusion), channel_id=1, source_target_pairs={{0,16},{4,52},{8,24},{12,60},{16,32},{20,4},{24,40},{28,12},{32,48... | collective-permute-start | bytes 786440 | tf_op jit(solution)/shard_map/ppermute | solution.py:21
  34.9 3.6 %pad_maximum_fusion = bf16[1792,2048]{1,0:T(8,128)(2,1)S(1)} fusion(bf16[448,2048]{1,0:T(8,128)(2,1)} %collective-permute-done.1, bf16[448,2048]{1,0:T(8,128)(2,1)} %bitcast.45, bf16[448,2048]{1,0:T(8,128)(2,1)S(1)} %collective-permute-done, bf16[448,2048]{1,0:T(8,128)(2,1)} %bitcast.47), kind=kLoop, calls=%fused_computation | loop fusion | flops 29360128 | bytes 14680064 | tf_op jit(solution)/shard_map/concatenate | solution.py:93
  38.5 2.7 %collective-permute-done.8 = bf16[4,16,2048]{2,1,0:T(8,128)(2,1)S(1)} collective-permute-done((bf16[4,16,2048]{2,1,0:T(8,128)(2,1)S(1)}, bf16[4,16,2048]{2,1,0:T(8,128)(2,1)S(1)}, u32[]{:S(2)}, u32[]{:S(2)}) %collective-permute-start.8) | collective-permute-done | bytes 262176 | tf_op jit(solution)/shard_map/ppermute | solution.py:21
  41.9 2.1 %collective-permute-start.13 = (bf16[4,16,2048]{2,1,0:T(8,128)(2,1)S(1)}, bf16[4,16,2048]{2,1,0:T(8,128)(2,1)S(1)}, u32[]{:S(2)}, u32[]{:S(2)}) collective-permute-start(bf16[4,16,2048]{2,1,0:T(8,128)(2,1)S(1)} %collective-permute-done.8), channel_id=1, source_target_pairs={{0,192},{64,0},{128,64},{192,128},{1,193},{65,1},{129,65},{193,129... | collective-permute-start | bytes 786440 | tf_op jit(solution)/shard_map/ppermute | solution.py:13
  44.3 2.1 %fusion.32 = (bf16[256,1792]{1,0:T(8,128)(2,1)S(1)}, f32[256,1792]{1,0:T(8,128)S(1)}) fusion(bf16[256,2048]{1,0:T(8,128)(2,1)S(1)} %bitcast.49, bf16[1792,2048]{1,0:T(8,128)(2,1)S(1)} %pad_maximum_fusion), kind=kOutput, calls=%fused_computation.65 | convolution fusion | flops 1879506944 | bytes 11141120 | tf_op jit(solution)/shard_map/dot_general | solution.py:54
  50.3 5.6 %collective-permute-done.13 = bf16[4,16,2048]{2,1,0:T(8,128)(2,1)S(1)} collective-permute-done((bf16[4,16,2048]{2,1,0:T(8,128)(2,1)S(1)}, bf16[4,16,2048]{2,1,0:T(8,128)(2,1)S(1)}, u32[]{:S(2)}, u32[]{:S(2)}) %collective-permute-start.13) | collective-permute-done | bytes 262176 | tf_op jit(solution)/shard_map/ppermute | solution.py:13
  56.7 2.1 %fusion.33 = (bf16[256,1792]{1,0:T(8,128)(2,1)S(1)}, f32[256,1792]{1,0:T(8,128)S(1)}) fusion(bf16[256,2048]{1,0:T(8,128)(2,1)S(1)} %bitcast.48, bf16[1792,2048]{1,0:T(8,128)(2,1)S(1)} %pad_maximum_fusion), kind=kOutput, calls=%fused_computation.66 | convolution fusion | flops 1879506944 | bytes 11141120 | tf_op jit(solution)/shard_map/dot_general | solution.py:54
  60.8 1.9 %collective-permute-start.23 = (bf16[64,896]{1,0:T(8,128)(2,1)S(1)}, bf16[64,896]{1,0:T(8,128)(2,1)S(1)}, u32[]{:S(2)}, u32[]{:S(2)}) collective-permute-start(bf16[64,896]{1,0:T(8,128)(2,1)S(1)} %fusion.17), channel_id=1, source_target_pairs={{0,1},{1,2},{2,3},{3,0},{4,5},{5,6},{6,7},{7,4},{8,9},{9,10},{10,1... | collective-permute-start | bytes 344072 | tf_op jit(solution)/shard_map/ppermute | solution.py:13
  62.7 1.7 %collective-permute-start.22 = (bf16[64,896]{1,0:T(8,128)(2,1)S(1)}, bf16[64,896]{1,0:T(8,128)(2,1)S(1)}, u32[]{:S(2)}, u32[]{:S(2)}) collective-permute-start(bf16[64,896]{1,0:T(8,128)(2,1)S(1)} %fusion.17), channel_id=1, source_target_pairs={{0,2},{1,3},{2,0},{3,1},{4,6},{5,7},{6,4},{7,5},{8,10},{9,11},{10,... | collective-permute-start | bytes 344072 | tf_op jit(solution)/shard_map/ppermute | solution.py:13
  67.2 3.7 %collective-permute-done.19 = bf16[64,1792]{1,0:T(8,128)(2,1)S(1)} collective-permute-done((bf16[64,1792]{1,0:T(8,128)(2,1)S(1)}, bf16[64,1792]{1,0:T(8,128)(2,1)S(1)}, u32[]{:S(2)}, u32[]{:S(2)}) %collective-permute-start.19) | collective-permute-done | bytes 229408 | tf_op jit(solution)/shard_map/ppermute | solution.py:13
  71.1 3.3 %collective-permute-start.25 = (bf16[64,896]{1,0:T(8,128)(2,1)S(1)}, bf16[64,896]{1,0:T(8,128)(2,1)S(1)}, u32[]{:S(2)}, u32[]{:S(2)}) collective-permute-start(bf16[64,896]{1,0:T(8,128)(2,1)S(1)} %fusion.16), channel_id=1, source_target_pairs={{0,2},{1,3},{2,0},{3,1},{4,6},{5,7},{6,4},{7,5},{8,10},{9,11},{10,... | collective-permute-start | bytes 344072 | tf_op jit(solution)/shard_map/ppermute | solution.py:13
  74.4 1.9 %collective-permute-done.23 = bf16[64,896]{1,0:T(8,128)(2,1)S(1)} collective-permute-done((bf16[64,896]{1,0:T(8,128)(2,1)S(1)}, bf16[64,896]{1,0:T(8,128)(2,1)S(1)}, u32[]{:S(2)}, u32[]{:S(2)}) %collective-permute-start.23) | collective-permute-done | bytes 114720 | tf_op jit(solution)/shard_map/ppermute | solution.py:13
  78.3 2.4 %collective-permute-start.28 = (bf16[4,16,2048]{2,1,0:T(8,128)(2,1)S(1)}, bf16[4,16,2048]{2,1,0:T(8,128)(2,1)S(1)}, u32[]{:S(2)}, u32[]{:S(2)}) collective-permute-start(bf16[4,16,2048]{2,1,0:T(8,128)(2,1)S(1)} %get-tuple-element.97), channel_id=1, source_target_pairs={{0,64},{64,128},{128,192},{192,0},{1,65},{65,129},{129,193},{193,1... | collective-permute-start | bytes 786440 | tf_op jit(solution)/shard_map/ppermute | solution.py:13
  81.7 2.2 %collective-permute-start.27 = (bf16[4,16,2048]{2,1,0:T(8,128)(2,1)S(1)}, bf16[4,16,2048]{2,1,0:T(8,128)(2,1)S(1)}, u32[]{:S(2)}, u32[]{:S(2)}) collective-permute-start(bf16[4,16,2048]{2,1,0:T(8,128)(2,1)S(1)} %get-tuple-element.98), channel_id=1, source_target_pairs={{0,192},{64,0},{128,64},{192,128},{1,193},{65,1},{129,65},{193,129... | collective-permute-start | bytes 786440 | tf_op jit(solution)/shard_map/ppermute | solution.py:13
  86.1 2.2 %collective-permute-start.32 = (bf16[4,16,2048]{2,1,0:T(8,128)(2,1)S(1)}, bf16[4,16,2048]{2,1,0:T(8,128)(2,1)S(1)}, u32[]{:S(2)}, u32[]{:S(2)}) collective-permute-start(bf16[4,16,2048]{2,1,0:T(8,128)(2,1)S(1)} %get-tuple-element.95), channel_id=1, source_target_pairs={{0,192},{64,0},{128,64},{192,128},{1,193},{65,1},{129,65},{193,129... | collective-permute-start | bytes 786440 | tf_op jit(solution)/shard_map/ppermute | solution.py:13
  88.3 4.3 %collective-permute-done.28 = bf16[4,16,2048]{2,1,0:T(8,128)(2,1)S(1)} collective-permute-done((bf16[4,16,2048]{2,1,0:T(8,128)(2,1)S(1)}, bf16[4,16,2048]{2,1,0:T(8,128)(2,1)S(1)}, u32[]{:S(2)}, u32[]{:S(2)}) %collective-permute-start.28) | collective-permute-done | bytes 262176 | tf_op jit(solution)/shard_map/ppermute | solution.py:13
  93.5 2.1 %collective-permute-start.31 = (bf16[4,8,2048]{2,1,0:T(8,128)(2,1)S(1)}, bf16[4,8,2048]{2,1,0:T(8,128)(2,1)S(1)}, u32[]{:S(2)}, u32[]{:S(2)}) collective-permute-start(bf16[4,8,2048]{2,1,0:T(8,128)(2,1)S(1)} %get-tuple-element.107), channel_id=1, source_target_pairs={{0,56},{4,12},{8,0},{12,20},{16,8},{20,28},{24,16},{28,36},{32,24}... | collective-permute-start | bytes 393224 | tf_op jit(solution)/shard_map/ppermute | solution.py:21
  95.6 3.8 %collective-permute-start.30 = (bf16[4,8,2048]{2,1,0:T(8,128)(2,1)S(1)}, bf16[4,8,2048]{2,1,0:T(8,128)(2,1)S(1)}, u32[]{:S(2)}, u32[]{:S(2)}) collective-permute-start(bf16[4,8,2048]{2,1,0:T(8,128)(2,1)S(1)} %get-tuple-element.108), channel_id=1, source_target_pairs={{0,0},{4,20},{8,8},{12,28},{16,16},{20,36},{24,24},{28,44},{32,32}... | collective-permute-start | bytes 393224 | tf_op jit(solution)/shard_map/ppermute | solution.py:21
  99.4 3.0 %collective-permute-done.33 = bf16[4,16,2048]{2,1,0:T(8,128)(2,1)S(1)} collective-permute-done((bf16[4,16,2048]{2,1,0:T(8,128)(2,1)S(1)}, bf16[4,16,2048]{2,1,0:T(8,128)(2,1)S(1)}, u32[]{:S(2)}, u32[]{:S(2)}) %collective-permute-start.33) | collective-permute-done | bytes 262176 | tf_op jit(solution)/shard_map/ppermute | solution.py:13
  103.8 3.8 %collective-permute-start.35 = (bf16[4,8,2048]{2,1,0:T(8,128)(2,1)S(1)}, bf16[4,8,2048]{2,1,0:T(8,128)(2,1)S(1)}, u32[]{:S(2)}, u32[]{:S(2)}) collective-permute-start(bf16[4,8,2048]{2,1,0:T(8,128)(2,1)S(1)} %get-tuple-element.105), channel_id=1, source_target_pairs={{0,48},{4,36},{8,56},{12,44},{16,0},{20,52},{24,8},{28,60},{32,16}... | collective-permute-start | bytes 393224 | tf_op jit(solution)/shard_map/ppermute | solution.py:21
  107.6 2.2 %collective-permute-start.36 = (bf16[4,8,2048]{2,1,0:T(8,128)(2,1)S(1)}, bf16[4,8,2048]{2,1,0:T(8,128)(2,1)S(1)}, u32[]{:S(2)}, u32[]{:S(2)}) collective-permute-start(bf16[4,8,2048]{2,1,0:T(8,128)(2,1)S(1)} %get-tuple-element.106), channel_id=1, source_target_pairs={{0,40},{4,28},{8,48},{12,36},{16,56},{20,44},{24,0},{28,52},{32,8}... | collective-permute-start | bytes 393224 | tf_op jit(solution)/shard_map/ppermute | solution.py:21
  109.8 3.3 %collective-permute-done.35 = bf16[4,8,2048]{2,1,0:T(8,128)(2,1)S(1)} collective-permute-done((bf16[4,8,2048]{2,1,0:T(8,128)(2,1)S(1)}, bf16[4,8,2048]{2,1,0:T(8,128)(2,1)S(1)}, u32[]{:S(2)}, u32[]{:S(2)}) %collective-permute-start.35) | collective-permute-done | bytes 131104 | tf_op jit(solution)/shard_map/ppermute | solution.py:21
  113.0 3.2 %collective-permute-done.36 = bf16[4,8,2048]{2,1,0:T(8,128)(2,1)S(1)} collective-permute-done((bf16[4,8,2048]{2,1,0:T(8,128)(2,1)S(1)}, bf16[4,8,2048]{2,1,0:T(8,128)(2,1)S(1)}, u32[]{:S(2)}, u32[]{:S(2)}) %collective-permute-start.36) | collective-permute-done | bytes 131104 | tf_op jit(solution)/shard_map/ppermute | solution.py:21
  116.4 2.3 %collective-permute-start.37 = (bf16[4,4,2048]{2,1,0:T(4,128)(2,1)S(1)}, bf16[4,4,2048]{2,1,0:T(4,128)(2,1)S(1)}, u32[]{:S(2)}, u32[]{:S(2)}) collective-permute-start(bf16[4,4,2048]{2,1,0:T(4,128)(2,1)S(1)} %select_convert_fusion), channel_id=1, source_target_pairs={{0,4},{4,0},{1,5},{5,1},{2,6},{6,2},{3,7},{7,3},{8,12},{12,8},{9,1... | collective-permute-start | bytes 196616 | tf_op jit(solution)/shard_map/ppermute | solution.py:13
  119.7 2.2 %collective-permute-start.40 = (f32[4,2048]{1,0:T(4,128)S(1)}, f32[4,2048]{1,0:T(4,128)S(1)}, u32[]{:S(2)}, u32[]{:S(2)}) collective-permute-start(f32[4,2048]{1,0:T(4,128)S(1)} %get-tuple-element.113), channel_id=1, source_target_pairs={{0,1},{1,2},{2,3},{3,0},{4,5},{5,6},{6,7},{7,4},{8,9},{9,10},{10,1... | collective-permute-start | bytes 98312 | tf_op jit(solution)/shard_map/ppermute | solution.py:13
  121.8 1.9 %collective-permute-start.39 = (f32[4,2048]{1,0:T(4,128)S(1)}, f32[4,2048]{1,0:T(4,128)S(1)}, u32[]{:S(2)}, u32[]{:S(2)}) collective-permute-start(f32[4,2048]{1,0:T(4,128)S(1)} %get-tuple-element.114), channel_id=1, source_target_pairs={{0,2},{1,3},{2,0},{3,1},{4,6},{5,7},{6,4},{7,5},{8,10},{9,11},{10,... | collective-permute-start | bytes 98312 | tf_op jit(solution)/shard_map/ppermute | solution.py:13
  124.3 1.8 %collective-permute-done.39 = f32[4,2048]{1,0:T(4,128)S(1)} collective-permute-done((f32[4,2048]{1,0:T(4,128)S(1)}, f32[4,2048]{1,0:T(4,128)S(1)}, u32[]{:S(2)}, u32[]{:S(2)}) %collective-permute-start.39) | collective-permute-done | bytes 32800 | tf_op jit(solution)/shard_map/ppermute | solution.py:13
  (97 shorter events, 32.8 us)
Async XLA Ops:
  0.0 32.2 %collective-permute-start = (bf16[448,2048]{1,0:T(8,128)(2,1)}, bf16[448,2048]{1,0:T(8,128)(2,1)S(1)}, u32[]{:S(2)}, u32[]{:S(2)}) collective-permute-start(bf16[448,2048]{1,0:T(8,128)(2,1)} %bitcast.46), channel_id=1, source_target_pairs={{0,4},{4,0},{1,5},{5,1},{2,6},{6,2},{3,7},{7,3},{8,12},{12,8},{9,1... | collective-permute-start | bytes 5505032 | tf_op jit(solution)/shard_map/ppermute | solution.py:13
  3.2 31.6 %collective-permute-start.1 = (bf16[448,2048]{1,0:T(8,128)(2,1)}, bf16[448,2048]{1,0:T(8,128)(2,1)}, u32[]{:S(2)}, u32[]{:S(2)}) collective-permute-start(bf16[448,2048]{1,0:T(8,128)(2,1)} %bitcast.44), channel_id=1, source_target_pairs={{0,4},{4,0},{1,5},{5,1},{2,6},{6,2},{3,7},{7,3},{8,12},{12,8},{9,1... | collective-permute-start | bytes 5505032 | tf_op jit(solution)/shard_map/ppermute | solution.py:13
  15.1 11.2 %collective-permute-start.5 = (bf16[4,8,2048]{2,1,0:T(8,128)(2,1)S(1)}, bf16[4,8,2048]{2,1,0:T(8,128)(2,1)S(1)}, u32[]{:S(2)}, u32[]{:S(2)}) collective-permute-start(bf16[4,8,2048]{2,1,0:T(8,128)(2,1)S(1)} %copy.11), channel_id=1, source_target_pairs={{0,0},{4,52},{8,8},{12,60},{16,16},{20,4},{24,24},{28,12},{32,32},... | collective-permute-start | bytes 393224 | tf_op jit(solution)/shard_map/ppermute | solution.py:21
  27.7 14.2 %collective-permute-start.11 = (bf16[4,16,2048]{2,1,0:T(8,128)(2,1)S(1)}, bf16[4,16,2048]{2,1,0:T(8,128)(2,1)S(1)}, u32[]{:S(2)}, u32[]{:S(2)}) collective-permute-start(bf16[4,16,2048]{2,1,0:T(8,128)(2,1)S(1)} %constant_dynamic-update-slice_fusion), channel_id=1, source_target_pairs={{0,128},{64,192},{128,0},{192,64},{1,129},{65,193},{129,1},{193,65... | collective-permute-start | bytes 786440 | tf_op jit(solution)/shard_map/ppermute | solution.py:13
  30.7 13.3 %collective-permute-start.10 = (bf16[4,16,2048]{2,1,0:T(8,128)(2,1)S(1)}, bf16[4,16,2048]{2,1,0:T(8,128)(2,1)S(1)}, u32[]{:S(2)}, u32[]{:S(2)}) collective-permute-start(bf16[4,16,2048]{2,1,0:T(8,128)(2,1)S(1)} %constant_dynamic-update-slice_fusion), channel_id=1, source_target_pairs={{0,192},{64,0},{128,64},{192,128},{1,193},{65,1},{129,65},{193,129... | collective-permute-start | bytes 786440 | tf_op jit(solution)/shard_map/ppermute | solution.py:13
  31.5 12.7 %collective-permute-start.9 = (bf16[4,16,2048]{2,1,0:T(8,128)(2,1)S(1)}, bf16[4,16,2048]{2,1,0:T(8,128)(2,1)S(1)}, u32[]{:S(2)}, u32[]{:S(2)}) collective-permute-start(bf16[4,16,2048]{2,1,0:T(8,128)(2,1)S(1)} %constant_dynamic-update-slice_fusion), channel_id=1, source_target_pairs={{0,64},{64,128},{128,192},{192,0},{1,65},{65,129},{129,193},{193,1... | collective-permute-start | bytes 786440 | tf_op jit(solution)/shard_map/ppermute | solution.py:13
  32.2 9.0 %collective-permute-start.8 = (bf16[4,16,2048]{2,1,0:T(8,128)(2,1)S(1)}, bf16[4,16,2048]{2,1,0:T(8,128)(2,1)S(1)}, u32[]{:S(2)}, u32[]{:S(2)}) collective-permute-start(bf16[4,16,2048]{2,1,0:T(8,128)(2,1)S(1)} %constant_dynamic-update-slice_fusion), channel_id=1, source_target_pairs={{0,16},{4,52},{8,24},{12,60},{16,32},{20,4},{24,40},{28,12},{32,48... | collective-permute-start | bytes 786440 | tf_op jit(solution)/shard_map/ppermute | solution.py:21
  34.9 11.8 %collective-permute-start.7 = (bf16[448,2048]{1,0:T(8,128)(2,1)}, bf16[448,2048]{1,0:T(8,128)(2,1)S(1)}, u32[]{:S(2)}, u32[]{:S(2)}) collective-permute-start(bf16[448,2048]{1,0:T(8,128)(2,1)} %param.9), channel_id=1, source_target_pairs={{0,4},{4,0},{1,5},{5,1},{2,6},{6,2},{3,7},{7,3},{8,12},{12,8},{9,1... | collective-permute-start | bytes 5505032 | tf_op jit(solution)/shard_map/ppermute | solution.py:13
  41.2 9.0 %collective-permute-start.14 = (bf16[4,16,2048]{2,1,0:T(8,128)(2,1)S(1)}, bf16[4,16,2048]{2,1,0:T(8,128)(2,1)S(1)}, u32[]{:S(2)}, u32[]{:S(2)}) collective-permute-start(bf16[4,16,2048]{2,1,0:T(8,128)(2,1)S(1)} %collective-permute-done.8), channel_id=1, source_target_pairs={{0,128},{64,192},{128,0},{192,64},{1,129},{65,193},{129,1},{193,65... | collective-permute-start | bytes 786440 | tf_op jit(solution)/shard_map/ppermute | solution.py:13
  41.9 13.9 %collective-permute-start.13 = (bf16[4,16,2048]{2,1,0:T(8,128)(2,1)S(1)}, bf16[4,16,2048]{2,1,0:T(8,128)(2,1)S(1)}, u32[]{:S(2)}, u32[]{:S(2)}) collective-permute-start(bf16[4,16,2048]{2,1,0:T(8,128)(2,1)S(1)} %collective-permute-done.8), channel_id=1, source_target_pairs={{0,192},{64,0},{128,64},{192,128},{1,193},{65,1},{129,65},{193,129... | collective-permute-start | bytes 786440 | tf_op jit(solution)/shard_map/ppermute | solution.py:13
  44.0 12.6 %collective-permute-start.12 = (bf16[4,16,2048]{2,1,0:T(8,128)(2,1)S(1)}, bf16[4,16,2048]{2,1,0:T(8,128)(2,1)S(1)}, u32[]{:S(2)}, u32[]{:S(2)}) collective-permute-start(bf16[4,16,2048]{2,1,0:T(8,128)(2,1)S(1)} %collective-permute-done.8), channel_id=1, source_target_pairs={{0,64},{64,128},{128,192},{192,0},{1,65},{65,129},{129,193},{193,1... | collective-permute-start | bytes 786440 | tf_op jit(solution)/shard_map/ppermute | solution.py:13
  46.5 13.9 %collective-permute-start.17 = (bf16[64,1792]{1,0:T(8,128)(2,1)S(1)}, bf16[64,1792]{1,0:T(8,128)(2,1)S(1)}, u32[]{:S(2)}, u32[]{:S(2)}) collective-permute-start(bf16[64,1792]{1,0:T(8,128)(2,1)S(1)} %get-tuple-element.102), channel_id=1, source_target_pairs={{0,3},{1,0},{2,1},{3,2},{4,7},{5,4},{6,5},{7,6},{8,11},{9,8},{10,9... | collective-permute-start | bytes 688136 | tf_op jit(solution)/shard_map/ppermute | solution.py:13
  46.7 13.9 %collective-permute-start.16 = (bf16[64,1792]{1,0:T(8,128)(2,1)S(1)}, bf16[64,1792]{1,0:T(8,128)(2,1)S(1)}, u32[]{:S(2)}, u32[]{:S(2)}) collective-permute-start(bf16[64,1792]{1,0:T(8,128)(2,1)S(1)} %get-tuple-element.103), channel_id=1, source_target_pairs={{0,1},{1,2},{2,3},{3,0},{4,5},{5,6},{6,7},{7,4},{8,9},{9,10},{10,1... | collective-permute-start | bytes 688136 | tf_op jit(solution)/shard_map/ppermute | solution.py:13
  50.3 10.3 %collective-permute-start.15 = (bf16[64,1792]{1,0:T(8,128)(2,1)S(1)}, bf16[64,1792]{1,0:T(8,128)(2,1)S(1)}, u32[]{:S(2)}, u32[]{:S(2)}) collective-permute-start(bf16[64,1792]{1,0:T(8,128)(2,1)S(1)} %get-tuple-element.104), channel_id=1, source_target_pairs={{0,2},{1,3},{2,0},{3,1},{4,6},{5,7},{6,4},{7,5},{8,10},{9,11},{10,... | collective-permute-start | bytes 688136 | tf_op jit(solution)/shard_map/ppermute | solution.py:13
  59.0 11.9 %collective-permute-start.19 = (bf16[64,1792]{1,0:T(8,128)(2,1)S(1)}, bf16[64,1792]{1,0:T(8,128)(2,1)S(1)}, u32[]{:S(2)}, u32[]{:S(2)}) collective-permute-start(bf16[64,1792]{1,0:T(8,128)(2,1)S(1)} %get-tuple-element.100), channel_id=1, source_target_pairs={{0,1},{1,2},{2,3},{3,0},{4,5},{5,6},{6,7},{7,4},{8,9},{9,10},{10,1... | collective-permute-start | bytes 688136 | tf_op jit(solution)/shard_map/ppermute | solution.py:13
  60.4 10.4 %collective-permute-start.18 = (bf16[64,1792]{1,0:T(8,128)(2,1)S(1)}, bf16[64,1792]{1,0:T(8,128)(2,1)S(1)}, u32[]{:S(2)}, u32[]{:S(2)}) collective-permute-start(bf16[64,1792]{1,0:T(8,128)(2,1)S(1)} %get-tuple-element.101), channel_id=1, source_target_pairs={{0,2},{1,3},{2,0},{3,1},{4,6},{5,7},{6,4},{7,5},{8,10},{9,11},{10,... | collective-permute-start | bytes 688136 | tf_op jit(solution)/shard_map/ppermute | solution.py:13
  60.8 15.5 %collective-permute-start.23 = (bf16[64,896]{1,0:T(8,128)(2,1)S(1)}, bf16[64,896]{1,0:T(8,128)(2,1)S(1)}, u32[]{:S(2)}, u32[]{:S(2)}) collective-permute-start(bf16[64,896]{1,0:T(8,128)(2,1)S(1)} %fusion.17), channel_id=1, source_target_pairs={{0,1},{1,2},{2,3},{3,0},{4,5},{5,6},{6,7},{7,4},{8,9},{9,10},{10,1... | collective-permute-start | bytes 344072 | tf_op jit(solution)/shard_map/ppermute | solution.py:13
  62.7 13.6 %collective-permute-start.22 = (bf16[64,896]{1,0:T(8,128)(2,1)S(1)}, bf16[64,896]{1,0:T(8,128)(2,1)S(1)}, u32[]{:S(2)}, u32[]{:S(2)}) collective-permute-start(bf16[64,896]{1,0:T(8,128)(2,1)S(1)} %fusion.17), channel_id=1, source_target_pairs={{0,2},{1,3},{2,0},{3,1},{4,6},{5,7},{6,4},{7,5},{8,10},{9,11},{10,... | collective-permute-start | bytes 344072 | tf_op jit(solution)/shard_map/ppermute | solution.py:13
  65.6 10.7 %collective-permute-start.21 = (bf16[64,896]{1,0:T(8,128)(2,1)S(1)}, bf16[64,896]{1,0:T(8,128)(2,1)S(1)}, u32[]{:S(2)}, u32[]{:S(2)}) collective-permute-start(bf16[64,896]{1,0:T(8,128)(2,1)S(1)} %fusion.17), channel_id=1, source_target_pairs={{0,3},{1,0},{2,1},{3,2},{4,7},{5,4},{6,5},{7,6},{8,11},{9,8},{10,9... | collective-permute-start | bytes 344072 | tf_op jit(solution)/shard_map/ppermute | solution.py:13
  71.1 10.6 %collective-permute-start.26 = (bf16[64,896]{1,0:T(8,128)(2,1)S(1)}, bf16[64,896]{1,0:T(8,128)(2,1)S(1)}, u32[]{:S(2)}, u32[]{:S(2)}) collective-permute-start(bf16[64,896]{1,0:T(8,128)(2,1)S(1)} %fusion.16), channel_id=1, source_target_pairs={{0,1},{1,2},{2,3},{3,0},{4,5},{5,6},{6,7},{7,4},{8,9},{9,10},{10,1... | collective-permute-start | bytes 344072 | tf_op jit(solution)/shard_map/ppermute | solution.py:13
  71.1 12.7 %collective-permute-start.25 = (bf16[64,896]{1,0:T(8,128)(2,1)S(1)}, bf16[64,896]{1,0:T(8,128)(2,1)S(1)}, u32[]{:S(2)}, u32[]{:S(2)}) collective-permute-start(bf16[64,896]{1,0:T(8,128)(2,1)S(1)} %fusion.16), channel_id=1, source_target_pairs={{0,2},{1,3},{2,0},{3,1},{4,6},{5,7},{6,4},{7,5},{8,10},{9,11},{10,... | collective-permute-start | bytes 344072 | tf_op jit(solution)/shard_map/ppermute | solution.py:13
  76.3 7.6 %collective-permute-start.24 = (bf16[64,896]{1,0:T(8,128)(2,1)S(1)}, bf16[64,896]{1,0:T(8,128)(2,1)S(1)}, u32[]{:S(2)}, u32[]{:S(2)}) collective-permute-start(bf16[64,896]{1,0:T(8,128)(2,1)S(1)} %fusion.16), channel_id=1, source_target_pairs={{0,3},{1,0},{2,1},{3,2},{4,7},{5,4},{6,5},{7,6},{8,11},{9,8},{10,9... | collective-permute-start | bytes 344072 | tf_op jit(solution)/shard_map/ppermute | solution.py:13
  77.9 8.2 %collective-permute-start.29 = (bf16[4,16,2048]{2,1,0:T(8,128)(2,1)S(1)}, bf16[4,16,2048]{2,1,0:T(8,128)(2,1)S(1)}, u32[]{:S(2)}, u32[]{:S(2)}) collective-permute-start(bf16[4,16,2048]{2,1,0:T(8,128)(2,1)S(1)} %get-tuple-element.96), channel_id=1, source_target_pairs={{0,128},{64,192},{128,0},{192,64},{1,129},{65,193},{129,1},{193,65... | collective-permute-start | bytes 786440 | tf_op jit(solution)/shard_map/ppermute | solution.py:13
  78.3 14.2 %collective-permute-start.28 = (bf16[4,16,2048]{2,1,0:T(8,128)(2,1)S(1)}, bf16[4,16,2048]{2,1,0:T(8,128)(2,1)S(1)}, u32[]{:S(2)}, u32[]{:S(2)}) collective-permute-start(bf16[4,16,2048]{2,1,0:T(8,128)(2,1)S(1)} %get-tuple-element.97), channel_id=1, source_target_pairs={{0,64},{64,128},{128,192},{192,0},{1,65},{65,129},{129,193},{193,1... | collective-permute-start | bytes 786440 | tf_op jit(solution)/shard_map/ppermute | solution.py:13
  81.7 11.7 %collective-permute-start.27 = (bf16[4,16,2048]{2,1,0:T(8,128)(2,1)S(1)}, bf16[4,16,2048]{2,1,0:T(8,128)(2,1)S(1)}, u32[]{:S(2)}, u32[]{:S(2)}) collective-permute-start(bf16[4,16,2048]{2,1,0:T(8,128)(2,1)S(1)} %get-tuple-element.98), channel_id=1, source_target_pairs={{0,192},{64,0},{128,64},{192,128},{1,193},{65,1},{129,65},{193,129... | collective-permute-start | bytes 786440 | tf_op jit(solution)/shard_map/ppermute | solution.py:13
  85.4 14.0 %collective-permute-start.34 = (bf16[4,16,2048]{2,1,0:T(8,128)(2,1)S(1)}, bf16[4,16,2048]{2,1,0:T(8,128)(2,1)S(1)}, u32[]{:S(2)}, u32[]{:S(2)}) collective-permute-start(bf16[4,16,2048]{2,1,0:T(8,128)(2,1)S(1)} %get-tuple-element.93), channel_id=1, source_target_pairs={{0,128},{64,192},{128,0},{192,64},{1,129},{65,193},{129,1},{193,65... | collective-permute-start | bytes 786440 | tf_op jit(solution)/shard_map/ppermute | solution.py:13
  85.5 16.9 %collective-permute-start.33 = (bf16[4,16,2048]{2,1,0:T(8,128)(2,1)S(1)}, bf16[4,16,2048]{2,1,0:T(8,128)(2,1)S(1)}, u32[]{:S(2)}, u32[]{:S(2)}) collective-permute-start(bf16[4,16,2048]{2,1,0:T(8,128)(2,1)S(1)} %get-tuple-element.94), channel_id=1, source_target_pairs={{0,64},{64,128},{128,192},{192,0},{1,65},{65,129},{129,193},{193,1... | collective-permute-start | bytes 786440 | tf_op jit(solution)/shard_map/ppermute | solution.py:13
  86.1 16.3 %collective-permute-start.32 = (bf16[4,16,2048]{2,1,0:T(8,128)(2,1)S(1)}, bf16[4,16,2048]{2,1,0:T(8,128)(2,1)S(1)}, u32[]{:S(2)}, u32[]{:S(2)}) collective-permute-start(bf16[4,16,2048]{2,1,0:T(8,128)(2,1)S(1)} %get-tuple-element.95), channel_id=1, source_target_pairs={{0,192},{64,0},{128,64},{192,128},{1,193},{65,1},{129,65},{193,129... | collective-permute-start | bytes 786440 | tf_op jit(solution)/shard_map/ppermute | solution.py:13
  93.5 8.9 %collective-permute-start.31 = (bf16[4,8,2048]{2,1,0:T(8,128)(2,1)S(1)}, bf16[4,8,2048]{2,1,0:T(8,128)(2,1)S(1)}, u32[]{:S(2)}, u32[]{:S(2)}) collective-permute-start(bf16[4,8,2048]{2,1,0:T(8,128)(2,1)S(1)} %get-tuple-element.107), channel_id=1, source_target_pairs={{0,56},{4,12},{8,0},{12,20},{16,8},{20,28},{24,16},{28,36},{32,24}... | collective-permute-start | bytes 393224 | tf_op jit(solution)/shard_map/ppermute | solution.py:21
  95.6 8.0 %collective-permute-start.30 = (bf16[4,8,2048]{2,1,0:T(8,128)(2,1)S(1)}, bf16[4,8,2048]{2,1,0:T(8,128)(2,1)S(1)}, u32[]{:S(2)}, u32[]{:S(2)}) collective-permute-start(bf16[4,8,2048]{2,1,0:T(8,128)(2,1)S(1)} %get-tuple-element.108), channel_id=1, source_target_pairs={{0,0},{4,20},{8,8},{12,28},{16,16},{20,36},{24,24},{28,44},{32,32}... | collective-permute-start | bytes 393224 | tf_op jit(solution)/shard_map/ppermute | solution.py:21
  103.8 9.3 %collective-permute-start.35 = (bf16[4,8,2048]{2,1,0:T(8,128)(2,1)S(1)}, bf16[4,8,2048]{2,1,0:T(8,128)(2,1)S(1)}, u32[]{:S(2)}, u32[]{:S(2)}) collective-permute-start(bf16[4,8,2048]{2,1,0:T(8,128)(2,1)S(1)} %get-tuple-element.105), channel_id=1, source_target_pairs={{0,48},{4,36},{8,56},{12,44},{16,0},{20,52},{24,8},{28,60},{32,16}... | collective-permute-start | bytes 393224 | tf_op jit(solution)/shard_map/ppermute | solution.py:21
  107.6 8.7 %collective-permute-start.36 = (bf16[4,8,2048]{2,1,0:T(8,128)(2,1)S(1)}, bf16[4,8,2048]{2,1,0:T(8,128)(2,1)S(1)}, u32[]{:S(2)}, u32[]{:S(2)}) collective-permute-start(bf16[4,8,2048]{2,1,0:T(8,128)(2,1)S(1)} %get-tuple-element.106), channel_id=1, source_target_pairs={{0,40},{4,28},{8,48},{12,36},{16,56},{20,44},{24,0},{28,52},{32,8}... | collective-permute-start | bytes 393224 | tf_op jit(solution)/shard_map/ppermute | solution.py:21
  (11 other events, 72.8 us)

commit v10 on v9

--- a/solution.py
+++ b/solution.py
@@ -105,18 +105,15 @@
     far_kept, *near_sums = together(far_partial[0], *near_sums)
     near_hidden = activate(near_kept, near_sums)
     near_spread = spread(near_hidden)
+    near_down = by_y(down(second, [near_hidden] + near_spread))
+    near_back = back_over_y(near_down)
 
-    near_hidden, *far_sums = together(near_hidden, *far_sums)
+    near_down[0], *far_sums = together(near_down[0], *far_sums)
     far_hidden = activate(far_kept, far_sums)
     far_spread = spread(far_hidden)
-    far_hidden, *near_spread = together(far_hidden, *near_spread)
-
-    near_down = by_y(down(second, [near_hidden] + near_spread))
-    near_back = back_over_y(near_down)
-    near_down[0], *far_spread = together(near_down[0], *far_spread)
+    far_hidden, *near_back = together(far_hidden, *near_back)
     far_down = by_y(down(second, [far_hidden] + far_spread))
     far_back = back_over_y(far_down)
-    far_down[0], *near_back = together(far_down[0], *near_back)
 
     near_total = sum_over_y(near_down, near_back)
     half = 2 * rows
@@ -126,11 +123,11 @@
     ]
     *near_pieces, back_1, back_3, back_2 = together(*near_pieces, *far_back)
     far_total = sum_over_y(far_down, (back_1, back_3, back_2))
-    far_pieces = [
-        along_z(far_total[:, :half].astype(BF16), -2, 4),
-        along_z(far_total[:, half:].astype(BF16), -3, 3),
-    ]
-    pair = sum(piece.astype(F32) for piece in near_pieces + far_pieces)
+    low, high = far_total[:, :half], far_total[:, half:]
+    passing = along_z(jnp.where(core == 0, high, low).astype(BF16), -1, 1).astype(F32)
+    joined = jnp.where(core == 0, low, high) + passing
+    far_piece = along_z(joined.astype(BF16), -2, 3)
+    pair = sum(piece.astype(F32) for piece in near_pieces + [far_piece])
     low, high = pair[:, :rows], pair[:, rows:]
     mine = jnp.where(core == 0, low, high)
     other = jnp.where(core == 0, high, low).astype(BF16)

time: 128 us -> 130 us (1.016)
  starting transfers between devices: 63.2 us -> 59.1 us
  waiting for transfers between devices: 44.7 us -> 48.6 us
  local copies, waits for them, and re-layouts: 0.59 us -> 1.94 us
    ppermute x7, waiting for transfers between devices: 14.3 us -> 27.3 us  [along_z(): return lax.ppermute(value, ('z', 'c'), pairs)]
    ppermute x34, waiting for transfers between devices: 30.4 us -> 21.3 us  [shift(): return lax.ppermute(value, axis, [(i, (i + step) % n) for i in range(n)])]
    ppermute x34, starting transfers between devices: 39.9 us -> 37.6 us  [shift(): return lax.ppermute(value, axis, [(i, (i + step) % n) for i in range(n)])]
    ppermute x7, starting transfers between devices: 23.3 us -> 21.6 us  [along_z(): return lax.ppermute(value, ('z', 'c'), pairs)]
  transfers between devices with their start and end apart: 41 -> 41, of which waited for: 21 -> 21; matrix products, arithmetic and copies ran while one was open for 11% -> 10% of each run, Pallas kernels for 0% -> 0%
where the time goes in v10:
time: 130 us
  starting transfers between devices  59.1 us (45%)
  waiting for transfers between devices  48.6 us (37%)
  other arithmetic  9.18 us (7%)
  matrix products  6.78 us (5%)
  blocking collectives  3.76 us (3%)
  local copies, waits for them, and re-layouts  1.94 us (1%)
    ppermute x34, starting transfers between devices, shift(): return lax.ppermute(value, axis, [(i, (i + step) % n) for i in range(n)])  37.6 us
    ppermute x7, waiting for transfers between devices, along_z(): return lax.ppermute(value, ('z', 'c'), pairs)  27.3 us
    ppermute x7, starting transfers between devices, along_z(): return lax.ppermute(value, ('z', 'c'), pairs)  21.6 us
    ppermute x34, waiting for transfers between devices, shift(): return lax.ppermute(value, axis, [(i, (i + step) % n) for i in range(n)])  21.3 us
    dot_general x2, matrix products, project(): lax.dot_general(block.reshape(-1, part), weights, (((1,), (1,)), ((), ())...  4.23 us
    all_gather x1, blocking collectives, local(): pair = lax.all_gather(own, 'c', axis=1, tiled=True)  3.76 us
    concatenate x1, other arithmetic, local(): first, far = together(jnp.concatenate(first, axis=0), far)  3.61 us
  transfers between devices with their start and end apart: 41, of which 21 were waited for; matrix products, arithmetic and copies ran while one was open for 10% of the time, Pallas kernels for 0%

profile of v10, /device:TPU:1, one launch (start us, length us, event | category | flops | bytes accessed | tf_op | source)
XLA Modules:
  0.0 129.8 jit_solution(2292979415006324751)
XLA Ops:
  0.0 3.2 %collective-permute-start = (bf16[448,2048]{1,0:T(8,128)(2,1)}, bf16[448,2048]{1,0:T(8,128)(2,1)S(1)}, u32[]{:S(2)}, u32[]{:S(2)}) collective-permute-start(bf16[448,2048]{1,0:T(8,128)(2,1)} %bitcast.46), channel_id=1, source_target_pairs={{0,4},{4,0},{1,5},{5,1},{2,6},{6,2},{3,7},{7,3},{8,12},{12,8},{9,1... | collective-permute-start | bytes 5505032 | tf_op jit(solution)/shard_map/ppermute | solution.py:13
  7.9 1.6 %collective-permute-done.3 = bf16[4,2048]{1,0:T(4,128)(2,1)S(1)} collective-permute-done((bf16[4,2048]{1,0:T(4,128)(2,1)S(1)}, bf16[4,2048]{1,0:T(4,128)(2,1)S(1)}, u32[]{:S(2)}, u32[]{:S(2)}) %collective-permute-start.3) | collective-permute-done | bytes 16416 | tf_op jit(solution)/shard_map/ppermute | solution.py:13
  9.6 1.6 %collective-permute-done.4 = bf16[4,2048]{1,0:T(4,128)(2,1)S(1)} collective-permute-done((bf16[4,2048]{1,0:T(4,128)(2,1)S(1)}, bf16[4,2048]{1,0:T(4,128)(2,1)S(1)}, u32[]{:S(2)}, u32[]{:S(2)}) %collective-permute-start.4) | collective-permute-done | bytes 16416 | tf_op jit(solution)/shard_map/ppermute | solution.py:13
  11.2 3.8 %all_gather.3 = bf16[4,8,2048]{2,0,1:T(4,128)(2,1)S(1)} all-gather(bf16[4,4,2048]{2,0,1:T(4,128)(2,1)S(1)} %copy.10), channel_id=1, replica_groups=mesh['y'=4,'z'=8,'c'=2,'x'=4] {'c'}, dimensions={1}, use_global_device_ids=true | all-gather | bytes 196608 | tf_op jit(solution)/shard_map/all_gather | solution.py:49
  15.1 7.9 %collective-permute-start.5 = (bf16[4,8,2048]{2,1,0:T(8,128)(2,1)S(1)}, bf16[4,8,2048]{2,1,0:T(8,128)(2,1)S(1)}, u32[]{:S(2)}, u32[]{:S(2)}) collective-permute-start(bf16[4,8,2048]{2,1,0:T(8,128)(2,1)S(1)} %copy.11), channel_id=1, source_target_pairs={{0,0},{4,52},{8,8},{12,60},{16,16},{20,4},{24,24},{28,12},{32,32},... | collective-permute-start | bytes 393224 | tf_op jit(solution)/shard_map/ppermute | solution.py:21
  23.8 2.5 %collective-permute-done.5 = bf16[4,8,2048]{2,1,0:T(8,128)(2,1)S(1)} collective-permute-done((bf16[4,8,2048]{2,1,0:T(8,128)(2,1)S(1)}, bf16[4,8,2048]{2,1,0:T(8,128)(2,1)S(1)}, u32[]{:S(2)}, u32[]{:S(2)}) %collective-permute-start.5) | collective-permute-done | bytes 131104 | tf_op jit(solution)/shard_map/ppermute | solution.py:21
  26.3 1.4 %collective-permute-done.6 = bf16[4,8,2048]{2,1,0:T(8,128)(2,1)S(1)} collective-permute-done((bf16[4,8,2048]{2,1,0:T(8,128)(2,1)S(1)}, bf16[4,8,2048]{2,1,0:T(8,128)(2,1)S(1)}, u32[]{:S(2)}, u32[]{:S(2)}) %collective-permute-start.6) | collective-permute-done | bytes 131104 | tf_op jit(solution)/shard_map/ppermute | solution.py:21
  27.7 3.0 %collective-permute-start.11 = (bf16[4,16,2048]{2,1,0:T(8,128)(2,1)S(1)}, bf16[4,16,2048]{2,1,0:T(8,128)(2,1)S(1)}, u32[]{:S(2)}, u32[]{:S(2)}) collective-permute-start(bf16[4,16,2048]{2,1,0:T(8,128)(2,1)S(1)} %constant_dynamic-update-slice_fusion), channel_id=1, source_target_pairs={{0,128},{64,192},{128,0},{192,64},{1,129},{65,193},{129,1},{193,65... | collective-permute-start | bytes 786440 | tf_op jit(solution)/shard_map/ppermute | solution.py:13
  32.2 2.6 %collective-permute-start.8 = (bf16[4,16,2048]{2,1,0:T(8,128)(2,1)S(1)}, bf16[4,16,2048]{2,1,0:T(8,128)(2,1)S(1)}, u32[]{:S(2)}, u32[]{:S(2)}) collective-permute-start(bf16[4,16,2048]{2,1,0:T(8,128)(2,1)S(1)} %constant_dynamic-update-slice_fusion), channel_id=1, source_target_pairs={{0,16},{4,52},{8,24},{12,60},{16,32},{20,4},{24,40},{28,12},{32,48... | collective-permute-start | bytes 786440 | tf_op jit(solution)/shard_map/ppermute | solution.py:21
  34.9 3.6 %pad_maximum_fusion = bf16[1792,2048]{1,0:T(8,128)(2,1)S(1)} fusion(bf16[448,2048]{1,0:T(8,128)(2,1)} %collective-permute-done.1, bf16[448,2048]{1,0:T(8,128)(2,1)} %bitcast.45, bf16[448,2048]{1,0:T(8,128)(2,1)S(1)} %collective-permute-done, bf16[448,2048]{1,0:T(8,128)(2,1)} %bitcast.47), kind=kLoop, calls=%fused_computation | loop fusion | flops 29360128 | bytes 14680064 | tf_op jit(solution)/shard_map/concatenate | solution.py:93
  38.5 2.7 %collective-permute-done.8 = bf16[4,16,2048]{2,1,0:T(8,128)(2,1)S(1)} collective-permute-done((bf16[4,16,2048]{2,1,0:T(8,128)(2,1)S(1)}, bf16[4,16,2048]{2,1,0:T(8,128)(2,1)S(1)}, u32[]{:S(2)}, u32[]{:S(2)}) %collective-permute-start.8) | collective-permute-done | bytes 262176 | tf_op jit(solution)/shard_map/ppermute | solution.py:21
  41.9 2.1 %collective-permute-start.13 = (bf16[4,16,2048]{2,1,0:T(8,128)(2,1)S(1)}, bf16[4,16,2048]{2,1,0:T(8,128)(2,1)S(1)}, u32[]{:S(2)}, u32[]{:S(2)}) collective-permute-start(bf16[4,16,2048]{2,1,0:T(8,128)(2,1)S(1)} %collective-permute-done.8), channel_id=1, source_target_pairs={{0,192},{64,0},{128,64},{192,128},{1,193},{65,1},{129,65},{193,129... | collective-permute-start | bytes 786440 | tf_op jit(solution)/shard_map/ppermute | solution.py:13
  44.3 2.1 %fusion.33 = (bf16[256,1792]{1,0:T(8,128)(2,1)S(1)}, f32[256,1792]{1,0:T(8,128)S(1)}) fusion(bf16[256,2048]{1,0:T(8,128)(2,1)S(1)} %bitcast.49, bf16[1792,2048]{1,0:T(8,128)(2,1)S(1)} %pad_maximum_fusion), kind=kOutput, calls=%fused_computation.68 | convolution fusion | flops 1879506944 | bytes 11141120 | tf_op jit(solution)/shard_map/dot_general | solution.py:54
  46.7 1.5 %collective-permute-start.16 = (bf16[64,1792]{1,0:T(8,128)(2,1)S(1)}, bf16[64,1792]{1,0:T(8,128)(2,1)S(1)}, u32[]{:S(2)}, u32[]{:S(2)}) collective-permute-start(bf16[64,1792]{1,0:T(8,128)(2,1)S(1)} %get-tuple-element.87), channel_id=1, source_target_pairs={{0,1},{1,2},{2,3},{3,0},{4,5},{5,6},{6,7},{7,4},{8,9},{9,10},{10,1... | collective-permute-start | bytes 688136 | tf_op jit(solution)/shard_map/ppermute | solution.py:13
  48.7 1.6 %collective-permute-done.14 = bf16[4,16,2048]{2,1,0:T(8,128)(2,1)S(1)} collective-permute-done((bf16[4,16,2048]{2,1,0:T(8,128)(2,1)S(1)}, bf16[4,16,2048]{2,1,0:T(8,128)(2,1)S(1)}, u32[]{:S(2)}, u32[]{:S(2)}) %collective-permute-start.14) | collective-permute-done | bytes 262176 | tf_op jit(solution)/shard_map/ppermute | solution.py:13
  50.3 5.6 %collective-permute-done.13 = bf16[4,16,2048]{2,1,0:T(8,128)(2,1)S(1)} collective-permute-done((bf16[4,16,2048]{2,1,0:T(8,128)(2,1)S(1)}, bf16[4,16,2048]{2,1,0:T(8,128)(2,1)S(1)}, u32[]{:S(2)}, u32[]{:S(2)}) %collective-permute-start.13) | collective-permute-done | bytes 262176 | tf_op jit(solution)/shard_map/ppermute | solution.py:13
  56.7 2.1 %fusion.34 = (bf16[256,1792]{1,0:T(8,128)(2,1)S(1)}, f32[256,1792]{1,0:T(8,128)S(1)}) fusion(bf16[256,2048]{1,0:T(8,128)(2,1)S(1)} %bitcast.48, bf16[1792,2048]{1,0:T(8,128)(2,1)S(1)} %pad_maximum_fusion), kind=kOutput, calls=%fused_computation.69 | convolution fusion | flops 1879506944 | bytes 11141120 | tf_op jit(solution)/shard_map/dot_general | solution.py:54
  59.2 2.6 %collective-permute-start.19 = (bf16[64,896]{1,0:T(8,128)(2,1)S(1)}, bf16[64,896]{1,0:T(8,128)(2,1)S(1)}, u32[]{:S(2)}, u32[]{:S(2)}) collective-permute-start(bf16[64,896]{1,0:T(8,128)(2,1)S(1)} %fusion.19), channel_id=1, source_target_pairs={{0,2},{1,3},{2,0},{3,1},{4,6},{5,7},{6,4},{7,5},{8,10},{9,11},{10,... | collective-permute-start | bytes 344072 | tf_op jit(solution)/shard_map/ppermute | solution.py:13
  63.1 1.5 %collective-permute-start.22 = (bf16[64,1792]{1,0:T(8,128)(2,1)S(1)}, bf16[64,1792]{1,0:T(8,128)(2,1)S(1)}, u32[]{:S(2)}, u32[]{:S(2)}) collective-permute-start(bf16[64,1792]{1,0:T(8,128)(2,1)S(1)} %get-tuple-element.84), channel_id=1, source_target_pairs={{0,1},{1,2},{2,3},{3,0},{4,5},{5,6},{6,7},{7,4},{8,9},{9,10},{10,1... | collective-permute-start | bytes 688136 | tf_op jit(solution)/shard_map/ppermute | solution.py:13
  68.3 2.3 %collective-permute-start.25 = (bf16[4,16,2048]{2,1,0:T(8,128)(2,1)S(1)}, bf16[4,16,2048]{2,1,0:T(8,128)(2,1)S(1)}, u32[]{:S(2)}, u32[]{:S(2)}) collective-permute-start(bf16[4,16,2048]{2,1,0:T(8,128)(2,1)S(1)} %get-tuple-element.81), channel_id=1, source_target_pairs={{0,64},{64,128},{128,192},{192,0},{1,65},{65,129},{129,193},{193,1... | collective-permute-start | bytes 786440 | tf_op jit(solution)/shard_map/ppermute | solution.py:13
  70.7 1.8 %collective-permute-start.24 = (bf16[4,16,2048]{2,1,0:T(8,128)(2,1)S(1)}, bf16[4,16,2048]{2,1,0:T(8,128)(2,1)S(1)}, u32[]{:S(2)}, u32[]{:S(2)}) collective-permute-start(bf16[4,16,2048]{2,1,0:T(8,128)(2,1)S(1)} %get-tuple-element.82), channel_id=1, source_target_pairs={{0,192},{64,0},{128,64},{192,128},{1,193},{65,1},{129,65},{193,129... | collective-permute-start | bytes 786440 | tf_op jit(solution)/shard_map/ppermute | solution.py:13
  72.5 2.1 %collective-permute-done.21 = bf16[64,1792]{1,0:T(8,128)(2,1)S(1)} collective-permute-done((bf16[64,1792]{1,0:T(8,128)(2,1)S(1)}, bf16[64,1792]{1,0:T(8,128)(2,1)S(1)}, u32[]{:S(2)}, u32[]{:S(2)}) %collective-permute-start.21) | collective-permute-done | bytes 229408 | tf_op jit(solution)/shard_map/ppermute | solution.py:13
  74.8 1.9 %collective-permute-start.31 = (bf16[64,896]{1,0:T(8,128)(2,1)S(1)}, bf16[64,896]{1,0:T(8,128)(2,1)S(1)}, u32[]{:S(2)}, u32[]{:S(2)}) collective-permute-start(bf16[64,896]{1,0:T(8,128)(2,1)S(1)} %fusion.18), channel_id=1, source_target_pairs={{0,1},{1,2},{2,3},{3,0},{4,5},{5,6},{6,7},{7,4},{8,9},{9,10},{10,1... | collective-permute-start | bytes 344072 | tf_op jit(solution)/shard_map/ppermute | solution.py:13
  76.7 2.3 %collective-permute-start.30 = (bf16[64,896]{1,0:T(8,128)(2,1)S(1)}, bf16[64,896]{1,0:T(8,128)(2,1)S(1)}, u32[]{:S(2)}, u32[]{:S(2)}) collective-permute-start(bf16[64,896]{1,0:T(8,128)(2,1)S(1)} %fusion.18), channel_id=1, source_target_pairs={{0,2},{1,3},{2,0},{3,1},{4,6},{5,7},{6,4},{7,5},{8,10},{9,11},{10,... | collective-permute-start | bytes 344072 | tf_op jit(solution)/shard_map/ppermute | solution.py:13
  80.4 2.1 %collective-permute-done.30 = bf16[64,896]{1,0:T(8,128)(2,1)S(1)} collective-permute-done((bf16[64,896]{1,0:T(8,128)(2,1)S(1)}, bf16[64,896]{1,0:T(8,128)(2,1)S(1)}, u32[]{:S(2)}, u32[]{:S(2)}) %collective-permute-start.30) | collective-permute-done | bytes 114720 | tf_op jit(solution)/shard_map/ppermute | solution.py:13
  85.6 2.1 %collective-permute-start.33 = (bf16[4,16,2048]{2,1,0:T(8,128)(2,1)S(1)}, bf16[4,16,2048]{2,1,0:T(8,128)(2,1)S(1)}, u32[]{:S(2)}, u32[]{:S(2)}) collective-permute-start(bf16[4,16,2048]{2,1,0:T(8,128)(2,1)S(1)} %get-tuple-element.78), channel_id=1, source_target_pairs={{0,64},{64,128},{128,192},{192,0},{1,65},{65,129},{129,193},{193,1... | collective-permute-start | bytes 786440 | tf_op jit(solution)/shard_map/ppermute | solution.py:13
  89.2 6.5 %collective-permute-start.28 = (bf16[4,8,2048]{2,1,0:T(8,128)(2,1)}, bf16[4,8,2048]{2,1,0:T(8,128)(2,1)}, u32[]{:S(2)}, u32[]{:S(2)}) collective-permute-start(bf16[4,8,2048]{2,1,0:T(8,128)(2,1)} %get-tuple-element.89), channel_id=1, source_target_pairs={{0,56},{4,12},{8,0},{12,20},{16,8},{20,28},{24,16},{28,36},{32,24}... | collective-permute-start | bytes 393224 | tf_op jit(solution)/shard_map/ppermute | solution.py:21
  95.6 3.3 %collective-permute-start.27 = (bf16[4,8,2048]{2,1,0:T(8,128)(2,1)}, bf16[4,8,2048]{2,1,0:T(8,128)(2,1)}, u32[]{:S(2)}, u32[]{:S(2)}) collective-permute-start(bf16[4,8,2048]{2,1,0:T(8,128)(2,1)} %get-tuple-element.90), channel_id=1, source_target_pairs={{0,0},{4,20},{8,8},{12,28},{16,16},{20,36},{24,24},{28,44},{32,32}... | collective-permute-start | bytes 393224 | tf_op jit(solution)/shard_map/ppermute | solution.py:21
  100.2 4.9 %collective-permute-done.27 = bf16[4,8,2048]{2,1,0:T(8,128)(2,1)} collective-permute-done((bf16[4,8,2048]{2,1,0:T(8,128)(2,1)}, bf16[4,8,2048]{2,1,0:T(8,128)(2,1)}, u32[]{:S(2)}, u32[]{:S(2)}) %collective-permute-start.27) | collective-permute-done | bytes 131104 | tf_op jit(solution)/shard_map/ppermute | solution.py:21
  105.4 5.1 %collective-permute-done.35 = bf16[4,8,2048]{2,1,0:T(8,128)(2,1)S(1)} collective-permute-done((bf16[4,8,2048]{2,1,0:T(8,128)(2,1)S(1)}, bf16[4,8,2048]{2,1,0:T(8,128)(2,1)S(1)}, u32[]{:S(2)}, u32[]{:S(2)}) %collective-permute-start.35) | collective-permute-done | bytes 131104 | tf_op jit(solution)/shard_map/ppermute | solution.py:21
  111.0 9.3 %collective-permute-done.36 = bf16[4,8,2048]{2,1,0:T(8,128)(2,1)S(1)} collective-permute-done((bf16[4,8,2048]{2,1,0:T(8,128)(2,1)S(1)}, bf16[4,8,2048]{2,1,0:T(8,128)(2,1)S(1)}, u32[]{:S(2)}, u32[]{:S(2)}) %collective-permute-start.36) | collective-permute-done | bytes 131104 | tf_op jit(solution)/shard_map/ppermute | solution.py:21
  123.2 3.1 %collective-permute-start.39 = (f32[4,2048]{1,0:T(4,128)S(1)}, f32[4,2048]{1,0:T(4,128)S(1)}, u32[]{:S(2)}, u32[]{:S(2)}) collective-permute-start(f32[4,2048]{1,0:T(4,128)S(1)} %get-tuple-element.96), channel_id=1, source_target_pairs={{0,2},{1,3},{2,0},{3,1},{4,6},{5,7},{6,4},{7,5},{8,10},{9,11},{10,... | collective-permute-start | bytes 98312 | tf_op jit(solution)/shard_map/ppermute | solution.py:13
  (97 shorter events, 29.4 us)
Async XLA Ops:
  0.0 32.2 %collective-permute-start = (bf16[448,2048]{1,0:T(8,128)(2,1)}, bf16[448,2048]{1,0:T(8,128)(2,1)S(1)}, u32[]{:S(2)}, u32[]{:S(2)}) collective-permute-start(bf16[448,2048]{1,0:T(8,128)(2,1)} %bitcast.46), channel_id=1, source_target_pairs={{0,4},{4,0},{1,5},{5,1},{2,6},{6,2},{3,7},{7,3},{8,12},{12,8},{9,1... | collective-permute-start | bytes 5505032 | tf_op jit(solution)/shard_map/ppermute | solution.py:13
  3.2 31.6 %collective-permute-start.1 = (bf16[448,2048]{1,0:T(8,128)(2,1)}, bf16[448,2048]{1,0:T(8,128)(2,1)}, u32[]{:S(2)}, u32[]{:S(2)}) collective-permute-start(bf16[448,2048]{1,0:T(8,128)(2,1)} %bitcast.44), channel_id=1, source_target_pairs={{0,4},{4,0},{1,5},{5,1},{2,6},{6,2},{3,7},{7,3},{8,12},{12,8},{9,1... | collective-permute-start | bytes 5505032 | tf_op jit(solution)/shard_map/ppermute | solution.py:13
  15.1 11.2 %collective-permute-start.5 = (bf16[4,8,2048]{2,1,0:T(8,128)(2,1)S(1)}, bf16[4,8,2048]{2,1,0:T(8,128)(2,1)S(1)}, u32[]{:S(2)}, u32[]{:S(2)}) collective-permute-start(bf16[4,8,2048]{2,1,0:T(8,128)(2,1)S(1)} %copy.11), channel_id=1, source_target_pairs={{0,0},{4,52},{8,8},{12,60},{16,16},{20,4},{24,24},{28,12},{32,32},... | collective-permute-start | bytes 393224 | tf_op jit(solution)/shard_map/ppermute | solution.py:21
  27.7 14.2 %collective-permute-start.11 = (bf16[4,16,2048]{2,1,0:T(8,128)(2,1)S(1)}, bf16[4,16,2048]{2,1,0:T(8,128)(2,1)S(1)}, u32[]{:S(2)}, u32[]{:S(2)}) collective-permute-start(bf16[4,16,2048]{2,1,0:T(8,128)(2,1)S(1)} %constant_dynamic-update-slice_fusion), channel_id=1, source_target_pairs={{0,128},{64,192},{128,0},{192,64},{1,129},{65,193},{129,1},{193,65... | collective-permute-start | bytes 786440 | tf_op jit(solution)/shard_map/ppermute | solution.py:13
  30.7 13.3 %collective-permute-start.10 = (bf16[4,16,2048]{2,1,0:T(8,128)(2,1)S(1)}, bf16[4,16,2048]{2,1,0:T(8,128)(2,1)S(1)}, u32[]{:S(2)}, u32[]{:S(2)}) collective-permute-start(bf16[4,16,2048]{2,1,0:T(8,128)(2,1)S(1)} %constant_dynamic-update-slice_fusion), channel_id=1, source_target_pairs={{0,192},{64,0},{128,64},{192,128},{1,193},{65,1},{129,65},{193,129... | collective-permute-start | bytes 786440 | tf_op jit(solution)/shard_map/ppermute | solution.py:13
  31.5 12.7 %collective-permute-start.9 = (bf16[4,16,2048]{2,1,0:T(8,128)(2,1)S(1)}, bf16[4,16,2048]{2,1,0:T(8,128)(2,1)S(1)}, u32[]{:S(2)}, u32[]{:S(2)}) collective-permute-start(bf16[4,16,2048]{2,1,0:T(8,128)(2,1)S(1)} %constant_dynamic-update-slice_fusion), channel_id=1, source_target_pairs={{0,64},{64,128},{128,192},{192,0},{1,65},{65,129},{129,193},{193,1... | collective-permute-start | bytes 786440 | tf_op jit(solution)/shard_map/ppermute | solution.py:13
  32.2 9.0 %collective-permute-start.8 = (bf16[4,16,2048]{2,1,0:T(8,128)(2,1)S(1)}, bf16[4,16,2048]{2,1,0:T(8,128)(2,1)S(1)}, u32[]{:S(2)}, u32[]{:S(2)}) collective-permute-start(bf16[4,16,2048]{2,1,0:T(8,128)(2,1)S(1)} %constant_dynamic-update-slice_fusion), channel_id=1, source_target_pairs={{0,16},{4,52},{8,24},{12,60},{16,32},{20,4},{24,40},{28,12},{32,48... | collective-permute-start | bytes 786440 | tf_op jit(solution)/shard_map/ppermute | solution.py:21
  34.9 11.8 %collective-permute-start.7 = (bf16[448,2048]{1,0:T(8,128)(2,1)}, bf16[448,2048]{1,0:T(8,128)(2,1)S(1)}, u32[]{:S(2)}, u32[]{:S(2)}) collective-permute-start(bf16[448,2048]{1,0:T(8,128)(2,1)} %param.9), channel_id=1, source_target_pairs={{0,4},{4,0},{1,5},{5,1},{2,6},{6,2},{3,7},{7,3},{8,12},{12,8},{9,1... | collective-permute-start | bytes 5505032 | tf_op jit(solution)/shard_map/ppermute | solution.py:13
  41.2 9.0 %collective-permute-start.14 = (bf16[4,16,2048]{2,1,0:T(8,128)(2,1)S(1)}, bf16[4,16,2048]{2,1,0:T(8,128)(2,1)S(1)}, u32[]{:S(2)}, u32[]{:S(2)}) collective-permute-start(bf16[4,16,2048]{2,1,0:T(8,128)(2,1)S(1)} %collective-permute-done.8), channel_id=1, source_target_pairs={{0,128},{64,192},{128,0},{192,64},{1,129},{65,193},{129,1},{193,65... | collective-permute-start | bytes 786440 | tf_op jit(solution)/shard_map/ppermute | solution.py:13
  41.9 13.9 %collective-permute-start.13 = (bf16[4,16,2048]{2,1,0:T(8,128)(2,1)S(1)}, bf16[4,16,2048]{2,1,0:T(8,128)(2,1)S(1)}, u32[]{:S(2)}, u32[]{:S(2)}) collective-permute-start(bf16[4,16,2048]{2,1,0:T(8,128)(2,1)S(1)} %collective-permute-done.8), channel_id=1, source_target_pairs={{0,192},{64,0},{128,64},{192,128},{1,193},{65,1},{129,65},{193,129... | collective-permute-start | bytes 786440 | tf_op jit(solution)/shard_map/ppermute | solution.py:13
  44.0 12.6 %collective-permute-start.12 = (bf16[4,16,2048]{2,1,0:T(8,128)(2,1)S(1)}, bf16[4,16,2048]{2,1,0:T(8,128)(2,1)S(1)}, u32[]{:S(2)}, u32[]{:S(2)}) collective-permute-start(bf16[4,16,2048]{2,1,0:T(8,128)(2,1)S(1)} %collective-permute-done.8), channel_id=1, source_target_pairs={{0,64},{64,128},{128,192},{192,0},{1,65},{65,129},{129,193},{193,1... | collective-permute-start | bytes 786440 | tf_op jit(solution)/shard_map/ppermute | solution.py:13
  46.5 12.3 %collective-permute-start.17 = (bf16[64,1792]{1,0:T(8,128)(2,1)S(1)}, bf16[64,1792]{1,0:T(8,128)(2,1)S(1)}, u32[]{:S(2)}, u32[]{:S(2)}) collective-permute-start(bf16[64,1792]{1,0:T(8,128)(2,1)S(1)} %get-tuple-element.86), channel_id=1, source_target_pairs={{0,3},{1,0},{2,1},{3,2},{4,7},{5,4},{6,5},{7,6},{8,11},{9,8},{10,9... | collective-permute-start | bytes 688136 | tf_op jit(solution)/shard_map/ppermute | solution.py:13
  46.7 12.2 %collective-permute-start.16 = (bf16[64,1792]{1,0:T(8,128)(2,1)S(1)}, bf16[64,1792]{1,0:T(8,128)(2,1)S(1)}, u32[]{:S(2)}, u32[]{:S(2)}) collective-permute-start(bf16[64,1792]{1,0:T(8,128)(2,1)S(1)} %get-tuple-element.87), channel_id=1, source_target_pairs={{0,1},{1,2},{2,3},{3,0},{4,5},{5,6},{6,7},{7,4},{8,9},{9,10},{10,1... | collective-permute-start | bytes 688136 | tf_op jit(solution)/shard_map/ppermute | solution.py:13
  50.3 8.6 %collective-permute-start.15 = (bf16[64,1792]{1,0:T(8,128)(2,1)S(1)}, bf16[64,1792]{1,0:T(8,128)(2,1)S(1)}, u32[]{:S(2)}, u32[]{:S(2)}) collective-permute-start(bf16[64,1792]{1,0:T(8,128)(2,1)S(1)} %get-tuple-element.88), channel_id=1, source_target_pairs={{0,2},{1,3},{2,0},{3,1},{4,6},{5,7},{6,4},{7,5},{8,10},{9,11},{10,... | collective-permute-start | bytes 688136 | tf_op jit(solution)/shard_map/ppermute | solution.py:13
  59.1 5.5 %collective-permute-start.20 = (bf16[64,896]{1,0:T(8,128)(2,1)S(1)}, bf16[64,896]{1,0:T(8,128)(2,1)S(1)}, u32[]{:S(2)}, u32[]{:S(2)}) collective-permute-start(bf16[64,896]{1,0:T(8,128)(2,1)S(1)} %fusion.19), channel_id=1, source_target_pairs={{0,1},{1,2},{2,3},{3,0},{4,5},{5,6},{6,7},{7,4},{8,9},{9,10},{10,1... | collective-permute-start | bytes 344072 | tf_op jit(solution)/shard_map/ppermute | solution.py:13
  59.2 6.6 %collective-permute-start.19 = (bf16[64,896]{1,0:T(8,128)(2,1)S(1)}, bf16[64,896]{1,0:T(8,128)(2,1)S(1)}, u32[]{:S(2)}, u32[]{:S(2)}) collective-permute-start(bf16[64,896]{1,0:T(8,128)(2,1)S(1)} %fusion.19), channel_id=1, source_target_pairs={{0,2},{1,3},{2,0},{3,1},{4,6},{5,7},{6,4},{7,5},{8,10},{9,11},{10,... | collective-permute-start | bytes 344072 | tf_op jit(solution)/shard_map/ppermute | solution.py:13
  63.0 7.6 %collective-permute-start.23 = (bf16[64,1792]{1,0:T(8,128)(2,1)S(1)}, bf16[64,1792]{1,0:T(8,128)(2,1)S(1)}, u32[]{:S(2)}, u32[]{:S(2)}) collective-permute-start(bf16[64,1792]{1,0:T(8,128)(2,1)S(1)} %get-tuple-element.83), channel_id=1, source_target_pairs={{0,3},{1,0},{2,1},{3,2},{4,7},{5,4},{6,5},{7,6},{8,11},{9,8},{10,9... | collective-permute-start | bytes 688136 | tf_op jit(solution)/shard_map/ppermute | solution.py:13
  63.1 9.4 %collective-permute-start.22 = (bf16[64,1792]{1,0:T(8,128)(2,1)S(1)}, bf16[64,1792]{1,0:T(8,128)(2,1)S(1)}, u32[]{:S(2)}, u32[]{:S(2)}) collective-permute-start(bf16[64,1792]{1,0:T(8,128)(2,1)S(1)} %get-tuple-element.84), channel_id=1, source_target_pairs={{0,1},{1,2},{2,3},{3,0},{4,5},{5,6},{6,7},{7,4},{8,9},{9,10},{10,1... | collective-permute-start | bytes 688136 | tf_op jit(solution)/shard_map/ppermute | solution.py:13
  64.6 10.1 %collective-permute-start.21 = (bf16[64,1792]{1,0:T(8,128)(2,1)S(1)}, bf16[64,1792]{1,0:T(8,128)(2,1)S(1)}, u32[]{:S(2)}, u32[]{:S(2)}) collective-permute-start(bf16[64,1792]{1,0:T(8,128)(2,1)S(1)} %get-tuple-element.85), channel_id=1, source_target_pairs={{0,2},{1,3},{2,0},{3,1},{4,6},{5,7},{6,4},{7,5},{8,10},{9,11},{10,... | collective-permute-start | bytes 688136 | tf_op jit(solution)/shard_map/ppermute | solution.py:13
  67.6 11.5 %collective-permute-start.26 = (bf16[4,16,2048]{2,1,0:T(8,128)(2,1)S(1)}, bf16[4,16,2048]{2,1,0:T(8,128)(2,1)S(1)}, u32[]{:S(2)}, u32[]{:S(2)}) collective-permute-start(bf16[4,16,2048]{2,1,0:T(8,128)(2,1)S(1)} %get-tuple-element.80), channel_id=1, source_target_pairs={{0,128},{64,192},{128,0},{192,64},{1,129},{65,193},{129,1},{193,65... | collective-permute-start | bytes 786440 | tf_op jit(solution)/shard_map/ppermute | solution.py:13
  68.3 10.9 %collective-permute-start.25 = (bf16[4,16,2048]{2,1,0:T(8,128)(2,1)S(1)}, bf16[4,16,2048]{2,1,0:T(8,128)(2,1)S(1)}, u32[]{:S(2)}, u32[]{:S(2)}) collective-permute-start(bf16[4,16,2048]{2,1,0:T(8,128)(2,1)S(1)} %get-tuple-element.81), channel_id=1, source_target_pairs={{0,64},{64,128},{128,192},{192,0},{1,65},{65,129},{129,193},{193,1... | collective-permute-start | bytes 786440 | tf_op jit(solution)/shard_map/ppermute | solution.py:13
  70.7 8.6 %collective-permute-start.24 = (bf16[4,16,2048]{2,1,0:T(8,128)(2,1)S(1)}, bf16[4,16,2048]{2,1,0:T(8,128)(2,1)S(1)}, u32[]{:S(2)}, u32[]{:S(2)}) collective-permute-start(bf16[4,16,2048]{2,1,0:T(8,128)(2,1)S(1)} %get-tuple-element.82), channel_id=1, source_target_pairs={{0,192},{64,0},{128,64},{192,128},{1,193},{65,1},{129,65},{193,129... | collective-permute-start | bytes 786440 | tf_op jit(solution)/shard_map/ppermute | solution.py:13
  74.8 5.6 %collective-permute-start.31 = (bf16[64,896]{1,0:T(8,128)(2,1)S(1)}, bf16[64,896]{1,0:T(8,128)(2,1)S(1)}, u32[]{:S(2)}, u32[]{:S(2)}) collective-permute-start(bf16[64,896]{1,0:T(8,128)(2,1)S(1)} %fusion.18), channel_id=1, source_target_pairs={{0,1},{1,2},{2,3},{3,0},{4,5},{5,6},{6,7},{7,4},{8,9},{9,10},{10,1... | collective-permute-start | bytes 344072 | tf_op jit(solution)/shard_map/ppermute | solution.py:13
  76.7 5.8 %collective-permute-start.30 = (bf16[64,896]{1,0:T(8,128)(2,1)S(1)}, bf16[64,896]{1,0:T(8,128)(2,1)S(1)}, u32[]{:S(2)}, u32[]{:S(2)}) collective-permute-start(bf16[64,896]{1,0:T(8,128)(2,1)S(1)} %fusion.18), channel_id=1, source_target_pairs={{0,2},{1,3},{2,0},{3,1},{4,6},{5,7},{6,4},{7,5},{8,10},{9,11},{10,... | collective-permute-start | bytes 344072 | tf_op jit(solution)/shard_map/ppermute | solution.py:13
  85.2 19.9 %collective-permute-start.34 = (bf16[4,16,2048]{2,1,0:T(8,128)(2,1)}, bf16[4,16,2048]{2,1,0:T(8,128)(2,1)S(1)}, u32[]{:S(2)}, u32[]{:S(2)}) collective-permute-start(bf16[4,16,2048]{2,1,0:T(8,128)(2,1)} %get-tuple-element.77), channel_id=1, source_target_pairs={{0,128},{64,192},{128,0},{192,64},{1,129},{65,193},{129,1},{193,65... | collective-permute-start | bytes 786440 | tf_op jit(solution)/shard_map/ppermute | solution.py:13
  85.6 19.6 %collective-permute-start.33 = (bf16[4,16,2048]{2,1,0:T(8,128)(2,1)S(1)}, bf16[4,16,2048]{2,1,0:T(8,128)(2,1)S(1)}, u32[]{:S(2)}, u32[]{:S(2)}) collective-permute-start(bf16[4,16,2048]{2,1,0:T(8,128)(2,1)S(1)} %get-tuple-element.78), channel_id=1, source_target_pairs={{0,64},{64,128},{128,192},{192,0},{1,65},{65,129},{129,193},{193,1... | collective-permute-start | bytes 786440 | tf_op jit(solution)/shard_map/ppermute | solution.py:13
  87.7 17.5 %collective-permute-start.32 = (bf16[4,16,2048]{2,1,0:T(8,128)(2,1)S(1)}, bf16[4,16,2048]{2,1,0:T(8,128)(2,1)S(1)}, u32[]{:S(2)}, u32[]{:S(2)}) collective-permute-start(bf16[4,16,2048]{2,1,0:T(8,128)(2,1)S(1)} %get-tuple-element.79), channel_id=1, source_target_pairs={{0,192},{64,0},{128,64},{192,128},{1,193},{65,1},{129,65},{193,129... | collective-permute-start | bytes 786440 | tf_op jit(solution)/shard_map/ppermute | solution.py:13
  89.2 11.1 %collective-permute-start.28 = (bf16[4,8,2048]{2,1,0:T(8,128)(2,1)}, bf16[4,8,2048]{2,1,0:T(8,128)(2,1)}, u32[]{:S(2)}, u32[]{:S(2)}) collective-permute-start(bf16[4,8,2048]{2,1,0:T(8,128)(2,1)} %get-tuple-element.89), channel_id=1, source_target_pairs={{0,56},{4,12},{8,0},{12,20},{16,8},{20,28},{24,16},{28,36},{32,24}... | collective-permute-start | bytes 393224 | tf_op jit(solution)/shard_map/ppermute | solution.py:21
  95.6 9.5 %collective-permute-start.27 = (bf16[4,8,2048]{2,1,0:T(8,128)(2,1)}, bf16[4,8,2048]{2,1,0:T(8,128)(2,1)}, u32[]{:S(2)}, u32[]{:S(2)}) collective-permute-start(bf16[4,8,2048]{2,1,0:T(8,128)(2,1)} %get-tuple-element.90), channel_id=1, source_target_pairs={{0,0},{4,20},{8,8},{12,28},{16,16},{20,36},{24,24},{28,44},{32,32}... | collective-permute-start | bytes 393224 | tf_op jit(solution)/shard_map/ppermute | solution.py:21
  105.3 5.2 %collective-permute-start.35 = (bf16[4,8,2048]{2,1,0:T(8,128)(2,1)S(1)}, bf16[4,8,2048]{2,1,0:T(8,128)(2,1)S(1)}, u32[]{:S(2)}, u32[]{:S(2)}) collective-permute-start(bf16[4,8,2048]{2,1,0:T(8,128)(2,1)S(1)} %select_convert_fusion), channel_id=1, source_target_pairs={{0,56},{4,12},{8,0},{12,20},{16,8},{20,28},{24,16},{28,36},{32,24}... | collective-permute-start | bytes 393224 | tf_op jit(solution)/shard_map/ppermute | solution.py:21
  110.6 9.7 %collective-permute-start.36 = (bf16[4,8,2048]{2,1,0:T(8,128)(2,1)S(1)}, bf16[4,8,2048]{2,1,0:T(8,128)(2,1)S(1)}, u32[]{:S(2)}, u32[]{:S(2)}) collective-permute-start(bf16[4,8,2048]{2,1,0:T(8,128)(2,1)S(1)} %add_convert_fusion.1), channel_id=1, source_target_pairs={{0,48},{4,28},{8,56},{12,36},{16,0},{20,44},{24,8},{28,52},{32,16}... | collective-permute-start | bytes 393224 | tf_op jit(solution)/shard_map/ppermute | solution.py:21
  123.2 4.9 %collective-permute-start.39 = (f32[4,2048]{1,0:T(4,128)S(1)}, f32[4,2048]{1,0:T(4,128)S(1)}, u32[]{:S(2)}, u32[]{:S(2)}) collective-permute-start(f32[4,2048]{1,0:T(4,128)S(1)} %get-tuple-element.96), channel_id=1, source_target_pairs={{0,2},{1,3},{2,0},{3,1},{4,6},{5,7},{6,4},{7,5},{8,10},{9,11},{10,... | collective-permute-start | bytes 98312 | tf_op jit(solution)/shard_map/ppermute | solution.py:13
  (11 other events, 64.2 us)

commit v11 on v9

--- a/solution.py
+++ b/solution.py
@@ -56,7 +56,7 @@
         ).reshape(4, -1, 2 * units)
 
     def exchange(partial):
-        return [shift(partial[k].astype(BF16), "x", k) for k in (2, 1, 3)]
+        return [shift(partial[k].astype(BF16), "x", k) for k in (1, 3, 2)]
 
     def activate(both, received):
         for value in received:
@@ -64,7 +64,8 @@
         return (jax.nn.silu(both[:, :units]) * both[:, units:]).astype(BF16)
 
     def spread(hidden):
-        return [shift(hidden, "x", -k) for k in (1, 2, 3)]
+        one, three, two = (shift(hidden, "x", -k) for k in (1, 3, 2))
+        return [one, two, three]
 
     def down(weights, everyone):
         return lax.dot_general(

time: 128 us -> 127 us (level)
  starting transfers between devices: 63.2 us -> 52.3 us
  waiting for transfers between devices: 44.7 us -> 54.5 us
    ppermute x34, waiting for transfers between devices: 30.4 us -> 37.3 us  [shift(): return lax.ppermute(value, axis, [(i, (i + step) % n) for i in range(n)])]
    ppermute x34, starting transfers between devices: 39.9 us -> 34 us  [shift(): return lax.ppermute(value, axis, [(i, (i + step) % n) for i in range(n)])]
    ppermute x7, starting transfers between devices: 23.3 us -> 18.4 us  [along_z(): return lax.ppermute(value, ('z', 'c'), pairs)]
    ppermute x7, waiting for transfers between devices: 14.3 us -> 17.2 us  [along_z(): return lax.ppermute(value, ('z', 'c'), pairs)]
  transfers between devices with their start and end apart: 41 -> 41, of which waited for: 21 -> 22; matrix products, arithmetic and copies ran while one was open for 11% -> 11% of each run, Pallas kernels for 0% -> 0%
where the time goes in v11:
time: 127 us
  waiting for transfers between devices  54.5 us (43%)
  starting transfers between devices  52.3 us (41%)
  other arithmetic  8.16 us (6%)
  matrix products  6.81 us (5%)
  blocking collectives  3.76 us (3%)
    ppermute x34, waiting for transfers between devices, shift(): return lax.ppermute(value, axis, [(i, (i + step) % n) for i in range(n)])  37.3 us
    ppermute x34, starting transfers between devices, shift(): return lax.ppermute(value, axis, [(i, (i + step) % n) for i in range(n)])  34 us
    ppermute x7, starting transfers between devices, along_z(): return lax.ppermute(value, ('z', 'c'), pairs)  18.4 us
    ppermute x7, waiting for transfers between devices, along_z(): return lax.ppermute(value, ('z', 'c'), pairs)  17.2 us
    dot_general x2, matrix products, project(): lax.dot_general(block.reshape(-1, part), weights, (((1,), (1,)), ((), ())...  4.23 us
    all_gather x1, blocking collectives, local(): pair = lax.all_gather(own, 'c', axis=1, tiled=True)  3.76 us
    concatenate x1, other arithmetic, local(): first, far = together(jnp.concatenate(first, axis=0), far)  3.61 us
    dot_general x2, matrix products, down(): lax.dot_general(jnp.concatenate(everyone, axis=0), weights, (((1,), (0,))...  2.58 us
  transfers between devices with their start and end apart: 41, of which 22 were waited for; matrix products, arithmetic and copies ran while one was open for 11% of the time, Pallas kernels for 0%

profile of v11, /device:TPU:1, one launch (start us, length us, event | category | flops | bytes accessed | tf_op | source)
XLA Modules:
  0.0 126.6 jit_solution(17898594921103592030)
XLA Ops:
  0.0 3.2 %collective-permute-start = (bf16[448,2048]{1,0:T(8,128)(2,1)}, bf16[448,2048]{1,0:T(8,128)(2,1)S(1)}, u32[]{:S(2)}, u32[]{:S(2)}) collective-permute-start(bf16[448,2048]{1,0:T(8,128)(2,1)} %bitcast.46), channel_id=1, source_target_pairs={{0,4},{4,0},{1,5},{5,1},{2,6},{6,2},{3,7},{7,3},{8,12},{12,8},{9,1... | collective-permute-start | bytes 5505032 | tf_op jit(solution)/shard_map/ppermute | solution.py:13
  7.9 1.6 %collective-permute-done.3 = bf16[4,2048]{1,0:T(4,128)(2,1)S(1)} collective-permute-done((bf16[4,2048]{1,0:T(4,128)(2,1)S(1)}, bf16[4,2048]{1,0:T(4,128)(2,1)S(1)}, u32[]{:S(2)}, u32[]{:S(2)}) %collective-permute-start.3) | collective-permute-done | bytes 16416 | tf_op jit(solution)/shard_map/ppermute | solution.py:13
  9.6 1.6 %collective-permute-done.4 = bf16[4,2048]{1,0:T(4,128)(2,1)S(1)} collective-permute-done((bf16[4,2048]{1,0:T(4,128)(2,1)S(1)}, bf16[4,2048]{1,0:T(4,128)(2,1)S(1)}, u32[]{:S(2)}, u32[]{:S(2)}) %collective-permute-start.4) | collective-permute-done | bytes 16416 | tf_op jit(solution)/shard_map/ppermute | solution.py:13
  11.2 3.8 %all_gather.3 = bf16[4,8,2048]{2,0,1:T(4,128)(2,1)S(1)} all-gather(bf16[4,4,2048]{2,0,1:T(4,128)(2,1)S(1)} %copy.10), channel_id=1, replica_groups=mesh['y'=4,'z'=8,'c'=2,'x'=4] {'c'}, dimensions={1}, use_global_device_ids=true | all-gather | bytes 196608 | tf_op jit(solution)/shard_map/all_gather | solution.py:49
  15.1 7.9 %collective-permute-start.5 = (bf16[4,8,2048]{2,1,0:T(8,128)(2,1)S(1)}, bf16[4,8,2048]{2,1,0:T(8,128)(2,1)S(1)}, u32[]{:S(2)}, u32[]{:S(2)}) collective-permute-start(bf16[4,8,2048]{2,1,0:T(8,128)(2,1)S(1)} %copy.11), channel_id=1, source_target_pairs={{0,0},{4,52},{8,8},{12,60},{16,16},{20,4},{24,24},{28,12},{32,32},... | collective-permute-start | bytes 393224 | tf_op jit(solution)/shard_map/ppermute | solution.py:21
  23.8 2.5 %collective-permute-done.5 = bf16[4,8,2048]{2,1,0:T(8,128)(2,1)S(1)} collective-permute-done((bf16[4,8,2048]{2,1,0:T(8,128)(2,1)S(1)}, bf16[4,8,2048]{2,1,0:T(8,128)(2,1)S(1)}, u32[]{:S(2)}, u32[]{:S(2)}) %collective-permute-start.5) | collective-permute-done | bytes 131104 | tf_op jit(solution)/shard_map/ppermute | solution.py:21
  26.3 1.4 %collective-permute-done.6 = bf16[4,8,2048]{2,1,0:T(8,128)(2,1)S(1)} collective-permute-done((bf16[4,8,2048]{2,1,0:T(8,128)(2,1)S(1)}, bf16[4,8,2048]{2,1,0:T(8,128)(2,1)S(1)}, u32[]{:S(2)}, u32[]{:S(2)}) %collective-permute-start.6) | collective-permute-done | bytes 131104 | tf_op jit(solution)/shard_map/ppermute | solution.py:21
  27.7 3.0 %collective-permute-start.11 = (bf16[4,16,2048]{2,1,0:T(8,128)(2,1)S(1)}, bf16[4,16,2048]{2,1,0:T(8,128)(2,1)S(1)}, u32[]{:S(2)}, u32[]{:S(2)}) collective-permute-start(bf16[4,16,2048]{2,1,0:T(8,128)(2,1)S(1)} %constant_dynamic-update-slice_fusion), channel_id=1, source_target_pairs={{0,128},{64,192},{128,0},{192,64},{1,129},{65,193},{129,1},{193,65... | collective-permute-start | bytes 786440 | tf_op jit(solution)/shard_map/ppermute | solution.py:13
  32.2 2.6 %collective-permute-start.8 = (bf16[4,16,2048]{2,1,0:T(8,128)(2,1)S(1)}, bf16[4,16,2048]{2,1,0:T(8,128)(2,1)S(1)}, u32[]{:S(2)}, u32[]{:S(2)}) collective-permute-start(bf16[4,16,2048]{2,1,0:T(8,128)(2,1)S(1)} %constant_dynamic-update-slice_fusion), channel_id=1, source_target_pairs={{0,16},{4,52},{8,24},{12,60},{16,32},{20,4},{24,40},{28,12},{32,48... | collective-permute-start | bytes 786440 | tf_op jit(solution)/shard_map/ppermute | solution.py:21
  34.9 3.6 %pad_maximum_fusion = bf16[1792,2048]{1,0:T(8,128)(2,1)S(1)} fusion(bf16[448,2048]{1,0:T(8,128)(2,1)} %collective-permute-done.1, bf16[448,2048]{1,0:T(8,128)(2,1)} %bitcast.45, bf16[448,2048]{1,0:T(8,128)(2,1)S(1)} %collective-permute-done, bf16[448,2048]{1,0:T(8,128)(2,1)} %bitcast.47), kind=kLoop, calls=%fused_computation | loop fusion | flops 29360128 | bytes 14680064 | tf_op jit(solution)/shard_map/concatenate | solution.py:94
  38.5 2.7 %collective-permute-done.8 = bf16[4,16,2048]{2,1,0:T(8,128)(2,1)S(1)} collective-permute-done((bf16[4,16,2048]{2,1,0:T(8,128)(2,1)S(1)}, bf16[4,16,2048]{2,1,0:T(8,128)(2,1)S(1)}, u32[]{:S(2)}, u32[]{:S(2)}) %collective-permute-start.8) | collective-permute-done | bytes 262176 | tf_op jit(solution)/shard_map/ppermute | solution.py:21
  41.9 2.1 %collective-permute-start.13 = (bf16[4,16,2048]{2,1,0:T(8,128)(2,1)S(1)}, bf16[4,16,2048]{2,1,0:T(8,128)(2,1)S(1)}, u32[]{:S(2)}, u32[]{:S(2)}) collective-permute-start(bf16[4,16,2048]{2,1,0:T(8,128)(2,1)S(1)} %collective-permute-done.8), channel_id=1, source_target_pairs={{0,192},{64,0},{128,64},{192,128},{1,193},{65,1},{129,65},{193,129... | collective-permute-start | bytes 786440 | tf_op jit(solution)/shard_map/ppermute | solution.py:13
  44.3 2.1 %fusion.32 = (bf16[256,1792]{1,0:T(8,128)(2,1)S(1)}, f32[256,1792]{1,0:T(8,128)S(1)}) fusion(bf16[256,2048]{1,0:T(8,128)(2,1)S(1)} %bitcast.49, bf16[1792,2048]{1,0:T(8,128)(2,1)S(1)} %pad_maximum_fusion), kind=kOutput, calls=%fused_computation.65 | convolution fusion | flops 1879506944 | bytes 11141120 | tf_op jit(solution)/shard_map/dot_general | solution.py:54
  46.7 1.8 %collective-permute-start.16 = (bf16[64,1792]{1,0:T(8,128)(2,1)S(1)}, bf16[64,1792]{1,0:T(8,128)(2,1)S(1)}, u32[]{:S(2)}, u32[]{:S(2)}) collective-permute-start(bf16[64,1792]{1,0:T(8,128)(2,1)S(1)} %get-tuple-element.103), channel_id=1, source_target_pairs={{0,3},{1,0},{2,1},{3,2},{4,7},{5,4},{6,5},{7,6},{8,11},{9,8},{10,9... | collective-permute-start | bytes 688136 | tf_op jit(solution)/shard_map/ppermute | solution.py:13
  50.3 5.6 %collective-permute-done.13 = bf16[4,16,2048]{2,1,0:T(8,128)(2,1)S(1)} collective-permute-done((bf16[4,16,2048]{2,1,0:T(8,128)(2,1)S(1)}, bf16[4,16,2048]{2,1,0:T(8,128)(2,1)S(1)}, u32[]{:S(2)}, u32[]{:S(2)}) %collective-permute-start.13) | collective-permute-done | bytes 262176 | tf_op jit(solution)/shard_map/ppermute | solution.py:13
  56.7 2.1 %fusion.33 = (bf16[256,1792]{1,0:T(8,128)(2,1)S(1)}, f32[256,1792]{1,0:T(8,128)S(1)}) fusion(bf16[256,2048]{1,0:T(8,128)(2,1)S(1)} %bitcast.48, bf16[1792,2048]{1,0:T(8,128)(2,1)S(1)} %pad_maximum_fusion), kind=kOutput, calls=%fused_computation.66 | convolution fusion | flops 1879506944 | bytes 11141120 | tf_op jit(solution)/shard_map/dot_general | solution.py:54
  59.0 1.8 %collective-permute-start.19 = (bf16[64,1792]{1,0:T(8,128)(2,1)S(1)}, bf16[64,1792]{1,0:T(8,128)(2,1)S(1)}, u32[]{:S(2)}, u32[]{:S(2)}) collective-permute-start(bf16[64,1792]{1,0:T(8,128)(2,1)S(1)} %get-tuple-element.100), channel_id=1, source_target_pairs={{0,3},{1,0},{2,1},{3,2},{4,7},{5,4},{6,5},{7,6},{8,11},{9,8},{10,9... | collective-permute-start | bytes 688136 | tf_op jit(solution)/shard_map/ppermute | solution.py:13
  62.0 3.0 %collective-permute-start.22 = (bf16[64,896]{1,0:T(8,128)(2,1)S(1)}, bf16[64,896]{1,0:T(8,128)(2,1)S(1)}, u32[]{:S(2)}, u32[]{:S(2)}) collective-permute-start(bf16[64,896]{1,0:T(8,128)(2,1)S(1)} %fusion.17), channel_id=1, source_target_pairs={{0,2},{1,3},{2,0},{3,1},{4,6},{5,7},{6,4},{7,5},{8,10},{9,11},{10,... | collective-permute-start | bytes 344072 | tf_op jit(solution)/shard_map/ppermute | solution.py:13
  65.0 2.2 %collective-permute-done.20 = bf16[64,1792]{1,0:T(8,128)(2,1)S(1)} collective-permute-done((bf16[64,1792]{1,0:T(8,128)(2,1)S(1)}, bf16[64,1792]{1,0:T(8,128)(2,1)S(1)}, u32[]{:S(2)}, u32[]{:S(2)}) %collective-permute-start.20) | collective-permute-done | bytes 229408 | tf_op jit(solution)/shard_map/ppermute | solution.py:13
  67.2 2.3 %collective-permute-done.19 = bf16[64,1792]{1,0:T(8,128)(2,1)S(1)} collective-permute-done((bf16[64,1792]{1,0:T(8,128)(2,1)S(1)}, bf16[64,1792]{1,0:T(8,128)(2,1)S(1)}, u32[]{:S(2)}, u32[]{:S(2)}) %collective-permute-start.19) | collective-permute-done | bytes 229408 | tf_op jit(solution)/shard_map/ppermute | solution.py:13
  69.5 3.4 %collective-permute-done.18 = bf16[64,1792]{1,0:T(8,128)(2,1)S(1)} collective-permute-done((bf16[64,1792]{1,0:T(8,128)(2,1)S(1)}, bf16[64,1792]{1,0:T(8,128)(2,1)S(1)}, u32[]{:S(2)}, u32[]{:S(2)}) %collective-permute-start.18) | collective-permute-done | bytes 229408 | tf_op jit(solution)/shard_map/ppermute | solution.py:13
  73.4 1.5 %collective-permute-start.25 = (bf16[64,896]{1,0:T(8,128)(2,1)S(1)}, bf16[64,896]{1,0:T(8,128)(2,1)S(1)}, u32[]{:S(2)}, u32[]{:S(2)}) collective-permute-start(bf16[64,896]{1,0:T(8,128)(2,1)S(1)} %fusion.16), channel_id=1, source_target_pairs={{0,2},{1,3},{2,0},{3,1},{4,6},{5,7},{6,4},{7,5},{8,10},{9,11},{10,... | collective-permute-start | bytes 344072 | tf_op jit(solution)/shard_map/ppermute | solution.py:13
  78.9 2.5 %collective-permute-start.28 = (bf16[4,16,2048]{2,1,0:T(8,128)(2,1)S(1)}, bf16[4,16,2048]{2,1,0:T(8,128)(2,1)S(1)}, u32[]{:S(2)}, u32[]{:S(2)}) collective-permute-start(bf16[4,16,2048]{2,1,0:T(8,128)(2,1)S(1)} %get-tuple-element.97), channel_id=1, source_target_pairs={{0,64},{64,128},{128,192},{192,0},{1,65},{65,129},{129,193},{193,1... | collective-permute-start | bytes 786440 | tf_op jit(solution)/shard_map/ppermute | solution.py:13
  84.9 1.5 %collective-permute-start.33 = (bf16[4,16,2048]{2,1,0:T(8,128)(2,1)S(1)}, bf16[4,16,2048]{2,1,0:T(8,128)(2,1)S(1)}, u32[]{:S(2)}, u32[]{:S(2)}) collective-permute-start(bf16[4,16,2048]{2,1,0:T(8,128)(2,1)S(1)} %get-tuple-element.94), channel_id=1, source_target_pairs={{0,64},{64,128},{128,192},{192,0},{1,65},{65,129},{129,193},{193,1... | collective-permute-start | bytes 786440 | tf_op jit(solution)/shard_map/ppermute | solution.py:13
  86.3 1.6 %collective-permute-start.32 = (bf16[4,16,2048]{2,1,0:T(8,128)(2,1)S(1)}, bf16[4,16,2048]{2,1,0:T(8,128)(2,1)S(1)}, u32[]{:S(2)}, u32[]{:S(2)}) collective-permute-start(bf16[4,16,2048]{2,1,0:T(8,128)(2,1)S(1)} %get-tuple-element.95), channel_id=1, source_target_pairs={{0,192},{64,0},{128,64},{192,128},{1,193},{65,1},{129,65},{193,129... | collective-permute-start | bytes 786440 | tf_op jit(solution)/shard_map/ppermute | solution.py:13
  87.9 7.5 %collective-permute-done.28 = bf16[4,16,2048]{2,1,0:T(8,128)(2,1)S(1)} collective-permute-done((bf16[4,16,2048]{2,1,0:T(8,128)(2,1)S(1)}, bf16[4,16,2048]{2,1,0:T(8,128)(2,1)S(1)}, u32[]{:S(2)}, u32[]{:S(2)}) %collective-permute-start.28) | collective-permute-done | bytes 262176 | tf_op jit(solution)/shard_map/ppermute | solution.py:13
  96.8 2.1 %collective-permute-start.30 = (bf16[4,8,2048]{2,1,0:T(8,128)(2,1)S(1)}, bf16[4,8,2048]{2,1,0:T(8,128)(2,1)S(1)}, u32[]{:S(2)}, u32[]{:S(2)}) collective-permute-start(bf16[4,8,2048]{2,1,0:T(8,128)(2,1)S(1)} %get-tuple-element.108), channel_id=1, source_target_pairs={{0,0},{4,20},{8,8},{12,28},{16,16},{20,36},{24,24},{28,44},{32,32}... | collective-permute-start | bytes 393224 | tf_op jit(solution)/shard_map/ppermute | solution.py:21
  98.9 5.7 %collective-permute-done.33 = bf16[4,16,2048]{2,1,0:T(8,128)(2,1)S(1)} collective-permute-done((bf16[4,16,2048]{2,1,0:T(8,128)(2,1)S(1)}, bf16[4,16,2048]{2,1,0:T(8,128)(2,1)S(1)}, u32[]{:S(2)}, u32[]{:S(2)}) %collective-permute-start.33) | collective-permute-done | bytes 262176 | tf_op jit(solution)/shard_map/ppermute | solution.py:13
  107.1 2.8 %collective-permute-start.36 = (bf16[4,8,2048]{2,1,0:T(8,128)(2,1)S(1)}, bf16[4,8,2048]{2,1,0:T(8,128)(2,1)S(1)}, u32[]{:S(2)}, u32[]{:S(2)}) collective-permute-start(bf16[4,8,2048]{2,1,0:T(8,128)(2,1)S(1)} %get-tuple-element.106), channel_id=1, source_target_pairs={{0,40},{4,28},{8,48},{12,36},{16,56},{20,44},{24,0},{28,52},{32,8}... | collective-permute-start | bytes 393224 | tf_op jit(solution)/shard_map/ppermute | solution.py:21
  109.9 7.1 %collective-permute-done.35 = bf16[4,8,2048]{2,1,0:T(8,128)(2,1)S(1)} collective-permute-done((bf16[4,8,2048]{2,1,0:T(8,128)(2,1)S(1)}, bf16[4,8,2048]{2,1,0:T(8,128)(2,1)S(1)}, u32[]{:S(2)}, u32[]{:S(2)}) %collective-permute-start.35) | collective-permute-done | bytes 131104 | tf_op jit(solution)/shard_map/ppermute | solution.py:21
  117.0 2.1 %collective-permute-done.36 = bf16[4,8,2048]{2,1,0:T(8,128)(2,1)S(1)} collective-permute-done((bf16[4,8,2048]{2,1,0:T(8,128)(2,1)S(1)}, bf16[4,8,2048]{2,1,0:T(8,128)(2,1)S(1)}, u32[]{:S(2)}, u32[]{:S(2)}) %collective-permute-start.36) | collective-permute-done | bytes 131104 | tf_op jit(solution)/shard_map/ppermute | solution.py:21
  121.9 2.0 %collective-permute-start.38 = (f32[4,2048]{1,0:T(4,128)S(1)}, f32[4,2048]{1,0:T(4,128)S(1)}, u32[]{:S(2)}, u32[]{:S(2)}) collective-permute-start(f32[4,2048]{1,0:T(4,128)S(1)} %get-tuple-element.115), channel_id=1, source_target_pairs={{0,3},{1,0},{2,1},{3,2},{4,7},{5,4},{6,5},{7,6},{8,11},{9,8},{10,9... | collective-permute-start | bytes 98312 | tf_op jit(solution)/shard_map/ppermute | solution.py:13
  (97 shorter events, 29.5 us)
Async XLA Ops:
  0.0 32.2 %collective-permute-start = (bf16[448,2048]{1,0:T(8,128)(2,1)}, bf16[448,2048]{1,0:T(8,128)(2,1)S(1)}, u32[]{:S(2)}, u32[]{:S(2)}) collective-permute-start(bf16[448,2048]{1,0:T(8,128)(2,1)} %bitcast.46), channel_id=1, source_target_pairs={{0,4},{4,0},{1,5},{5,1},{2,6},{6,2},{3,7},{7,3},{8,12},{12,8},{9,1... | collective-permute-start | bytes 5505032 | tf_op jit(solution)/shard_map/ppermute | solution.py:13
  3.2 31.6 %collective-permute-start.1 = (bf16[448,2048]{1,0:T(8,128)(2,1)}, bf16[448,2048]{1,0:T(8,128)(2,1)}, u32[]{:S(2)}, u32[]{:S(2)}) collective-permute-start(bf16[448,2048]{1,0:T(8,128)(2,1)} %bitcast.44), channel_id=1, source_target_pairs={{0,4},{4,0},{1,5},{5,1},{2,6},{6,2},{3,7},{7,3},{8,12},{12,8},{9,1... | collective-permute-start | bytes 5505032 | tf_op jit(solution)/shard_map/ppermute | solution.py:13
  15.1 11.2 %collective-permute-start.5 = (bf16[4,8,2048]{2,1,0:T(8,128)(2,1)S(1)}, bf16[4,8,2048]{2,1,0:T(8,128)(2,1)S(1)}, u32[]{:S(2)}, u32[]{:S(2)}) collective-permute-start(bf16[4,8,2048]{2,1,0:T(8,128)(2,1)S(1)} %copy.11), channel_id=1, source_target_pairs={{0,0},{4,52},{8,8},{12,60},{16,16},{20,4},{24,24},{28,12},{32,32},... | collective-permute-start | bytes 393224 | tf_op jit(solution)/shard_map/ppermute | solution.py:21
  27.7 14.2 %collective-permute-start.11 = (bf16[4,16,2048]{2,1,0:T(8,128)(2,1)S(1)}, bf16[4,16,2048]{2,1,0:T(8,128)(2,1)S(1)}, u32[]{:S(2)}, u32[]{:S(2)}) collective-permute-start(bf16[4,16,2048]{2,1,0:T(8,128)(2,1)S(1)} %constant_dynamic-update-slice_fusion), channel_id=1, source_target_pairs={{0,128},{64,192},{128,0},{192,64},{1,129},{65,193},{129,1},{193,65... | collective-permute-start | bytes 786440 | tf_op jit(solution)/shard_map/ppermute | solution.py:13
  30.7 13.3 %collective-permute-start.10 = (bf16[4,16,2048]{2,1,0:T(8,128)(2,1)S(1)}, bf16[4,16,2048]{2,1,0:T(8,128)(2,1)S(1)}, u32[]{:S(2)}, u32[]{:S(2)}) collective-permute-start(bf16[4,16,2048]{2,1,0:T(8,128)(2,1)S(1)} %constant_dynamic-update-slice_fusion), channel_id=1, source_target_pairs={{0,192},{64,0},{128,64},{192,128},{1,193},{65,1},{129,65},{193,129... | collective-permute-start | bytes 786440 | tf_op jit(solution)/shard_map/ppermute | solution.py:13
  31.5 12.7 %collective-permute-start.9 = (bf16[4,16,2048]{2,1,0:T(8,128)(2,1)S(1)}, bf16[4,16,2048]{2,1,0:T(8,128)(2,1)S(1)}, u32[]{:S(2)}, u32[]{:S(2)}) collective-permute-start(bf16[4,16,2048]{2,1,0:T(8,128)(2,1)S(1)} %constant_dynamic-update-slice_fusion), channel_id=1, source_target_pairs={{0,64},{64,128},{128,192},{192,0},{1,65},{65,129},{129,193},{193,1... | collective-permute-start | bytes 786440 | tf_op jit(solution)/shard_map/ppermute | solution.py:13
  32.2 9.0 %collective-permute-start.8 = (bf16[4,16,2048]{2,1,0:T(8,128)(2,1)S(1)}, bf16[4,16,2048]{2,1,0:T(8,128)(2,1)S(1)}, u32[]{:S(2)}, u32[]{:S(2)}) collective-permute-start(bf16[4,16,2048]{2,1,0:T(8,128)(2,1)S(1)} %constant_dynamic-update-slice_fusion), channel_id=1, source_target_pairs={{0,16},{4,52},{8,24},{12,60},{16,32},{20,4},{24,40},{28,12},{32,48... | collective-permute-start | bytes 786440 | tf_op jit(solution)/shard_map/ppermute | solution.py:21
  34.9 11.8 %collective-permute-start.7 = (bf16[448,2048]{1,0:T(8,128)(2,1)}, bf16[448,2048]{1,0:T(8,128)(2,1)S(1)}, u32[]{:S(2)}, u32[]{:S(2)}) collective-permute-start(bf16[448,2048]{1,0:T(8,128)(2,1)} %param.9), channel_id=1, source_target_pairs={{0,4},{4,0},{1,5},{5,1},{2,6},{6,2},{3,7},{7,3},{8,12},{12,8},{9,1... | collective-permute-start | bytes 5505032 | tf_op jit(solution)/shard_map/ppermute | solution.py:13
  41.2 9.0 %collective-permute-start.14 = (bf16[4,16,2048]{2,1,0:T(8,128)(2,1)S(1)}, bf16[4,16,2048]{2,1,0:T(8,128)(2,1)S(1)}, u32[]{:S(2)}, u32[]{:S(2)}) collective-permute-start(bf16[4,16,2048]{2,1,0:T(8,128)(2,1)S(1)} %collective-permute-done.8), channel_id=1, source_target_pairs={{0,128},{64,192},{128,0},{192,64},{1,129},{65,193},{129,1},{193,65... | collective-permute-start | bytes 786440 | tf_op jit(solution)/shard_map/ppermute | solution.py:13
  41.9 13.9 %collective-permute-start.13 = (bf16[4,16,2048]{2,1,0:T(8,128)(2,1)S(1)}, bf16[4,16,2048]{2,1,0:T(8,128)(2,1)S(1)}, u32[]{:S(2)}, u32[]{:S(2)}) collective-permute-start(bf16[4,16,2048]{2,1,0:T(8,128)(2,1)S(1)} %collective-permute-done.8), channel_id=1, source_target_pairs={{0,192},{64,0},{128,64},{192,128},{1,193},{65,1},{129,65},{193,129... | collective-permute-start | bytes 786440 | tf_op jit(solution)/shard_map/ppermute | solution.py:13
  44.0 12.6 %collective-permute-start.12 = (bf16[4,16,2048]{2,1,0:T(8,128)(2,1)S(1)}, bf16[4,16,2048]{2,1,0:T(8,128)(2,1)S(1)}, u32[]{:S(2)}, u32[]{:S(2)}) collective-permute-start(bf16[4,16,2048]{2,1,0:T(8,128)(2,1)S(1)} %collective-permute-done.8), channel_id=1, source_target_pairs={{0,64},{64,128},{128,192},{192,0},{1,65},{65,129},{129,193},{193,1... | collective-permute-start | bytes 786440 | tf_op jit(solution)/shard_map/ppermute | solution.py:13
  46.5 14.2 %collective-permute-start.17 = (bf16[64,1792]{1,0:T(8,128)(2,1)S(1)}, bf16[64,1792]{1,0:T(8,128)(2,1)S(1)}, u32[]{:S(2)}, u32[]{:S(2)}) collective-permute-start(bf16[64,1792]{1,0:T(8,128)(2,1)S(1)} %get-tuple-element.102), channel_id=1, source_target_pairs={{0,2},{1,3},{2,0},{3,1},{4,6},{5,7},{6,4},{7,5},{8,10},{9,11},{10,... | collective-permute-start | bytes 688136 | tf_op jit(solution)/shard_map/ppermute | solution.py:13
  46.7 14.2 %collective-permute-start.16 = (bf16[64,1792]{1,0:T(8,128)(2,1)S(1)}, bf16[64,1792]{1,0:T(8,128)(2,1)S(1)}, u32[]{:S(2)}, u32[]{:S(2)}) collective-permute-start(bf16[64,1792]{1,0:T(8,128)(2,1)S(1)} %get-tuple-element.103), channel_id=1, source_target_pairs={{0,3},{1,0},{2,1},{3,2},{4,7},{5,4},{6,5},{7,6},{8,11},{9,8},{10,9... | collective-permute-start | bytes 688136 | tf_op jit(solution)/shard_map/ppermute | solution.py:13
  50.3 10.6 %collective-permute-start.15 = (bf16[64,1792]{1,0:T(8,128)(2,1)S(1)}, bf16[64,1792]{1,0:T(8,128)(2,1)S(1)}, u32[]{:S(2)}, u32[]{:S(2)}) collective-permute-start(bf16[64,1792]{1,0:T(8,128)(2,1)S(1)} %get-tuple-element.104), channel_id=1, source_target_pairs={{0,1},{1,2},{2,3},{3,0},{4,5},{5,6},{6,7},{7,4},{8,9},{9,10},{10,1... | collective-permute-start | bytes 688136 | tf_op jit(solution)/shard_map/ppermute | solution.py:13
  58.9 8.3 %collective-permute-start.20 = (bf16[64,1792]{1,0:T(8,128)(2,1)S(1)}, bf16[64,1792]{1,0:T(8,128)(2,1)S(1)}, u32[]{:S(2)}, u32[]{:S(2)}) collective-permute-start(bf16[64,1792]{1,0:T(8,128)(2,1)S(1)} %get-tuple-element.99), channel_id=1, source_target_pairs={{0,2},{1,3},{2,0},{3,1},{4,6},{5,7},{6,4},{7,5},{8,10},{9,11},{10,... | collective-permute-start | bytes 688136 | tf_op jit(solution)/shard_map/ppermute | solution.py:13
  59.0 10.5 %collective-permute-start.19 = (bf16[64,1792]{1,0:T(8,128)(2,1)S(1)}, bf16[64,1792]{1,0:T(8,128)(2,1)S(1)}, u32[]{:S(2)}, u32[]{:S(2)}) collective-permute-start(bf16[64,1792]{1,0:T(8,128)(2,1)S(1)} %get-tuple-element.100), channel_id=1, source_target_pairs={{0,3},{1,0},{2,1},{3,2},{4,7},{5,4},{6,5},{7,6},{8,11},{9,8},{10,9... | collective-permute-start | bytes 688136 | tf_op jit(solution)/shard_map/ppermute | solution.py:13
  60.8 12.1 %collective-permute-start.18 = (bf16[64,1792]{1,0:T(8,128)(2,1)S(1)}, bf16[64,1792]{1,0:T(8,128)(2,1)S(1)}, u32[]{:S(2)}, u32[]{:S(2)}) collective-permute-start(bf16[64,1792]{1,0:T(8,128)(2,1)S(1)} %get-tuple-element.101), channel_id=1, source_target_pairs={{0,1},{1,2},{2,3},{3,0},{4,5},{5,6},{6,7},{7,4},{8,9},{9,10},{10,1... | collective-permute-start | bytes 688136 | tf_op jit(solution)/shard_map/ppermute | solution.py:13
  61.1 15.1 %collective-permute-start.23 = (bf16[64,896]{1,0:T(8,128)(2,1)S(1)}, bf16[64,896]{1,0:T(8,128)(2,1)S(1)}, u32[]{:S(2)}, u32[]{:S(2)}) collective-permute-start(bf16[64,896]{1,0:T(8,128)(2,1)S(1)} %fusion.17), channel_id=1, source_target_pairs={{0,1},{1,2},{2,3},{3,0},{4,5},{5,6},{6,7},{7,4},{8,9},{9,10},{10,1... | collective-permute-start | bytes 344072 | tf_op jit(solution)/shard_map/ppermute | solution.py:13
  62.0 15.0 %collective-permute-start.22 = (bf16[64,896]{1,0:T(8,128)(2,1)S(1)}, bf16[64,896]{1,0:T(8,128)(2,1)S(1)}, u32[]{:S(2)}, u32[]{:S(2)}) collective-permute-start(bf16[64,896]{1,0:T(8,128)(2,1)S(1)} %fusion.17), channel_id=1, source_target_pairs={{0,2},{1,3},{2,0},{3,1},{4,6},{5,7},{6,4},{7,5},{8,10},{9,11},{10,... | collective-permute-start | bytes 344072 | tf_op jit(solution)/shard_map/ppermute | solution.py:13
  67.2 9.8 %collective-permute-start.21 = (bf16[64,896]{1,0:T(8,128)(2,1)S(1)}, bf16[64,896]{1,0:T(8,128)(2,1)S(1)}, u32[]{:S(2)}, u32[]{:S(2)}) collective-permute-start(bf16[64,896]{1,0:T(8,128)(2,1)S(1)} %fusion.17), channel_id=1, source_target_pairs={{0,3},{1,0},{2,1},{3,2},{4,7},{5,4},{6,5},{7,6},{8,11},{9,8},{10,9... | collective-permute-start | bytes 344072 | tf_op jit(solution)/shard_map/ppermute | solution.py:13
  73.1 8.4 %collective-permute-start.26 = (bf16[64,896]{1,0:T(8,128)(2,1)S(1)}, bf16[64,896]{1,0:T(8,128)(2,1)S(1)}, u32[]{:S(2)}, u32[]{:S(2)}) collective-permute-start(bf16[64,896]{1,0:T(8,128)(2,1)S(1)} %fusion.16), channel_id=1, source_target_pairs={{0,1},{1,2},{2,3},{3,0},{4,5},{5,6},{6,7},{7,4},{8,9},{9,10},{10,1... | collective-permute-start | bytes 344072 | tf_op jit(solution)/shard_map/ppermute | solution.py:13
  73.4 9.1 %collective-permute-start.25 = (bf16[64,896]{1,0:T(8,128)(2,1)S(1)}, bf16[64,896]{1,0:T(8,128)(2,1)S(1)}, u32[]{:S(2)}, u32[]{:S(2)}) collective-permute-start(bf16[64,896]{1,0:T(8,128)(2,1)S(1)} %fusion.16), channel_id=1, source_target_pairs={{0,2},{1,3},{2,0},{3,1},{4,6},{5,7},{6,4},{7,5},{8,10},{9,11},{10,... | collective-permute-start | bytes 344072 | tf_op jit(solution)/shard_map/ppermute | solution.py:13
  78.6 7.7 %collective-permute-start.29 = (bf16[4,16,2048]{2,1,0:T(8,128)(2,1)S(1)}, bf16[4,16,2048]{2,1,0:T(8,128)(2,1)S(1)}, u32[]{:S(2)}, u32[]{:S(2)}) collective-permute-start(bf16[4,16,2048]{2,1,0:T(8,128)(2,1)S(1)} %get-tuple-element.96), channel_id=1, source_target_pairs={{0,128},{64,192},{128,0},{192,64},{1,129},{65,193},{129,1},{193,65... | collective-permute-start | bytes 786440 | tf_op jit(solution)/shard_map/ppermute | solution.py:13
  78.9 16.5 %collective-permute-start.28 = (bf16[4,16,2048]{2,1,0:T(8,128)(2,1)S(1)}, bf16[4,16,2048]{2,1,0:T(8,128)(2,1)S(1)}, u32[]{:S(2)}, u32[]{:S(2)}) collective-permute-start(bf16[4,16,2048]{2,1,0:T(8,128)(2,1)S(1)} %get-tuple-element.97), channel_id=1, source_target_pairs={{0,64},{64,128},{128,192},{192,0},{1,65},{65,129},{129,193},{193,1... | collective-permute-start | bytes 786440 | tf_op jit(solution)/shard_map/ppermute | solution.py:13
  81.4 14.0 %collective-permute-start.27 = (bf16[4,16,2048]{2,1,0:T(8,128)(2,1)S(1)}, bf16[4,16,2048]{2,1,0:T(8,128)(2,1)S(1)}, u32[]{:S(2)}, u32[]{:S(2)}) collective-permute-start(bf16[4,16,2048]{2,1,0:T(8,128)(2,1)S(1)} %get-tuple-element.98), channel_id=1, source_target_pairs={{0,192},{64,0},{128,64},{192,128},{1,193},{65,1},{129,65},{193,129... | collective-permute-start | bytes 786440 | tf_op jit(solution)/shard_map/ppermute | solution.py:13
  84.1 14.9 %collective-permute-start.34 = (bf16[4,16,2048]{2,1,0:T(8,128)(2,1)S(1)}, bf16[4,16,2048]{2,1,0:T(8,128)(2,1)S(1)}, u32[]{:S(2)}, u32[]{:S(2)}) collective-permute-start(bf16[4,16,2048]{2,1,0:T(8,128)(2,1)S(1)} %get-tuple-element.93), channel_id=1, source_target_pairs={{0,128},{64,192},{128,0},{192,64},{1,129},{65,193},{129,1},{193,65... | collective-permute-start | bytes 786440 | tf_op jit(solution)/shard_map/ppermute | solution.py:13
  84.9 19.8 %collective-permute-start.33 = (bf16[4,16,2048]{2,1,0:T(8,128)(2,1)S(1)}, bf16[4,16,2048]{2,1,0:T(8,128)(2,1)S(1)}, u32[]{:S(2)}, u32[]{:S(2)}) collective-permute-start(bf16[4,16,2048]{2,1,0:T(8,128)(2,1)S(1)} %get-tuple-element.94), channel_id=1, source_target_pairs={{0,64},{64,128},{128,192},{192,0},{1,65},{65,129},{129,193},{193,1... | collective-permute-start | bytes 786440 | tf_op jit(solution)/shard_map/ppermute | solution.py:13
  86.3 18.3 %collective-permute-start.32 = (bf16[4,16,2048]{2,1,0:T(8,128)(2,1)S(1)}, bf16[4,16,2048]{2,1,0:T(8,128)(2,1)S(1)}, u32[]{:S(2)}, u32[]{:S(2)}) collective-permute-start(bf16[4,16,2048]{2,1,0:T(8,128)(2,1)S(1)} %get-tuple-element.95), channel_id=1, source_target_pairs={{0,192},{64,0},{128,64},{192,128},{1,193},{65,1},{129,65},{193,129... | collective-permute-start | bytes 786440 | tf_op jit(solution)/shard_map/ppermute | solution.py:13
  95.6 9.1 %collective-permute-start.31 = (bf16[4,8,2048]{2,1,0:T(8,128)(2,1)S(1)}, bf16[4,8,2048]{2,1,0:T(8,128)(2,1)S(1)}, u32[]{:S(2)}, u32[]{:S(2)}) collective-permute-start(bf16[4,8,2048]{2,1,0:T(8,128)(2,1)S(1)} %get-tuple-element.107), channel_id=1, source_target_pairs={{0,56},{4,12},{8,0},{12,20},{16,8},{20,28},{24,16},{28,36},{32,24}... | collective-permute-start | bytes 393224 | tf_op jit(solution)/shard_map/ppermute | solution.py:21
  96.8 9.2 %collective-permute-start.30 = (bf16[4,8,2048]{2,1,0:T(8,128)(2,1)S(1)}, bf16[4,8,2048]{2,1,0:T(8,128)(2,1)S(1)}, u32[]{:S(2)}, u32[]{:S(2)}) collective-permute-start(bf16[4,8,2048]{2,1,0:T(8,128)(2,1)S(1)} %get-tuple-element.108), channel_id=1, source_target_pairs={{0,0},{4,20},{8,8},{12,28},{16,16},{20,36},{24,24},{28,44},{32,32}... | collective-permute-start | bytes 393224 | tf_op jit(solution)/shard_map/ppermute | solution.py:21
  106.2 10.8 %collective-permute-start.35 = (bf16[4,8,2048]{2,1,0:T(8,128)(2,1)S(1)}, bf16[4,8,2048]{2,1,0:T(8,128)(2,1)S(1)}, u32[]{:S(2)}, u32[]{:S(2)}) collective-permute-start(bf16[4,8,2048]{2,1,0:T(8,128)(2,1)S(1)} %get-tuple-element.105), channel_id=1, source_target_pairs={{0,48},{4,36},{8,56},{12,44},{16,0},{20,52},{24,8},{28,60},{32,16}... | collective-permute-start | bytes 393224 | tf_op jit(solution)/shard_map/ppermute | solution.py:21
  107.1 12.0 %collective-permute-start.36 = (bf16[4,8,2048]{2,1,0:T(8,128)(2,1)S(1)}, bf16[4,8,2048]{2,1,0:T(8,128)(2,1)S(1)}, u32[]{:S(2)}, u32[]{:S(2)}) collective-permute-start(bf16[4,8,2048]{2,1,0:T(8,128)(2,1)S(1)} %get-tuple-element.106), channel_id=1, source_target_pairs={{0,40},{4,28},{8,48},{12,36},{16,56},{20,44},{24,0},{28,52},{32,8}... | collective-permute-start | bytes 393224 | tf_op jit(solution)/shard_map/ppermute | solution.py:21
  (11 other events, 68.3 us)

commit v12 on v11

--- a/solution.py
+++ b/solution.py
@@ -64,8 +64,7 @@
         return (jax.nn.silu(both[:, :units]) * both[:, units:]).astype(BF16)
 
     def spread(hidden):
-        one, three, two = (shift(hidden, "x", -k) for k in (1, 3, 2))
-        return [one, two, three]
+        return [shift(hidden, "x", -k) for k in (1, 3, 2)]
 
     def down(weights, everyone):
         return lax.dot_general(
@@ -136,7 +135,7 @@
     mine = jnp.where(core == 0, low, high)
     other = jnp.where(core == 0, high, low).astype(BF16)
     mine = mine + shift(other, "c", 1).astype(F32)
-    columns = [mine[0]] + [shift(mine[k], "x", k) for k in (1, 2, 3)]
+    columns = [mine[0]] + [shift(mine[place], "x", k) for k, place in ((1, 1), (2, 3), (3, 2))]
     ordered = [columns[0]] * 4
     for k in (1, 2, 3):
         ordered = [

time: 127 us -> 127 us (level)
    ppermute x34, waiting for transfers between devices: 37.3 us -> 38.8 us  [shift(): return lax.ppermute(value, axis, [(i, (i + step) % n) for i in range(n)])]
  transfers between devices with their start and end apart: 41 -> 41, of which waited for: 22 -> 23; matrix products, arithmetic and copies ran while one was open for 11% -> 11% of each run, Pallas kernels for 0% -> 0%
where the time goes in v12:
time: 127 us
  waiting for transfers between devices  55.3 us (44%)
  starting transfers between devices  51.8 us (41%)
  other arithmetic  8.16 us (6%)
  matrix products  6.81 us (5%)
  blocking collectives  3.76 us (3%)
    ppermute x34, waiting for transfers between devices, shift(): return lax.ppermute(value, axis, [(i, (i + step) % n) for i in range(n)])  38.8 us
    ppermute x34, starting transfers between devices, shift(): return lax.ppermute(value, axis, [(i, (i + step) % n) for i in range(n)])  34.1 us
    ppermute x7, starting transfers between devices, along_z(): return lax.ppermute(value, ('z', 'c'), pairs)  17.8 us
    ppermute x7, waiting for transfers between devices, along_z(): return lax.ppermute(value, ('z', 'c'), pairs)  16.5 us
    dot_general x2, matrix products, project(): lax.dot_general(block.reshape(-1, part), weights, (((1,), (1,)), ((), ())...  4.23 us
    all_gather x1, blocking collectives, local(): pair = lax.all_gather(own, 'c', axis=1, tiled=True)  3.76 us
    concatenate x1, other arithmetic, local(): first, far = together(jnp.concatenate(first, axis=0), far)  3.61 us
    dot_general x2, matrix products, down(): lax.dot_general(jnp.concatenate(everyone, axis=0), weights, (((1,), (0,))...  2.57 us
  transfers between devices with their start and end apart: 41, of which 23 were waited for; matrix products, arithmetic and copies ran while one was open for 11% of the time, Pallas kernels for 0%

profile of v12, /device:TPU:1, one launch (start us, length us, event | category | flops | bytes accessed | tf_op | source)
XLA Modules:
  0.0 126.9 jit_solution(17021758378709861070)
XLA Ops:
  0.0 3.2 %collective-permute-start = (bf16[448,2048]{1,0:T(8,128)(2,1)}, bf16[448,2048]{1,0:T(8,128)(2,1)S(1)}, u32[]{:S(2)}, u32[]{:S(2)}) collective-permute-start(bf16[448,2048]{1,0:T(8,128)(2,1)} %bitcast.46), channel_id=1, source_target_pairs={{0,4},{4,0},{1,5},{5,1},{2,6},{6,2},{3,7},{7,3},{8,12},{12,8},{9,1... | collective-permute-start | bytes 5505032 | tf_op jit(solution)/shard_map/ppermute | solution.py:13
  7.9 1.6 %collective-permute-done.3 = bf16[4,2048]{1,0:T(4,128)(2,1)S(1)} collective-permute-done((bf16[4,2048]{1,0:T(4,128)(2,1)S(1)}, bf16[4,2048]{1,0:T(4,128)(2,1)S(1)}, u32[]{:S(2)}, u32[]{:S(2)}) %collective-permute-start.3) | collective-permute-done | bytes 16416 | tf_op jit(solution)/shard_map/ppermute | solution.py:13
  9.6 1.6 %collective-permute-done.4 = bf16[4,2048]{1,0:T(4,128)(2,1)S(1)} collective-permute-done((bf16[4,2048]{1,0:T(4,128)(2,1)S(1)}, bf16[4,2048]{1,0:T(4,128)(2,1)S(1)}, u32[]{:S(2)}, u32[]{:S(2)}) %collective-permute-start.4) | collective-permute-done | bytes 16416 | tf_op jit(solution)/shard_map/ppermute | solution.py:13
  11.2 3.8 %all_gather.3 = bf16[4,8,2048]{2,0,1:T(4,128)(2,1)S(1)} all-gather(bf16[4,4,2048]{2,0,1:T(4,128)(2,1)S(1)} %copy.10), channel_id=1, replica_groups=mesh['y'=4,'z'=8,'c'=2,'x'=4] {'c'}, dimensions={1}, use_global_device_ids=true | all-gather | bytes 196608 | tf_op jit(solution)/shard_map/all_gather | solution.py:49
  15.1 7.9 %collective-permute-start.5 = (bf16[4,8,2048]{2,1,0:T(8,128)(2,1)S(1)}, bf16[4,8,2048]{2,1,0:T(8,128)(2,1)S(1)}, u32[]{:S(2)}, u32[]{:S(2)}) collective-permute-start(bf16[4,8,2048]{2,1,0:T(8,128)(2,1)S(1)} %copy.11), channel_id=1, source_target_pairs={{0,0},{4,52},{8,8},{12,60},{16,16},{20,4},{24,24},{28,12},{32,32},... | collective-permute-start | bytes 393224 | tf_op jit(solution)/shard_map/ppermute | solution.py:21
  23.8 2.5 %collective-permute-done.5 = bf16[4,8,2048]{2,1,0:T(8,128)(2,1)S(1)} collective-permute-done((bf16[4,8,2048]{2,1,0:T(8,128)(2,1)S(1)}, bf16[4,8,2048]{2,1,0:T(8,128)(2,1)S(1)}, u32[]{:S(2)}, u32[]{:S(2)}) %collective-permute-start.5) | collective-permute-done | bytes 131104 | tf_op jit(solution)/shard_map/ppermute | solution.py:21
  26.3 1.4 %collective-permute-done.6 = bf16[4,8,2048]{2,1,0:T(8,128)(2,1)S(1)} collective-permute-done((bf16[4,8,2048]{2,1,0:T(8,128)(2,1)S(1)}, bf16[4,8,2048]{2,1,0:T(8,128)(2,1)S(1)}, u32[]{:S(2)}, u32[]{:S(2)}) %collective-permute-start.6) | collective-permute-done | bytes 131104 | tf_op jit(solution)/shard_map/ppermute | solution.py:21
  27.7 3.0 %collective-permute-start.11 = (bf16[4,16,2048]{2,1,0:T(8,128)(2,1)S(1)}, bf16[4,16,2048]{2,1,0:T(8,128)(2,1)S(1)}, u32[]{:S(2)}, u32[]{:S(2)}) collective-permute-start(bf16[4,16,2048]{2,1,0:T(8,128)(2,1)S(1)} %constant_dynamic-update-slice_fusion), channel_id=1, source_target_pairs={{0,128},{64,192},{128,0},{192,64},{1,129},{65,193},{129,1},{193,65... | collective-permute-start | bytes 786440 | tf_op jit(solution)/shard_map/ppermute | solution.py:13
  32.2 2.6 %collective-permute-start.8 = (bf16[4,16,2048]{2,1,0:T(8,128)(2,1)S(1)}, bf16[4,16,2048]{2,1,0:T(8,128)(2,1)S(1)}, u32[]{:S(2)}, u32[]{:S(2)}) collective-permute-start(bf16[4,16,2048]{2,1,0:T(8,128)(2,1)S(1)} %constant_dynamic-update-slice_fusion), channel_id=1, source_target_pairs={{0,16},{4,52},{8,24},{12,60},{16,32},{20,4},{24,40},{28,12},{32,48... | collective-permute-start | bytes 786440 | tf_op jit(solution)/shard_map/ppermute | solution.py:21
  34.9 3.6 %pad_maximum_fusion = bf16[1792,2048]{1,0:T(8,128)(2,1)S(1)} fusion(bf16[448,2048]{1,0:T(8,128)(2,1)} %collective-permute-done.1, bf16[448,2048]{1,0:T(8,128)(2,1)} %bitcast.45, bf16[448,2048]{1,0:T(8,128)(2,1)S(1)} %collective-permute-done, bf16[448,2048]{1,0:T(8,128)(2,1)} %bitcast.47), kind=kLoop, calls=%fused_computation | loop fusion | flops 29360128 | bytes 14680064 | tf_op jit(solution)/shard_map/concatenate | solution.py:93
  38.5 2.7 %collective-permute-done.8 = bf16[4,16,2048]{2,1,0:T(8,128)(2,1)S(1)} collective-permute-done((bf16[4,16,2048]{2,1,0:T(8,128)(2,1)S(1)}, bf16[4,16,2048]{2,1,0:T(8,128)(2,1)S(1)}, u32[]{:S(2)}, u32[]{:S(2)}) %collective-permute-start.8) | collective-permute-done | bytes 262176 | tf_op jit(solution)/shard_map/ppermute | solution.py:21
  41.9 2.1 %collective-permute-start.13 = (bf16[4,16,2048]{2,1,0:T(8,128)(2,1)S(1)}, bf16[4,16,2048]{2,1,0:T(8,128)(2,1)S(1)}, u32[]{:S(2)}, u32[]{:S(2)}) collective-permute-start(bf16[4,16,2048]{2,1,0:T(8,128)(2,1)S(1)} %collective-permute-done.8), channel_id=1, source_target_pairs={{0,192},{64,0},{128,64},{192,128},{1,193},{65,1},{129,65},{193,129... | collective-permute-start | bytes 786440 | tf_op jit(solution)/shard_map/ppermute | solution.py:13
  44.3 2.1 %fusion.32 = (bf16[256,1792]{1,0:T(8,128)(2,1)S(1)}, f32[256,1792]{1,0:T(8,128)S(1)}) fusion(bf16[256,2048]{1,0:T(8,128)(2,1)S(1)} %bitcast.49, bf16[1792,2048]{1,0:T(8,128)(2,1)S(1)} %pad_maximum_fusion), kind=kOutput, calls=%fused_computation.65 | convolution fusion | flops 1879506944 | bytes 11141120 | tf_op jit(solution)/shard_map/dot_general | solution.py:54
  46.7 1.8 %collective-permute-start.16 = (bf16[64,1792]{1,0:T(8,128)(2,1)S(1)}, bf16[64,1792]{1,0:T(8,128)(2,1)S(1)}, u32[]{:S(2)}, u32[]{:S(2)}) collective-permute-start(bf16[64,1792]{1,0:T(8,128)(2,1)S(1)} %get-tuple-element.103), channel_id=1, source_target_pairs={{0,3},{1,0},{2,1},{3,2},{4,7},{5,4},{6,5},{7,6},{8,11},{9,8},{10,9... | collective-permute-start | bytes 688136 | tf_op jit(solution)/shard_map/ppermute | solution.py:13
  50.3 5.6 %collective-permute-done.13 = bf16[4,16,2048]{2,1,0:T(8,128)(2,1)S(1)} collective-permute-done((bf16[4,16,2048]{2,1,0:T(8,128)(2,1)S(1)}, bf16[4,16,2048]{2,1,0:T(8,128)(2,1)S(1)}, u32[]{:S(2)}, u32[]{:S(2)}) %collective-permute-start.13) | collective-permute-done | bytes 262176 | tf_op jit(solution)/shard_map/ppermute | solution.py:13
  56.7 2.1 %fusion.33 = (bf16[256,1792]{1,0:T(8,128)(2,1)S(1)}, f32[256,1792]{1,0:T(8,128)S(1)}) fusion(bf16[256,2048]{1,0:T(8,128)(2,1)S(1)} %bitcast.48, bf16[1792,2048]{1,0:T(8,128)(2,1)S(1)} %pad_maximum_fusion), kind=kOutput, calls=%fused_computation.66 | convolution fusion | flops 1879506944 | bytes 11141120 | tf_op jit(solution)/shard_map/dot_general | solution.py:54
  59.0 1.8 %collective-permute-start.19 = (bf16[64,1792]{1,0:T(8,128)(2,1)S(1)}, bf16[64,1792]{1,0:T(8,128)(2,1)S(1)}, u32[]{:S(2)}, u32[]{:S(2)}) collective-permute-start(bf16[64,1792]{1,0:T(8,128)(2,1)S(1)} %get-tuple-element.100), channel_id=1, source_target_pairs={{0,3},{1,0},{2,1},{3,2},{4,7},{5,4},{6,5},{7,6},{8,11},{9,8},{10,9... | collective-permute-start | bytes 688136 | tf_op jit(solution)/shard_map/ppermute | solution.py:13
  61.1 2.7 %collective-permute-start.23 = (bf16[64,896]{1,0:T(8,128)(2,1)S(1)}, bf16[64,896]{1,0:T(8,128)(2,1)S(1)}, u32[]{:S(2)}, u32[]{:S(2)}) collective-permute-start(bf16[64,896]{1,0:T(8,128)(2,1)S(1)} %fusion.17), channel_id=1, source_target_pairs={{0,2},{1,3},{2,0},{3,1},{4,6},{5,7},{6,4},{7,5},{8,10},{9,11},{10,... | collective-permute-start | bytes 344072 | tf_op jit(solution)/shard_map/ppermute | solution.py:13
  64.4 2.8 %collective-permute-done.20 = bf16[64,1792]{1,0:T(8,128)(2,1)S(1)} collective-permute-done((bf16[64,1792]{1,0:T(8,128)(2,1)S(1)}, bf16[64,1792]{1,0:T(8,128)(2,1)S(1)}, u32[]{:S(2)}, u32[]{:S(2)}) %collective-permute-start.20) | collective-permute-done | bytes 229408 | tf_op jit(solution)/shard_map/ppermute | solution.py:13
  67.2 2.3 %collective-permute-done.19 = bf16[64,1792]{1,0:T(8,128)(2,1)S(1)} collective-permute-done((bf16[64,1792]{1,0:T(8,128)(2,1)S(1)}, bf16[64,1792]{1,0:T(8,128)(2,1)S(1)}, u32[]{:S(2)}, u32[]{:S(2)}) %collective-permute-start.19) | collective-permute-done | bytes 229408 | tf_op jit(solution)/shard_map/ppermute | solution.py:13
  69.5 4.2 %collective-permute-done.18 = bf16[64,1792]{1,0:T(8,128)(2,1)S(1)} collective-permute-done((bf16[64,1792]{1,0:T(8,128)(2,1)S(1)}, bf16[64,1792]{1,0:T(8,128)(2,1)S(1)}, u32[]{:S(2)}, u32[]{:S(2)}) %collective-permute-start.18) | collective-permute-done | bytes 229408 | tf_op jit(solution)/shard_map/ppermute | solution.py:13
  74.6 2.2 %collective-permute-start.24 = (bf16[64,896]{1,0:T(8,128)(2,1)S(1)}, bf16[64,896]{1,0:T(8,128)(2,1)S(1)}, u32[]{:S(2)}, u32[]{:S(2)}) collective-permute-start(bf16[64,896]{1,0:T(8,128)(2,1)S(1)} %fusion.16), channel_id=1, source_target_pairs={{0,3},{1,0},{2,1},{3,2},{4,7},{5,4},{6,5},{7,6},{8,11},{9,8},{10,9... | collective-permute-start | bytes 344072 | tf_op jit(solution)/shard_map/ppermute | solution.py:13
  80.2 2.0 %collective-permute-start.28 = (bf16[4,16,2048]{2,1,0:T(8,128)(2,1)S(1)}, bf16[4,16,2048]{2,1,0:T(8,128)(2,1)S(1)}, u32[]{:S(2)}, u32[]{:S(2)}) collective-permute-start(bf16[4,16,2048]{2,1,0:T(8,128)(2,1)S(1)} %get-tuple-element.97), channel_id=1, source_target_pairs={{0,64},{64,128},{128,192},{192,0},{1,65},{65,129},{129,193},{193,1... | collective-permute-start | bytes 786440 | tf_op jit(solution)/shard_map/ppermute | solution.py:13
  87.0 1.4 %collective-permute-done.29 = bf16[4,16,2048]{2,1,0:T(8,128)(2,1)S(1)} collective-permute-done((bf16[4,16,2048]{2,1,0:T(8,128)(2,1)S(1)}, bf16[4,16,2048]{2,1,0:T(8,128)(2,1)S(1)}, u32[]{:S(2)}, u32[]{:S(2)}) %collective-permute-start.29) | collective-permute-done | bytes 262176 | tf_op jit(solution)/shard_map/ppermute | solution.py:13
  88.4 2.2 %collective-permute-start.32 = (bf16[4,16,2048]{2,1,0:T(8,128)(2,1)S(1)}, bf16[4,16,2048]{2,1,0:T(8,128)(2,1)S(1)}, u32[]{:S(2)}, u32[]{:S(2)}) collective-permute-start(bf16[4,16,2048]{2,1,0:T(8,128)(2,1)S(1)} %get-tuple-element.95), channel_id=1, source_target_pairs={{0,192},{64,0},{128,64},{192,128},{1,193},{65,1},{129,65},{193,129... | collective-permute-start | bytes 786440 | tf_op jit(solution)/shard_map/ppermute | solution.py:13
  90.6 5.0 %collective-permute-done.28 = bf16[4,16,2048]{2,1,0:T(8,128)(2,1)S(1)} collective-permute-done((bf16[4,16,2048]{2,1,0:T(8,128)(2,1)S(1)}, bf16[4,16,2048]{2,1,0:T(8,128)(2,1)S(1)}, u32[]{:S(2)}, u32[]{:S(2)}) %collective-permute-start.28) | collective-permute-done | bytes 262176 | tf_op jit(solution)/shard_map/ppermute | solution.py:13
  95.9 3.0 %collective-permute-start.30 = (bf16[4,8,2048]{2,1,0:T(8,128)(2,1)S(1)}, bf16[4,8,2048]{2,1,0:T(8,128)(2,1)S(1)}, u32[]{:S(2)}, u32[]{:S(2)}) collective-permute-start(bf16[4,8,2048]{2,1,0:T(8,128)(2,1)S(1)} %get-tuple-element.108), channel_id=1, source_target_pairs={{0,0},{4,20},{8,8},{12,28},{16,16},{20,36},{24,24},{28,44},{32,32}... | collective-permute-start | bytes 393224 | tf_op jit(solution)/shard_map/ppermute | solution.py:21
  99.7 6.4 %collective-permute-done.33 = bf16[4,16,2048]{2,1,0:T(8,128)(2,1)S(1)} collective-permute-done((bf16[4,16,2048]{2,1,0:T(8,128)(2,1)S(1)}, bf16[4,16,2048]{2,1,0:T(8,128)(2,1)S(1)}, u32[]{:S(2)}, u32[]{:S(2)}) %collective-permute-start.33) | collective-permute-done | bytes 262176 | tf_op jit(solution)/shard_map/ppermute | solution.py:13
  107.0 2.5 %collective-permute-start.36 = (bf16[4,8,2048]{2,1,0:T(8,128)(2,1)S(1)}, bf16[4,8,2048]{2,1,0:T(8,128)(2,1)S(1)}, u32[]{:S(2)}, u32[]{:S(2)}) collective-permute-start(bf16[4,8,2048]{2,1,0:T(8,128)(2,1)S(1)} %get-tuple-element.106), channel_id=1, source_target_pairs={{0,40},{4,28},{8,48},{12,36},{16,56},{20,44},{24,0},{28,52},{32,8}... | collective-permute-start | bytes 393224 | tf_op jit(solution)/shard_map/ppermute | solution.py:21
  109.5 4.9 %collective-permute-done.35 = bf16[4,8,2048]{2,1,0:T(8,128)(2,1)S(1)} collective-permute-done((bf16[4,8,2048]{2,1,0:T(8,128)(2,1)S(1)}, bf16[4,8,2048]{2,1,0:T(8,128)(2,1)S(1)}, u32[]{:S(2)}, u32[]{:S(2)}) %collective-permute-start.35) | collective-permute-done | bytes 131104 | tf_op jit(solution)/shard_map/ppermute | solution.py:21
  114.3 5.0 %collective-permute-done.36 = bf16[4,8,2048]{2,1,0:T(8,128)(2,1)S(1)} collective-permute-done((bf16[4,8,2048]{2,1,0:T(8,128)(2,1)S(1)}, bf16[4,8,2048]{2,1,0:T(8,128)(2,1)S(1)}, u32[]{:S(2)}, u32[]{:S(2)}) %collective-permute-start.36) | collective-permute-done | bytes 131104 | tf_op jit(solution)/shard_map/ppermute | solution.py:21
  122.2 1.5 %collective-permute-start.38 = (f32[4,2048]{1,0:T(4,128)S(1)}, f32[4,2048]{1,0:T(4,128)S(1)}, u32[]{:S(2)}, u32[]{:S(2)}) collective-permute-start(f32[4,2048]{1,0:T(4,128)S(1)} %get-tuple-element.115), channel_id=1, source_target_pairs={{0,3},{1,0},{2,1},{3,2},{4,7},{5,4},{6,5},{7,6},{8,11},{9,8},{10,9... | collective-permute-start | bytes 98312 | tf_op jit(solution)/shard_map/ppermute | solution.py:13
  (97 shorter events, 28.9 us)
Async XLA Ops:
  0.0 32.2 %collective-permute-start = (bf16[448,2048]{1,0:T(8,128)(2,1)}, bf16[448,2048]{1,0:T(8,128)(2,1)S(1)}, u32[]{:S(2)}, u32[]{:S(2)}) collective-permute-start(bf16[448,2048]{1,0:T(8,128)(2,1)} %bitcast.46), channel_id=1, source_target_pairs={{0,4},{4,0},{1,5},{5,1},{2,6},{6,2},{3,7},{7,3},{8,12},{12,8},{9,1... | collective-permute-start | bytes 5505032 | tf_op jit(solution)/shard_map/ppermute | solution.py:13
  3.2 31.6 %collective-permute-start.1 = (bf16[448,2048]{1,0:T(8,128)(2,1)}, bf16[448,2048]{1,0:T(8,128)(2,1)}, u32[]{:S(2)}, u32[]{:S(2)}) collective-permute-start(bf16[448,2048]{1,0:T(8,128)(2,1)} %bitcast.44), channel_id=1, source_target_pairs={{0,4},{4,0},{1,5},{5,1},{2,6},{6,2},{3,7},{7,3},{8,12},{12,8},{9,1... | collective-permute-start | bytes 5505032 | tf_op jit(solution)/shard_map/ppermute | solution.py:13
  15.1 11.2 %collective-permute-start.5 = (bf16[4,8,2048]{2,1,0:T(8,128)(2,1)S(1)}, bf16[4,8,2048]{2,1,0:T(8,128)(2,1)S(1)}, u32[]{:S(2)}, u32[]{:S(2)}) collective-permute-start(bf16[4,8,2048]{2,1,0:T(8,128)(2,1)S(1)} %copy.11), channel_id=1, source_target_pairs={{0,0},{4,52},{8,8},{12,60},{16,16},{20,4},{24,24},{28,12},{32,32},... | collective-permute-start | bytes 393224 | tf_op jit(solution)/shard_map/ppermute | solution.py:21
  27.7 14.2 %collective-permute-start.11 = (bf16[4,16,2048]{2,1,0:T(8,128)(2,1)S(1)}, bf16[4,16,2048]{2,1,0:T(8,128)(2,1)S(1)}, u32[]{:S(2)}, u32[]{:S(2)}) collective-permute-start(bf16[4,16,2048]{2,1,0:T(8,128)(2,1)S(1)} %constant_dynamic-update-slice_fusion), channel_id=1, source_target_pairs={{0,128},{64,192},{128,0},{192,64},{1,129},{65,193},{129,1},{193,65... | collective-permute-start | bytes 786440 | tf_op jit(solution)/shard_map/ppermute | solution.py:13
  30.7 13.3 %collective-permute-start.10 = (bf16[4,16,2048]{2,1,0:T(8,128)(2,1)S(1)}, bf16[4,16,2048]{2,1,0:T(8,128)(2,1)S(1)}, u32[]{:S(2)}, u32[]{:S(2)}) collective-permute-start(bf16[4,16,2048]{2,1,0:T(8,128)(2,1)S(1)} %constant_dynamic-update-slice_fusion), channel_id=1, source_target_pairs={{0,192},{64,0},{128,64},{192,128},{1,193},{65,1},{129,65},{193,129... | collective-permute-start | bytes 786440 | tf_op jit(solution)/shard_map/ppermute | solution.py:13
  31.5 12.7 %collective-permute-start.9 = (bf16[4,16,2048]{2,1,0:T(8,128)(2,1)S(1)}, bf16[4,16,2048]{2,1,0:T(8,128)(2,1)S(1)}, u32[]{:S(2)}, u32[]{:S(2)}) collective-permute-start(bf16[4,16,2048]{2,1,0:T(8,128)(2,1)S(1)} %constant_dynamic-update-slice_fusion), channel_id=1, source_target_pairs={{0,64},{64,128},{128,192},{192,0},{1,65},{65,129},{129,193},{193,1... | collective-permute-start | bytes 786440 | tf_op jit(solution)/shard_map/ppermute | solution.py:13
  32.2 9.0 %collective-permute-start.8 = (bf16[4,16,2048]{2,1,0:T(8,128)(2,1)S(1)}, bf16[4,16,2048]{2,1,0:T(8,128)(2,1)S(1)}, u32[]{:S(2)}, u32[]{:S(2)}) collective-permute-start(bf16[4,16,2048]{2,1,0:T(8,128)(2,1)S(1)} %constant_dynamic-update-slice_fusion), channel_id=1, source_target_pairs={{0,16},{4,52},{8,24},{12,60},{16,32},{20,4},{24,40},{28,12},{32,48... | collective-permute-start | bytes 786440 | tf_op jit(solution)/shard_map/ppermute | solution.py:21
  34.9 11.8 %collective-permute-start.7 = (bf16[448,2048]{1,0:T(8,128)(2,1)}, bf16[448,2048]{1,0:T(8,128)(2,1)S(1)}, u32[]{:S(2)}, u32[]{:S(2)}) collective-permute-start(bf16[448,2048]{1,0:T(8,128)(2,1)} %param.9), channel_id=1, source_target_pairs={{0,4},{4,0},{1,5},{5,1},{2,6},{6,2},{3,7},{7,3},{8,12},{12,8},{9,1... | collective-permute-start | bytes 5505032 | tf_op jit(solution)/shard_map/ppermute | solution.py:13
  41.2 9.0 %collective-permute-start.14 = (bf16[4,16,2048]{2,1,0:T(8,128)(2,1)S(1)}, bf16[4,16,2048]{2,1,0:T(8,128)(2,1)S(1)}, u32[]{:S(2)}, u32[]{:S(2)}) collective-permute-start(bf16[4,16,2048]{2,1,0:T(8,128)(2,1)S(1)} %collective-permute-done.8), channel_id=1, source_target_pairs={{0,128},{64,192},{128,0},{192,64},{1,129},{65,193},{129,1},{193,65... | collective-permute-start | bytes 786440 | tf_op jit(solution)/shard_map/ppermute | solution.py:13
  41.9 13.9 %collective-permute-start.13 = (bf16[4,16,2048]{2,1,0:T(8,128)(2,1)S(1)}, bf16[4,16,2048]{2,1,0:T(8,128)(2,1)S(1)}, u32[]{:S(2)}, u32[]{:S(2)}) collective-permute-start(bf16[4,16,2048]{2,1,0:T(8,128)(2,1)S(1)} %collective-permute-done.8), channel_id=1, source_target_pairs={{0,192},{64,0},{128,64},{192,128},{1,193},{65,1},{129,65},{193,129... | collective-permute-start | bytes 786440 | tf_op jit(solution)/shard_map/ppermute | solution.py:13
  44.0 12.6 %collective-permute-start.12 = (bf16[4,16,2048]{2,1,0:T(8,128)(2,1)S(1)}, bf16[4,16,2048]{2,1,0:T(8,128)(2,1)S(1)}, u32[]{:S(2)}, u32[]{:S(2)}) collective-permute-start(bf16[4,16,2048]{2,1,0:T(8,128)(2,1)S(1)} %collective-permute-done.8), channel_id=1, source_target_pairs={{0,64},{64,128},{128,192},{192,0},{1,65},{65,129},{129,193},{193,1... | collective-permute-start | bytes 786440 | tf_op jit(solution)/shard_map/ppermute | solution.py:13
  46.5 14.2 %collective-permute-start.17 = (bf16[64,1792]{1,0:T(8,128)(2,1)S(1)}, bf16[64,1792]{1,0:T(8,128)(2,1)S(1)}, u32[]{:S(2)}, u32[]{:S(2)}) collective-permute-start(bf16[64,1792]{1,0:T(8,128)(2,1)S(1)} %get-tuple-element.102), channel_id=1, source_target_pairs={{0,2},{1,3},{2,0},{3,1},{4,6},{5,7},{6,4},{7,5},{8,10},{9,11},{10,... | collective-permute-start | bytes 688136 | tf_op jit(solution)/shard_map/ppermute | solution.py:13
  46.7 14.2 %collective-permute-start.16 = (bf16[64,1792]{1,0:T(8,128)(2,1)S(1)}, bf16[64,1792]{1,0:T(8,128)(2,1)S(1)}, u32[]{:S(2)}, u32[]{:S(2)}) collective-permute-start(bf16[64,1792]{1,0:T(8,128)(2,1)S(1)} %get-tuple-element.103), channel_id=1, source_target_pairs={{0,3},{1,0},{2,1},{3,2},{4,7},{5,4},{6,5},{7,6},{8,11},{9,8},{10,9... | collective-permute-start | bytes 688136 | tf_op jit(solution)/shard_map/ppermute | solution.py:13
  50.3 10.6 %collective-permute-start.15 = (bf16[64,1792]{1,0:T(8,128)(2,1)S(1)}, bf16[64,1792]{1,0:T(8,128)(2,1)S(1)}, u32[]{:S(2)}, u32[]{:S(2)}) collective-permute-start(bf16[64,1792]{1,0:T(8,128)(2,1)S(1)} %get-tuple-element.104), channel_id=1, source_target_pairs={{0,1},{1,2},{2,3},{3,0},{4,5},{5,6},{6,7},{7,4},{8,9},{9,10},{10,1... | collective-permute-start | bytes 688136 | tf_op jit(solution)/shard_map/ppermute | solution.py:13
  58.9 8.3 %collective-permute-start.20 = (bf16[64,1792]{1,0:T(8,128)(2,1)S(1)}, bf16[64,1792]{1,0:T(8,128)(2,1)S(1)}, u32[]{:S(2)}, u32[]{:S(2)}) collective-permute-start(bf16[64,1792]{1,0:T(8,128)(2,1)S(1)} %get-tuple-element.99), channel_id=1, source_target_pairs={{0,2},{1,3},{2,0},{3,1},{4,6},{5,7},{6,4},{7,5},{8,10},{9,11},{10,... | collective-permute-start | bytes 688136 | tf_op jit(solution)/shard_map/ppermute | solution.py:13
  59.0 10.5 %collective-permute-start.19 = (bf16[64,1792]{1,0:T(8,128)(2,1)S(1)}, bf16[64,1792]{1,0:T(8,128)(2,1)S(1)}, u32[]{:S(2)}, u32[]{:S(2)}) collective-permute-start(bf16[64,1792]{1,0:T(8,128)(2,1)S(1)} %get-tuple-element.100), channel_id=1, source_target_pairs={{0,3},{1,0},{2,1},{3,2},{4,7},{5,4},{6,5},{7,6},{8,11},{9,8},{10,9... | collective-permute-start | bytes 688136 | tf_op jit(solution)/shard_map/ppermute | solution.py:13
  60.8 12.9 %collective-permute-start.18 = (bf16[64,1792]{1,0:T(8,128)(2,1)S(1)}, bf16[64,1792]{1,0:T(8,128)(2,1)S(1)}, u32[]{:S(2)}, u32[]{:S(2)}) collective-permute-start(bf16[64,1792]{1,0:T(8,128)(2,1)S(1)} %get-tuple-element.101), channel_id=1, source_target_pairs={{0,1},{1,2},{2,3},{3,0},{4,5},{5,6},{6,7},{7,4},{8,9},{9,10},{10,1... | collective-permute-start | bytes 688136 | tf_op jit(solution)/shard_map/ppermute | solution.py:13
  61.1 13.5 %collective-permute-start.23 = (bf16[64,896]{1,0:T(8,128)(2,1)S(1)}, bf16[64,896]{1,0:T(8,128)(2,1)S(1)}, u32[]{:S(2)}, u32[]{:S(2)}) collective-permute-start(bf16[64,896]{1,0:T(8,128)(2,1)S(1)} %fusion.17), channel_id=1, source_target_pairs={{0,2},{1,3},{2,0},{3,1},{4,6},{5,7},{6,4},{7,5},{8,10},{9,11},{10,... | collective-permute-start | bytes 344072 | tf_op jit(solution)/shard_map/ppermute | solution.py:13
  63.8 14.0 %collective-permute-start.22 = (bf16[64,896]{1,0:T(8,128)(2,1)S(1)}, bf16[64,896]{1,0:T(8,128)(2,1)S(1)}, u32[]{:S(2)}, u32[]{:S(2)}) collective-permute-start(bf16[64,896]{1,0:T(8,128)(2,1)S(1)} %fusion.17), channel_id=1, source_target_pairs={{0,1},{1,2},{2,3},{3,0},{4,5},{5,6},{6,7},{7,4},{8,9},{9,10},{10,1... | collective-permute-start | bytes 344072 | tf_op jit(solution)/shard_map/ppermute | solution.py:13
  67.2 10.6 %collective-permute-start.21 = (bf16[64,896]{1,0:T(8,128)(2,1)S(1)}, bf16[64,896]{1,0:T(8,128)(2,1)S(1)}, u32[]{:S(2)}, u32[]{:S(2)}) collective-permute-start(bf16[64,896]{1,0:T(8,128)(2,1)S(1)} %fusion.17), channel_id=1, source_target_pairs={{0,3},{1,0},{2,1},{3,2},{4,7},{5,4},{6,5},{7,6},{8,11},{9,8},{10,9... | collective-permute-start | bytes 344072 | tf_op jit(solution)/shard_map/ppermute | solution.py:13
  73.9 8.4 %collective-permute-start.26 = (bf16[64,896]{1,0:T(8,128)(2,1)S(1)}, bf16[64,896]{1,0:T(8,128)(2,1)S(1)}, u32[]{:S(2)}, u32[]{:S(2)}) collective-permute-start(bf16[64,896]{1,0:T(8,128)(2,1)S(1)} %fusion.16), channel_id=1, source_target_pairs={{0,2},{1,3},{2,0},{3,1},{4,6},{5,7},{6,4},{7,5},{8,10},{9,11},{10,... | collective-permute-start | bytes 344072 | tf_op jit(solution)/shard_map/ppermute | solution.py:13
  74.0 8.9 %collective-permute-start.25 = (bf16[64,896]{1,0:T(8,128)(2,1)S(1)}, bf16[64,896]{1,0:T(8,128)(2,1)S(1)}, u32[]{:S(2)}, u32[]{:S(2)}) collective-permute-start(bf16[64,896]{1,0:T(8,128)(2,1)S(1)} %fusion.16), channel_id=1, source_target_pairs={{0,1},{1,2},{2,3},{3,0},{4,5},{5,6},{6,7},{7,4},{8,9},{9,10},{10,1... | collective-permute-start | bytes 344072 | tf_op jit(solution)/shard_map/ppermute | solution.py:13
  74.6 8.3 %collective-permute-start.24 = (bf16[64,896]{1,0:T(8,128)(2,1)S(1)}, bf16[64,896]{1,0:T(8,128)(2,1)S(1)}, u32[]{:S(2)}, u32[]{:S(2)}) collective-permute-start(bf16[64,896]{1,0:T(8,128)(2,1)S(1)} %fusion.16), channel_id=1, source_target_pairs={{0,3},{1,0},{2,1},{3,2},{4,7},{5,4},{6,5},{7,6},{8,11},{9,8},{10,9... | collective-permute-start | bytes 344072 | tf_op jit(solution)/shard_map/ppermute | solution.py:13
  79.4 9.0 %collective-permute-start.29 = (bf16[4,16,2048]{2,1,0:T(8,128)(2,1)S(1)}, bf16[4,16,2048]{2,1,0:T(8,128)(2,1)S(1)}, u32[]{:S(2)}, u32[]{:S(2)}) collective-permute-start(bf16[4,16,2048]{2,1,0:T(8,128)(2,1)S(1)} %get-tuple-element.96), channel_id=1, source_target_pairs={{0,128},{64,192},{128,0},{192,64},{1,129},{65,193},{129,1},{193,65... | collective-permute-start | bytes 786440 | tf_op jit(solution)/shard_map/ppermute | solution.py:13
  80.2 15.4 %collective-permute-start.28 = (bf16[4,16,2048]{2,1,0:T(8,128)(2,1)S(1)}, bf16[4,16,2048]{2,1,0:T(8,128)(2,1)S(1)}, u32[]{:S(2)}, u32[]{:S(2)}) collective-permute-start(bf16[4,16,2048]{2,1,0:T(8,128)(2,1)S(1)} %get-tuple-element.97), channel_id=1, source_target_pairs={{0,64},{64,128},{128,192},{192,0},{1,65},{65,129},{129,193},{193,1... | collective-permute-start | bytes 786440 | tf_op jit(solution)/shard_map/ppermute | solution.py:13
  82.2 13.4 %collective-permute-start.27 = (bf16[4,16,2048]{2,1,0:T(8,128)(2,1)S(1)}, bf16[4,16,2048]{2,1,0:T(8,128)(2,1)S(1)}, u32[]{:S(2)}, u32[]{:S(2)}) collective-permute-start(bf16[4,16,2048]{2,1,0:T(8,128)(2,1)S(1)} %get-tuple-element.98), channel_id=1, source_target_pairs={{0,192},{64,0},{128,64},{192,128},{1,193},{65,1},{129,65},{193,129... | collective-permute-start | bytes 786440 | tf_op jit(solution)/shard_map/ppermute | solution.py:13
  84.4 15.3 %collective-permute-start.34 = (bf16[4,16,2048]{2,1,0:T(8,128)(2,1)S(1)}, bf16[4,16,2048]{2,1,0:T(8,128)(2,1)S(1)}, u32[]{:S(2)}, u32[]{:S(2)}) collective-permute-start(bf16[4,16,2048]{2,1,0:T(8,128)(2,1)S(1)} %get-tuple-element.93), channel_id=1, source_target_pairs={{0,128},{64,192},{128,0},{192,64},{1,129},{65,193},{129,1},{193,65... | collective-permute-start | bytes 786440 | tf_op jit(solution)/shard_map/ppermute | solution.py:13
  85.7 20.4 %collective-permute-start.33 = (bf16[4,16,2048]{2,1,0:T(8,128)(2,1)S(1)}, bf16[4,16,2048]{2,1,0:T(8,128)(2,1)S(1)}, u32[]{:S(2)}, u32[]{:S(2)}) collective-permute-start(bf16[4,16,2048]{2,1,0:T(8,128)(2,1)S(1)} %get-tuple-element.94), channel_id=1, source_target_pairs={{0,64},{64,128},{128,192},{192,0},{1,65},{65,129},{129,193},{193,1... | collective-permute-start | bytes 786440 | tf_op jit(solution)/shard_map/ppermute | solution.py:13
  88.4 17.7 %collective-permute-start.32 = (bf16[4,16,2048]{2,1,0:T(8,128)(2,1)S(1)}, bf16[4,16,2048]{2,1,0:T(8,128)(2,1)S(1)}, u32[]{:S(2)}, u32[]{:S(2)}) collective-permute-start(bf16[4,16,2048]{2,1,0:T(8,128)(2,1)S(1)} %get-tuple-element.95), channel_id=1, source_target_pairs={{0,192},{64,0},{128,64},{192,128},{1,193},{65,1},{129,65},{193,129... | collective-permute-start | bytes 786440 | tf_op jit(solution)/shard_map/ppermute | solution.py:13
  95.8 10.3 %collective-permute-start.31 = (bf16[4,8,2048]{2,1,0:T(8,128)(2,1)S(1)}, bf16[4,8,2048]{2,1,0:T(8,128)(2,1)S(1)}, u32[]{:S(2)}, u32[]{:S(2)}) collective-permute-start(bf16[4,8,2048]{2,1,0:T(8,128)(2,1)S(1)} %get-tuple-element.107), channel_id=1, source_target_pairs={{0,56},{4,12},{8,0},{12,20},{16,8},{20,28},{24,16},{28,36},{32,24}... | collective-permute-start | bytes 393224 | tf_op jit(solution)/shard_map/ppermute | solution.py:21
  95.9 10.1 %collective-permute-start.30 = (bf16[4,8,2048]{2,1,0:T(8,128)(2,1)S(1)}, bf16[4,8,2048]{2,1,0:T(8,128)(2,1)S(1)}, u32[]{:S(2)}, u32[]{:S(2)}) collective-permute-start(bf16[4,8,2048]{2,1,0:T(8,128)(2,1)S(1)} %get-tuple-element.108), channel_id=1, source_target_pairs={{0,0},{4,20},{8,8},{12,28},{16,16},{20,36},{24,24},{28,44},{32,32}... | collective-permute-start | bytes 393224 | tf_op jit(solution)/shard_map/ppermute | solution.py:21
  107.0 12.3 %collective-permute-start.36 = (bf16[4,8,2048]{2,1,0:T(8,128)(2,1)S(1)}, bf16[4,8,2048]{2,1,0:T(8,128)(2,1)S(1)}, u32[]{:S(2)}, u32[]{:S(2)}) collective-permute-start(bf16[4,8,2048]{2,1,0:T(8,128)(2,1)S(1)} %get-tuple-element.106), channel_id=1, source_target_pairs={{0,40},{4,28},{8,48},{12,36},{16,56},{20,44},{24,0},{28,52},{32,8}... | collective-permute-start | bytes 393224 | tf_op jit(solution)/shard_map/ppermute | solution.py:21
  (11 other events, 70.1 us)

commit v13 on v11

--- a/solution.py
+++ b/solution.py
@@ -136,7 +136,7 @@
     mine = jnp.where(core == 0, low, high)
     other = jnp.where(core == 0, high, low).astype(BF16)
     mine = mine + shift(other, "c", 1).astype(F32)
-    columns = [mine[0]] + [shift(mine[k], "x", k) for k in (1, 2, 3)]
+    columns = [mine[0]] + [shift(mine[k].astype(BF16), "x", k).astype(F32) for k in (1, 2, 3)]
     ordered = [columns[0]] * 4
     for k in (1, 2, 3):
         ordered = [

time: 127 us -> 127 us (level)
  no operation moved by 1% of the time
where the time goes in v13:
time: 127 us; the launch traced here: 126 us
  waiting for transfers between devices  54.2 us (43%)
  starting transfers between devices  52.3 us (41%)
  other arithmetic  8.17 us (6%)
  matrix products  6.81 us (5%)
  blocking collectives  3.76 us (3%)
    ppermute x34, waiting for transfers between devices, shift(): return lax.ppermute(value, axis, [(i, (i + step) % n) for i in range(n)])  37 us
    ppermute x34, starting transfers between devices, shift(): return lax.ppermute(value, axis, [(i, (i + step) % n) for i in range(n)])  34 us
    ppermute x7, starting transfers between devices, along_z(): return lax.ppermute(value, ('z', 'c'), pairs)  18.4 us
    ppermute x7, waiting for transfers between devices, along_z(): return lax.ppermute(value, ('z', 'c'), pairs)  17.2 us
    dot_general x2, matrix products, project(): lax.dot_general(block.reshape(-1, part), weights, (((1,), (1,)), ((), ())...  4.23 us
    all_gather x1, blocking collectives, local(): pair = lax.all_gather(own, 'c', axis=1, tiled=True)  3.76 us
    concatenate x1, other arithmetic, local(): first, far = together(jnp.concatenate(first, axis=0), far)  3.61 us
    dot_general x2, matrix products, down(): lax.dot_general(jnp.concatenate(everyone, axis=0), weights, (((1,), (0,))...  2.58 us
  transfers between devices with their start and end apart: 41, of which 22 were waited for; matrix products, arithmetic and copies ran while one was open for 11% of the time, Pallas kernels for 0%

profile of v13, /device:TPU:1, one launch (start us, length us, event | category | flops | bytes accessed | tf_op | source)
XLA Modules:
  0.0 126.3 jit_solution(10922962425136830670)
XLA Ops:
  0.0 3.2 %collective-permute-start = (bf16[448,2048]{1,0:T(8,128)(2,1)}, bf16[448,2048]{1,0:T(8,128)(2,1)S(1)}, u32[]{:S(2)}, u32[]{:S(2)}) collective-permute-start(bf16[448,2048]{1,0:T(8,128)(2,1)} %bitcast.46), channel_id=1, source_target_pairs={{0,4},{4,0},{1,5},{5,1},{2,6},{6,2},{3,7},{7,3},{8,12},{12,8},{9,1... | collective-permute-start | bytes 5505032 | tf_op jit(solution)/shard_map/ppermute | solution.py:13
  7.9 1.6 %collective-permute-done.3 = bf16[4,2048]{1,0:T(4,128)(2,1)S(1)} collective-permute-done((bf16[4,2048]{1,0:T(4,128)(2,1)S(1)}, bf16[4,2048]{1,0:T(4,128)(2,1)S(1)}, u32[]{:S(2)}, u32[]{:S(2)}) %collective-permute-start.3) | collective-permute-done | bytes 16416 | tf_op jit(solution)/shard_map/ppermute | solution.py:13
  9.6 1.6 %collective-permute-done.4 = bf16[4,2048]{1,0:T(4,128)(2,1)S(1)} collective-permute-done((bf16[4,2048]{1,0:T(4,128)(2,1)S(1)}, bf16[4,2048]{1,0:T(4,128)(2,1)S(1)}, u32[]{:S(2)}, u32[]{:S(2)}) %collective-permute-start.4) | collective-permute-done | bytes 16416 | tf_op jit(solution)/shard_map/ppermute | solution.py:13
  11.2 3.8 %all_gather.3 = bf16[4,8,2048]{2,0,1:T(4,128)(2,1)S(1)} all-gather(bf16[4,4,2048]{2,0,1:T(4,128)(2,1)S(1)} %copy.10), channel_id=1, replica_groups=mesh['y'=4,'z'=8,'c'=2,'x'=4] {'c'}, dimensions={1}, use_global_device_ids=true | all-gather | bytes 196608 | tf_op jit(solution)/shard_map/all_gather | solution.py:49
  15.1 7.9 %collective-permute-start.5 = (bf16[4,8,2048]{2,1,0:T(8,128)(2,1)S(1)}, bf16[4,8,2048]{2,1,0:T(8,128)(2,1)S(1)}, u32[]{:S(2)}, u32[]{:S(2)}) collective-permute-start(bf16[4,8,2048]{2,1,0:T(8,128)(2,1)S(1)} %copy.11), channel_id=1, source_target_pairs={{0,0},{4,52},{8,8},{12,60},{16,16},{20,4},{24,24},{28,12},{32,32},... | collective-permute-start | bytes 393224 | tf_op jit(solution)/shard_map/ppermute | solution.py:21
  23.8 2.5 %collective-permute-done.5 = bf16[4,8,2048]{2,1,0:T(8,128)(2,1)S(1)} collective-permute-done((bf16[4,8,2048]{2,1,0:T(8,128)(2,1)S(1)}, bf16[4,8,2048]{2,1,0:T(8,128)(2,1)S(1)}, u32[]{:S(2)}, u32[]{:S(2)}) %collective-permute-start.5) | collective-permute-done | bytes 131104 | tf_op jit(solution)/shard_map/ppermute | solution.py:21
  26.3 1.4 %collective-permute-done.6 = bf16[4,8,2048]{2,1,0:T(8,128)(2,1)S(1)} collective-permute-done((bf16[4,8,2048]{2,1,0:T(8,128)(2,1)S(1)}, bf16[4,8,2048]{2,1,0:T(8,128)(2,1)S(1)}, u32[]{:S(2)}, u32[]{:S(2)}) %collective-permute-start.6) | collective-permute-done | bytes 131104 | tf_op jit(solution)/shard_map/ppermute | solution.py:21
  27.7 3.0 %collective-permute-start.11 = (bf16[4,16,2048]{2,1,0:T(8,128)(2,1)S(1)}, bf16[4,16,2048]{2,1,0:T(8,128)(2,1)S(1)}, u32[]{:S(2)}, u32[]{:S(2)}) collective-permute-start(bf16[4,16,2048]{2,1,0:T(8,128)(2,1)S(1)} %constant_dynamic-update-slice_fusion), channel_id=1, source_target_pairs={{0,128},{64,192},{128,0},{192,64},{1,129},{65,193},{129,1},{193,65... | collective-permute-start | bytes 786440 | tf_op jit(solution)/shard_map/ppermute | solution.py:13
  32.2 2.6 %collective-permute-start.8 = (bf16[4,16,2048]{2,1,0:T(8,128)(2,1)S(1)}, bf16[4,16,2048]{2,1,0:T(8,128)(2,1)S(1)}, u32[]{:S(2)}, u32[]{:S(2)}) collective-permute-start(bf16[4,16,2048]{2,1,0:T(8,128)(2,1)S(1)} %constant_dynamic-update-slice_fusion), channel_id=1, source_target_pairs={{0,16},{4,52},{8,24},{12,60},{16,32},{20,4},{24,40},{28,12},{32,48... | collective-permute-start | bytes 786440 | tf_op jit(solution)/shard_map/ppermute | solution.py:21
  34.9 3.6 %pad_maximum_fusion = bf16[1792,2048]{1,0:T(8,128)(2,1)S(1)} fusion(bf16[448,2048]{1,0:T(8,128)(2,1)} %collective-permute-done.1, bf16[448,2048]{1,0:T(8,128)(2,1)} %bitcast.45, bf16[448,2048]{1,0:T(8,128)(2,1)S(1)} %collective-permute-done, bf16[448,2048]{1,0:T(8,128)(2,1)} %bitcast.47), kind=kLoop, calls=%fused_computation | loop fusion | flops 29360128 | bytes 14680064 | tf_op jit(solution)/shard_map/concatenate | solution.py:94
  38.5 2.7 %collective-permute-done.8 = bf16[4,16,2048]{2,1,0:T(8,128)(2,1)S(1)} collective-permute-done((bf16[4,16,2048]{2,1,0:T(8,128)(2,1)S(1)}, bf16[4,16,2048]{2,1,0:T(8,128)(2,1)S(1)}, u32[]{:S(2)}, u32[]{:S(2)}) %collective-permute-start.8) | collective-permute-done | bytes 262176 | tf_op jit(solution)/shard_map/ppermute | solution.py:21
  41.9 2.1 %collective-permute-start.13 = (bf16[4,16,2048]{2,1,0:T(8,128)(2,1)S(1)}, bf16[4,16,2048]{2,1,0:T(8,128)(2,1)S(1)}, u32[]{:S(2)}, u32[]{:S(2)}) collective-permute-start(bf16[4,16,2048]{2,1,0:T(8,128)(2,1)S(1)} %collective-permute-done.8), channel_id=1, source_target_pairs={{0,192},{64,0},{128,64},{192,128},{1,193},{65,1},{129,65},{193,129... | collective-permute-start | bytes 786440 | tf_op jit(solution)/shard_map/ppermute | solution.py:13
  44.3 2.1 %fusion.33 = (bf16[256,1792]{1,0:T(8,128)(2,1)S(1)}, f32[256,1792]{1,0:T(8,128)S(1)}) fusion(bf16[256,2048]{1,0:T(8,128)(2,1)S(1)} %bitcast.49, bf16[1792,2048]{1,0:T(8,128)(2,1)S(1)} %pad_maximum_fusion), kind=kOutput, calls=%fused_computation.74 | convolution fusion | flops 1879506944 | bytes 11141120 | tf_op jit(solution)/shard_map/dot_general | solution.py:54
  46.7 1.8 %collective-permute-start.16 = (bf16[64,1792]{1,0:T(8,128)(2,1)S(1)}, bf16[64,1792]{1,0:T(8,128)(2,1)S(1)}, u32[]{:S(2)}, u32[]{:S(2)}) collective-permute-start(bf16[64,1792]{1,0:T(8,128)(2,1)S(1)} %get-tuple-element.105), channel_id=1, source_target_pairs={{0,3},{1,0},{2,1},{3,2},{4,7},{5,4},{6,5},{7,6},{8,11},{9,8},{10,9... | collective-permute-start | bytes 688136 | tf_op jit(solution)/shard_map/ppermute | solution.py:13
  50.3 5.6 %collective-permute-done.13 = bf16[4,16,2048]{2,1,0:T(8,128)(2,1)S(1)} collective-permute-done((bf16[4,16,2048]{2,1,0:T(8,128)(2,1)S(1)}, bf16[4,16,2048]{2,1,0:T(8,128)(2,1)S(1)}, u32[]{:S(2)}, u32[]{:S(2)}) %collective-permute-start.13) | collective-permute-done | bytes 262176 | tf_op jit(solution)/shard_map/ppermute | solution.py:13
  56.7 2.1 %fusion.34 = (bf16[256,1792]{1,0:T(8,128)(2,1)S(1)}, f32[256,1792]{1,0:T(8,128)S(1)}) fusion(bf16[256,2048]{1,0:T(8,128)(2,1)S(1)} %bitcast.48, bf16[1792,2048]{1,0:T(8,128)(2,1)S(1)} %pad_maximum_fusion), kind=kOutput, calls=%fused_computation.75 | convolution fusion | flops 1879506944 | bytes 11141120 | tf_op jit(solution)/shard_map/dot_general | solution.py:54
  59.0 1.8 %collective-permute-start.19 = (bf16[64,1792]{1,0:T(8,128)(2,1)S(1)}, bf16[64,1792]{1,0:T(8,128)(2,1)S(1)}, u32[]{:S(2)}, u32[]{:S(2)}) collective-permute-start(bf16[64,1792]{1,0:T(8,128)(2,1)S(1)} %get-tuple-element.102), channel_id=1, source_target_pairs={{0,3},{1,0},{2,1},{3,2},{4,7},{5,4},{6,5},{7,6},{8,11},{9,8},{10,9... | collective-permute-start | bytes 688136 | tf_op jit(solution)/shard_map/ppermute | solution.py:13
  62.0 3.0 %collective-permute-start.22 = (bf16[64,896]{1,0:T(8,128)(2,1)S(1)}, bf16[64,896]{1,0:T(8,128)(2,1)S(1)}, u32[]{:S(2)}, u32[]{:S(2)}) collective-permute-start(bf16[64,896]{1,0:T(8,128)(2,1)S(1)} %fusion.17), channel_id=1, source_target_pairs={{0,2},{1,3},{2,0},{3,1},{4,6},{5,7},{6,4},{7,5},{8,10},{9,11},{10,... | collective-permute-start | bytes 344072 | tf_op jit(solution)/shard_map/ppermute | solution.py:13
  65.0 2.2 %collective-permute-done.20 = bf16[64,1792]{1,0:T(8,128)(2,1)S(1)} collective-permute-done((bf16[64,1792]{1,0:T(8,128)(2,1)S(1)}, bf16[64,1792]{1,0:T(8,128)(2,1)S(1)}, u32[]{:S(2)}, u32[]{:S(2)}) %collective-permute-start.20) | collective-permute-done | bytes 229408 | tf_op jit(solution)/shard_map/ppermute | solution.py:13
  67.2 2.3 %collective-permute-done.19 = bf16[64,1792]{1,0:T(8,128)(2,1)S(1)} collective-permute-done((bf16[64,1792]{1,0:T(8,128)(2,1)S(1)}, bf16[64,1792]{1,0:T(8,128)(2,1)S(1)}, u32[]{:S(2)}, u32[]{:S(2)}) %collective-permute-start.19) | collective-permute-done | bytes 229408 | tf_op jit(solution)/shard_map/ppermute | solution.py:13
  69.5 3.4 %collective-permute-done.18 = bf16[64,1792]{1,0:T(8,128)(2,1)S(1)} collective-permute-done((bf16[64,1792]{1,0:T(8,128)(2,1)S(1)}, bf16[64,1792]{1,0:T(8,128)(2,1)S(1)}, u32[]{:S(2)}, u32[]{:S(2)}) %collective-permute-start.18) | collective-permute-done | bytes 229408 | tf_op jit(solution)/shard_map/ppermute | solution.py:13
  73.4 1.5 %collective-permute-start.25 = (bf16[64,896]{1,0:T(8,128)(2,1)S(1)}, bf16[64,896]{1,0:T(8,128)(2,1)S(1)}, u32[]{:S(2)}, u32[]{:S(2)}) collective-permute-start(bf16[64,896]{1,0:T(8,128)(2,1)S(1)} %fusion.16), channel_id=1, source_target_pairs={{0,2},{1,3},{2,0},{3,1},{4,6},{5,7},{6,4},{7,5},{8,10},{9,11},{10,... | collective-permute-start | bytes 344072 | tf_op jit(solution)/shard_map/ppermute | solution.py:13
  78.9 2.5 %collective-permute-start.28 = (bf16[4,16,2048]{2,1,0:T(8,128)(2,1)S(1)}, bf16[4,16,2048]{2,1,0:T(8,128)(2,1)S(1)}, u32[]{:S(2)}, u32[]{:S(2)}) collective-permute-start(bf16[4,16,2048]{2,1,0:T(8,128)(2,1)S(1)} %get-tuple-element.99), channel_id=1, source_target_pairs={{0,64},{64,128},{128,192},{192,0},{1,65},{65,129},{129,193},{193,1... | collective-permute-start | bytes 786440 | tf_op jit(solution)/shard_map/ppermute | solution.py:13
  84.9 1.5 %collective-permute-start.33 = (bf16[4,16,2048]{2,1,0:T(8,128)(2,1)S(1)}, bf16[4,16,2048]{2,1,0:T(8,128)(2,1)S(1)}, u32[]{:S(2)}, u32[]{:S(2)}) collective-permute-start(bf16[4,16,2048]{2,1,0:T(8,128)(2,1)S(1)} %get-tuple-element.96), channel_id=1, source_target_pairs={{0,64},{64,128},{128,192},{192,0},{1,65},{65,129},{129,193},{193,1... | collective-permute-start | bytes 786440 | tf_op jit(solution)/shard_map/ppermute | solution.py:13
  86.3 1.6 %collective-permute-start.32 = (bf16[4,16,2048]{2,1,0:T(8,128)(2,1)S(1)}, bf16[4,16,2048]{2,1,0:T(8,128)(2,1)S(1)}, u32[]{:S(2)}, u32[]{:S(2)}) collective-permute-start(bf16[4,16,2048]{2,1,0:T(8,128)(2,1)S(1)} %get-tuple-element.97), channel_id=1, source_target_pairs={{0,192},{64,0},{128,64},{192,128},{1,193},{65,1},{129,65},{193,129... | collective-permute-start | bytes 786440 | tf_op jit(solution)/shard_map/ppermute | solution.py:13
  87.9 7.5 %collective-permute-done.28 = bf16[4,16,2048]{2,1,0:T(8,128)(2,1)S(1)} collective-permute-done((bf16[4,16,2048]{2,1,0:T(8,128)(2,1)S(1)}, bf16[4,16,2048]{2,1,0:T(8,128)(2,1)S(1)}, u32[]{:S(2)}, u32[]{:S(2)}) %collective-permute-start.28) | collective-permute-done | bytes 262176 | tf_op jit(solution)/shard_map/ppermute | solution.py:13
  96.8 2.1 %collective-permute-start.30 = (bf16[4,8,2048]{2,1,0:T(8,128)(2,1)S(1)}, bf16[4,8,2048]{2,1,0:T(8,128)(2,1)S(1)}, u32[]{:S(2)}, u32[]{:S(2)}) collective-permute-start(bf16[4,8,2048]{2,1,0:T(8,128)(2,1)S(1)} %get-tuple-element.110), channel_id=1, source_target_pairs={{0,0},{4,20},{8,8},{12,28},{16,16},{20,36},{24,24},{28,44},{32,32}... | collective-permute-start | bytes 393224 | tf_op jit(solution)/shard_map/ppermute | solution.py:21
  98.9 5.7 %collective-permute-done.33 = bf16[4,16,2048]{2,1,0:T(8,128)(2,1)S(1)} collective-permute-done((bf16[4,16,2048]{2,1,0:T(8,128)(2,1)S(1)}, bf16[4,16,2048]{2,1,0:T(8,128)(2,1)S(1)}, u32[]{:S(2)}, u32[]{:S(2)}) %collective-permute-start.33) | collective-permute-done | bytes 262176 | tf_op jit(solution)/shard_map/ppermute | solution.py:13
  107.1 2.8 %collective-permute-start.36 = (bf16[4,8,2048]{2,1,0:T(8,128)(2,1)S(1)}, bf16[4,8,2048]{2,1,0:T(8,128)(2,1)S(1)}, u32[]{:S(2)}, u32[]{:S(2)}) collective-permute-start(bf16[4,8,2048]{2,1,0:T(8,128)(2,1)S(1)} %get-tuple-element.108), channel_id=1, source_target_pairs={{0,40},{4,28},{8,48},{12,36},{16,56},{20,44},{24,0},{28,52},{32,8}... | collective-permute-start | bytes 393224 | tf_op jit(solution)/shard_map/ppermute | solution.py:21
  109.9 7.1 %collective-permute-done.35 = bf16[4,8,2048]{2,1,0:T(8,128)(2,1)S(1)} collective-permute-done((bf16[4,8,2048]{2,1,0:T(8,128)(2,1)S(1)}, bf16[4,8,2048]{2,1,0:T(8,128)(2,1)S(1)}, u32[]{:S(2)}, u32[]{:S(2)}) %collective-permute-start.35) | collective-permute-done | bytes 131104 | tf_op jit(solution)/shard_map/ppermute | solution.py:21
  117.0 2.1 %collective-permute-done.36 = bf16[4,8,2048]{2,1,0:T(8,128)(2,1)S(1)} collective-permute-done((bf16[4,8,2048]{2,1,0:T(8,128)(2,1)S(1)}, bf16[4,8,2048]{2,1,0:T(8,128)(2,1)S(1)}, u32[]{:S(2)}, u32[]{:S(2)}) %collective-permute-start.36) | collective-permute-done | bytes 131104 | tf_op jit(solution)/shard_map/ppermute | solution.py:21
  121.9 2.0 %collective-permute-start.38 = (bf16[4,2048]{1,0:T(4,128)(2,1)S(1)}, bf16[4,2048]{1,0:T(4,128)(2,1)S(1)}, u32[]{:S(2)}, u32[]{:S(2)}) collective-permute-start(bf16[4,2048]{1,0:T(4,128)(2,1)S(1)} %get-tuple-element.117), channel_id=1, source_target_pairs={{0,3},{1,0},{2,1},{3,2},{4,7},{5,4},{6,5},{7,6},{8,11},{9,8},{10,9... | collective-permute-start | bytes 49160 | tf_op jit(solution)/shard_map/ppermute | solution.py:13
  (97 shorter events, 29.2 us)
Async XLA Ops:
  0.0 32.2 %collective-permute-start = (bf16[448,2048]{1,0:T(8,128)(2,1)}, bf16[448,2048]{1,0:T(8,128)(2,1)S(1)}, u32[]{:S(2)}, u32[]{:S(2)}) collective-permute-start(bf16[448,2048]{1,0:T(8,128)(2,1)} %bitcast.46), channel_id=1, source_target_pairs={{0,4},{4,0},{1,5},{5,1},{2,6},{6,2},{3,7},{7,3},{8,12},{12,8},{9,1... | collective-permute-start | bytes 5505032 | tf_op jit(solution)/shard_map/ppermute | solution.py:13
  3.2 31.6 %collective-permute-start.1 = (bf16[448,2048]{1,0:T(8,128)(2,1)}, bf16[448,2048]{1,0:T(8,128)(2,1)}, u32[]{:S(2)}, u32[]{:S(2)}) collective-permute-start(bf16[448,2048]{1,0:T(8,128)(2,1)} %bitcast.44), channel_id=1, source_target_pairs={{0,4},{4,0},{1,5},{5,1},{2,6},{6,2},{3,7},{7,3},{8,12},{12,8},{9,1... | collective-permute-start | bytes 5505032 | tf_op jit(solution)/shard_map/ppermute | solution.py:13
  15.1 11.2 %collective-permute-start.5 = (bf16[4,8,2048]{2,1,0:T(8,128)(2,1)S(1)}, bf16[4,8,2048]{2,1,0:T(8,128)(2,1)S(1)}, u32[]{:S(2)}, u32[]{:S(2)}) collective-permute-start(bf16[4,8,2048]{2,1,0:T(8,128)(2,1)S(1)} %copy.11), channel_id=1, source_target_pairs={{0,0},{4,52},{8,8},{12,60},{16,16},{20,4},{24,24},{28,12},{32,32},... | collective-permute-start | bytes 393224 | tf_op jit(solution)/shard_map/ppermute | solution.py:21
  27.7 14.2 %collective-permute-start.11 = (bf16[4,16,2048]{2,1,0:T(8,128)(2,1)S(1)}, bf16[4,16,2048]{2,1,0:T(8,128)(2,1)S(1)}, u32[]{:S(2)}, u32[]{:S(2)}) collective-permute-start(bf16[4,16,2048]{2,1,0:T(8,128)(2,1)S(1)} %constant_dynamic-update-slice_fusion), channel_id=1, source_target_pairs={{0,128},{64,192},{128,0},{192,64},{1,129},{65,193},{129,1},{193,65... | collective-permute-start | bytes 786440 | tf_op jit(solution)/shard_map/ppermute | solution.py:13
  30.7 13.3 %collective-permute-start.10 = (bf16[4,16,2048]{2,1,0:T(8,128)(2,1)S(1)}, bf16[4,16,2048]{2,1,0:T(8,128)(2,1)S(1)}, u32[]{:S(2)}, u32[]{:S(2)}) collective-permute-start(bf16[4,16,2048]{2,1,0:T(8,128)(2,1)S(1)} %constant_dynamic-update-slice_fusion), channel_id=1, source_target_pairs={{0,192},{64,0},{128,64},{192,128},{1,193},{65,1},{129,65},{193,129... | collective-permute-start | bytes 786440 | tf_op jit(solution)/shard_map/ppermute | solution.py:13
  31.5 12.7 %collective-permute-start.9 = (bf16[4,16,2048]{2,1,0:T(8,128)(2,1)S(1)}, bf16[4,16,2048]{2,1,0:T(8,128)(2,1)S(1)}, u32[]{:S(2)}, u32[]{:S(2)}) collective-permute-start(bf16[4,16,2048]{2,1,0:T(8,128)(2,1)S(1)} %constant_dynamic-update-slice_fusion), channel_id=1, source_target_pairs={{0,64},{64,128},{128,192},{192,0},{1,65},{65,129},{129,193},{193,1... | collective-permute-start | bytes 786440 | tf_op jit(solution)/shard_map/ppermute | solution.py:13
  32.2 9.0 %collective-permute-start.8 = (bf16[4,16,2048]{2,1,0:T(8,128)(2,1)S(1)}, bf16[4,16,2048]{2,1,0:T(8,128)(2,1)S(1)}, u32[]{:S(2)}, u32[]{:S(2)}) collective-permute-start(bf16[4,16,2048]{2,1,0:T(8,128)(2,1)S(1)} %constant_dynamic-update-slice_fusion), channel_id=1, source_target_pairs={{0,16},{4,52},{8,24},{12,60},{16,32},{20,4},{24,40},{28,12},{32,48... | collective-permute-start | bytes 786440 | tf_op jit(solution)/shard_map/ppermute | solution.py:21
  34.9 11.8 %collective-permute-start.7 = (bf16[448,2048]{1,0:T(8,128)(2,1)}, bf16[448,2048]{1,0:T(8,128)(2,1)S(1)}, u32[]{:S(2)}, u32[]{:S(2)}) collective-permute-start(bf16[448,2048]{1,0:T(8,128)(2,1)} %param.9), channel_id=1, source_target_pairs={{0,4},{4,0},{1,5},{5,1},{2,6},{6,2},{3,7},{7,3},{8,12},{12,8},{9,1... | collective-permute-start | bytes 5505032 | tf_op jit(solution)/shard_map/ppermute | solution.py:13
  41.2 9.0 %collective-permute-start.14 = (bf16[4,16,2048]{2,1,0:T(8,128)(2,1)S(1)}, bf16[4,16,2048]{2,1,0:T(8,128)(2,1)S(1)}, u32[]{:S(2)}, u32[]{:S(2)}) collective-permute-start(bf16[4,16,2048]{2,1,0:T(8,128)(2,1)S(1)} %collective-permute-done.8), channel_id=1, source_target_pairs={{0,128},{64,192},{128,0},{192,64},{1,129},{65,193},{129,1},{193,65... | collective-permute-start | bytes 786440 | tf_op jit(solution)/shard_map/ppermute | solution.py:13
  41.9 13.9 %collective-permute-start.13 = (bf16[4,16,2048]{2,1,0:T(8,128)(2,1)S(1)}, bf16[4,16,2048]{2,1,0:T(8,128)(2,1)S(1)}, u32[]{:S(2)}, u32[]{:S(2)}) collective-permute-start(bf16[4,16,2048]{2,1,0:T(8,128)(2,1)S(1)} %collective-permute-done.8), channel_id=1, source_target_pairs={{0,192},{64,0},{128,64},{192,128},{1,193},{65,1},{129,65},{193,129... | collective-permute-start | bytes 786440 | tf_op jit(solution)/shard_map/ppermute | solution.py:13
  44.0 12.6 %collective-permute-start.12 = (bf16[4,16,2048]{2,1,0:T(8,128)(2,1)S(1)}, bf16[4,16,2048]{2,1,0:T(8,128)(2,1)S(1)}, u32[]{:S(2)}, u32[]{:S(2)}) collective-permute-start(bf16[4,16,2048]{2,1,0:T(8,128)(2,1)S(1)} %collective-permute-done.8), channel_id=1, source_target_pairs={{0,64},{64,128},{128,192},{192,0},{1,65},{65,129},{129,193},{193,1... | collective-permute-start | bytes 786440 | tf_op jit(solution)/shard_map/ppermute | solution.py:13
  46.5 14.2 %collective-permute-start.17 = (bf16[64,1792]{1,0:T(8,128)(2,1)S(1)}, bf16[64,1792]{1,0:T(8,128)(2,1)S(1)}, u32[]{:S(2)}, u32[]{:S(2)}) collective-permute-start(bf16[64,1792]{1,0:T(8,128)(2,1)S(1)} %get-tuple-element.104), channel_id=1, source_target_pairs={{0,2},{1,3},{2,0},{3,1},{4,6},{5,7},{6,4},{7,5},{8,10},{9,11},{10,... | collective-permute-start | bytes 688136 | tf_op jit(solution)/shard_map/ppermute | solution.py:13
  46.7 14.2 %collective-permute-start.16 = (bf16[64,1792]{1,0:T(8,128)(2,1)S(1)}, bf16[64,1792]{1,0:T(8,128)(2,1)S(1)}, u32[]{:S(2)}, u32[]{:S(2)}) collective-permute-start(bf16[64,1792]{1,0:T(8,128)(2,1)S(1)} %get-tuple-element.105), channel_id=1, source_target_pairs={{0,3},{1,0},{2,1},{3,2},{4,7},{5,4},{6,5},{7,6},{8,11},{9,8},{10,9... | collective-permute-start | bytes 688136 | tf_op jit(solution)/shard_map/ppermute | solution.py:13
  50.3 10.6 %collective-permute-start.15 = (bf16[64,1792]{1,0:T(8,128)(2,1)S(1)}, bf16[64,1792]{1,0:T(8,128)(2,1)S(1)}, u32[]{:S(2)}, u32[]{:S(2)}) collective-permute-start(bf16[64,1792]{1,0:T(8,128)(2,1)S(1)} %get-tuple-element.106), channel_id=1, source_target_pairs={{0,1},{1,2},{2,3},{3,0},{4,5},{5,6},{6,7},{7,4},{8,9},{9,10},{10,1... | collective-permute-start | bytes 688136 | tf_op jit(solution)/shard_map/ppermute | solution.py:13
  58.9 8.3 %collective-permute-start.20 = (bf16[64,1792]{1,0:T(8,128)(2,1)S(1)}, bf16[64,1792]{1,0:T(8,128)(2,1)S(1)}, u32[]{:S(2)}, u32[]{:S(2)}) collective-permute-start(bf16[64,1792]{1,0:T(8,128)(2,1)S(1)} %get-tuple-element.101), channel_id=1, source_target_pairs={{0,2},{1,3},{2,0},{3,1},{4,6},{5,7},{6,4},{7,5},{8,10},{9,11},{10,... | collective-permute-start | bytes 688136 | tf_op jit(solution)/shard_map/ppermute | solution.py:13
  59.0 10.5 %collective-permute-start.19 = (bf16[64,1792]{1,0:T(8,128)(2,1)S(1)}, bf16[64,1792]{1,0:T(8,128)(2,1)S(1)}, u32[]{:S(2)}, u32[]{:S(2)}) collective-permute-start(bf16[64,1792]{1,0:T(8,128)(2,1)S(1)} %get-tuple-element.102), channel_id=1, source_target_pairs={{0,3},{1,0},{2,1},{3,2},{4,7},{5,4},{6,5},{7,6},{8,11},{9,8},{10,9... | collective-permute-start | bytes 688136 | tf_op jit(solution)/shard_map/ppermute | solution.py:13
  60.8 12.1 %collective-permute-start.18 = (bf16[64,1792]{1,0:T(8,128)(2,1)S(1)}, bf16[64,1792]{1,0:T(8,128)(2,1)S(1)}, u32[]{:S(2)}, u32[]{:S(2)}) collective-permute-start(bf16[64,1792]{1,0:T(8,128)(2,1)S(1)} %get-tuple-element.103), channel_id=1, source_target_pairs={{0,1},{1,2},{2,3},{3,0},{4,5},{5,6},{6,7},{7,4},{8,9},{9,10},{10,1... | collective-permute-start | bytes 688136 | tf_op jit(solution)/shard_map/ppermute | solution.py:13
  61.1 15.1 %collective-permute-start.23 = (bf16[64,896]{1,0:T(8,128)(2,1)S(1)}, bf16[64,896]{1,0:T(8,128)(2,1)S(1)}, u32[]{:S(2)}, u32[]{:S(2)}) collective-permute-start(bf16[64,896]{1,0:T(8,128)(2,1)S(1)} %fusion.17), channel_id=1, source_target_pairs={{0,1},{1,2},{2,3},{3,0},{4,5},{5,6},{6,7},{7,4},{8,9},{9,10},{10,1... | collective-permute-start | bytes 344072 | tf_op jit(solution)/shard_map/ppermute | solution.py:13
  62.0 15.0 %collective-permute-start.22 = (bf16[64,896]{1,0:T(8,128)(2,1)S(1)}, bf16[64,896]{1,0:T(8,128)(2,1)S(1)}, u32[]{:S(2)}, u32[]{:S(2)}) collective-permute-start(bf16[64,896]{1,0:T(8,128)(2,1)S(1)} %fusion.17), channel_id=1, source_target_pairs={{0,2},{1,3},{2,0},{3,1},{4,6},{5,7},{6,4},{7,5},{8,10},{9,11},{10,... | collective-permute-start | bytes 344072 | tf_op jit(solution)/shard_map/ppermute | solution.py:13
  67.2 9.8 %collective-permute-start.21 = (bf16[64,896]{1,0:T(8,128)(2,1)S(1)}, bf16[64,896]{1,0:T(8,128)(2,1)S(1)}, u32[]{:S(2)}, u32[]{:S(2)}) collective-permute-start(bf16[64,896]{1,0:T(8,128)(2,1)S(1)} %fusion.17), channel_id=1, source_target_pairs={{0,3},{1,0},{2,1},{3,2},{4,7},{5,4},{6,5},{7,6},{8,11},{9,8},{10,9... | collective-permute-start | bytes 344072 | tf_op jit(solution)/shard_map/ppermute | solution.py:13
  73.1 8.4 %collective-permute-start.26 = (bf16[64,896]{1,0:T(8,128)(2,1)S(1)}, bf16[64,896]{1,0:T(8,128)(2,1)S(1)}, u32[]{:S(2)}, u32[]{:S(2)}) collective-permute-start(bf16[64,896]{1,0:T(8,128)(2,1)S(1)} %fusion.16), channel_id=1, source_target_pairs={{0,1},{1,2},{2,3},{3,0},{4,5},{5,6},{6,7},{7,4},{8,9},{9,10},{10,1... | collective-permute-start | bytes 344072 | tf_op jit(solution)/shard_map/ppermute | solution.py:13
  73.4 9.1 %collective-permute-start.25 = (bf16[64,896]{1,0:T(8,128)(2,1)S(1)}, bf16[64,896]{1,0:T(8,128)(2,1)S(1)}, u32[]{:S(2)}, u32[]{:S(2)}) collective-permute-start(bf16[64,896]{1,0:T(8,128)(2,1)S(1)} %fusion.16), channel_id=1, source_target_pairs={{0,2},{1,3},{2,0},{3,1},{4,6},{5,7},{6,4},{7,5},{8,10},{9,11},{10,... | collective-permute-start | bytes 344072 | tf_op jit(solution)/shard_map/ppermute | solution.py:13
  78.6 7.7 %collective-permute-start.29 = (bf16[4,16,2048]{2,1,0:T(8,128)(2,1)S(1)}, bf16[4,16,2048]{2,1,0:T(8,128)(2,1)S(1)}, u32[]{:S(2)}, u32[]{:S(2)}) collective-permute-start(bf16[4,16,2048]{2,1,0:T(8,128)(2,1)S(1)} %get-tuple-element.98), channel_id=1, source_target_pairs={{0,128},{64,192},{128,0},{192,64},{1,129},{65,193},{129,1},{193,65... | collective-permute-start | bytes 786440 | tf_op jit(solution)/shard_map/ppermute | solution.py:13
  78.9 16.5 %collective-permute-start.28 = (bf16[4,16,2048]{2,1,0:T(8,128)(2,1)S(1)}, bf16[4,16,2048]{2,1,0:T(8,128)(2,1)S(1)}, u32[]{:S(2)}, u32[]{:S(2)}) collective-permute-start(bf16[4,16,2048]{2,1,0:T(8,128)(2,1)S(1)} %get-tuple-element.99), channel_id=1, source_target_pairs={{0,64},{64,128},{128,192},{192,0},{1,65},{65,129},{129,193},{193,1... | collective-permute-start | bytes 786440 | tf_op jit(solution)/shard_map/ppermute | solution.py:13
  81.4 14.0 %collective-permute-start.27 = (bf16[4,16,2048]{2,1,0:T(8,128)(2,1)S(1)}, bf16[4,16,2048]{2,1,0:T(8,128)(2,1)S(1)}, u32[]{:S(2)}, u32[]{:S(2)}) collective-permute-start(bf16[4,16,2048]{2,1,0:T(8,128)(2,1)S(1)} %get-tuple-element.100), channel_id=1, source_target_pairs={{0,192},{64,0},{128,64},{192,128},{1,193},{65,1},{129,65},{193,129... | collective-permute-start | bytes 786440 | tf_op jit(solution)/shard_map/ppermute | solution.py:13
  84.1 14.9 %collective-permute-start.34 = (bf16[4,16,2048]{2,1,0:T(8,128)(2,1)S(1)}, bf16[4,16,2048]{2,1,0:T(8,128)(2,1)S(1)}, u32[]{:S(2)}, u32[]{:S(2)}) collective-permute-start(bf16[4,16,2048]{2,1,0:T(8,128)(2,1)S(1)} %get-tuple-element.95), channel_id=1, source_target_pairs={{0,128},{64,192},{128,0},{192,64},{1,129},{65,193},{129,1},{193,65... | collective-permute-start | bytes 786440 | tf_op jit(solution)/shard_map/ppermute | solution.py:13
  84.9 19.8 %collective-permute-start.33 = (bf16[4,16,2048]{2,1,0:T(8,128)(2,1)S(1)}, bf16[4,16,2048]{2,1,0:T(8,128)(2,1)S(1)}, u32[]{:S(2)}, u32[]{:S(2)}) collective-permute-start(bf16[4,16,2048]{2,1,0:T(8,128)(2,1)S(1)} %get-tuple-element.96), channel_id=1, source_target_pairs={{0,64},{64,128},{128,192},{192,0},{1,65},{65,129},{129,193},{193,1... | collective-permute-start | bytes 786440 | tf_op jit(solution)/shard_map/ppermute | solution.py:13
  86.3 18.3 %collective-permute-start.32 = (bf16[4,16,2048]{2,1,0:T(8,128)(2,1)S(1)}, bf16[4,16,2048]{2,1,0:T(8,128)(2,1)S(1)}, u32[]{:S(2)}, u32[]{:S(2)}) collective-permute-start(bf16[4,16,2048]{2,1,0:T(8,128)(2,1)S(1)} %get-tuple-element.97), channel_id=1, source_target_pairs={{0,192},{64,0},{128,64},{192,128},{1,193},{65,1},{129,65},{193,129... | collective-permute-start | bytes 786440 | tf_op jit(solution)/shard_map/ppermute | solution.py:13
  95.6 9.1 %collective-permute-start.31 = (bf16[4,8,2048]{2,1,0:T(8,128)(2,1)S(1)}, bf16[4,8,2048]{2,1,0:T(8,128)(2,1)S(1)}, u32[]{:S(2)}, u32[]{:S(2)}) collective-permute-start(bf16[4,8,2048]{2,1,0:T(8,128)(2,1)S(1)} %get-tuple-element.109), channel_id=1, source_target_pairs={{0,56},{4,12},{8,0},{12,20},{16,8},{20,28},{24,16},{28,36},{32,24}... | collective-permute-start | bytes 393224 | tf_op jit(solution)/shard_map/ppermute | solution.py:21
  96.8 9.2 %collective-permute-start.30 = (bf16[4,8,2048]{2,1,0:T(8,128)(2,1)S(1)}, bf16[4,8,2048]{2,1,0:T(8,128)(2,1)S(1)}, u32[]{:S(2)}, u32[]{:S(2)}) collective-permute-start(bf16[4,8,2048]{2,1,0:T(8,128)(2,1)S(1)} %get-tuple-element.110), channel_id=1, source_target_pairs={{0,0},{4,20},{8,8},{12,28},{16,16},{20,36},{24,24},{28,44},{32,32}... | collective-permute-start | bytes 393224 | tf_op jit(solution)/shard_map/ppermute | solution.py:21
  106.2 10.8 %collective-permute-start.35 = (bf16[4,8,2048]{2,1,0:T(8,128)(2,1)S(1)}, bf16[4,8,2048]{2,1,0:T(8,128)(2,1)S(1)}, u32[]{:S(2)}, u32[]{:S(2)}) collective-permute-start(bf16[4,8,2048]{2,1,0:T(8,128)(2,1)S(1)} %get-tuple-element.107), channel_id=1, source_target_pairs={{0,48},{4,36},{8,56},{12,44},{16,0},{20,52},{24,8},{28,60},{32,16}... | collective-permute-start | bytes 393224 | tf_op jit(solution)/shard_map/ppermute | solution.py:21
  107.1 12.0 %collective-permute-start.36 = (bf16[4,8,2048]{2,1,0:T(8,128)(2,1)S(1)}, bf16[4,8,2048]{2,1,0:T(8,128)(2,1)S(1)}, u32[]{:S(2)}, u32[]{:S(2)}) collective-permute-start(bf16[4,8,2048]{2,1,0:T(8,128)(2,1)S(1)} %get-tuple-element.108), channel_id=1, source_target_pairs={{0,40},{4,28},{8,48},{12,36},{16,56},{20,44},{24,0},{28,52},{32,8}... | collective-permute-start | bytes 393224 | tf_op jit(solution)/shard_map/ppermute | solution.py:21
  (11 other events, 67.2 us)
